TPU v7x, 128 devices: a whole 4x4x4 slice. The times are simulated.
128 devices in a mesh: req: 8 (over z, core), unit: 16 (over x, y).
Axes of the slice: x: 4, y: 4, z: 4, core: 2. Of those that a mesh axis runs over, the one named last changes fastest.
Arguments:
- tokens: bfloat16 [128, 384, 1536], P('req'), may hold values from -6 to 6
- lengths: int32 [128], P('req'), may hold values from 1 to 384, 30720 in all
- gate_proj: float32 [1536, 3072], P(('req', 'unit')), may hold values from -0.15625 to 0.15625
- input_proj: float32 [1536, 3072], P(('req', 'unit')), may hold values from -0.15625 to 0.15625
- state_proj: float32 [1536, 256], P(('req', 'unit')), may hold values from -0.15625 to 0.15625
- step_proj: float32 [1536, 48], P(('req', 'unit')), may hold values from -0.15625 to 0.15625
- out_proj: float32 [1536, 3072], P(('req', 'unit')), may hold values from -0.109375 to 0.109375
- conv_weight: float32 [4, 3328], replicated, may hold values from -3 to 3
- step_bias: float32 [48], replicated, may hold values from -4 to -1
- log_rate: float32 [48], replicated, may hold values from -3.5 to 0
- skip_gain: float32 [48], replicated, may hold values from 0.5 to 3
- norm_gain: float32 [3072], replicated, may hold values from 0.1 to 1.9
Outputs:
- mixed: bfloat16 [128, 384, 1536], P(('req', 'unit'))
- final_state: float32 [128, 48, 64, 128], P(('req', 'unit'))
All inputs are finite; a program needn't handle non-finite values. No bound on the sum of `lengths` on one device may be relied on, other than what follows from the above.
Results may differ from a plain program's by a relative error of at most 0.0084.
Values may be sent and summed in bfloat16 or wider, within the bound.
No kernel may reach another device: no remote copies, remote signals or barrier semaphores. Data moves between devices by JAX's collectives and lax.ppermute only.
A program may use at most 192 MiB of HBM per device.

v0:
```python
import jax
import jax.numpy as jnp
from jax import lax
from jax.sharding import PartitionSpec as P

SPAN = 128


EPSILON = 1e-05
HIGHEST = lax.Precision.HIGHEST


def causal_conv(values, kernel):
    kernel_len = kernel.shape[0]
    seq_len = values.shape[-2]
    axis_time = values.ndim - 2
    padding = [(0, 0)] * axis_time + [(kernel_len - 1, 0), (0, 0)]
    padded = jnp.pad(values.astype(jnp.float32), padding)
    running = jnp.zeros(values.shape, jnp.float32)
    for offset in range(kernel_len):
        running = running + kernel[offset] * lax.slice_in_dim(
            padded, offset, offset + seq_len, axis=axis_time
        )
    return jax.nn.silu(running)


def ssd_scan(head_in, step_size, b_matrix, c_matrix, rate_per, skip_gain, block_len):
    req_count, seq_len, head_count, head_dim = head_in.shape
    state_dim = b_matrix.shape[-1]
    blocks = seq_len // block_len
    b_short = b_matrix.astype(jnp.bfloat16)
    c_short = c_matrix.astype(jnp.bfloat16)
    b_wide = lax.optimization_barrier(b_short).astype(jnp.float32)
    c_wide = lax.optimization_barrier(c_short).astype(jnp.float32)
    shaped_x = jnp.moveaxis(
        head_in.reshape(req_count, blocks, block_len, head_count, head_dim), 1, 0
    )
    shaped_dt = jnp.moveaxis(step_size.reshape(req_count, blocks, block_len, head_count), 1, 0)
    shaped_bs = jnp.moveaxis(b_short.reshape(req_count, blocks, block_len, state_dim), 1, 0)
    shaped_cs = jnp.moveaxis(c_short.reshape(req_count, blocks, block_len, state_dim), 1, 0)
    shaped_b = jnp.moveaxis(b_wide.reshape(req_count, blocks, block_len, state_dim), 1, 0)
    shaped_c = jnp.moveaxis(c_wide.reshape(req_count, blocks, block_len, state_dim), 1, 0)
    decays = jnp.cumsum(shaped_dt * rate_per, axis=2)
    where_lower = jnp.arange(block_len)[:, None] >= jnp.arange(block_len)[None, :]

    def advance(carried, pieces):
        piece_x, piece_dt, piece_bs, piece_cs, piece_b, piece_c, piece_log = pieces
        intersection = jnp.einsum(
            "rtn,rsn->rts", piece_cs, piece_bs, preferred_element_type=jnp.float32
        )
        log_gaps = piece_log[:, :, None, :] - piece_log[:, None, :, :]
        factor = jnp.exp(jnp.where(where_lower[None, :, :, None], log_gaps, -jnp.inf))
        mixing = intersection[..., None] * factor * piece_dt[:, None, :, :]
        inside = jnp.einsum("rtsh,rshp->rthp", mixing, piece_x, precision=HIGHEST)
        earlier = (
            jnp.einsum("rtn,rhpn->rthp", piece_c, carried, precision=HIGHEST)
            * jnp.exp(piece_log)[..., None]
        )
        ending = piece_log[:, -1, :]
        weight_in = jnp.exp(ending[:, None, :] - piece_log) * piece_dt
        fresh_state = jnp.einsum(
            "rsh,rshp,rsn->rhpn", weight_in, piece_x, piece_b, precision=HIGHEST
        )
        carried = jnp.exp(ending)[:, :, None, None] * carried + fresh_state
        return (carried, inside + earlier)

    start_state = jnp.zeros((req_count, head_count, head_dim, state_dim), jnp.float32)
    final_state, outputs = lax.scan(
        advance,
        start_state,
        (shaped_x, shaped_dt, shaped_bs, shaped_cs, shaped_b, shaped_c, decays),
    )
    scanned = jnp.moveaxis(outputs, 0, 1).reshape(req_count, seq_len, head_count, head_dim)
    return (scanned + skip_gain[:, None] * head_in, final_state)


def body(
    tokens,
    lengths,
    gate_proj,
    input_proj,
    state_proj,
    step_proj,
    out_proj,
    conv_weight,
    step_bias,
    log_rate,
    skip_gain,
    norm_gain,
):
    unit_count = lax.axis_size("unit")
    unit_id = lax.axis_index("unit")
    group_reqs, seq_len, model_dim = tokens.shape
    own_reqs = group_reqs // unit_count
    inner_dim = gate_proj.shape[1]
    head_count = log_rate.shape[0]
    head_dim = inner_dim // head_count
    state_dim = state_proj.shape[1] // 2
    flat_tokens = tokens.reshape(group_reqs * seq_len, model_dim)
    rate_per = -jnp.exp(log_rate)
    position = jnp.arange(seq_len)
    moved = (
        lax.all_to_all(
            gate_proj.astype(jnp.bfloat16), "unit", split_axis=1, concat_axis=0, tiled=True
        ),
        lax.all_to_all(
            input_proj.astype(jnp.bfloat16), "unit", split_axis=1, concat_axis=0, tiled=True
        ),
        lax.all_to_all(
            state_proj.astype(jnp.bfloat16), "unit", split_axis=1, concat_axis=0, tiled=True
        ),
        lax.all_to_all(
            step_proj.astype(jnp.bfloat16), "unit", split_axis=1, concat_axis=0, tiled=True
        ),
        lax.all_to_all(
            out_proj.astype(jnp.bfloat16), "unit", split_axis=1, concat_axis=0, tiled=True
        ),
    )
    pieces = (
        lax.all_gather(moved[0], "req", axis=0, tiled=True),
        lax.all_gather(moved[1], "req", axis=0, tiled=True),
        lax.all_gather(moved[2], "req", axis=0, tiled=True),
        lax.all_gather(moved[3], "req", axis=0, tiled=True),
        lax.all_gather(moved[4], "req", axis=0, tiled=True),
    )
    projected = tuple(
        (
            jnp.dot(flat_tokens, weight_piece, preferred_element_type=jnp.float32)
            for weight_piece in pieces[:4]
        )
    )
    out_piece = pieces[4]
    gate_sum, input_sum, state_sum, step_sum, out_block = projected + (out_piece,)

    def as_cols(summed):
        return summed.astype(jnp.bfloat16).reshape(group_reqs, seq_len, summed.shape[1])

    gate_cols = as_cols(gate_sum)
    input_cols = as_cols(input_sum)
    state_cols = as_cols(state_sum)
    step_cols = as_cols(step_sum)
    own_len = lax.dynamic_slice_in_dim(lengths, unit_id * own_reqs, own_reqs, 0)
    own_live = (position[None, :] < own_len[:, None]).astype(jnp.float32)
    gate_all, input_all, state_all, step_all = (
        lax.all_to_all(gate_cols, "unit", split_axis=0, concat_axis=2, tiled=True),
        lax.all_to_all(input_cols, "unit", split_axis=0, concat_axis=2, tiled=True),
        lax.all_to_all(state_cols, "unit", split_axis=0, concat_axis=2, tiled=True),
        lax.all_to_all(step_cols, "unit", split_axis=0, concat_axis=2, tiled=True),
    )
    x_conv = causal_conv(input_all, conv_weight[:, :inner_dim])
    s_conv = causal_conv(state_all, conv_weight[:, inner_dim:])
    step_size = jax.nn.softplus(step_all.astype(jnp.float32) + step_bias) * own_live[..., None]
    scanned, final_state = ssd_scan(
        x_conv.reshape(own_reqs, seq_len, head_count, head_dim),
        step_size,
        s_conv[..., :state_dim],
        s_conv[..., state_dim:],
        rate_per,
        skip_gain,
        SPAN,
    )
    gated = scanned.reshape(own_reqs, seq_len, inner_dim) * jax.nn.silu(
        gate_all.astype(jnp.float32)
    )
    spread = jnp.mean(gated * gated, axis=-1, keepdims=True)
    normed = (gated * lax.rsqrt(spread + EPSILON) * norm_gain).astype(jnp.bfloat16)
    returned = lax.all_to_all(normed, "unit", split_axis=2, concat_axis=0, tiled=True)
    mixed = lax.psum_scatter(
        jnp.einsum("rse,de->rsd", returned, out_block, preferred_element_type=jnp.float32),
        "unit",
        scatter_dimension=0,
        tiled=True,
    )
    mixed_out = (mixed * own_live[..., None]).astype(jnp.bfloat16)
    return (mixed_out, final_state)


def solution(mesh):
    placed = (
        P("req", None, None),
        P("req"),
        P(("req", "unit"), None),
        P(("req", "unit"), None),
        P(("req", "unit"), None),
        P(("req", "unit"), None),
        P(("req", "unit"), None),
        P(),
        P(),
        P(),
        P(),
        P(),
    )
    return jax.shard_map(
        body,
        mesh=mesh,
        in_specs=placed,
        out_specs=(P(("req", "unit"), None, None), P(("req", "unit"), None, None, None)),
        check_vma=False,
    )
```

profile of v0, /device:TPU:1, one launch (start us, length us, event | category | flops | bytes accessed | tf_op | source)
XLA Modules:
  0.0 799.3 jit_solution(10832921844835051563)
XLA Ops:
  8.6 7.6 all-to-all-start
  34.9 14.1 %all-gather = bf16[8,192,3]{1,2,0:T(4,128)(2,1)S(1)} all-gather(bf16[1,192,3]{1,2,0:T(4,128)(2,1)S(1)} %reshape.481), channel_id=1, replica_groups=mesh['req'=8,'unit'=16] {'req'}, dimensions={0}, use_global_device_ids=true | all-gather | bytes 10368 | tf_op jit(solution)/shard_map/all_gather | solution.py:123
  49.1 12.0 %convolution_convert_fusion.3 = bf16[6144,3]{0,1:T(4,128)(2,1)} fusion(bf16[6144,1536]{1,0:T(8,128)(2,1)} %bitcast.188, bf16[1536,3]{0,1:T(4,128)(2,1)S(1)} %reshape.482), kind=kOutput, calls=%fused_computation.50 | convolution fusion | flops 56641536 | bytes 18920448 | tf_op jit(solution)/shard_map/dot_general | solution.py:128
  68.2 13.0 %all-gather.1 = bf16[8,192,16]{1,2,0:T(8,128)(2,1)S(1)} all-gather(bf16[1,192,16]{1,2,0:T(8,128)(2,1)S(1)} %reshape.483), channel_id=1, replica_groups=mesh['req'=8,'unit'=16] {'req'}, dimensions={0}, use_global_device_ids=true | all-gather | bytes 55296 | tf_op jit(solution)/shard_map/all_gather | solution.py:122
  81.4 11.3 %convolution_convert_fusion.2 = bf16[6144,16]{0,1:T(8,128)(2,1)S(1)} fusion(bf16[6144,1536]{1,0:T(8,128)(2,1)} %bitcast.189, bf16[1536,16]{0,1:T(8,128)(2,1)S(1)} %reshape.484), kind=kOutput, calls=%fused_computation.49 | convolution fusion | flops 302088192 | bytes 19120128 | tf_op jit(solution)/shard_map/dot_general | solution.py:128
  110.7 14.9 %all_gather.16 = bf16[1536,192]{1,0:T(8,128)(2,1)S(1)} all-gather(bf16[192,192]{1,0:T(8,128)(2,1)S(1)} %all_to_all.119), channel_id=1, replica_groups=mesh['req'=8,'unit'=16] {'req'}, dimensions={0}, use_global_device_ids=true | all-gather | bytes 663552 | tf_op jit(solution)/shard_map/all_gather | solution.py:121
  132.6 10.6 %convolution_convert_fusion.1 = bf16[6144,192]{0,1:T(8,128)(2,1)S(1)} fusion(bf16[6144,1536]{1,0:T(8,128)(2,1)} %bitcast.190, bf16[1536,192]{1,0:T(8,128)(2,1)S(1)} %all_gather.16), kind=kOutput, calls=%fused_computation.45 | convolution fusion | flops 3625058304 | bytes 21823488 | tf_op jit(solution)/shard_map/dot_general | solution.py:128
  152.2 14.2 %all_gather.18 = bf16[1536,192]{1,0:T(8,128)(2,1)S(1)} all-gather(bf16[192,192]{1,0:T(8,128)(2,1)S(1)} %all_to_all.129), channel_id=1, replica_groups=mesh['req'=8,'unit'=16] {'req'}, dimensions={0}, use_global_device_ids=true | all-gather | bytes 663552 | tf_op jit(solution)/shard_map/all_gather | solution.py:120
  166.4 10.6 %convolution_convert_fusion = bf16[6144,192]{0,1:T(8,128)(2,1)S(1)} fusion(bf16[6144,1536]{1,0:T(8,128)(2,1)} %bitcast.191, bf16[1536,192]{1,0:T(8,128)(2,1)S(1)} %all_gather.18), kind=kOutput, calls=%fused_computation.44 | convolution fusion | flops 3625058304 | bytes 21823488 | tf_op jit(solution)/shard_map/dot_general | solution.py:128
  199.8 8.0 transpose_reshape_reshape.3
  207.8 173.0 %while.13 = (s32[]{:T(128)}, f32[1,48,64,128]{3,2,1,0:T(8,128)S(1)}, f32[3,1,128,48,64]{2,0,4,3,1:T(4,128)}, f32[3,1,128,48]{2,3,1,0:T(8,128)S(1)}, f32[3,1,128,...) while((s32[]{:T(128)}, ...), condition=%wide.region_2.3_spmd.clone, body=%wide.region_1.2_spmd.clone.sunk | while | flops 1822060544 | bytes 19582040 | solution.py:68
  223.8 39.1 %dynamic_update_slice.6 = f32[3,1,128,48,64]{2,0,4,3,1:T(4,128)} dynamic-update-slice(f32[3,1,128,48,64]{2,0,4,3,1:T(4,128)} %get-tuple-element.262, f32[1,1,128,48,64]{2,0,4,3,1:T(1,128)} %bitcast.194, s32[]{:T(128)} %get-tuple-element.260, s32[]{:T(128)} %constant.43.clone.1..sunk, s32[]{:T(128)} %constant.43.clone.1..sunk, s32[]{:T(128)} %constant.43.clone.1..sunk, s32[]{:T(128)} %constant.43.clone.1..sunk) | dynamic-update-slice | bytes 3145732 | tf_op jit(solution)/shard_map/while/body/jit(dynamic_update_index_in_dim)/dynamic_update_slice | solution.py:68
  274.1 7.4 bitcast_add_fusion.5
  281.5 39.1 %dynamic_update_slice.6 = f32[3,1,128,48,64]{2,0,4,3,1:T(4,128)} dynamic-update-slice(f32[3,1,128,48,64]{2,0,4,3,1:T(4,128)} %get-tuple-element.262, f32[1,1,128,48,64]{2,0,4,3,1:T(1,128)} %bitcast.194, s32[]{:T(128)} %get-tuple-element.260, s32[]{:T(128)} %constant.43.clone.1..sunk, s32[]{:T(128)} %constant.43.clone.1..sunk, s32[]{:T(128)} %constant.43.clone.1..sunk, s32[]{:T(128)} %constant.43.clone.1..sunk) | dynamic-update-slice | bytes 3145732 | tf_op jit(solution)/shard_map/while/body/jit(dynamic_update_index_in_dim)/dynamic_update_slice | solution.py:68
  331.8 7.4 bitcast_add_fusion.5
  339.2 39.1 %dynamic_update_slice.6 = f32[3,1,128,48,64]{2,0,4,3,1:T(4,128)} dynamic-update-slice(f32[3,1,128,48,64]{2,0,4,3,1:T(4,128)} %get-tuple-element.262, f32[1,1,128,48,64]{2,0,4,3,1:T(1,128)} %bitcast.194, s32[]{:T(128)} %get-tuple-element.260, s32[]{:T(128)} %constant.43.clone.1..sunk, s32[]{:T(128)} %constant.43.clone.1..sunk, s32[]{:T(128)} %constant.43.clone.1..sunk, s32[]{:T(128)} %constant.43.clone.1..sunk) | dynamic-update-slice | bytes 3145732 | tf_op jit(solution)/shard_map/while/body/jit(dynamic_update_index_in_dim)/dynamic_update_slice | solution.py:68
  380.8 9.1 %reshape_transpose.3 = f32[1,384,3072]{1,2,0:T(8,128)} reshape(f32[3,1,128,48,64]{2,0,4,3,1:T(4,128)} %get-tuple-element.60) | data formatting | bytes 9437184 | tf_op jit(solution)/shard_map/reshape;transpose | solution.py:73
  396.7 15.3 %multiply_reduce_fusion = (f32[384]{0:T(512)S(1)}, f32[1,384,3072]{1,2,0:T(8,128)S(1)}) fusion(bf16[16,384,192]{1,2,0:T(8,128)(2,1)} %all-to-all-done.7, f32[1,384,3072]{1,2,0:T(8,128)} %reshape_transpose.3, f32[3072]{0:T(1024)S(1)} %mul.288, f32[1,384,3072]{1,2,0:T(8,128)} %bitcast.193, f32[3072]{0:T(1024)S(1)} %bitcast.216, f32[3072]{0:T(1024)S(1)} %bitcast.218, ...), kind=kLoop, calls=%fused_computation.64 | loop fusion | flops 24772224 | bytes 16578048 | tf_op jit(solution)/shard_map/reduce_sum | solution.py:165
  412.5 44.7 %copy.164 = bf16[1,384,3072]{1,0,2:T(2,128)(2,1)} copy(bf16[1,384,3072]{1,2,0:T(8,128)(2,1)S(1)} %multiply_convert_fusion) | data formatting | bytes 4718592 | tf_op jit(solution)/shard_map/convert_element_type | solution.py:166
  457.7 50.8 %reduce.4 = bf16[3072,384]{1,0:T(8,128)(2,1)S(1)} reduce(bf16[3072,1,384]{2,1,0:T(2,128)(2,1)} %bitcast.195, bf16[]{:T(256)} %broadcast.240), dimensions={1}, to_apply=%bitcast.159.reduce_sub_computation | reduce | bytes 4718594
  517.6 16.9 %all_gather.19 = bf16[1536,192]{1,0:T(8,128)(2,1)S(1)} all-gather(bf16[192,192]{1,0:T(8,128)(2,1)S(1)} %all_to_all.138), channel_id=1, replica_groups=mesh['req'=8,'unit'=16] {'req'}, dimensions={0}, use_global_device_ids=true | all-gather | bytes 663552 | tf_op jit(solution)/shard_map/all_gather | solution.py:124
  534.5 10.7 %all-to-all-done.8 = bf16[16,2,36864]{2,1,0:T(2,128)(2,1)S(1)} async-done(((bf16[16,2,36864]{2,1,0:T(2,128)(2,1)}), bf16[16,2,36864]{2,1,0:T(2,128)(2,1)S(1)}, u32[]{:S(2)}, u32[]{:S(2)}) %all-to-all-start.8) | async-done | bytes 2359328 | tf_op jit(solution)/shard_map/all_to_all | solution.py:167
  554.9 14.9 %fusion.50 = f32[16,384,1536]{2,1,0:T(8,128)} fusion(bf16[16,384,192]{1,2,0:T(8,128)(2,1)S(1)} %bitcast.197, bf16[1536,192]{1,0:T(8,128)(2,1)S(1)} %all_gather.19), kind=kOutput, calls=%fused_computation.70 | convolution fusion | flops 3623878656 | bytes 40697856 | tf_op jit(solution)/shard_map/rse,de->rsd/dot_general | solution.py:169
  570.4 219.0 %reduce-scatter.4.cloned.1.call-done = f32[1,384,1536]{2,1,0:T(8,128)} async-done(((f32[16,384,1536]{2,1,0:T(8,128)}), f32[1,384,1536]{2,1,0:T(8,128)}) %reduce-scatter.4.cloned.1.call-update) | async-done | bytes 2359312
  (123 shorter events, 154.7 us)
Async XLA Ops:
  8.6 19.6 %all-to-all-start = ((bf16[12,16,3]{0,2,1:T(4,128)(2,1)}), bf16[12,16,3]{0,2,1:T(4,128)(2,1)S(1)}, u32[]{:S(2)}, u32[]{:S(2)}) async-start(bf16[12,16,3]{0,2,1:T(4,128)(2,1)} %all_to_all.111), calls=%async_computation | async-start | bytes 32768 | tf_op jit(solution)/shard_map/all_to_all | solution.py:112
  28.2 32.9 %all-to-all-start.4 = ((bf16[12,16,16]{0,2,1:T(8,128)(2,1)}), bf16[12,16,16]{0,2,1:T(8,128)(2,1)S(1)}, u32[]{:S(2)}, u32[]{:S(2)}) async-start(bf16[12,16,16]{0,2,1:T(8,128)(2,1)} %bitcast.17), calls=%async_computation.4 | async-start | bytes 131072 | tf_op jit(solution)/shard_map/all_to_all | solution.py:109
  61.1 32.3 %all-to-all-start.1 = ((bf16[16,384,3]{1,2,0:T(4,128)(2,1)}), bf16[16,384,3]{1,2,0:T(4,128)(2,1)S(1)}, u32[]{:S(2)}, u32[]{:S(2)}) async-start(bf16[16,384,3]{1,2,0:T(4,128)(2,1)} %bitcast.2), calls=%async_computation.1 | async-start | bytes 98304 | tf_op jit(solution)/shard_map/all_to_all | solution.py:148
  81.4 19.1 %copy-start.3 = (f32[48]{0:T(128)S(1)}, f32[48]{0:T(128)}, u32[]{:S(2)}) copy-start(f32[48]{0:T(128)} %param.22) | copy-start | bytes 580
  93.4 13.7 %all-to-all-start.2 = ((bf16[12,16,192]{2,0,1:T(8,128)(2,1)}), bf16[12,16,192]{2,0,1:T(8,128)(2,1)S(1)}, u32[]{:S(2)}, u32[]{:S(2)}) async-start(bf16[12,16,192]{2,0,1:T(8,128)(2,1)} %copy.121), calls=%async_computation.2 | async-start | bytes 262144 | tf_op jit(solution)/shard_map/all_to_all | solution.py:106
  107.1 18.5 %all-to-all-start.6 = ((bf16[12,16,192]{2,0,1:T(8,128)(2,1)}), bf16[12,16,192]{2,0,1:T(8,128)(2,1)S(1)}, u32[]{:S(2)}, u32[]{:S(2)}) async-start(bf16[12,16,192]{2,0,1:T(8,128)(2,1)} %copy.139), calls=%async_computation.6 | async-start | bytes 262144 | tf_op jit(solution)/shard_map/all_to_all | solution.py:103
  125.6 19.4 %all-to-all-start.5 = ((bf16[16,384,16]{1,2,0:T(8,128)(2,1)}), bf16[16,384,16]{1,2,0:T(8,128)(2,1)S(1)}, u32[]{:S(2)}, u32[]{:S(2)}) async-start(bf16[16,384,16]{1,2,0:T(8,128)(2,1)} %bitcast.158), calls=%async_computation.5 | async-start | bytes 393216 | tf_op jit(solution)/shard_map/all_to_all | solution.py:147
  145.1 38.7 %all-to-all-start.3 = ((bf16[16,384,192]{1,2,0:T(8,128)(2,1)}), bf16[16,384,192]{1,2,0:T(8,128)(2,1)}, u32[]{:S(2)}, u32[]{:S(2)}) async-start(bf16[16,384,192]{1,2,0:T(8,128)(2,1)} %bitcast.199), calls=%async_computation.3 | async-start | bytes 4718592 | tf_op jit(solution)/shard_map/all_to_all | solution.py:146
  183.8 206.1 %all-to-all-start.7 = ((bf16[16,384,192]{1,2,0:T(8,128)(2,1)}), bf16[16,384,192]{1,2,0:T(8,128)(2,1)}, u32[]{:S(2)}, u32[]{:S(2)}) async-start(bf16[16,384,192]{1,2,0:T(8,128)(2,1)} %bitcast.198), calls=%async_computation.7 | async-start | bytes 4718592 | tf_op jit(solution)/shard_map/all_to_all | solution.py:145
  190.8 2.1 copy-start.1
  380.8 9.1 %copy-start = (f32[1,48,64,128]{3,2,1,0:T(8,128)}, f32[1,48,64,128]{3,2,1,0:T(8,128)S(1)}, u32[]{:S(2)}) copy-start(f32[1,48,64,128]{3,2,1,0:T(8,128)S(1)} %get-tuple-element.59) | copy-start | bytes 4718596
  389.9 120.8 %all-to-all-start.9 = ((bf16[12,16,192]{2,0,1:T(8,128)(2,1)}), bf16[12,16,192]{2,0,1:T(8,128)(2,1)S(1)}, u32[]{:S(2)}, u32[]{:S(2)}) async-start(bf16[12,16,192]{2,0,1:T(8,128)(2,1)} %copy.142), calls=%async_computation.9 | async-start | bytes 262144 | tf_op jit(solution)/shard_map/all_to_all | solution.py:115
  396.7 15.3 %copy-start.2 = (f32[3072]{0:T(1024)S(1)}, f32[3072]{0:T(1024)}, u32[]{:S(2)}) copy-start(f32[3072]{0:T(1024)} %param.25) | copy-start | bytes 36868
  510.7 34.5 %all-to-all-start.8 = ((bf16[16,2,36864]{2,1,0:T(2,128)(2,1)}), bf16[16,2,36864]{2,1,0:T(2,128)(2,1)S(1)}, u32[]{:S(2)}, u32[]{:S(2)}) async-start(bf16[16,2,36864]{2,1,0:T(2,128)(2,1)} %reshape.500), calls=%async_computation.8 | async-start | bytes 4718592 | tf_op jit(solution)/shard_map/all_to_all | solution.py:167
  517.5 271.9 %reduce-scatter.4.cloned.1.call-start = ((), (), s32[]{:S(2)}) async-start(), calls=%async_computation.11 | async-start | bytes 40108032
Sparse Core Ops, SparseCore 0:
  569.9 219.3 reduce-scatter.3
where the time goes:
time: 813 us; the launch traced here: 799 us
  waiting for transfers between devices  237 us (29%)
  local copies, waits for them, and re-layouts  226 us (28%)
  matrix products  97.7 us (12%)
  other arithmetic  86.5 us (11%)
  blocking collectives  73.2 us (9%)
  starting transfers between devices  64.1 us (8%)
  between operations  14.6 us (2%)
    unnamed x2, waiting for transfers between devices  219 us
    dynamic_update_slice x3, local copies, waits for them, and re-layouts, ssd_scan(): lax.scan(advance, start_state, (shaped_x, shaped_dt, shaped_bs, shaped_cs...  117 us
    unnamed x2, other arithmetic  50.8 us
    convert_element_type x1, local copies, waits for them, and re-layouts, body(): (gated * lax.rsqrt(spread + EPSILON) * norm_gain).astype(jnp.bfloat16)  44.7 us
    dot_general x4, matrix products, body(): jnp.dot(flat_tokens, weight_piece, preferred_element_type=jnp.float32)  44.5 us
    dot_general x3, matrix products, advance(): inside = jnp.einsum('rtsh,rshp->rthp', mixing, piece_x, precision=HIGHEST)  22.1 us
    all_gather x1, blocking collectives, body(): lax.all_gather(moved[4], 'req', axis=0, tiled=True)  16.9 us
  transfers between devices with their start and end apart: 11, of which 4 were waited for; matrix products, arithmetic and copies ran while one was open for 47% of the time, Pallas kernels for 0%

commit v1 on v0

v1 whole, which is shorter than its diff:
```python
import jax
import jax.numpy as jnp
from jax import lax
from jax.experimental import pallas as pl
from jax.experimental.pallas import tpu as pltpu
from jax.sharding import PartitionSpec as P

SPAN = 128
LANES = 128
HEADS_STEP = 8
EPSILON = 1e-05
BF = jnp.bfloat16
F32 = jnp.float32


def silu(v):
    h = 0.5 * v
    return h + h * jnp.tanh(h)


def causal_conv(values, taps):
    rows = lax.broadcasted_iota(jnp.int32, values.shape, 0)
    count = taps.shape[0]
    total = values * taps[count - 1 : count]
    for back in range(1, count):
        moved = jnp.where(rows >= back, pltpu.roll(values, back, 0), 0.0)
        total = total + moved * taps[count - 1 - back : count - back]
    return silu(total)


def scan_kernel(
    len_ref,
    input_ref,
    gate_ref,
    side_ref,
    taps_ref,
    side_taps_ref,
    bias_ref,
    log_rate_ref,
    skip_ref,
    gain_ref,
    gated_ref,
    state_ref,
    scale_ref,
    decay_col,
    delta_col,
    decay_row,
    b_scr,
    c_scr,
    cb_scr,
    square_scr,
):
    step = pl.program_id(0)
    seq = input_ref.shape[0]
    state_dim = side_taps_ref.shape[1] // 2
    groups = decay_col.shape[0]
    blocks = seq // SPAN
    inner = groups * input_ref.shape[1]
    position = lax.broadcasted_iota(jnp.int32, (seq, LANES), 0)
    live = (position < len_ref[0]).astype(F32)

    @pl.when(step == 0)
    def _():
        side = side_ref[...].astype(F32)
        conv = causal_conv(side[:, : 2 * state_dim], side_taps_ref[...])
        b_short = conv[:, :state_dim].astype(BF)
        c_short = conv[:, state_dim:].astype(BF)
        b_scr[...] = b_short
        c_scr[...] = c_short
        for block in range(blocks):
            at = slice(block * SPAN, (block + 1) * SPAN)
            cb_scr[block] = lax.dot_general(
                c_short[at], b_short[at], (((1,), (1,)), ((), ())), preferred_element_type=F32
            )
        raw = side[:, 2 * state_dim :] + bias_ref[...]
        delta = (jnp.maximum(raw, 0.0) + jnp.log1p(jnp.exp(-jnp.abs(raw)))) * live
        total = delta * -jnp.exp(log_rate_ref[...])
        within = position % SPAN
        reach = 1
        while reach < SPAN:
            total = total + jnp.where(within >= reach, pltpu.roll(total, reach, 0), 0.0)
            reach *= 2
        turned = jnp.transpose(total)
        for group in range(groups):
            at = slice(group * HEADS_STEP, (group + 1) * HEADS_STEP)
            decay_col[group] = total[:, at]
            delta_col[group] = delta[:, at]
            decay_row[group] = turned[at]
        square_scr[...] = jnp.zeros_like(square_scr)

    decays = decay_col[step]
    deltas = delta_col[step]
    rows_of = decay_row[step]
    lower = lax.broadcasted_iota(jnp.int32, (SPAN, SPAN), 0) >= lax.broadcasted_iota(
        jnp.int32, (SPAN, SPAN), 1
    )
    left = lax.broadcasted_iota(jnp.int32, (SPAN, LANES), 1) < LANES // 2
    top = lax.broadcasted_iota(jnp.int32, (LANES, state_dim), 0) < LANES // 2
    for pair in range(HEADS_STEP // 2):
        cols = slice(pair * LANES, (pair + 1) * LANES)
        one, two = 2 * pair, 2 * pair + 1
        x_conv = causal_conv(input_ref[:, cols].astype(F32), taps_ref[:, cols])
        gate = silu(gate_ref[:, cols].astype(F32))
        skip = skip_ref[:, cols]
        gain = gain_ref[:, cols]
        state = jnp.zeros((LANES, state_dim), F32)
        for block in range(blocks):
            at = slice(block * SPAN, (block + 1) * SPAN)
            x_here = x_conv[at]
            cb = cb_scr[block]
            d_one, d_two = decays[at, one : one + 1], decays[at, two : two + 1]
            mix_one = cb * jnp.exp(
                jnp.where(lower, d_one - rows_of[one : one + 1, at], -jnp.inf)
            )
            mix_two = cb * jnp.exp(
                jnp.where(lower, d_two - rows_of[two : two + 1, at], -jnp.inf)
            )
            decay = jnp.where(left, d_one, d_two)
            x_step = x_here * jnp.where(
                left, deltas[at, one : one + 1], deltas[at, two : two + 1]
            )
            short = x_step.astype(BF)
            zero = jnp.zeros_like(short)
            mixing = jnp.concatenate([mix_one.astype(BF), mix_two.astype(BF)], axis=1)
            spread = jnp.concatenate(
                [jnp.where(left, short, zero), jnp.where(left, zero, short)], axis=0
            )
            out = jnp.dot(mixing, spread, preferred_element_type=F32)
            if block:
                out = out + jnp.exp(decay) * lax.dot_general(
                    c_scr[at],
                    state.astype(BF),
                    (((1,), (1,)), ((), ())),
                    preferred_element_type=F32,
                )
            ending = decay[SPAN - 1 : SPAN]
            weighted = (x_step * jnp.exp(ending - decay)).astype(BF)
            fresh = lax.dot_general(
                weighted, b_scr[at], (((0,), (0,)), ((), ())), preferred_element_type=F32
            )
            if block:
                fade = jnp.where(
                    top,
                    jnp.exp(d_one[SPAN - 1 : SPAN]),
                    jnp.exp(d_two[SPAN - 1 : SPAN]),
                )
                fresh = fade * state + fresh
            state = fresh
            gated = (out + skip * x_here) * gate[at]
            square_scr[at, :] += gated * gated
            gated_ref[at, cols] = (gated * gain).astype(BF)
        state_ref[cols, :] = state

    @pl.when(step == groups - 1)
    def _():
        mean = jnp.sum(square_scr[...], axis=1, keepdims=True) / inner
        scale_ref[...] = lax.rsqrt(mean + EPSILON) * live


def scan_gate(length, inputs, gate, side, taps, side_taps, bias, log_rate, skip, gain):
    seq, inner = inputs.shape
    width = side_taps.shape[1]
    state_dim = width // 2
    cols = HEADS_STEP * LANES // 2
    groups = inner // cols
    whole = lambda i: (0, 0)
    part = lambda i: (0, i)
    return pl.pallas_call(
        scan_kernel,
        grid=(groups,),
        in_specs=[
            pl.BlockSpec(memory_space=pltpu.SMEM),
            pl.BlockSpec((seq, cols), part),
            pl.BlockSpec((seq, cols), part),
            pl.BlockSpec((seq, width + LANES), whole),
            pl.BlockSpec((taps.shape[0], cols), part),
            pl.BlockSpec((taps.shape[0], width), whole),
            pl.BlockSpec((1, LANES), whole),
            pl.BlockSpec((1, LANES), whole),
            pl.BlockSpec((1, cols), part),
            pl.BlockSpec((1, cols), part),
        ],
        out_specs=[
            pl.BlockSpec((seq, cols), part),
            pl.BlockSpec((cols, state_dim), lambda i: (i, 0)),
            pl.BlockSpec((seq, LANES), whole),
        ],
        out_shape=[
            jax.ShapeDtypeStruct((seq, inner), BF),
            jax.ShapeDtypeStruct((inner, state_dim), F32),
            jax.ShapeDtypeStruct((seq, LANES), F32),
        ],
        scratch_shapes=[
            pltpu.VMEM((groups, seq, HEADS_STEP), F32),
            pltpu.VMEM((groups, seq, HEADS_STEP), F32),
            pltpu.VMEM((groups, HEADS_STEP, seq), F32),
            pltpu.VMEM((seq, state_dim), BF),
            pltpu.VMEM((seq, state_dim), BF),
            pltpu.VMEM((seq // SPAN, SPAN, SPAN), F32),
            pltpu.VMEM((seq, LANES), F32),
        ],
        compiler_params=pltpu.CompilerParams(
            dimension_semantics=("arbitrary",), vmem_limit_bytes=40 << 20
        ),
        cost_estimate=pl.CostEstimate(
            flops=2 * inner * seq * 640, transcendentals=inner * seq * 6, bytes_accessed=9 << 20
        ),
        name="scan_gate",
    )(length, inputs, gate, side, taps, side_taps, bias, log_rate, skip, gain)


def body(
    tokens,
    lengths,
    gate_proj,
    input_proj,
    state_proj,
    step_proj,
    out_proj,
    conv_weight,
    step_bias,
    log_rate,
    skip_gain,
    norm_gain,
):
    unit_id = lax.axis_index("unit")
    group_reqs, seq_len, model_dim = tokens.shape
    inner_dim = gate_proj.shape[1]
    head_count = log_rate.shape[0]
    head_dim = inner_dim // head_count
    state_dim = state_proj.shape[1] // 2
    everyone = ("req", "unit")

    side_proj = jnp.concatenate([state_proj, step_proj], axis=1)
    spare = LANES - head_count
    side_proj = jnp.pad(side_proj, ((0, 0), (0, spare)))
    first = jnp.concatenate([side_proj.astype(BF), input_proj.astype(BF)], axis=1)
    first = lax.all_gather(first, everyone, axis=0, tiled=True)
    second = lax.all_gather(gate_proj.astype(BF), everyone, axis=0, tiled=True)
    third = lax.all_gather(out_proj.astype(BF), everyone, axis=0, tiled=True)

    own = lax.dynamic_index_in_dim(tokens, unit_id, 0, keepdims=False)
    length = lax.dynamic_slice_in_dim(lengths, unit_id, 1, 0)
    width = side_proj.shape[1]
    projected = jnp.dot(own, first, preferred_element_type=F32).astype(BF)
    side, inputs = projected[:, :width], projected[:, width:]
    gate = jnp.dot(own, second, preferred_element_type=F32).astype(BF)
    gated, state, scale = scan_gate(
        length,
        inputs,
        gate,
        side,
        conv_weight[:, :inner_dim],
        conv_weight[:, inner_dim:],
        jnp.pad(step_bias, (0, spare))[None],
        jnp.pad(log_rate, (0, spare))[None],
        jnp.repeat(skip_gain, head_dim)[None],
        norm_gain[None],
    )
    mixed = lax.dot_general(gated, third, (((1,), (1,)), ((), ())), preferred_element_type=F32)
    mixed = (mixed * scale[:, :1]).astype(BF)
    return (mixed[None], state.reshape(1, head_count, head_dim, state_dim))


def solution(mesh):
    placed = (
        P("req", None, None),
        P("req"),
        P(("req", "unit"), None),
        P(("req", "unit"), None),
        P(("req", "unit"), None),
        P(("req", "unit"), None),
        P(("req", "unit"), None),
        P(),
        P(),
        P(),
        P(),
        P(),
    )
    return jax.shard_map(
        body,
        mesh=mesh,
        in_specs=placed,
        out_specs=(P(("req", "unit"), None, None), P(("req", "unit"), None, None, None)),
        check_vma=False,
    )
```

time: 813 us -> 299 us (0.37); the launches traced: 799 us -> 297 us
  local copies, waits for them, and re-layouts: 226 us -> 49.5 us
  other arithmetic: 86.5 us -> 6.18 us
  matrix products: 97.7 us -> 21.7 us
  blocking collectives: 73.2 us -> 0 us
  starting transfers between devices: 64.1 us -> 0.12 us
  waiting for transfers between devices: 237 us -> 190 us
  Pallas kernels: 0 us -> 15.7 us
    unnamed x2 -> x3, waiting for transfers between devices: 219 us -> 0.05 us
    all_gather x0 -> x3, waiting for transfers between devices: none -> 190 us  [the longest x1 70.7 us: body(): second = lax.all_gather(gate_proj.astype(BF), everyone, axis=0, tiled=True)]
    dynamic_update_slice x3 -> x0, local copies, waits for them, and re-layouts: 117 us -> none  [ssd_scan(): lax.scan(advance, start_state, (shaped_x, shaped_dt, shaped_bs, shaped_cs...]
    dot_general x17 -> x3, matrix products: 97.7 us -> 21.7 us  [the longest x1 8.94 us: body(): projected = jnp.dot(own, first, preferred_element_type=F32).astype(BF)]
    all_gather x5 -> x0, blocking collectives: 73.2 us -> none  [the longest x1 16.9 us: body(): lax.all_gather(moved[4], 'req', axis=0, tiled=True)]
    all_to_all x10 -> x0, starting transfers between devices: 64.1 us -> none  [the longest x1 7.58 us: body(): lax.all_to_all(step_proj.astype(jnp.bfloat16), 'unit', split_axis=1, conc...]
    unnamed x2 -> x4, other arithmetic: 50.8 us -> 3.81 us
    convert_element_type x4 -> x0, local copies, waits for them, and re-layouts: 45.6 us -> none  [the longest x1 44.7 us: body(): (gated * lax.rsqrt(spread + EPSILON) * norm_gain).astype(jnp.bfloat16)]
  transfers between devices with their start and end apart: 11 -> 3, of which waited for: 4 -> 3; matrix products, arithmetic and copies ran while one was open for 47% -> 15% of each run, Pallas kernels for 0% -> 0%
where the time goes in v1:
time: 299 us; the launch traced here: 297 us
  waiting for transfers between devices  190 us (64%)
  local copies, waits for them, and re-layouts  49.5 us (17%)
  matrix products  21.7 us (7%)
  Pallas kernels  15.7 us (5%)
  between operations  13.8 us (5%)
  other arithmetic  6.18 us (2%)
    all_gather x1, waiting for transfers between devices, body(): second = lax.all_gather(gate_proj.astype(BF), everyone, axis=0, tiled=True)  70.7 us
    all_gather x1, waiting for transfers between devices, body(): third = lax.all_gather(out_proj.astype(BF), everyone, axis=0, tiled=True)  62.1 us
    all_gather x1, waiting for transfers between devices, body(): first = lax.all_gather(first, everyone, axis=0, tiled=True)  57.5 us
    unnamed x11, local copies, waits for them, and re-layouts  44.7 us
    pallas_call x1, Pallas kernels, scan_gate(): pl.pallas_call(scan_kernel, grid=(groups,), in_specs=[pl.BlockSpec(memory...  15.7 us
    dot_general x1, matrix products, body(): projected = jnp.dot(own, first, preferred_element_type=F32).astype(BF)  8.94 us
    dot_general x1, matrix products, body(): gate = jnp.dot(own, second, preferred_element_type=F32).astype(BF)  7.88 us
  transfers between devices with their start and end apart: 3, of which 3 were waited for; matrix products, arithmetic and copies ran while one was open for 15% of the time, Pallas kernels for 0%

profile of v1, /device:TPU:1, one launch (start us, length us, event | category | flops | bytes accessed | tf_op | source)
XLA Modules:
  0.0 297.3 jit_solution(8553150779537826751)
XLA Ops:
  7.2 1.6 convert_bitcast_fusion.1
  8.9 1.6 convert_bitcast_fusion
  10.5 0.9 convert_element_type.24
  11.5 0.7 convert.8
  12.2 0.7 convert.9
  12.9 0.7 maximum_bitcast_fusion
  13.6 0.8 slice.17.taps_ref
  14.4 0.7 slice.18.side_taps_ref
  15.1 0.7 broadcast_in_dim.17
  15.9 1.3 dynamic_slice.7.len_ref
  17.2 0.7 pad_bitcast_fusion
  17.8 70.7 %all-gather.9.cloned.1.call-done = bf16[128,12,3072]{2,1,0:T(8,128)(2,1)} async-done(((bf16[1,12,3072]{2,1,0:T(8,128)(2,1)}), bf16[128,12,3072]{2,1,0:T(8,128)(2,1)}) %all-gather.9.cloned.1.call-update) | async-done | bytes 9437200 | tf_op jit(solution)/shard_map/all_gather | solution.py:239
  88.6 13.8 %reshape.11 = bf16[1536,3072]{1,0:T(8,128)(2,1)} reshape(bf16[128,12,3072]{2,1,0:T(8,128)(2,1)} %all-gather.9.cloned.1.call-done) | data formatting | bytes 18874368
  102.3 62.1 %all-gather.11.cloned.1.call-done = bf16[128,12,3072]{2,1,0:T(8,128)(2,1)} async-done(((bf16[1,12,3072]{2,1,0:T(8,128)(2,1)}), bf16[128,12,3072]{2,1,0:T(8,128)(2,1)}) %all-gather.11.cloned.1.call-update) | async-done | bytes 9437200 | tf_op jit(solution)/shard_map/all_gather | solution.py:240
  164.4 13.7 %reshape.13 = bf16[1536,3072]{1,0:T(8,128)(2,1)} reshape(bf16[128,12,3072]{2,1,0:T(8,128)(2,1)} %all-gather.11.cloned.1.call-done) | data formatting | bytes 18874368
  178.1 7.9 %convolution_convert_fusion.1.gate_ref = bf16[384,3072]{1,0:T(8,128)(2,1)S(1)} fusion(bf16[1536,3072]{1,0:T(8,128)(2,1)} %reshape.11, bf16[16,384,1536]{2,1,0:T(8,128)(2,1)} %param.12, s32[]{:T(128)S(6)} %select_n.5), kind=kOutput, calls=%fused_computation.1 | convolution fusion | flops 3625058304 | bytes 12976132 | tf_op jit(solution)/shard_map/dot_general | solution.py:247
  186.0 57.5 %all-gather.7.cloned.1.call-done = bf16[128,12,3456]{2,1,0:T(8,128)(2,1)} async-done(((bf16[1,12,3456]{2,1,0:T(8,128)(2,1)}), bf16[128,12,3456]{2,1,0:T(8,128)(2,1)}) %all-gather.7.cloned.1.call-update) | async-done | bytes 10616848 | tf_op jit(solution)/shard_map/all_gather | solution.py:238
  243.5 16.9 %reshape.9 = bf16[1536,3456]{1,0:T(8,128)(2,1)} reshape(bf16[128,12,3456]{2,1,0:T(8,128)(2,1)} %all-gather.7.cloned.1.call-done) | data formatting | bytes 21233664
  260.4 8.9 %convolution_convert_fusion = bf16[384,3456]{1,0:T(8,128)(2,1)S(1)} fusion(bf16[1536,3456]{1,0:T(8,128)(2,1)} %reshape.9, bf16[16,384,1536]{2,1,0:T(8,128)(2,1)} %param.12, s32[]{:T(128)S(6)} %select_n.5), kind=kOutput, calls=%fused_computation | convolution fusion | flops 4078190592 | bytes 14450692 | tf_op jit(solution)/shard_map/dot_general | solution.py:245
  269.4 0.3 slice.20.input_ref
  269.7 0.3 copy-done
  270.1 15.7 %scan_gate.1 = (bf16[384,3072]{1,0:T(8,128)(2,1)S(1)}, f32[3072,128]{1,0:T(8,128)}, f32[384,128]{1,0:T(8,128)S(1)}) custom-call(s32[1]{0:T(128)} %dynamic_slice.7.len_ref, bf16[384,3072]{1,0:T(8,128)(2,1)S(1)} %slice.20.input_ref, bf16[384,3072]{1,0:T(8,128)(2,1)S(1)} %convolution_convert_fusion.1.gate_ref, bf16[384,384]{1,0:T(8,128)(2,1)S(1)} %slice.21.side_ref, ...), custom_call_target="tpu_custom_call" | custom-call | flops 1509949440 | bytes 9437184 | tf_op jit(solution)/shard_map/scan_gate/pallas_call | solution.py:168
  285.7 0.1 slice_reduce_fusion
  285.9 4.9 %fusion.1 = bf16[1,384,1536]{2,1,0:T(8,128)(2,1)} fusion(bf16[384,3072]{1,0:T(8,128)(2,1)S(1)} %get-tuple-element.5, bf16[1536,3072]{1,0:T(8,128)(2,1)S(1)} %bitcast.25, f32[384]{0:T(512)S(1)} %slice_reduce_fusion), kind=kOutput, calls=%fused_computation.4 | convolution fusion | flops 3625058304 | bytes 12977664 | tf_op jit(solution)/shard_map/dot_general | solution.py:260
  (17 shorter events, 0.3 us)
Async XLA Ops:
  7.2 81.4 %all-gather.9.cloned.1.call-start = ((), (), s32[]{:S(2)}) async-start(), calls=%async_computation.1 | async-start | bytes 12681216 | tf_op jit(solution)/shard_map/all_gather | solution.py:239
  8.8 155.6 %all-gather.11.cloned.1.call-start = ((), (), s32[]{:S(2)}) async-start(), calls=%async_computation.2 | async-start | bytes 12681216 | tf_op jit(solution)/shard_map/all_gather | solution.py:240
  10.5 233.0 %all-gather.7.cloned.1.call-start = ((), (), s32[]{:S(2)}) async-start(), calls=%async_computation | async-start | bytes 14266368 | tf_op jit(solution)/shard_map/all_gather | solution.py:238
  260.4 25.5 %slice-start = ((s8[9437184]{0:T(1024)(128)(4,1)}), s8[4194304]{0:T(1024)(128)(4,1)S(1)}, s32[]{:S(2)}) async-start(s8[9437184]{0:T(1024)(128)(4,1)} %bitcast.24), calls=%async_computation.3 | async-start | bytes 8388608
  260.4 25.5 %slice-start.1 = ((s8[9437184]{0:T(1024)(128)(4,1)}), s8[4194304]{0:T(1024)(128)(4,1)S(1)}, s32[]{:S(2)}) async-start(s8[9437184]{0:T(1024)(128)(4,1)} %bitcast.24), calls=%async_computation.4 | async-start | bytes 8388608
  269.3 0.7 copy-start
  269.4 16.5 %slice-start.2 = ((s8[9437184]{0:T(1024)(128)(4,1)}), s8[1048576]{0:T(1024)(128)(4,1)S(1)}, s32[]{:S(2)}) async-start(s8[9437184]{0:T(1024)(128)(4,1)} %bitcast.24), calls=%async_computation.5 | async-start | bytes 2097152
Sparse Core Ops, SparseCore 0:
  11.6 76.9 all-gather.8
  91.6 72.8 all-gather.10
  168.0 75.4 all-gather.6

commit v2 on v1

--- a/solution.py
+++ b/solution.py
@@ -29,7 +29,7 @@
 
 
 def scan_kernel(
-    len_ref,
+    meta_ref,
     input_ref,
     gate_ref,
     side_ref,
@@ -41,23 +41,22 @@
     gain_ref,
     gated_ref,
     state_ref,
-    scale_ref,
+    square_ref,
     decay_col,
     delta_col,
     decay_row,
     b_scr,
     c_scr,
     cb_scr,
-    square_scr,
 ):
-    step = pl.program_id(0)
+    which = pl.program_id(0)
+    step = pl.program_id(1)
     seq = input_ref.shape[0]
     state_dim = side_taps_ref.shape[1] // 2
     groups = decay_col.shape[0]
     blocks = seq // SPAN
-    inner = groups * input_ref.shape[1]
     position = lax.broadcasted_iota(jnp.int32, (seq, LANES), 0)
-    live = (position < len_ref[0]).astype(F32)
+    group_here = meta_ref[0] * pl.num_programs(1) + step
 
     @pl.when(step == 0)
     def _():
@@ -73,6 +72,7 @@
                 c_short[at], b_short[at], (((1,), (1,)), ((), ())), preferred_element_type=F32
             )
         raw = side[:, 2 * state_dim :] + bias_ref[...]
+        live = (position < meta_ref[1 + which]).astype(F32)
         delta = (jnp.maximum(raw, 0.0) + jnp.log1p(jnp.exp(-jnp.abs(raw)))) * live
         total = delta * -jnp.exp(log_rate_ref[...])
         within = position % SPAN
@@ -86,11 +86,11 @@
             decay_col[group] = total[:, at]
             delta_col[group] = delta[:, at]
             decay_row[group] = turned[at]
-        square_scr[...] = jnp.zeros_like(square_scr)
-
-    decays = decay_col[step]
-    deltas = delta_col[step]
-    rows_of = decay_row[step]
+        square_ref[...] = jnp.zeros_like(square_ref)
+
+    decays = decay_col[group_here]
+    deltas = delta_col[group_here]
+    rows_of = decay_row[group_here]
     lower = lax.broadcasted_iota(jnp.int32, (SPAN, SPAN), 0) >= lax.broadcasted_iota(
         jnp.int32, (SPAN, SPAN), 1
     )
@@ -147,66 +147,194 @@
                 fresh = fade * state + fresh
             state = fresh
             gated = (out + skip * x_here) * gate[at]
-            square_scr[at, :] += gated * gated
+            square_ref[at, :] += gated * gated
             gated_ref[at, cols] = (gated * gain).astype(BF)
         state_ref[cols, :] = state
 
-    @pl.when(step == groups - 1)
-    def _():
-        mean = jnp.sum(square_scr[...], axis=1, keepdims=True) / inner
-        scale_ref[...] = lax.rsqrt(mean + EPSILON) * live
-
-
-def scan_gate(length, inputs, gate, side, taps, side_taps, bias, log_rate, skip, gain):
-    seq, inner = inputs.shape
-    width = side_taps.shape[1]
+
+def scan_gate(meta, projected, conv_weight, bias, log_rate, skip, gain, width):
+    rows, total = projected.shape
+    seq = rows // 2
     state_dim = width // 2
+    half = (total - width - LANES) // 2
+    inner = 2 * half
     cols = HEADS_STEP * LANES // 2
-    groups = inner // cols
-    whole = lambda i: (0, 0)
-    part = lambda i: (0, i)
-    return pl.pallas_call(
-        scan_kernel,
-        grid=(groups,),
+    groups = half // cols
+    taps = conv_weight.shape[0]
+    here = lambda r, g, m: (0, m[0] * groups + g)
+    fixed = lambda r, g, m: (0, 0)
+    grid_spec = pltpu.PrefetchScalarGridSpec(
+        num_scalar_prefetch=1,
+        grid=(2, groups),
         in_specs=[
-            pl.BlockSpec(memory_space=pltpu.SMEM),
-            pl.BlockSpec((seq, cols), part),
-            pl.BlockSpec((seq, cols), part),
-            pl.BlockSpec((seq, width + LANES), whole),
-            pl.BlockSpec((taps.shape[0], cols), part),
-            pl.BlockSpec((taps.shape[0], width), whole),
-            pl.BlockSpec((1, LANES), whole),
-            pl.BlockSpec((1, LANES), whole),
-            pl.BlockSpec((1, cols), part),
-            pl.BlockSpec((1, cols), part),
+            pl.BlockSpec((seq, cols), lambda r, g, m: (r, g)),
+            pl.BlockSpec((seq, cols), lambda r, g, m: (r, groups + g)),
+            pl.BlockSpec((seq, width + LANES), lambda r, g, m: (r, inner // (width + LANES))),
+            pl.BlockSpec((taps, cols), here),
+            pl.BlockSpec((taps, width), lambda r, g, m: (0, inner // width)),
+            pl.BlockSpec((1, LANES), fixed),
+            pl.BlockSpec((1, LANES), fixed),
+            pl.BlockSpec((1, cols), here),
+            pl.BlockSpec((1, cols), here),
         ],
         out_specs=[
-            pl.BlockSpec((seq, cols), part),
-            pl.BlockSpec((cols, state_dim), lambda i: (i, 0)),
-            pl.BlockSpec((seq, LANES), whole),
-        ],
-        out_shape=[
-            jax.ShapeDtypeStruct((seq, inner), BF),
-            jax.ShapeDtypeStruct((inner, state_dim), F32),
-            jax.ShapeDtypeStruct((seq, LANES), F32),
+            pl.BlockSpec((None, seq, cols), lambda r, g, m: (r, 0, g)),
+            pl.BlockSpec((None, cols, state_dim), lambda r, g, m: (r, g, 0)),
+            pl.BlockSpec((None, seq, LANES), lambda r, g, m: (r, 0, 0)),
         ],
         scratch_shapes=[
-            pltpu.VMEM((groups, seq, HEADS_STEP), F32),
-            pltpu.VMEM((groups, seq, HEADS_STEP), F32),
-            pltpu.VMEM((groups, HEADS_STEP, seq), F32),
+            pltpu.VMEM((2 * groups, seq, HEADS_STEP), F32),
+            pltpu.VMEM((2 * groups, seq, HEADS_STEP), F32),
+            pltpu.VMEM((2 * groups, HEADS_STEP, seq), F32),
             pltpu.VMEM((seq, state_dim), BF),
             pltpu.VMEM((seq, state_dim), BF),
             pltpu.VMEM((seq // SPAN, SPAN, SPAN), F32),
-            pltpu.VMEM((seq, LANES), F32),
+        ],
+    )
+    return pl.pallas_call(
+        scan_kernel,
+        grid_spec=grid_spec,
+        out_shape=[
+            jax.ShapeDtypeStruct((2, seq, half), BF),
+            jax.ShapeDtypeStruct((2, half, state_dim), F32),
+            jax.ShapeDtypeStruct((2, seq, LANES), F32),
         ],
         compiler_params=pltpu.CompilerParams(
-            dimension_semantics=("arbitrary",), vmem_limit_bytes=40 << 20
+            dimension_semantics=("arbitrary", "arbitrary"), vmem_limit_bytes=40 << 20
         ),
         cost_estimate=pl.CostEstimate(
             flops=2 * inner * seq * 640, transcendentals=inner * seq * 6, bytes_accessed=9 << 20
         ),
         name="scan_gate",
-    )(length, inputs, gate, side, taps, side_taps, bias, log_rate, skip, gain)
+    )(meta, projected, projected, projected, conv_weight, conv_weight, bias, log_rate, skip, gain)
+
+
+def project_kernel(tokens_ref, *refs):
+    pieces, out_ref = refs[:-1], refs[-1]
+    depth = pieces[0].shape[0]
+    total = None
+    for index, piece in enumerate(pieces):
+        part = jnp.dot(
+            tokens_ref[:, index * depth : (index + 1) * depth],
+            piece[...],
+            preferred_element_type=F32,
+        )
+        total = part if total is None else total + part
+    out_ref[...] = total.astype(BF)
+
+
+def project(tokens, pieces):
+    rows, model = tokens.shape
+    depth, total = pieces[0].shape
+    tile = total // 3
+    return pl.pallas_call(
+        project_kernel,
+        grid=(3,),
+        in_specs=[pl.BlockSpec((rows, model), lambda n: (0, 0))]
+        + [pl.BlockSpec((depth, tile), lambda n: (0, n)) for _ in pieces],
+        out_specs=pl.BlockSpec((rows, tile), lambda n: (0, n)),
+        out_shape=jax.ShapeDtypeStruct((rows, total), BF),
+        compiler_params=pltpu.CompilerParams(
+            dimension_semantics=("arbitrary",), vmem_limit_bytes=40 << 20
+        ),
+        cost_estimate=pl.CostEstimate(
+            flops=2 * rows * model * total, transcendentals=0, bytes_accessed=20 << 20
+        ),
+        name="project",
+    )(tokens, *pieces)
+
+
+def mix_kernel(meta_ref, mine_ref, other_ref, w_mine_ref, w_other_ref, sq_mine, sq_other, out_ref):
+    seq = mine_ref.shape[0]
+    dims = (((1,), (1,)), ((), ()))
+    inner = 2 * mine_ref.shape[1]
+    wide = lax.dot_general(mine_ref[...], w_mine_ref[...], dims, preferred_element_type=F32)
+    wide += lax.dot_general(other_ref[...], w_other_ref[...], dims, preferred_element_type=F32)
+    mean = jnp.sum(sq_mine[...] + sq_other[...], axis=1, keepdims=True) / inner
+    live = lax.broadcasted_iota(jnp.int32, (seq, 1), 0) < meta_ref[1]
+    scale = jnp.where(live, lax.rsqrt(mean + EPSILON), 0.0)
+    short = (wide * scale).astype(BF)
+    padded, kept = wide.shape[1], out_ref.shape[1]
+    row = lax.broadcasted_iota(jnp.int32, (padded, kept), 0)
+    col = lax.broadcasted_iota(jnp.int32, (padded, kept), 1)
+    part = row & (PADDED_ROWS - 1)
+    place = (row >> PADDED_SHIFT) * SHARD_ROWS + part
+    pick = jnp.where((place == col) & (part < SHARD_ROWS), 1.0, 0.0).astype(BF)
+    out_ref[...] = jnp.dot(short, pick, preferred_element_type=F32).astype(BF)
+
+
+def mix(meta, mine, other, weight, sq_mine, sq_other, model):
+    seq, half = mine.shape
+    padded = weight.shape[0]
+    steps = 4
+    fixed = lambda n, m: (0, 0)
+    return pl.pallas_call(
+        mix_kernel,
+        grid_spec=pltpu.PrefetchScalarGridSpec(
+            num_scalar_prefetch=1,
+            grid=(steps,),
+            in_specs=[
+                pl.BlockSpec((seq, half), fixed),
+                pl.BlockSpec((seq, half), fixed),
+                pl.BlockSpec((padded // steps, half), lambda n, m: (n, m[0])),
+                pl.BlockSpec((padded // steps, half), lambda n, m: (n, 1 - m[0])),
+                pl.BlockSpec((seq, LANES), fixed),
+                pl.BlockSpec((seq, LANES), fixed),
+            ],
+            out_specs=pl.BlockSpec((seq, model // steps), lambda n, m: (0, n)),
+        ),
+        out_shape=jax.ShapeDtypeStruct((seq, model), BF),
+        compiler_params=pltpu.CompilerParams(
+            dimension_semantics=("arbitrary",), vmem_limit_bytes=40 << 20
+        ),
+        cost_estimate=pl.CostEstimate(
+            flops=6 * seq * half * padded, transcendentals=0, bytes_accessed=16 << 20
+        ),
+        name="mix",
+    )(meta, mine, other, weight, weight, sq_mine, sq_other)
+
+
+EVERYONE = ("req", "unit")
+DEVICES = 128
+CORE = 16
+SHARD_ROWS = 12
+PADDED_ROWS = 16
+PADDED_SHIFT = 4
+COLOURS = 3
+LINKS = (1 << 2, 1, 1 << 5, 3 << 2, 3, 3 << 5)
+
+
+def link_of(colour, core, step):
+    return LINKS[(colour + 3 * core + step) % 6]
+
+
+def hop(value, mask_of):
+    return lax.ppermute(
+        value, EVERYONE, [(d, d ^ mask_of((d // CORE) % 2)) for d in range(DEVICES)]
+    )
+
+
+def swap(value):
+    return hop(value, lambda core: CORE)
+
+
+def row_sources(me, core):
+    sources = []
+    block = jnp.arange(64, dtype=jnp.int32)
+    row = jnp.arange(8, dtype=jnp.int32)
+    for colour in range(COLOURS):
+        masks = []
+        for side in range(2):
+            mask = jnp.zeros_like(block)
+            for step in range(6):
+                mask = mask ^ (((block >> step) & 1) * link_of(colour, side, step))
+            masks.append(mask)
+        chip = (me ^ jnp.where(core == 0, masks[0], masks[1])) & ~CORE
+        local = colour * 8 + row
+        upper = (local >= SHARD_ROWS).astype(jnp.int32)
+        device = chip[:, None] + CORE * upper[None]
+        sources.append((device * SHARD_ROWS + (local - SHARD_ROWS * upper)[None]).reshape(-1))
+    return jnp.concatenate(sources)
 
 
 def body(
@@ -224,42 +352,65 @@
     norm_gain,
 ):
     unit_id = lax.axis_index("unit")
-    group_reqs, seq_len, model_dim = tokens.shape
+    me = lax.axis_index(EVERYONE).astype(jnp.int32)
+    core = (me // CORE) % 2
+    first_core = core == 0
+    seq_len, model_dim = tokens.shape[1:]
     inner_dim = gate_proj.shape[1]
     head_count = log_rate.shape[0]
     head_dim = inner_dim // head_count
-    state_dim = state_proj.shape[1] // 2
-    everyone = ("req", "unit")
-
-    side_proj = jnp.concatenate([state_proj, step_proj], axis=1)
+    width = state_proj.shape[1]
+    half = inner_dim // 2
     spare = LANES - head_count
-    side_proj = jnp.pad(side_proj, ((0, 0), (0, spare)))
-    first = jnp.concatenate([side_proj.astype(BF), input_proj.astype(BF)], axis=1)
-    first = lax.all_gather(first, everyone, axis=0, tiled=True)
-    second = lax.all_gather(gate_proj.astype(BF), everyone, axis=0, tiled=True)
-    third = lax.all_gather(out_proj.astype(BF), everyone, axis=0, tiled=True)
+
+    padded_out = jnp.pad(out_proj.astype(BF), ((0, PADDED_ROWS - SHARD_ROWS), (0, 0)))
+    out_weight = lax.all_gather(padded_out, EVERYONE, axis=0, tiled=True)
+
+    side = jnp.pad(jnp.concatenate([state_proj, step_proj], axis=1), ((0, 0), (0, spare)))
+    low = jnp.concatenate([input_proj[:, :half], gate_proj[:, :half], side], axis=1).astype(BF)
+    high = jnp.concatenate([input_proj[:, half:], gate_proj[:, half:], side], axis=1).astype(BF)
+    received = swap(jnp.where(first_core, high, low))
+    kept = jnp.where(first_core, low, high)
+    pair = jnp.concatenate(
+        [jnp.where(first_core, kept, received), jnp.where(first_core, received, kept)], axis=0
+    )
+    held = [pair[8 * c : 8 * c + 8] for c in range(COLOURS)]
+    for step in range(5):
+        moved = [
+            hop(held[c], lambda core, c=c: link_of(c, core, step)) for c in range(COLOURS)
+        ]
+        held = [jnp.concatenate([h, m], axis=0) for h, m in zip(held, moved)]
+    moved = [hop(held[c], lambda core, c=c: link_of(c, core, 5)) for c in range(COLOURS)]
+    pieces = [piece for both in zip(held, moved) for piece in both]
 
     own = lax.dynamic_index_in_dim(tokens, unit_id, 0, keepdims=False)
     length = lax.dynamic_slice_in_dim(lengths, unit_id, 1, 0)
-    width = side_proj.shape[1]
-    projected = jnp.dot(own, first, preferred_element_type=F32).astype(BF)
-    side, inputs = projected[:, :width], projected[:, width:]
-    gate = jnp.dot(own, second, preferred_element_type=F32).astype(BF)
-    gated, state, scale = scan_gate(
-        length,
-        inputs,
-        gate,
-        side,
-        conv_weight[:, :inner_dim],
-        conv_weight[:, inner_dim:],
+    coded = jnp.stack([length // 16, length % 16], axis=1).astype(BF)
+    coded = jnp.pad(coded, ((0, 7), (0, model_dim - 2)))
+    other = swap(jnp.concatenate([own, coded], axis=0))
+    code = other[seq_len, :2].astype(jnp.int32)
+    meta = jnp.stack([core, length[0], code[0] * 16 + code[1]])
+    both = jnp.concatenate([own, other[:seq_len]], axis=0)
+    pick = jnp.arange(model_dim, dtype=jnp.int32)[:, None] == row_sources(me, core)[None]
+    both = jnp.dot(both, pick.astype(BF), preferred_element_type=F32).astype(BF)
+
+    projected = project(both, pieces)
+    gated, state, squares = scan_gate(
+        meta,
+        projected,
+        conv_weight,
         jnp.pad(step_bias, (0, spare))[None],
         jnp.pad(log_rate, (0, spare))[None],
         jnp.repeat(skip_gain, head_dim)[None],
         norm_gain[None],
-    )
-    mixed = lax.dot_general(gated, third, (((1,), (1,)), ((), ())), preferred_element_type=F32)
-    mixed = (mixed * scale[:, :1]).astype(BF)
-    return (mixed[None], state.reshape(1, head_count, head_dim, state_dim))
+        width,
+    )
+    gated_other, squares_other, state_other = swap(gated[1]), swap(squares[1]), swap(state[1])
+    mixed = mix(meta, gated[0], gated_other, out_weight, squares[0], squares_other, model_dim)
+    state = jnp.concatenate(
+        [jnp.where(first_core, state[0], state_other), jnp.where(first_core, state_other, state[0])]
+    )
+    return (mixed[None], state.reshape(1, head_count, head_dim, width // 2))
 
 
 def solution(mesh):

time: 299 us -> 160 us (0.54)
  waiting for transfers between devices: 190 us -> 56.4 us
  local copies, waits for them, and re-layouts: 49.5 us -> 17.3 us
  Pallas kernels: 15.7 us -> 39.2 us
  starting transfers between devices: 0.12 us -> 18 us
  matrix products: 21.7 us -> 4.12 us
  between operations: 13.8 us -> 18.3 us
    all_gather x3 -> x1, waiting for transfers between devices: 190 us -> 0.01 us  [body(): out_weight = lax.all_gather(padded_out, EVERYONE, axis=0, tiled=True)]
    ppermute x0 -> x23, waiting for transfers between devices: none -> 56.4 us  [hop(): lax.ppermute(value, EVERYONE, [(d, d ^ mask_of(d // CORE % 2)) for d in r...]
    unnamed x11 -> x30, local copies, waits for them, and re-layouts: 44.7 us -> 7.24 us
    pallas_call x1 -> x3, Pallas kernels: 15.7 us -> 39.2 us  [the longest x1 16 us: scan_gate(): pl.pallas_call(scan_kernel, grid_spec=grid_spec, out_shape=[jax.ShapeDtyp...]
    ppermute x0 -> x23, starting transfers between devices: none -> 18 us  [hop(): lax.ppermute(value, EVERYONE, [(d, d ^ mask_of(d // CORE % 2)) for d in r...]
    dot_general x3 -> x1, matrix products: 21.7 us -> 4.12 us  [body(): both = jnp.dot(both, pick.astype(BF), preferred_element_type=F32).astype(BF)]
    concatenate x0 -> x6, local copies, waits for them, and re-layouts: none -> 3.89 us  [body(): held = [jnp.concatenate([h, m], axis=0) for h, m in zip(held, moved)]]
    unnamed x4 -> x1, other arithmetic: 3.81 us -> 0.65 us
  transfers between devices with their start and end apart: 3 -> 24, of which waited for: 3 -> 11; matrix products, arithmetic and copies ran while one was open for 15% -> 15% of each run, Pallas kernels for 0% -> 18%
where the time goes in v2:
time: 160 us
  waiting for transfers between devices  56.4 us (35%)
  Pallas kernels  39.2 us (25%)
  between operations  18.3 us (11%)
  starting transfers between devices  18 us (11%)
  local copies, waits for them, and re-layouts  17.3 us (11%)
  other arithmetic  6.1 us (4%)
  matrix products  4.12 us (3%)
    ppermute x23, waiting for transfers between devices, hop(): lax.ppermute(value, EVERYONE, [(d, d ^ mask_of(d // CORE % 2)) for d in r...  56.4 us
    ppermute x23, starting transfers between devices, hop(): lax.ppermute(value, EVERYONE, [(d, d ^ mask_of(d // CORE % 2)) for d in r...  18 us
    pallas_call x1, Pallas kernels, scan_gate(): pl.pallas_call(scan_kernel, grid_spec=grid_spec, out_shape=[jax.ShapeDtyp...  16 us
    pallas_call x1, Pallas kernels, project(): pl.pallas_call(project_kernel, grid=(3,), in_specs=[pl.BlockSpec((rows, m...  12.9 us
    pallas_call x1, Pallas kernels, mix(): pl.pallas_call(mix_kernel, grid_spec=pltpu.PrefetchScalarGridSpec(num_sca...  10.3 us
    unnamed x30, local copies, waits for them, and re-layouts  7.24 us
    dot_general x1, matrix products, body(): both = jnp.dot(both, pick.astype(BF), preferred_element_type=F32).astype(BF)  4.12 us
    concatenate x6, local copies, waits for them, and re-layouts, body(): held = [jnp.concatenate([h, m], axis=0) for h, m in zip(held, moved)]  3.89 us
  transfers between devices with their start and end apart: 24, of which 11 were waited for; matrix products, arithmetic and copies ran while one was open for 15% of the time, Pallas kernels for 18%

profile of v2, /device:TPU:1, one launch (start us, length us, event | category | flops | bytes accessed | tf_op | source)
XLA Modules:
  0.0 159.5 jit_solution(9764168140902731634)
XLA Ops:
  8.8 1.3 dynamic_slice.7
  12.7 1.3 dynamic-slice_bitcast_fusion
  14.1 1.1 pad_maximum_fusion.1
  15.2 1.4 collective-permute-start
  17.0 2.3 %collective-permute-done.1 = bf16[12,3456]{1,0:T(8,128)(2,1)S(1)} collective-permute-done((bf16[12,3456]{1,0:T(8,128)(2,1)S(1)}, bf16[12,3456]{1,0:T(8,128)(2,1)S(1)}, u32[]{:S(2)}, u32[]{:S(2)}) %collective-permute-start.1) | collective-permute-done | bytes 82976 | tf_op jit(solution)/shard_map/ppermute | solution.py:312
  20.0 2.6 %collective-permute-start.2 = (bf16[8,3456]{1,0:T(8,128)(2,1)S(1)}, bf16[8,3456]{1,0:T(8,128)(2,1)S(1)}, u32[]{:S(2)}, u32[]{:S(2)}) collective-permute-start(bf16[8,3456]{1,0:T(8,128)(2,1)S(1)} %get-tuple-element.39), channel_id=1, source_target_pairs={{0,4},{1,5},{2,6},{3,7},{4,0},{5,1},{6,2},{7,3},{8,12},{9,13},{10,... | collective-permute-start | bytes 165896 | tf_op jit(solution)/shard_map/ppermute | solution.py:312
  22.6 2.7 %collective-permute-start.8 = (bf16[8,3456]{1,0:T(8,128)(2,1)S(1)}, bf16[8,3456]{1,0:T(8,128)(2,1)S(1)}, u32[]{:S(2)}, u32[]{:S(2)}) collective-permute-start(bf16[8,3456]{1,0:T(8,128)(2,1)S(1)} %get-tuple-element.36), channel_id=1, source_target_pairs={{0,1},{1,0},{2,3},{3,2},{4,5},{5,4},{6,7},{7,6},{8,9},{9,8},{10,11... | collective-permute-start | bytes 165896 | tf_op jit(solution)/shard_map/ppermute | solution.py:312
  26.0 3.8 %collective-permute-start.14 = (bf16[8,3456]{1,0:T(8,128)(2,1)S(1)}, bf16[8,3456]{1,0:T(8,128)(2,1)S(1)}, u32[]{:S(2)}, u32[]{:S(2)}) collective-permute-start(bf16[8,3456]{1,0:T(8,128)(2,1)S(1)} %get-tuple-element.34), channel_id=1, source_target_pairs={{0,32},{1,33},{2,34},{3,35},{4,36},{5,37},{6,38},{7,39},{8,40},{9,... | collective-permute-start | bytes 165896 | tf_op jit(solution)/shard_map/ppermute | solution.py:312
  29.9 1.2 collective-permute-start.9
  33.3 2.0 %collective-permute-done.3 = bf16[16,3456]{1,0:T(8,128)(2,1)S(1)} collective-permute-done((bf16[16,3456]{1,0:T(8,128)(2,1)S(1)}, bf16[16,3456]{1,0:T(8,128)(2,1)S(1)}, u32[]{:S(2)}, u32[]{:S(2)}) %collective-permute-start.3) | collective-permute-done | bytes 110624 | tf_op jit(solution)/shard_map/ppermute | solution.py:312
  35.8 1.3 collective-permute-start.10
  38.7 3.1 %collective-permute-done.4 = bf16[32,3456]{1,0:T(8,128)(2,1)S(1)} collective-permute-done((bf16[32,3456]{1,0:T(8,128)(2,1)S(1)}, bf16[32,3456]{1,0:T(8,128)(2,1)S(1)}, u32[]{:S(2)}, u32[]{:S(2)}) %collective-permute-start.4) | collective-permute-done | bytes 221216 | tf_op jit(solution)/shard_map/ppermute | solution.py:312
  43.7 7.2 %collective-permute-done.5 = bf16[64,3456]{1,0:T(8,128)(2,1)S(1)} collective-permute-done((bf16[64,3456]{1,0:T(8,128)(2,1)S(1)}, bf16[64,3456]{1,0:T(8,128)(2,1)S(1)}, u32[]{:S(2)}, u32[]{:S(2)}) %collective-permute-start.5) | collective-permute-done | bytes 442400 | tf_op jit(solution)/shard_map/ppermute | solution.py:312
  52.8 12.7 %collective-permute-done.6 = bf16[128,3456]{1,0:T(8,128)(2,1)S(1)} collective-permute-done((bf16[128,3456]{1,0:T(8,128)(2,1)S(1)}, bf16[128,3456]{1,0:T(8,128)(2,1)S(1)}, u32[]{:S(2)}, u32[]{:S(2)}) %collective-permute-start.6) | collective-permute-done | bytes 884768 | tf_op jit(solution)/shard_map/ppermute | solution.py:312
  67.9 1.5 collective-permute-start.19
  72.9 1.4 slice.76
  75.0 4.1 %fusion.2.tokens_ref = bf16[768,1536]{1,0:T(8,128)(2,1)S(1)} fusion(s32[1536]{0:T(1024)S(1)} %pad_add_fusion, bf16[384,1536]{1,0:T(8,128)(2,1)S(1)} %slice.76, bf16[384,1536]{1,0:T(8,128)(2,1)S(1)} %dynamic-slice_bitcast_fusion), kind=kOutput, calls=%fused_computation.3 | convolution fusion | flops 3632136192 | bytes 4724736 | tf_op jit(solution)/shard_map/dot_general | solution.py:395
  79.2 26.0 %collective-permute-done.7.refs_1_ = bf16[256,3456]{1,0:T(8,128)(2,1)} collective-permute-done((bf16[256,3456]{1,0:T(8,128)(2,1)}, bf16[256,3456]{1,0:T(8,128)(2,1)}, u32[]{:S(2)}, u32[]{:S(2)}) %collective-permute-start.7) | collective-permute-done | bytes 1769504 | tf_op jit(solution)/shard_map/ppermute | solution.py:312
  105.2 1.1 collective-permute-done.13.refs_3_
  106.4 12.9 %project.1.input_ref.gate_ref.side_ref = bf16[768,3456]{1,0:T(8,128)(2,1)} custom-call(bf16[768,1536]{1,0:T(8,128)(2,1)S(1)} %fusion.2.tokens_ref, bf16[256,3456]{1,0:T(8,128)(2,1)} %constant_dynamic-update-slice_fusion.5.refs_0_, bf16[256,3456]{1,0:T(8,128)(2,1)} %collective-permute-done.7.refs_1_, ...), custom_call_target="tpu_custom_call" | custom-call | flops 8153726976 | bytes 20971520 | tf_op jit(solution)/shard_map/project/pallas_call | solution.py:230
  119.3 2.5 %copy-done = bf16[768,3456]{1,0:T(8,128)(2,1)S(1)} copy-done((bf16[768,3456]{1,0:T(8,128)(2,1)S(1)}, bf16[768,3456]{1,0:T(8,128)(2,1)}, u32[]{:S(2)}) %copy-start) | copy-done | bytes 5308440
  121.8 16.0 %scan_gate.1 = (bf16[2,384,1536]{2,1,0:T(8,128)(2,1)S(1)}, f32[2,1536,128]{2,1,0:T(8,128)S(1)}, f32[2,384,128]{2,1,0:T(8,128)S(1)}) custom-call(s32[3]{0:T(128)S(1)} %pad_add_fusion.1.meta_ref, bf16[768,3456]{1,0:T(8,128)(2,1)S(1)} %copy-done, bf16[768,3456]{1,0:T(8,128)(2,1)S(1)} %copy-done, bf16[768,3456]{1,0:T(8,128)(2,1)S(1)} %copy-done, ...), custom_call_target="tpu_custom_call" | custom-call | flops 1509949440 | bytes 9437184 | tf_op jit(solution)/shard_map/scan_gate/pallas_call | solution.py:194
  140.6 1.2 pad_maximum_fusion
  142.4 10.3 %mix.1 = bf16[384,1536]{1,0:T(8,128)(2,1)} custom-call(s32[3]{0:T(128)S(1)} %pad_add_fusion.1.meta_ref, bf16[384,1536]{1,0:T(8,128)(2,1)S(1)} %get-tuple-element.13.mine_ref, bf16[384,1536]{1,0:T(8,128)(2,1)S(1)} %collective-permute-done.20.other_ref, bf16[2048,3072]{1,0:T(8,128)(2,1)} %all-gather.2.cloned.1.call-done.w_mine_ref.w_other_ref, ...), custom_call_target="tpu_custom_call" | custom-call | flops 7247757312 | bytes 16777216 | tf_op jit(solution)/shard_map/mix/pallas_call | solution.py:271
  (114 shorter events, 20.3 us)
Async XLA Ops:
  7.2 135.3 %all-gather.2.cloned.1.call-start = ((), (), s32[]{:S(2)}) async-start(), calls=%async_computation | async-start | bytes 12681216 | tf_op jit(solution)/shard_map/all_gather | solution.py:367
  15.2 55.1 %collective-permute-start = (bf16[392,1536]{1,0:T(8,128)(2,1)}, bf16[392,1536]{1,0:T(8,128)(2,1)}, u32[]{:S(2)}, u32[]{:S(2)}) collective-permute-start(bf16[392,1536]{1,0:T(8,128)(2,1)} %pad_maximum_fusion.1), channel_id=1, source_target_pairs={{0,16},{1,17},{2,18},{3,19},{4,20},{5,21},{6,22},{7,23},{8,24},{9,... | collective-permute-start | bytes 3612680 | tf_op jit(solution)/shard_map/ppermute | solution.py:312
  16.8 2.5 %collective-permute-start.1 = (bf16[12,3456]{1,0:T(8,128)(2,1)S(1)}, bf16[12,3456]{1,0:T(8,128)(2,1)S(1)}, u32[]{:S(2)}, u32[]{:S(2)}) collective-permute-start(bf16[12,3456]{1,0:T(8,128)(2,1)S(1)} %broadcast_select_fusion.2), channel_id=1, source_target_pairs={{0,16},{1,17},{2,18},{3,19},{4,20},{5,21},{6,22},{7,23},{8,24},{9,... | collective-permute-start | bytes 248840 | tf_op jit(solution)/shard_map/ppermute | solution.py:312
  20.0 9.7 %collective-permute-start.2 = (bf16[8,3456]{1,0:T(8,128)(2,1)S(1)}, bf16[8,3456]{1,0:T(8,128)(2,1)S(1)}, u32[]{:S(2)}, u32[]{:S(2)}) collective-permute-start(bf16[8,3456]{1,0:T(8,128)(2,1)S(1)} %get-tuple-element.39), channel_id=1, source_target_pairs={{0,4},{1,5},{2,6},{3,7},{4,0},{5,1},{6,2},{7,3},{8,12},{9,13},{10,... | collective-permute-start | bytes 165896 | tf_op jit(solution)/shard_map/ppermute | solution.py:312
  22.6 7.2 %collective-permute-start.8 = (bf16[8,3456]{1,0:T(8,128)(2,1)S(1)}, bf16[8,3456]{1,0:T(8,128)(2,1)S(1)}, u32[]{:S(2)}, u32[]{:S(2)}) collective-permute-start(bf16[8,3456]{1,0:T(8,128)(2,1)S(1)} %get-tuple-element.36), channel_id=1, source_target_pairs={{0,1},{1,0},{2,3},{3,2},{4,5},{5,4},{6,7},{7,6},{8,9},{9,8},{10,11... | collective-permute-start | bytes 165896 | tf_op jit(solution)/shard_map/ppermute | solution.py:312
  26.0 5.3 %collective-permute-start.14 = (bf16[8,3456]{1,0:T(8,128)(2,1)S(1)}, bf16[8,3456]{1,0:T(8,128)(2,1)S(1)}, u32[]{:S(2)}, u32[]{:S(2)}) collective-permute-start(bf16[8,3456]{1,0:T(8,128)(2,1)S(1)} %get-tuple-element.34), channel_id=1, source_target_pairs={{0,32},{1,33},{2,34},{3,35},{4,36},{5,37},{6,38},{7,39},{8,40},{9,... | collective-permute-start | bytes 165896 | tf_op jit(solution)/shard_map/ppermute | solution.py:312
  29.7 5.6 %collective-permute-start.3 = (bf16[16,3456]{1,0:T(8,128)(2,1)S(1)}, bf16[16,3456]{1,0:T(8,128)(2,1)S(1)}, u32[]{:S(2)}, u32[]{:S(2)}) collective-permute-start(bf16[16,3456]{1,0:T(8,128)(2,1)S(1)} %pad_maximum_fusion.10), channel_id=1, source_target_pairs={{0,1},{1,0},{2,3},{3,2},{4,5},{5,4},{6,7},{7,6},{8,9},{9,8},{10,11... | collective-permute-start | bytes 331784 | tf_op jit(solution)/shard_map/ppermute | solution.py:312
  29.9 5.9 %collective-permute-start.9 = (bf16[16,3456]{1,0:T(8,128)(2,1)S(1)}, bf16[16,3456]{1,0:T(8,128)(2,1)S(1)}, u32[]{:S(2)}, u32[]{:S(2)}) collective-permute-start(bf16[16,3456]{1,0:T(8,128)(2,1)S(1)} %pad_maximum_fusion.11), channel_id=1, source_target_pairs={{0,32},{1,33},{2,34},{3,35},{4,36},{5,37},{6,38},{7,39},{8,40},{9,... | collective-permute-start | bytes 331784 | tf_op jit(solution)/shard_map/ppermute | solution.py:312
  31.3 5.8 %collective-permute-start.15 = (bf16[16,3456]{1,0:T(8,128)(2,1)S(1)}, bf16[16,3456]{1,0:T(8,128)(2,1)S(1)}, u32[]{:S(2)}, u32[]{:S(2)}) collective-permute-start(bf16[16,3456]{1,0:T(8,128)(2,1)S(1)} %pad_maximum_fusion.12), channel_id=1, source_target_pairs={{0,12},{1,13},{2,14},{3,15},{4,8},{5,9},{6,10},{7,11},{8,4},{9,5},... | collective-permute-start | bytes 331784 | tf_op jit(solution)/shard_map/ppermute | solution.py:312
  35.3 6.5 %collective-permute-start.4 = (bf16[32,3456]{1,0:T(8,128)(2,1)S(1)}, bf16[32,3456]{1,0:T(8,128)(2,1)S(1)}, u32[]{:S(2)}, u32[]{:S(2)}) collective-permute-start(bf16[32,3456]{1,0:T(8,128)(2,1)S(1)} %pad_maximum_fusion.5), channel_id=1, source_target_pairs={{0,32},{1,33},{2,34},{3,35},{4,36},{5,37},{6,38},{7,39},{8,40},{9,... | collective-permute-start | bytes 663560 | tf_op jit(solution)/shard_map/ppermute | solution.py:312
  35.8 6.2 %collective-permute-start.10 = (bf16[32,3456]{1,0:T(8,128)(2,1)S(1)}, bf16[32,3456]{1,0:T(8,128)(2,1)S(1)}, u32[]{:S(2)}, u32[]{:S(2)}) collective-permute-start(bf16[32,3456]{1,0:T(8,128)(2,1)S(1)} %pad_maximum_fusion.6), channel_id=1, source_target_pairs={{0,12},{1,13},{2,14},{3,15},{4,8},{5,9},{6,10},{7,11},{8,4},{9,5},... | collective-permute-start | bytes 663560 | tf_op jit(solution)/shard_map/ppermute | solution.py:312
  37.1 5.0 %collective-permute-start.16 = (bf16[32,3456]{1,0:T(8,128)(2,1)S(1)}, bf16[32,3456]{1,0:T(8,128)(2,1)S(1)}, u32[]{:S(2)}, u32[]{:S(2)}) collective-permute-start(bf16[32,3456]{1,0:T(8,128)(2,1)S(1)} %pad_maximum_fusion.7), channel_id=1, source_target_pairs={{0,3},{1,2},{2,1},{3,0},{4,7},{5,6},{6,5},{7,4},{8,11},{9,10},{10,... | collective-permute-start | bytes 663560 | tf_op jit(solution)/shard_map/ppermute | solution.py:312
  41.9 9.0 %collective-permute-start.5 = (bf16[64,3456]{1,0:T(8,128)(2,1)S(1)}, bf16[64,3456]{1,0:T(8,128)(2,1)S(1)}, u32[]{:S(2)}, u32[]{:S(2)}) collective-permute-start(bf16[64,3456]{1,0:T(8,128)(2,1)S(1)} %pad_maximum_fusion.2), channel_id=1, source_target_pairs={{0,12},{1,13},{2,14},{3,15},{4,8},{5,9},{6,10},{7,11},{8,4},{9,5},... | collective-permute-start | bytes 1327112 | tf_op jit(solution)/shard_map/ppermute | solution.py:312
  42.0 9.7 %collective-permute-start.11 = (bf16[64,3456]{1,0:T(8,128)(2,1)S(1)}, bf16[64,3456]{1,0:T(8,128)(2,1)S(1)}, u32[]{:S(2)}, u32[]{:S(2)}) collective-permute-start(bf16[64,3456]{1,0:T(8,128)(2,1)S(1)} %pad_maximum_fusion.3), channel_id=1, source_target_pairs={{0,3},{1,2},{2,1},{3,0},{4,7},{5,6},{6,5},{7,4},{8,11},{9,10},{10,... | collective-permute-start | bytes 1327112 | tf_op jit(solution)/shard_map/ppermute | solution.py:312
  42.1 10.4 %collective-permute-start.17 = (bf16[64,3456]{1,0:T(8,128)(2,1)S(1)}, bf16[64,3456]{1,0:T(8,128)(2,1)S(1)}, u32[]{:S(2)}, u32[]{:S(2)}) collective-permute-start(bf16[64,3456]{1,0:T(8,128)(2,1)S(1)} %pad_maximum_fusion.4), channel_id=1, source_target_pairs={{0,96},{1,97},{2,98},{3,99},{4,100},{5,101},{6,102},{7,103},{8,104... | collective-permute-start | bytes 1327112 | tf_op jit(solution)/shard_map/ppermute | solution.py:312
  51.7 13.7 %collective-permute-start.6 = (bf16[128,3456]{1,0:T(8,128)(2,1)S(1)}, bf16[128,3456]{1,0:T(8,128)(2,1)S(1)}, u32[]{:S(2)}, u32[]{:S(2)}) collective-permute-start(bf16[128,3456]{1,0:T(8,128)(2,1)S(1)} %get-tuple-element.18), channel_id=1, source_target_pairs={{0,3},{1,2},{2,1},{3,0},{4,7},{5,6},{6,5},{7,4},{8,11},{9,10},{10,... | collective-permute-start | bytes 2654216 | tf_op jit(solution)/shard_map/ppermute | solution.py:312
  52.6 13.9 %collective-permute-start.12 = (bf16[128,3456]{1,0:T(8,128)(2,1)S(1)}, bf16[128,3456]{1,0:T(8,128)(2,1)S(1)}, u32[]{:S(2)}, u32[]{:S(2)}) collective-permute-start(bf16[128,3456]{1,0:T(8,128)(2,1)S(1)} %get-tuple-element.16), channel_id=1, source_target_pairs={{0,96},{1,97},{2,98},{3,99},{4,100},{5,101},{6,102},{7,103},{8,104... | collective-permute-start | bytes 2654216 | tf_op jit(solution)/shard_map/ppermute | solution.py:312
  52.7 15.2 %collective-permute-start.18 = (bf16[128,3456]{1,0:T(8,128)(2,1)S(1)}, bf16[128,3456]{1,0:T(8,128)(2,1)S(1)}, u32[]{:S(2)}, u32[]{:S(2)}) collective-permute-start(bf16[128,3456]{1,0:T(8,128)(2,1)S(1)} %get-tuple-element.14), channel_id=1, source_target_pairs={{0,4},{1,5},{2,6},{3,7},{4,0},{5,1},{6,2},{7,3},{8,12},{9,13},{10,... | collective-permute-start | bytes 2654216 | tf_op jit(solution)/shard_map/ppermute | solution.py:312
  66.4 38.7 %collective-permute-start.7 = (bf16[256,3456]{1,0:T(8,128)(2,1)}, bf16[256,3456]{1,0:T(8,128)(2,1)}, u32[]{:S(2)}, u32[]{:S(2)}) collective-permute-start(bf16[256,3456]{1,0:T(8,128)(2,1)} %constant_dynamic-update-slice_fusion.5.refs_0_), channel_id=1, source_target_pairs={{0,96},{1,97},{2,98},{3,99},{4,100},{5,101},{6,102},{7,103},{8,104... | collective-permute-start | bytes 5308424 | tf_op jit(solution)/shard_map/ppermute | solution.py:312
  67.5 38.8 %collective-permute-start.13 = (bf16[256,3456]{1,0:T(8,128)(2,1)}, bf16[256,3456]{1,0:T(8,128)(2,1)}, u32[]{:S(2)}, u32[]{:S(2)}) collective-permute-start(bf16[256,3456]{1,0:T(8,128)(2,1)} %constant_dynamic-update-slice_fusion.16.refs_2_), channel_id=1, source_target_pairs={{0,4},{1,5},{2,6},{3,7},{4,0},{5,1},{6,2},{7,3},{8,12},{9,13},{10,... | collective-permute-start | bytes 5308424 | tf_op jit(solution)/shard_map/ppermute | solution.py:312
  67.9 38.5 %collective-permute-start.19 = (bf16[256,3456]{1,0:T(8,128)(2,1)S(1)}, bf16[256,3456]{1,0:T(8,128)(2,1)}, u32[]{:S(2)}, u32[]{:S(2)}) collective-permute-start(bf16[256,3456]{1,0:T(8,128)(2,1)S(1)} %constant_dynamic-update-slice_fusion.27.refs_4_), channel_id=1, source_target_pairs={{0,1},{1,0},{2,3},{3,2},{4,5},{5,4},{6,7},{7,6},{8,9},{9,8},{10,11... | collective-permute-start | bytes 5308424 | tf_op jit(solution)/shard_map/ppermute | solution.py:312
  137.9 2.6 %collective-permute-start.22 = (f32[1536,128]{1,0:T(8,128)S(1)}, f32[1536,128]{1,0:T(8,128)S(1)}, u32[]{:S(2)}, u32[]{:S(2)}) collective-permute-start(f32[1536,128]{1,0:T(8,128)S(1)} %slice_bitcast_fusion.2), channel_id=1, source_target_pairs={{0,16},{1,17},{2,18},{3,19},{4,20},{5,21},{6,22},{7,23},{8,24},{9,... | collective-permute-start | bytes 2359304 | tf_op jit(solution)/shard_map/ppermute | solution.py:312
  138.7 3.7 %collective-permute-start.20 = (bf16[384,1536]{1,0:T(8,128)(2,1)S(1)}, bf16[384,1536]{1,0:T(8,128)(2,1)S(1)}, u32[]{:S(2)}, u32[]{:S(2)}) collective-permute-start(bf16[384,1536]{1,0:T(8,128)(2,1)S(1)} %get-tuple-element.12), channel_id=1, source_target_pairs={{0,16},{1,17},{2,18},{3,19},{4,20},{5,21},{6,22},{7,23},{8,24},{9,... | collective-permute-start | bytes 3538952 | tf_op jit(solution)/shard_map/ppermute | solution.py:312
  138.8 3.6 %collective-permute-start.21 = (f32[384,128]{1,0:T(8,128)S(1)}, f32[384,128]{1,0:T(8,128)S(1)}, u32[]{:S(2)}, u32[]{:S(2)}) collective-permute-start(f32[384,128]{1,0:T(8,128)S(1)} %get-tuple-element.20), channel_id=1, source_target_pairs={{0,16},{1,17},{2,18},{3,19},{4,20},{5,21},{6,22},{7,23},{8,24},{9,... | collective-permute-start | bytes 589832 | tf_op jit(solution)/shard_map/ppermute | solution.py:312
  (10 other events, 104.4 us)
Sparse Core Ops, SparseCore 0:
  11.6 86.1 all-gather.1

commit v3 on v2

--- a/solution.py
+++ b/solution.py
@@ -31,17 +31,14 @@
 def scan_kernel(
     meta_ref,
     input_ref,
-    gate_ref,
     side_ref,
     taps_ref,
     side_taps_ref,
     bias_ref,
     log_rate_ref,
     skip_ref,
-    gain_ref,
-    gated_ref,
+    scanned_ref,
     state_ref,
-    square_ref,
     decay_col,
     delta_col,
     decay_row,
@@ -86,7 +83,6 @@
             decay_col[group] = total[:, at]
             delta_col[group] = delta[:, at]
             decay_row[group] = turned[at]
-        square_ref[...] = jnp.zeros_like(square_ref)
 
     decays = decay_col[group_here]
     deltas = delta_col[group_here]
@@ -100,9 +96,7 @@
         cols = slice(pair * LANES, (pair + 1) * LANES)
         one, two = 2 * pair, 2 * pair + 1
         x_conv = causal_conv(input_ref[:, cols].astype(F32), taps_ref[:, cols])
-        gate = silu(gate_ref[:, cols].astype(F32))
         skip = skip_ref[:, cols]
-        gain = gain_ref[:, cols]
         state = jnp.zeros((LANES, state_dim), F32)
         for block in range(blocks):
             at = slice(block * SPAN, (block + 1) * SPAN)
@@ -146,17 +140,15 @@
                 )
                 fresh = fade * state + fresh
             state = fresh
-            gated = (out + skip * x_here) * gate[at]
-            square_ref[at, :] += gated * gated
-            gated_ref[at, cols] = (gated * gain).astype(BF)
+            scanned_ref[at, cols] = out + skip * x_here
         state_ref[cols, :] = state
 
 
-def scan_gate(meta, projected, conv_weight, bias, log_rate, skip, gain, width):
+def scan(meta, projected, conv_weight, bias, log_rate, skip, width):
     rows, total = projected.shape
     seq = rows // 2
     state_dim = width // 2
-    half = (total - width - LANES) // 2
+    half = total - width - LANES
     inner = 2 * half
     cols = HEADS_STEP * LANES // 2
     groups = half // cols
@@ -168,19 +160,16 @@
         grid=(2, groups),
         in_specs=[
             pl.BlockSpec((seq, cols), lambda r, g, m: (r, g)),
-            pl.BlockSpec((seq, cols), lambda r, g, m: (r, groups + g)),
-            pl.BlockSpec((seq, width + LANES), lambda r, g, m: (r, inner // (width + LANES))),
+            pl.BlockSpec((seq, width + LANES), lambda r, g, m: (r, half // (width + LANES))),
             pl.BlockSpec((taps, cols), here),
             pl.BlockSpec((taps, width), lambda r, g, m: (0, inner // width)),
             pl.BlockSpec((1, LANES), fixed),
             pl.BlockSpec((1, LANES), fixed),
             pl.BlockSpec((1, cols), here),
-            pl.BlockSpec((1, cols), here),
         ],
         out_specs=[
             pl.BlockSpec((None, seq, cols), lambda r, g, m: (r, 0, g)),
             pl.BlockSpec((None, cols, state_dim), lambda r, g, m: (r, g, 0)),
-            pl.BlockSpec((None, seq, LANES), lambda r, g, m: (r, 0, 0)),
         ],
         scratch_shapes=[
             pltpu.VMEM((2 * groups, seq, HEADS_STEP), F32),
@@ -195,9 +184,8 @@
         scan_kernel,
         grid_spec=grid_spec,
         out_shape=[
-            jax.ShapeDtypeStruct((2, seq, half), BF),
+            jax.ShapeDtypeStruct((2, seq, half), F32),
             jax.ShapeDtypeStruct((2, half, state_dim), F32),
-            jax.ShapeDtypeStruct((2, seq, LANES), F32),
         ],
         compiler_params=pltpu.CompilerParams(
             dimension_semantics=("arbitrary", "arbitrary"), vmem_limit_bytes=40 << 20
@@ -205,31 +193,23 @@
         cost_estimate=pl.CostEstimate(
             flops=2 * inner * seq * 640, transcendentals=inner * seq * 6, bytes_accessed=9 << 20
         ),
-        name="scan_gate",
-    )(meta, projected, projected, projected, conv_weight, conv_weight, bias, log_rate, skip, gain)
+        name="scan",
+    )(meta, projected, projected, conv_weight, conv_weight, bias, log_rate, skip)
 
 
 def project_kernel(tokens_ref, *refs):
-    pieces, out_ref = refs[:-1], refs[-1]
-    depth = pieces[0].shape[0]
-    total = None
-    for index, piece in enumerate(pieces):
-        part = jnp.dot(
-            tokens_ref[:, index * depth : (index + 1) * depth],
-            piece[...],
-            preferred_element_type=F32,
-        )
-        total = part if total is None else total + part
-    out_ref[...] = total.astype(BF)
+    weight = jnp.concatenate([piece[...] for piece in refs[:-1]], axis=0)
+    refs[-1][...] = jnp.dot(tokens_ref[...], weight, preferred_element_type=F32).astype(BF)
 
 
 def project(tokens, pieces):
     rows, model = tokens.shape
     depth, total = pieces[0].shape
-    tile = total // 3
+    steps = 3
+    tile = total // steps
     return pl.pallas_call(
         project_kernel,
-        grid=(3,),
+        grid=(steps,),
         in_specs=[pl.BlockSpec((rows, model), lambda n: (0, 0))]
         + [pl.BlockSpec((depth, tile), lambda n: (0, n)) for _ in pieces],
         out_specs=pl.BlockSpec((rows, tile), lambda n: (0, n)),
@@ -238,10 +218,62 @@
             dimension_semantics=("arbitrary",), vmem_limit_bytes=40 << 20
         ),
         cost_estimate=pl.CostEstimate(
-            flops=2 * rows * model * total, transcendentals=0, bytes_accessed=20 << 20
+            flops=2 * rows * model * total, transcendentals=0, bytes_accessed=10 << 20
         ),
         name="project",
     )(tokens, *pieces)
+
+
+def gate_kernel(meta_ref, tokens_ref, scanned_ref, gain_ref, *refs):
+    gated_ref, square_ref = refs[-2:]
+    weight = jnp.concatenate([piece[...] for piece in refs[:-2]], axis=0)
+    gate = jnp.dot(tokens_ref[...], weight, preferred_element_type=F32).astype(BF)
+    gated = scanned_ref[...] * silu(gate.astype(F32))
+    gated_ref[...] = (gated * gain_ref[...]).astype(BF)
+
+    @pl.when(pl.program_id(0) == 0)
+    def _():
+        square_ref[...] = jnp.zeros_like(square_ref)
+
+    square = gated * gated
+    for at in range(0, square.shape[1], LANES):
+        square_ref[...] += square[:, at : at + LANES]
+
+
+def gating(which, meta, tokens, scanned, gain, pieces):
+    _, seq, half = scanned.shape
+    model = tokens.shape[1]
+    depth = pieces[0].shape[0]
+    steps = 3
+    tile = half // steps
+    return pl.pallas_call(
+        gate_kernel,
+        grid_spec=pltpu.PrefetchScalarGridSpec(
+            num_scalar_prefetch=1,
+            grid=(steps,),
+            in_specs=[
+                pl.BlockSpec((seq, model), lambda n, m: (which, 0)),
+                pl.BlockSpec((None, seq, tile), lambda n, m: (which, 0, n)),
+                pl.BlockSpec((1, tile), lambda n, m: (0, m[0] * steps + n)),
+            ]
+            + [pl.BlockSpec((depth, tile), lambda n, m: (0, n)) for _ in pieces],
+            out_specs=[
+                pl.BlockSpec((seq, tile), lambda n, m: (0, n)),
+                pl.BlockSpec((seq, LANES), lambda n, m: (0, 0)),
+            ],
+        ),
+        out_shape=[
+            jax.ShapeDtypeStruct((seq, half), BF),
+            jax.ShapeDtypeStruct((seq, LANES), F32),
+        ],
+        compiler_params=pltpu.CompilerParams(
+            dimension_semantics=("arbitrary",), vmem_limit_bytes=40 << 20
+        ),
+        cost_estimate=pl.CostEstimate(
+            flops=2 * seq * model * half, transcendentals=seq * half, bytes_accessed=10 << 20
+        ),
+        name="gating",
+    )(meta, tokens, scanned, gain, *pieces)
 
 
 def mix_kernel(meta_ref, mine_ref, other_ref, w_mine_ref, w_other_ref, sq_mine, sq_other, out_ref):
@@ -316,6 +348,12 @@
 
 def swap(value):
     return hop(value, lambda core: CORE)
+
+
+def double(held, step):
+    return held, [
+        hop(piece, lambda core, c=c: link_of(c, core, step)) for c, piece in enumerate(held)
+    ]
 
 
 def row_sources(me, core):
@@ -363,25 +401,34 @@
     half = inner_dim // 2
     spare = LANES - head_count
 
+    side = jnp.pad(jnp.concatenate([state_proj, step_proj], axis=1), ((0, 0), (0, spare)))
+    low = jnp.concatenate([input_proj[:, :half], side, gate_proj[:, :half]], axis=1).astype(BF)
+    high = jnp.concatenate([input_proj[:, half:], side, gate_proj[:, half:]], axis=1).astype(BF)
+    sent, out_proj = lax.optimization_barrier((jnp.where(first_core, high, low), out_proj))
+    received = swap(sent)
     padded_out = jnp.pad(out_proj.astype(BF), ((0, PADDED_ROWS - SHARD_ROWS), (0, 0)))
     out_weight = lax.all_gather(padded_out, EVERYONE, axis=0, tiled=True)
 
-    side = jnp.pad(jnp.concatenate([state_proj, step_proj], axis=1), ((0, 0), (0, spare)))
-    low = jnp.concatenate([input_proj[:, :half], gate_proj[:, :half], side], axis=1).astype(BF)
-    high = jnp.concatenate([input_proj[:, half:], gate_proj[:, half:], side], axis=1).astype(BF)
-    received = swap(jnp.where(first_core, high, low))
     kept = jnp.where(first_core, low, high)
     pair = jnp.concatenate(
         [jnp.where(first_core, kept, received), jnp.where(first_core, received, kept)], axis=0
     )
     held = [pair[8 * c : 8 * c + 8] for c in range(COLOURS)]
-    for step in range(5):
-        moved = [
-            hop(held[c], lambda core, c=c: link_of(c, core, step)) for c in range(COLOURS)
-        ]
+    for step in range(3):
+        held, moved = double(held, step)
         held = [jnp.concatenate([h, m], axis=0) for h, m in zip(held, moved)]
-    moved = [hop(held[c], lambda core, c=c: link_of(c, core, 5)) for c in range(COLOURS)]
-    pieces = [piece for both in zip(held, moved) for piece in both]
+    held, moved = double(held, 3)
+    moved, unit_id = lax.optimization_barrier((moved, unit_id))
+    held = [jnp.concatenate([h, m], axis=0) for h, m in zip(held, moved)]
+    cut = half + width + LANES
+    early, late = [h[:, :cut] for h in held], [h[:, cut:] for h in held]
+    early, moved = double(early, 4)
+    moved, late = lax.optimization_barrier((moved, late))
+    early, moved = double([jnp.concatenate([h, m], axis=0) for h, m in zip(early, moved)], 5)
+    early = [piece for both in zip(early, moved) for piece in both]
+    late, moved = double(late, 4)
+    late, moved = double([jnp.concatenate([h, m], axis=0) for h, m in zip(late, moved)], 5)
+    late = [piece for both in zip(late, moved) for piece in both]
 
     own = lax.dynamic_index_in_dim(tokens, unit_id, 0, keepdims=False)
     length = lax.dynamic_slice_in_dim(lengths, unit_id, 1, 0)
@@ -394,19 +441,22 @@
     pick = jnp.arange(model_dim, dtype=jnp.int32)[:, None] == row_sources(me, core)[None]
     both = jnp.dot(both, pick.astype(BF), preferred_element_type=F32).astype(BF)
 
-    projected = project(both, pieces)
-    gated, state, squares = scan_gate(
+    projected = project(both, early)
+    scanned, state = scan(
         meta,
         projected,
         conv_weight,
         jnp.pad(step_bias, (0, spare))[None],
         jnp.pad(log_rate, (0, spare))[None],
         jnp.repeat(skip_gain, head_dim)[None],
-        norm_gain[None],
         width,
     )
-    gated_other, squares_other, state_other = swap(gated[1]), swap(squares[1]), swap(state[1])
-    mixed = mix(meta, gated[0], gated_other, out_weight, squares[0], squares_other, model_dim)
+    state_other = swap(state[1])
+    gain = norm_gain[None]
+    sent, square_sent = gating(1, meta, both, scanned, gain, late)
+    other, square_other = swap(sent), swap(square_sent)
+    mine, square = gating(0, meta, both, scanned, gain, late)
+    mixed = mix(meta, mine, other, out_weight, square, square_other, model_dim)
     state = jnp.concatenate(
         [jnp.where(first_core, state[0], state_other), jnp.where(first_core, state_other, state[0])]
     )

time: 160 us -> 165 us (1.031)
  waiting for transfers between devices: 56.4 us -> 36.4 us
  starting transfers between devices: 18 us -> 36.3 us
  other arithmetic: 6.1 us -> 10.7 us
    ppermute x23 -> x29, waiting for transfers between devices: 56.4 us -> 36.4 us  [hop(): lax.ppermute(value, EVERYONE, [(d, d ^ mask_of(d // CORE % 2)) for d in r...]
    ppermute x23 -> x29, starting transfers between devices: 18 us -> 36.3 us  [hop(): lax.ppermute(value, EVERYONE, [(d, d ^ mask_of(d // CORE % 2)) for d in r...]
    concatenate x0 -> x3, other arithmetic: none -> 3.31 us  [body(): jnp.concatenate([h, m], axis=0)]
    another operation x3, other arithmetic: 0.04 us -> 2.63 us
    slice x1 -> x7, local copies, waits for them, and re-layouts: 0.02 us -> 2.23 us  [the longest x6 2.22 us: body(): early, late = ([h[:, :cut] for h in held], [h[:, cut:] for h in held])]
    pallas_call x2 -> x4, Pallas kernels: 28.9 us -> 30.3 us  [the longest x1 15.3 us: scan(): pl.pallas_call(scan_kernel, grid_spec=grid_spec, out_shape=[jax.ShapeDtyp...]
    unnamed x30 -> x40, local copies, waits for them, and re-layouts: 7.24 us -> 8.31 us
    concatenate x6 -> x3, local copies, waits for them, and re-layouts: 3.89 us -> 2.89 us  [body(): held = [jnp.concatenate([h, m], axis=0) for h, m in zip(held, moved)]]
  transfers between devices with their start and end apart: 24 -> 30, of which waited for: 11 -> 15; matrix products, arithmetic and copies ran while one was open for 15% -> 13% of each run, Pallas kernels for 18% -> 18%
where the time goes in v3:
time: 165 us; the launch traced here: 164 us
  Pallas kernels  40.6 us (25%)
  waiting for transfers between devices  36.4 us (22%)
  starting transfers between devices  36.3 us (22%)
  between operations  18.5 us (11%)
  local copies, waits for them, and re-layouts  17.5 us (11%)
  other arithmetic  10.7 us (6%)
  matrix products  4.12 us (2%)
    ppermute x29, waiting for transfers between devices, hop(): lax.ppermute(value, EVERYONE, [(d, d ^ mask_of(d // CORE % 2)) for d in r...  36.4 us
    ppermute x29, starting transfers between devices, hop(): lax.ppermute(value, EVERYONE, [(d, d ^ mask_of(d // CORE % 2)) for d in r...  36.3 us
    pallas_call x1, Pallas kernels, scan(): pl.pallas_call(scan_kernel, grid_spec=grid_spec, out_shape=[jax.ShapeDtyp...  15.3 us
    pallas_call x1, Pallas kernels, mix(): pl.pallas_call(mix_kernel, grid_spec=pltpu.PrefetchScalarGridSpec(num_sca...  10.2 us
    unnamed x40, local copies, waits for them, and re-layouts  8.31 us
    pallas_call x2, Pallas kernels, gating(): pl.pallas_call(gate_kernel, grid_spec=pltpu.PrefetchScalarGridSpec(num_sc...  8.27 us
    pallas_call x1, Pallas kernels, project(): pl.pallas_call(project_kernel, grid=(steps,), in_specs=[pl.BlockSpec((row...  6.78 us
    dot_general x1, matrix products, body(): both = jnp.dot(both, pick.astype(BF), preferred_element_type=F32).astype(BF)  4.12 us
  transfers between devices with their start and end apart: 30, of which 15 were waited for; matrix products, arithmetic and copies ran while one was open for 13% of the time, Pallas kernels for 18%

profile of v3, /device:TPU:1, one launch (start us, length us, event | category | flops | bytes accessed | tf_op | source)
XLA Modules:
  0.0 164.1 jit_solution(7385836853102517971)
XLA Ops:
  11.6 1.5 collective-permute-start
  14.8 3.9 %collective-permute-start.9 = (bf16[8,3456]{1,0:T(8,128)(2,1)S(1)}, bf16[8,3456]{1,0:T(8,128)(2,1)S(1)}, u32[]{:S(2)}, u32[]{:S(2)}) collective-permute-start(bf16[8,3456]{1,0:T(8,128)(2,1)S(1)} %get-tuple-element.45), channel_id=1, source_target_pairs={{0,32},{1,33},{2,34},{3,35},{4,36},{5,37},{6,38},{7,39},{8,40},{9,... | collective-permute-start | bytes 165896 | tf_op jit(solution)/shard_map/ppermute | solution.py:344
  18.8 2.8 %collective-permute-start.5 = (bf16[8,3456]{1,0:T(8,128)(2,1)S(1)}, bf16[8,3456]{1,0:T(8,128)(2,1)S(1)}, u32[]{:S(2)}, u32[]{:S(2)}) collective-permute-start(bf16[8,3456]{1,0:T(8,128)(2,1)S(1)} %get-tuple-element.47), channel_id=1, source_target_pairs={{0,1},{1,0},{2,3},{3,2},{4,5},{5,4},{6,7},{7,6},{8,9},{9,8},{10,11... | collective-permute-start | bytes 165896 | tf_op jit(solution)/shard_map/ppermute | solution.py:344
  21.6 2.5 %collective-permute-start.1 = (bf16[8,3456]{1,0:T(8,128)(2,1)S(1)}, bf16[8,3456]{1,0:T(8,128)(2,1)S(1)}, u32[]{:S(2)}, u32[]{:S(2)}) collective-permute-start(bf16[8,3456]{1,0:T(8,128)(2,1)S(1)} %get-tuple-element.49), channel_id=1, source_target_pairs={{0,4},{1,5},{2,6},{3,7},{4,0},{5,1},{6,2},{7,3},{8,12},{9,13},{10,... | collective-permute-start | bytes 165896 | tf_op jit(solution)/shard_map/ppermute | solution.py:344
  24.3 2.3 %collective-permute-done.1 = bf16[8,3456]{1,0:T(8,128)(2,1)S(1)} collective-permute-done((bf16[8,3456]{1,0:T(8,128)(2,1)S(1)}, bf16[8,3456]{1,0:T(8,128)(2,1)S(1)}, u32[]{:S(2)}, u32[]{:S(2)}) %collective-permute-start.1) | collective-permute-done | bytes 55328 | tf_op jit(solution)/shard_map/ppermute | solution.py:344
  29.2 1.5 collective-permute-start.7
  35.3 3.1 %collective-permute-done.3 = bf16[32,3456]{1,0:T(8,128)(2,1)S(1)} collective-permute-done((bf16[32,3456]{1,0:T(8,128)(2,1)S(1)}, bf16[32,3456]{1,0:T(8,128)(2,1)S(1)}, u32[]{:S(2)}, u32[]{:S(2)}) %collective-permute-start.3) | collective-permute-done | bytes 221216 | tf_op jit(solution)/shard_map/ppermute | solution.py:344
  39.3 3.0 %collective-permute-done.12 = bf16[64,3456]{1,0:T(8,128)(2,1)} collective-permute-done((bf16[64,3456]{1,0:T(8,128)(2,1)S(1)}, bf16[64,3456]{1,0:T(8,128)(2,1)}, u32[]{:S(2)}, u32[]{:S(2)}) %collective-permute-start.12) | collective-permute-done | bytes 442400 | tf_op jit(solution)/shard_map/ppermute | solution.py:344
  42.6 3.5 %collective-permute-done.4 = bf16[64,3456]{1,0:T(8,128)(2,1)S(1)} collective-permute-done((bf16[64,3456]{1,0:T(8,128)(2,1)S(1)}, bf16[64,3456]{1,0:T(8,128)(2,1)S(1)}, u32[]{:S(2)}, u32[]{:S(2)}) %collective-permute-start.4) | collective-permute-done | bytes 442400 | tf_op jit(solution)/shard_map/ppermute | solution.py:344
  46.1 1.8 %constant_dynamic-update-slice_fusion.10 = bf16[128,3456]{1,0:T(8,128)(2,1)} fusion(bf16[128,3456]{1,0:T(8,128)(2,1)} %constant_dynamic-update-slice_fusion.11, bf16[64,3456]{1,0:T(8,128)(2,1)} %collective-permute-done.12), kind=kLoop, calls=%fused_computation.49 | loop fusion | bytes 884736 | tf_op jit(solution)/shard_map/concatenate | solution.py:422
  48.9 3.2 %collective-permute-start.16 = (bf16[128,1920]{1,0:T(8,128)(2,1)S(1)}, bf16[128,1920]{1,0:T(8,128)(2,1)}, u32[]{:S(2)}, u32[]{:S(2)}) collective-permute-start(bf16[128,1920]{1,0:T(8,128)(2,1)S(1)} %slice.93), channel_id=1, source_target_pairs={{0,4},{1,5},{2,6},{3,7},{4,0},{5,1},{6,2},{7,3},{8,12},{9,13},{10,... | collective-permute-start | bytes 1474568 | tf_op jit(solution)/shard_map/ppermute | solution.py:344
  59.4 6.7 %collective-permute-start.13 = (bf16[392,1536]{1,0:T(8,128)(2,1)S(1)}, bf16[392,1536]{1,0:T(8,128)(2,1)S(1)}, u32[]{:S(2)}, u32[]{:S(2)}) collective-permute-start(bf16[392,1536]{1,0:T(8,128)(2,1)S(1)} %pad_maximum_fusion.1), channel_id=1, source_target_pairs={{0,16},{1,17},{2,18},{3,19},{4,20},{5,21},{6,22},{7,23},{8,24},{9,... | collective-permute-start | bytes 3612680 | tf_op jit(solution)/shard_map/ppermute | solution.py:344
  67.2 3.0 %collective-permute-start.19 = (bf16[256,1920]{1,0:T(8,128)(2,1)S(1)}, bf16[256,1920]{1,0:T(8,128)(2,1)S(1)}, u32[]{:S(2)}, u32[]{:S(2)}) collective-permute-start(bf16[256,1920]{1,0:T(8,128)(2,1)S(1)} %pad_maximum_fusion.4.refs_4_), channel_id=1, source_target_pairs={{0,1},{1,0},{2,3},{3,2},{4,5},{5,4},{6,7},{7,6},{8,9},{9,8},{10,11... | collective-permute-start | bytes 2949128 | tf_op jit(solution)/shard_map/ppermute | solution.py:344
  72.9 14.0 %collective-permute-done.24 = bf16[128,1536]{1,0:T(8,128)(2,1)S(1)} collective-permute-done((bf16[128,1536]{1,0:T(8,128)(2,1)S(1)}, bf16[128,1536]{1,0:T(8,128)(2,1)S(1)}, u32[]{:S(2)}, u32[]{:S(2)}) %collective-permute-start.24) | collective-permute-done | bytes 393248 | tf_op jit(solution)/shard_map/ppermute | solution.py:344
  87.9 4.2 %collective-permute-done.20 = bf16[128,1536]{1,0:T(8,128)(2,1)S(1)} collective-permute-done((bf16[128,1536]{1,0:T(8,128)(2,1)S(1)}, bf16[128,1536]{1,0:T(8,128)(2,1)S(1)}, u32[]{:S(2)}, u32[]{:S(2)}) %collective-permute-start.20) | collective-permute-done | bytes 393248 | tf_op jit(solution)/shard_map/ppermute | solution.py:344
  93.4 1.8 %collective-permute-start.23 = (bf16[256,1536]{1,0:T(8,128)(2,1)S(1)}, bf16[256,1536]{1,0:T(8,128)(2,1)S(1)}, u32[]{:S(2)}, u32[]{:S(2)}) collective-permute-start(bf16[256,1536]{1,0:T(8,128)(2,1)S(1)} %constant_dynamic-update-slice_fusion.17.refs_2_), channel_id=1, source_target_pairs={{0,4},{1,5},{2,6},{3,7},{4,0},{5,1},{6,2},{7,3},{8,12},{9,13},{10,... | collective-permute-start | bytes 2359304 | tf_op jit(solution)/shard_map/ppermute | solution.py:344
  97.9 4.1 %fusion.2.tokens_ref = bf16[768,1536]{1,0:T(8,128)(2,1)S(1)} fusion(s32[1536]{0:T(1024)S(1)} %pad_add_fusion, bf16[384,1536]{1,0:T(8,128)(2,1)S(1)} %slice.90, bf16[384,1536]{1,0:T(8,128)(2,1)S(1)} %dynamic-slice_bitcast_fusion), kind=kOutput, calls=%fused_computation.3 | convolution fusion | flops 3632136192 | bytes 4724736 | tf_op jit(solution)/shard_map/dot_general | solution.py:442
  103.7 6.8 %project.1.input_ref.side_ref = bf16[768,1920]{1,0:T(8,128)(2,1)S(1)} custom-call(bf16[768,1536]{1,0:T(8,128)(2,1)S(1)} %fusion.2.tokens_ref, bf16[256,1920]{1,0:T(8,128)(2,1)S(1)} %pad_maximum_fusion.2.refs_0_, bf16[256,1920]{1,0:T(8,128)(2,1)S(1)} %collective-permute-done.17.refs_1_, bf16[256,1920]{1,0:T(8,128)(2,1)S(1)} %pad_maximum_fusion.3.refs_2_, ...), custom_call_target="tpu_custom_call" | custom-call | flops 4529848320 | bytes 10485760 | tf_op jit(solution)/shard_map/project/pallas_call | solution.py:210
  110.5 15.3 %scan.1 = (f32[2,384,1536]{2,1,0:T(8,128)S(1)}, f32[2,1536,128]{2,1,0:T(8,128)S(1)}) custom-call(s32[3]{0:T(128)S(1)} %pad_add_fusion.1.meta_ref, bf16[768,1920]{1,0:T(8,128)(2,1)S(1)} %project.1.input_ref.side_ref, bf16[768,1920]{1,0:T(8,128)(2,1)S(1)} %project.1.input_ref.side_ref, f32[4,3328]{1,0:T(4,128)S(1)} %copy-done.9, f32[4,3328]{1,0:T(4,128)S(1)} %copy-done.9, ...), custom_call_target="tpu_custom_call" | custom-call | flops 1509949440 | bytes 9437184 | tf_op jit(solution)/shard_map/scan/pallas_call | solution.py:183
  125.8 4.4 %collective-permute-start.28 = (f32[1536,128]{1,0:T(8,128)S(1)}, f32[1536,128]{1,0:T(8,128)S(1)}, u32[]{:S(2)}, u32[]{:S(2)}) collective-permute-start(f32[1536,128]{1,0:T(8,128)S(1)} %slice_bitcast_fusion), channel_id=1, source_target_pairs={{0,16},{1,17},{2,18},{3,19},{4,20},{5,21},{6,22},{7,23},{8,24},{9,... | collective-permute-start | bytes 2359304 | tf_op jit(solution)/shard_map/ppermute | solution.py:344
  130.3 4.1 %gating.3 = (bf16[384,1536]{1,0:T(8,128)(2,1)S(1)}, f32[384,128]{1,0:T(8,128)S(1)}) custom-call(s32[3]{0:T(128)S(1)} %pad_add_fusion.1.meta_ref, bf16[768,1536]{1,0:T(8,128)(2,1)S(1)} %fusion.2.tokens_ref, f32[2,384,1536]{2,1,0:T(8,128)S(1)} %get-tuple-element.28.scanned_ref, f32[1,3072]{1,0:T(1,128)S(1)} %bitcast.18, ...), custom_call_target="tpu_custom_call" | custom-call | flops 1811939328 | bytes 10485760 | tf_op jit(solution)/shard_map/gating/pallas_call | solution.py:249
  135.0 4.1 %gating.2 = (bf16[384,1536]{1,0:T(8,128)(2,1)S(1)}, f32[384,128]{1,0:T(8,128)S(1)}) custom-call(s32[3]{0:T(128)S(1)} %pad_add_fusion.1.meta_ref, bf16[768,1536]{1,0:T(8,128)(2,1)S(1)} %fusion.2.tokens_ref, f32[2,384,1536]{2,1,0:T(8,128)S(1)} %get-tuple-element.28.scanned_ref, f32[1,3072]{1,0:T(1,128)S(1)} %bitcast.19, ...), custom_call_target="tpu_custom_call" | custom-call | flops 1811939328 | bytes 10485760 | tf_op jit(solution)/shard_map/gating/pallas_call | solution.py:249
  139.3 1.5 pad_maximum_fusion
  147.0 10.2 %mix.1 = bf16[384,1536]{1,0:T(8,128)(2,1)} custom-call(s32[3]{0:T(128)S(1)} %pad_add_fusion.1.meta_ref, bf16[384,1536]{1,0:T(8,128)(2,1)S(1)} %copy-done.3, bf16[384,1536]{1,0:T(8,128)(2,1)S(1)} %copy-done.1, bf16[2048,3072]{1,0:T(8,128)(2,1)} %all-gather.2.cloned.1.call-done.w_mine_ref.w_other_ref, ...), custom_call_target="tpu_custom_call" | custom-call | flops 7247757312 | bytes 16777216 | tf_op jit(solution)/shard_map/mix/pallas_call | solution.py:303
  (145 shorter events, 36.2 us)
Async XLA Ops:
  7.2 135.4 %all-gather.2.cloned.1.call-start = ((), (), s32[]{:S(2)}) async-start(), calls=%async_computation | async-start | bytes 12681216 | tf_op jit(solution)/shard_map/all_gather | solution.py:410
  14.8 9.3 %collective-permute-start.9 = (bf16[8,3456]{1,0:T(8,128)(2,1)S(1)}, bf16[8,3456]{1,0:T(8,128)(2,1)S(1)}, u32[]{:S(2)}, u32[]{:S(2)}) collective-permute-start(bf16[8,3456]{1,0:T(8,128)(2,1)S(1)} %get-tuple-element.45), channel_id=1, source_target_pairs={{0,32},{1,33},{2,34},{3,35},{4,36},{5,37},{6,38},{7,39},{8,40},{9,... | collective-permute-start | bytes 165896 | tf_op jit(solution)/shard_map/ppermute | solution.py:344
  28.1 5.5 %collective-permute-start.11 = (bf16[32,3456]{1,0:T(8,128)(2,1)S(1)}, bf16[32,3456]{1,0:T(8,128)(2,1)S(1)}, u32[]{:S(2)}, u32[]{:S(2)}) collective-permute-start(bf16[32,3456]{1,0:T(8,128)(2,1)S(1)} %pad_maximum_fusion.10), channel_id=1, source_target_pairs={{0,3},{1,2},{2,1},{3,0},{4,7},{5,6},{6,5},{7,4},{8,11},{9,10},{10,... | collective-permute-start | bytes 663560 | tf_op jit(solution)/shard_map/ppermute | solution.py:344
  29.2 5.6 %collective-permute-start.7 = (bf16[32,3456]{1,0:T(8,128)(2,1)S(1)}, bf16[32,3456]{1,0:T(8,128)(2,1)S(1)}, u32[]{:S(2)}, u32[]{:S(2)}) collective-permute-start(bf16[32,3456]{1,0:T(8,128)(2,1)S(1)} %pad_maximum_fusion.9), channel_id=1, source_target_pairs={{0,12},{1,13},{2,14},{3,15},{4,8},{5,9},{6,10},{7,11},{8,4},{9,5},... | collective-permute-start | bytes 663560 | tf_op jit(solution)/shard_map/ppermute | solution.py:344
  32.1 6.2 %collective-permute-start.3 = (bf16[32,3456]{1,0:T(8,128)(2,1)S(1)}, bf16[32,3456]{1,0:T(8,128)(2,1)S(1)}, u32[]{:S(2)}, u32[]{:S(2)}) collective-permute-start(bf16[32,3456]{1,0:T(8,128)(2,1)S(1)} %pad_maximum_fusion.8), channel_id=1, source_target_pairs={{0,32},{1,33},{2,34},{3,35},{4,36},{5,37},{6,38},{7,39},{8,40},{9,... | collective-permute-start | bytes 663560 | tf_op jit(solution)/shard_map/ppermute | solution.py:344
  33.6 8.6 %collective-permute-start.12 = (bf16[64,3456]{1,0:T(8,128)(2,1)S(1)}, bf16[64,3456]{1,0:T(8,128)(2,1)}, u32[]{:S(2)}, u32[]{:S(2)}) collective-permute-start(bf16[64,3456]{1,0:T(8,128)(2,1)S(1)} %pad_maximum_fusion.7), channel_id=1, source_target_pairs={{0,96},{1,97},{2,98},{3,99},{4,100},{5,101},{6,102},{7,103},{8,104... | collective-permute-start | bytes 1327112 | tf_op jit(solution)/shard_map/ppermute | solution.py:344
  34.8 7.8 %collective-permute-start.8 = (bf16[64,3456]{1,0:T(8,128)(2,1)S(1)}, bf16[64,3456]{1,0:T(8,128)(2,1)}, u32[]{:S(2)}, u32[]{:S(2)}) collective-permute-start(bf16[64,3456]{1,0:T(8,128)(2,1)S(1)} %pad_maximum_fusion.6), channel_id=1, source_target_pairs={{0,3},{1,2},{2,1},{3,0},{4,7},{5,6},{6,5},{7,4},{8,11},{9,10},{10,... | collective-permute-start | bytes 1327112 | tf_op jit(solution)/shard_map/ppermute | solution.py:344
  38.4 7.6 %collective-permute-start.4 = (bf16[64,3456]{1,0:T(8,128)(2,1)S(1)}, bf16[64,3456]{1,0:T(8,128)(2,1)S(1)}, u32[]{:S(2)}, u32[]{:S(2)}) collective-permute-start(bf16[64,3456]{1,0:T(8,128)(2,1)S(1)} %pad_maximum_fusion.5), channel_id=1, source_target_pairs={{0,12},{1,13},{2,14},{3,15},{4,8},{5,9},{6,10},{7,11},{8,4},{9,5},... | collective-permute-start | bytes 1327112 | tf_op jit(solution)/shard_map/ppermute | solution.py:344
  48.9 17.2 %collective-permute-start.16 = (bf16[128,1920]{1,0:T(8,128)(2,1)S(1)}, bf16[128,1920]{1,0:T(8,128)(2,1)}, u32[]{:S(2)}, u32[]{:S(2)}) collective-permute-start(bf16[128,1920]{1,0:T(8,128)(2,1)S(1)} %slice.93), channel_id=1, source_target_pairs={{0,4},{1,5},{2,6},{3,7},{4,0},{5,1},{6,2},{7,3},{8,12},{9,13},{10,... | collective-permute-start | bytes 1474568 | tf_op jit(solution)/shard_map/ppermute | solution.py:344
  53.3 12.9 %collective-permute-start.15 = (bf16[128,1920]{1,0:T(8,128)(2,1)S(1)}, bf16[128,1920]{1,0:T(8,128)(2,1)}, u32[]{:S(2)}, u32[]{:S(2)}) collective-permute-start(bf16[128,1920]{1,0:T(8,128)(2,1)S(1)} %slice.92), channel_id=1, source_target_pairs={{0,96},{1,97},{2,98},{3,99},{4,100},{5,101},{6,102},{7,103},{8,104... | collective-permute-start | bytes 1474568 | tf_op jit(solution)/shard_map/ppermute | solution.py:344
  53.4 12.7 %collective-permute-start.14 = (bf16[128,1920]{1,0:T(8,128)(2,1)S(1)}, bf16[128,1920]{1,0:T(8,128)(2,1)}, u32[]{:S(2)}, u32[]{:S(2)}) collective-permute-start(bf16[128,1920]{1,0:T(8,128)(2,1)S(1)} %slice.91), channel_id=1, source_target_pairs={{0,3},{1,2},{2,1},{3,0},{4,7},{5,6},{6,5},{7,4},{8,11},{9,10},{10,... | collective-permute-start | bytes 1474568 | tf_op jit(solution)/shard_map/ppermute | solution.py:344
  59.4 34.0 %collective-permute-start.13 = (bf16[392,1536]{1,0:T(8,128)(2,1)S(1)}, bf16[392,1536]{1,0:T(8,128)(2,1)S(1)}, u32[]{:S(2)}, u32[]{:S(2)}) collective-permute-start(bf16[392,1536]{1,0:T(8,128)(2,1)S(1)} %pad_maximum_fusion.1), channel_id=1, source_target_pairs={{0,16},{1,17},{2,18},{3,19},{4,20},{5,21},{6,22},{7,23},{8,24},{9,... | collective-permute-start | bytes 3612680 | tf_op jit(solution)/shard_map/ppermute | solution.py:344
  67.2 35.2 %collective-permute-start.19 = (bf16[256,1920]{1,0:T(8,128)(2,1)S(1)}, bf16[256,1920]{1,0:T(8,128)(2,1)S(1)}, u32[]{:S(2)}, u32[]{:S(2)}) collective-permute-start(bf16[256,1920]{1,0:T(8,128)(2,1)S(1)} %pad_maximum_fusion.4.refs_4_), channel_id=1, source_target_pairs={{0,1},{1,0},{2,3},{3,2},{4,5},{5,4},{6,7},{7,6},{8,9},{9,8},{10,11... | collective-permute-start | bytes 2949128 | tf_op jit(solution)/shard_map/ppermute | solution.py:344
  70.2 16.6 %collective-permute-start.24 = (bf16[128,1536]{1,0:T(8,128)(2,1)S(1)}, bf16[128,1536]{1,0:T(8,128)(2,1)S(1)}, u32[]{:S(2)}, u32[]{:S(2)}) collective-permute-start(bf16[128,1536]{1,0:T(8,128)(2,1)S(1)} %slice.96), channel_id=1, source_target_pairs={{0,4},{1,5},{2,6},{3,7},{4,0},{5,1},{6,2},{7,3},{8,12},{9,13},{10,... | collective-permute-start | bytes 1179656 | tf_op jit(solution)/shard_map/ppermute | solution.py:344
  72.5 15.4 %collective-permute-start.22 = (bf16[128,1536]{1,0:T(8,128)(2,1)S(1)}, bf16[128,1536]{1,0:T(8,128)(2,1)S(1)}, u32[]{:S(2)}, u32[]{:S(2)}) collective-permute-start(bf16[128,1536]{1,0:T(8,128)(2,1)S(1)} %slice.95), channel_id=1, source_target_pairs={{0,96},{1,97},{2,98},{3,99},{4,100},{5,101},{6,102},{7,103},{8,104... | collective-permute-start | bytes 1179656 | tf_op jit(solution)/shard_map/ppermute | solution.py:344
  72.6 19.5 %collective-permute-start.20 = (bf16[128,1536]{1,0:T(8,128)(2,1)S(1)}, bf16[128,1536]{1,0:T(8,128)(2,1)S(1)}, u32[]{:S(2)}, u32[]{:S(2)}) collective-permute-start(bf16[128,1536]{1,0:T(8,128)(2,1)S(1)} %slice.94), channel_id=1, source_target_pairs={{0,3},{1,2},{2,1},{3,0},{4,7},{5,6},{6,5},{7,4},{8,11},{9,10},{10,... | collective-permute-start | bytes 1179656 | tf_op jit(solution)/shard_map/ppermute | solution.py:344
  86.9 16.8 %collective-permute-start.18 = (bf16[256,1920]{1,0:T(8,128)(2,1)S(1)}, bf16[256,1920]{1,0:T(8,128)(2,1)S(1)}, u32[]{:S(2)}, u32[]{:S(2)}) collective-permute-start(bf16[256,1920]{1,0:T(8,128)(2,1)S(1)} %pad_maximum_fusion.3.refs_2_), channel_id=1, source_target_pairs={{0,4},{1,5},{2,6},{3,7},{4,0},{5,1},{6,2},{7,3},{8,12},{9,13},{10,... | collective-permute-start | bytes 2949128 | tf_op jit(solution)/shard_map/ppermute | solution.py:344
  87.9 15.8 %collective-permute-start.17 = (bf16[256,1920]{1,0:T(8,128)(2,1)S(1)}, bf16[256,1920]{1,0:T(8,128)(2,1)S(1)}, u32[]{:S(2)}, u32[]{:S(2)}) collective-permute-start(bf16[256,1920]{1,0:T(8,128)(2,1)S(1)} %pad_maximum_fusion.2.refs_0_), channel_id=1, source_target_pairs={{0,96},{1,97},{2,98},{3,99},{4,100},{5,101},{6,102},{7,103},{8,104... | collective-permute-start | bytes 2949128 | tf_op jit(solution)/shard_map/ppermute | solution.py:344
  92.1 38.1 %collective-permute-start.25 = (bf16[256,1536]{1,0:T(8,128)(2,1)S(1)}, bf16[256,1536]{1,0:T(8,128)(2,1)S(1)}, u32[]{:S(2)}, u32[]{:S(2)}) collective-permute-start(bf16[256,1536]{1,0:T(8,128)(2,1)S(1)} %constant_dynamic-update-slice_fusion.19.refs_4_), channel_id=1, source_target_pairs={{0,1},{1,0},{2,3},{3,2},{4,5},{5,4},{6,7},{7,6},{8,9},{9,8},{10,11... | collective-permute-start | bytes 2359304 | tf_op jit(solution)/shard_map/ppermute | solution.py:344
  93.4 36.9 %collective-permute-start.23 = (bf16[256,1536]{1,0:T(8,128)(2,1)S(1)}, bf16[256,1536]{1,0:T(8,128)(2,1)S(1)}, u32[]{:S(2)}, u32[]{:S(2)}) collective-permute-start(bf16[256,1536]{1,0:T(8,128)(2,1)S(1)} %constant_dynamic-update-slice_fusion.17.refs_2_), channel_id=1, source_target_pairs={{0,4},{1,5},{2,6},{3,7},{4,0},{5,1},{6,2},{7,3},{8,12},{9,13},{10,... | collective-permute-start | bytes 2359304 | tf_op jit(solution)/shard_map/ppermute | solution.py:344
  102.4 27.8 %collective-permute-start.21 = (bf16[256,1536]{1,0:T(8,128)(2,1)S(1)}, bf16[256,1536]{1,0:T(8,128)(2,1)S(1)}, u32[]{:S(2)}, u32[]{:S(2)}) collective-permute-start(bf16[256,1536]{1,0:T(8,128)(2,1)S(1)} %constant_dynamic-update-slice_fusion.15.refs_0_), channel_id=1, source_target_pairs={{0,96},{1,97},{2,98},{3,99},{4,100},{5,101},{6,102},{7,103},{8,104... | collective-permute-start | bytes 2359304 | tf_op jit(solution)/shard_map/ppermute | solution.py:344
  125.8 13.3 %collective-permute-start.28 = (f32[1536,128]{1,0:T(8,128)S(1)}, f32[1536,128]{1,0:T(8,128)S(1)}, u32[]{:S(2)}, u32[]{:S(2)}) collective-permute-start(f32[1536,128]{1,0:T(8,128)S(1)} %slice_bitcast_fusion), channel_id=1, source_target_pairs={{0,16},{1,17},{2,18},{3,19},{4,20},{5,21},{6,22},{7,23},{8,24},{9,... | collective-permute-start | bytes 2359304 | tf_op jit(solution)/shard_map/ppermute | solution.py:344
  134.4 7.1 %collective-permute-start.26 = (bf16[384,1536]{1,0:T(8,128)(2,1)S(1)}, bf16[384,1536]{1,0:T(8,128)(2,1)S(1)}, u32[]{:S(2)}, u32[]{:S(2)}) collective-permute-start(bf16[384,1536]{1,0:T(8,128)(2,1)S(1)} %get-tuple-element.33), channel_id=1, source_target_pairs={{0,16},{1,17},{2,18},{3,19},{4,20},{5,21},{6,22},{7,23},{8,24},{9,... | collective-permute-start | bytes 3538952 | tf_op jit(solution)/shard_map/ppermute | solution.py:344
  134.5 6.3 %collective-permute-start.27 = (f32[384,128]{1,0:T(8,128)S(1)}, f32[384,128]{1,0:T(8,128)S(1)}, u32[]{:S(2)}, u32[]{:S(2)}) collective-permute-start(f32[384,128]{1,0:T(8,128)S(1)} %get-tuple-element.36), channel_id=1, source_target_pairs={{0,16},{1,17},{2,18},{3,19},{4,20},{5,21},{6,22},{7,23},{8,24},{9,... | collective-permute-start | bytes 589832 | tf_op jit(solution)/shard_map/ppermute | solution.py:344
  (20 other events, 101.9 us)
Sparse Core Ops, SparseCore 0:
  11.7 90.4 all-gather.1

commit v4 on v3

--- a/solution.py
+++ b/solution.py
@@ -11,6 +11,10 @@
 EPSILON = 1e-05
 BF = jnp.bfloat16
 F32 = jnp.float32
+
+
+def in_hbm(value):
+    return pltpu.with_memory_space_constraint(value, pltpu.HBM)
 
 
 def silu(v):
@@ -96,7 +100,8 @@
         cols = slice(pair * LANES, (pair + 1) * LANES)
         one, two = 2 * pair, 2 * pair + 1
         x_conv = causal_conv(input_ref[:, cols].astype(F32), taps_ref[:, cols])
-        skip = skip_ref[:, cols]
+        head = group_here * HEADS_STEP + one
+        skip = jnp.where(left[:1], skip_ref[head], skip_ref[head + 1])
         state = jnp.zeros((LANES, state_dim), F32)
         for block in range(blocks):
             at = slice(block * SPAN, (block + 1) * SPAN)
@@ -165,7 +170,7 @@
             pl.BlockSpec((taps, width), lambda r, g, m: (0, inner // width)),
             pl.BlockSpec((1, LANES), fixed),
             pl.BlockSpec((1, LANES), fixed),
-            pl.BlockSpec((1, cols), here),
+            pl.BlockSpec(memory_space=pltpu.SMEM),
         ],
         out_specs=[
             pl.BlockSpec((None, seq, cols), lambda r, g, m: (r, 0, g)),
@@ -184,11 +189,11 @@
         scan_kernel,
         grid_spec=grid_spec,
         out_shape=[
-            jax.ShapeDtypeStruct((2, seq, half), F32),
-            jax.ShapeDtypeStruct((2, half, state_dim), F32),
+            pltpu.HBM((2, seq, half), F32),
+            pltpu.HBM((2, half, state_dim), F32),
         ],
         compiler_params=pltpu.CompilerParams(
-            dimension_semantics=("arbitrary", "arbitrary"), vmem_limit_bytes=40 << 20
+            dimension_semantics=("arbitrary", "arbitrary"), vmem_limit_bytes=24 << 20
         ),
         cost_estimate=pl.CostEstimate(
             flops=2 * inner * seq * 640, transcendentals=inner * seq * 6, bytes_accessed=9 << 20
@@ -215,7 +220,7 @@
         out_specs=pl.BlockSpec((rows, tile), lambda n: (0, n)),
         out_shape=jax.ShapeDtypeStruct((rows, total), BF),
         compiler_params=pltpu.CompilerParams(
-            dimension_semantics=("arbitrary",), vmem_limit_bytes=40 << 20
+            dimension_semantics=("arbitrary",), vmem_limit_bytes=24 << 20
         ),
         cost_estimate=pl.CostEstimate(
             flops=2 * rows * model * total, transcendentals=0, bytes_accessed=10 << 20
@@ -263,42 +268,71 @@
             ],
         ),
         out_shape=[
-            jax.ShapeDtypeStruct((seq, half), BF),
-            jax.ShapeDtypeStruct((seq, LANES), F32),
+            pltpu.HBM((seq, half), BF),
+            pltpu.HBM((seq, LANES), F32),
         ],
         compiler_params=pltpu.CompilerParams(
-            dimension_semantics=("arbitrary",), vmem_limit_bytes=40 << 20
+            dimension_semantics=("arbitrary",), vmem_limit_bytes=24 << 20
         ),
         cost_estimate=pl.CostEstimate(
             flops=2 * seq * model * half, transcendentals=seq * half, bytes_accessed=10 << 20
         ),
         name="gating",
-    )(meta, tokens, scanned, gain, *pieces)
-
-
-def mix_kernel(meta_ref, mine_ref, other_ref, w_mine_ref, w_other_ref, sq_mine, sq_other, out_ref):
+    )(meta, tokens, in_hbm(scanned), gain, *map(in_hbm, pieces))
+
+
+def share_kernel(gated_ref, weight_ref, out_ref):
+    out_ref[...] = lax.dot_general(
+        gated_ref[...], weight_ref[...], (((1,), (1,)), ((), ())), preferred_element_type=F32
+    )
+
+
+def out_share(gated, weight):
+    seq, half = gated.shape
+    model = weight.shape[0]
+    steps = 4
+    tile = model // steps
+    return pl.pallas_call(
+        share_kernel,
+        grid=(steps,),
+        in_specs=[
+            pl.BlockSpec((seq, half), lambda n: (0, 0)),
+            pl.BlockSpec((tile, half), lambda n: (n, 0)),
+        ],
+        out_specs=pl.BlockSpec((seq, tile), lambda n: (0, n)),
+        out_shape=jax.ShapeDtypeStruct((seq, model), F32),
+        compiler_params=pltpu.CompilerParams(
+            dimension_semantics=("arbitrary",), vmem_limit_bytes=24 << 20
+        ),
+        cost_estimate=pl.CostEstimate(
+            flops=2 * seq * half * model, transcendentals=0, bytes_accessed=8 << 20
+        ),
+        name="out_share",
+    )(in_hbm(gated), in_hbm(weight))
+
+
+def mix_kernel(meta_ref, mine_ref, weight_ref, share_ref, sq_mine, sq_other, pick_ref, out_ref):
     seq = mine_ref.shape[0]
-    dims = (((1,), (1,)), ((), ()))
     inner = 2 * mine_ref.shape[1]
-    wide = lax.dot_general(mine_ref[...], w_mine_ref[...], dims, preferred_element_type=F32)
-    wide += lax.dot_general(other_ref[...], w_other_ref[...], dims, preferred_element_type=F32)
+    total = share_ref[...] + lax.dot_general(
+        mine_ref[...], weight_ref[...], (((1,), (1,)), ((), ())), preferred_element_type=F32
+    )
     mean = jnp.sum(sq_mine[...] + sq_other[...], axis=1, keepdims=True) / inner
     live = lax.broadcasted_iota(jnp.int32, (seq, 1), 0) < meta_ref[1]
     scale = jnp.where(live, lax.rsqrt(mean + EPSILON), 0.0)
-    short = (wide * scale).astype(BF)
-    padded, kept = wide.shape[1], out_ref.shape[1]
-    row = lax.broadcasted_iota(jnp.int32, (padded, kept), 0)
-    col = lax.broadcasted_iota(jnp.int32, (padded, kept), 1)
-    part = row & (PADDED_ROWS - 1)
-    place = (row >> PADDED_SHIFT) * SHARD_ROWS + part
-    pick = jnp.where((place == col) & (part < SHARD_ROWS), 1.0, 0.0).astype(BF)
-    out_ref[...] = jnp.dot(short, pick, preferred_element_type=F32).astype(BF)
-
-
-def mix(meta, mine, other, weight, sq_mine, sq_other, model):
+    short = (total * scale).astype(BF)
+    out_ref[...] = jnp.dot(short, pick_ref[...], preferred_element_type=F32).astype(BF)
+
+
+def mix(meta, mine, weight, share, sq_mine, sq_other):
     seq, half = mine.shape
-    padded = weight.shape[0]
+    model = weight.shape[0]
     steps = 4
+    tile = model // steps
+    column = jnp.arange(tile, dtype=jnp.int32)
+    chip, rest = column // (2 * SHARD_ROWS), column % (2 * SHARD_ROWS)
+    place = rest // SHARD_ROWS * (tile // 2) + chip * SHARD_ROWS + rest % SHARD_ROWS
+    pick = (place[:, None] == column[None]).astype(BF)
     fixed = lambda n, m: (0, 0)
     return pl.pallas_call(
         mix_kernel,
@@ -307,32 +341,31 @@
             grid=(steps,),
             in_specs=[
                 pl.BlockSpec((seq, half), fixed),
-                pl.BlockSpec((seq, half), fixed),
-                pl.BlockSpec((padded // steps, half), lambda n, m: (n, m[0])),
-                pl.BlockSpec((padded // steps, half), lambda n, m: (n, 1 - m[0])),
+                pl.BlockSpec((tile, half), lambda n, m: (n, 0)),
+                pl.BlockSpec((seq, tile), lambda n, m: (0, n)),
                 pl.BlockSpec((seq, LANES), fixed),
                 pl.BlockSpec((seq, LANES), fixed),
+                pl.BlockSpec((tile, tile), fixed),
             ],
-            out_specs=pl.BlockSpec((seq, model // steps), lambda n, m: (0, n)),
+            out_specs=pl.BlockSpec((seq, tile), lambda n, m: (0, n)),
         ),
         out_shape=jax.ShapeDtypeStruct((seq, model), BF),
         compiler_params=pltpu.CompilerParams(
-            dimension_semantics=("arbitrary",), vmem_limit_bytes=40 << 20
+            dimension_semantics=("arbitrary",), vmem_limit_bytes=24 << 20
         ),
         cost_estimate=pl.CostEstimate(
-            flops=6 * seq * half * padded, transcendentals=0, bytes_accessed=16 << 20
+            flops=2 * seq * half * model, transcendentals=0, bytes_accessed=8 << 20
         ),
         name="mix",
-    )(meta, mine, other, weight, weight, sq_mine, sq_other)
+    )(meta, in_hbm(mine), in_hbm(weight), share, sq_mine, sq_other, pick)
 
 
 EVERYONE = ("req", "unit")
 DEVICES = 128
 CORE = 16
 SHARD_ROWS = 12
-PADDED_ROWS = 16
-PADDED_SHIFT = 4
 COLOURS = 3
+SAME_CORE = [[d for d in range(DEVICES) if d // CORE % 2 == core] for core in range(2)]
 LINKS = (1 << 2, 1, 1 << 5, 3 << 2, 3, 3 << 5)
 
 
@@ -350,9 +383,13 @@
     return hop(value, lambda core: CORE)
 
 
-def double(held, step):
-    return held, [
-        hop(piece, lambda core, c=c: link_of(c, core, step)) for c, piece in enumerate(held)
+def moved_over(held, step):
+    return [hop(piece, lambda core, c=c: link_of(c, core, step)) for c, piece in enumerate(held)]
+
+
+def joined(held, moved):
+    return [
+        lax.optimization_barrier(jnp.concatenate([h, m], axis=0)) for h, m in zip(held, moved)
     ]
 
 
@@ -401,35 +438,31 @@
     half = inner_dim // 2
     spare = LANES - head_count
 
+    cut = half + width + LANES
     side = jnp.pad(jnp.concatenate([state_proj, step_proj], axis=1), ((0, 0), (0, spare)))
-    low = jnp.concatenate([input_proj[:, :half], side, gate_proj[:, :half]], axis=1).astype(BF)
-    high = jnp.concatenate([input_proj[:, half:], side, gate_proj[:, half:]], axis=1).astype(BF)
-    sent, out_proj = lax.optimization_barrier((jnp.where(first_core, high, low), out_proj))
-    received = swap(sent)
-    padded_out = jnp.pad(out_proj.astype(BF), ((0, PADDED_ROWS - SHARD_ROWS), (0, 0)))
-    out_weight = lax.all_gather(padded_out, EVERYONE, axis=0, tiled=True)
-
+    low = [input_proj[:, :half], side, gate_proj[:, :half], out_proj[:, :half]]
+    high = [input_proj[:, half:], side, gate_proj[:, half:], out_proj[:, half:]]
+    low = jnp.concatenate(low, axis=1).astype(BF)
+    high = jnp.concatenate(high, axis=1).astype(BF)
+    received = swap(jnp.where(first_core, high, low))
     kept = jnp.where(first_core, low, high)
     pair = jnp.concatenate(
         [jnp.where(first_core, kept, received), jnp.where(first_core, received, kept)], axis=0
     )
+    out_weight = lax.all_gather(
+        pair[:, cut + half :], EVERYONE, axis=0, tiled=True, axis_index_groups=SAME_CORE
+    )
+    pair = pair[:, : cut + half]
     held = [pair[8 * c : 8 * c + 8] for c in range(COLOURS)]
     for step in range(3):
-        held, moved = double(held, step)
-        held = [jnp.concatenate([h, m], axis=0) for h, m in zip(held, moved)]
-    held, moved = double(held, 3)
-    moved, unit_id = lax.optimization_barrier((moved, unit_id))
-    held = [jnp.concatenate([h, m], axis=0) for h, m in zip(held, moved)]
-    cut = half + width + LANES
+        held = joined(held, moved_over(held, step))
+    moved, unit_id = lax.optimization_barrier((moved_over(held, 3), unit_id))
+    held = joined(held, moved)
     early, late = [h[:, :cut] for h in held], [h[:, cut:] for h in held]
-    early, moved = double(early, 4)
-    moved, late = lax.optimization_barrier((moved, late))
-    early, moved = double([jnp.concatenate([h, m], axis=0) for h, m in zip(early, moved)], 5)
+    early = joined(early, moved_over(early, 4))
+    moved, late = lax.optimization_barrier((moved_over(early, 5), late))
     early = [piece for both in zip(early, moved) for piece in both]
-    late, moved = double(late, 4)
-    late, moved = double([jnp.concatenate([h, m], axis=0) for h, m in zip(late, moved)], 5)
-    late = [piece for both in zip(late, moved) for piece in both]
-
+    late = joined(late, moved_over(late, 4))
     own = lax.dynamic_index_in_dim(tokens, unit_id, 0, keepdims=False)
     length = lax.dynamic_slice_in_dim(lengths, unit_id, 1, 0)
     coded = jnp.stack([length // 16, length % 16], axis=1).astype(BF)
@@ -441,22 +474,23 @@
     pick = jnp.arange(model_dim, dtype=jnp.int32)[:, None] == row_sources(me, core)[None]
     both = jnp.dot(both, pick.astype(BF), preferred_element_type=F32).astype(BF)
 
-    projected = project(both, early)
+    projected, late = lax.optimization_barrier((project(both, early), late))
+    late = [piece for two in zip(late, moved_over(late, 5)) for piece in two]
     scanned, state = scan(
         meta,
         projected,
         conv_weight,
         jnp.pad(step_bias, (0, spare))[None],
         jnp.pad(log_rate, (0, spare))[None],
-        jnp.repeat(skip_gain, head_dim)[None],
+        skip_gain,
         width,
     )
     state_other = swap(state[1])
     gain = norm_gain[None]
     sent, square_sent = gating(1, meta, both, scanned, gain, late)
-    other, square_other = swap(sent), swap(square_sent)
+    share, square_other = swap(out_share(sent, out_weight)), swap(square_sent)
     mine, square = gating(0, meta, both, scanned, gain, late)
-    mixed = mix(meta, mine, other, out_weight, square, square_other, model_dim)
+    mixed = mix(meta, mine, out_weight, share, square, square_other)
     state = jnp.concatenate(
         [jnp.where(first_core, state[0], state_other), jnp.where(first_core, state_other, state[0])]
     )

time: 165 us -> 179 us (1.085); the launches traced: 164 us -> 176 us
  Pallas kernels: 40.6 us -> 50.4 us
  waiting for transfers between devices: 36.4 us -> 45.2 us
  local copies, waits for them, and re-layouts: 17.5 us -> 8.95 us
    ppermute x29, waiting for transfers between devices: 36.4 us -> 45.2 us  [hop(): lax.ppermute(value, EVERYONE, [(d, d ^ mask_of(d // CORE % 2)) for d in r...]
    pallas_call x1 -> x2, Pallas kernels: 15.3 us -> 22.1 us  [the longest x1 16.5 us: scan(): pl.pallas_call(scan_kernel, grid_spec=grid_spec, out_shape=[pltpu.HBM((2,...]
    unnamed x40 -> x42, local copies, waits for them, and re-layouts: 8.31 us -> 3.01 us
    pallas_call x2, Pallas kernels: 8.27 us -> 13 us  [gating(): pl.pallas_call(gate_kernel, grid_spec=pltpu.PrefetchScalarGridSpec(num_sc...]
    concatenate x6 -> x0, local copies, waits for them, and re-layouts: 2.97 us -> none  [the longest x3 2.89 us: body(): held = [jnp.concatenate([h, m], axis=0) for h, m in zip(held, moved)]]
    pallas_call x1, Pallas kernels: 10.2 us -> 7.61 us  [mix(): pl.pallas_call(mix_kernel, grid_spec=pltpu.PrefetchScalarGridSpec(num_sca...]
  transfers between devices with their start and end apart: 30 -> 30, of which waited for: 15 -> 12; matrix products, arithmetic and copies ran while one was open for 13% -> 10% of each run, Pallas kernels for 18% -> 21%
where the time goes in v4:
time: 179 us; the launch traced here: 176 us
  Pallas kernels  50.4 us (28%)
  waiting for transfers between devices  45.2 us (25%)
  starting transfers between devices  36.8 us (21%)
  between operations  18.5 us (10%)
  other arithmetic  12.2 us (7%)
  local copies, waits for them, and re-layouts  8.95 us (5%)
  matrix products  4.14 us (2%)
    ppermute x29, waiting for transfers between devices, hop(): lax.ppermute(value, EVERYONE, [(d, d ^ mask_of(d // CORE % 2)) for d in r...  45.2 us
    ppermute x29, starting transfers between devices, hop(): lax.ppermute(value, EVERYONE, [(d, d ^ mask_of(d // CORE % 2)) for d in r...  36.8 us
    pallas_call x1, Pallas kernels, scan(): pl.pallas_call(scan_kernel, grid_spec=grid_spec, out_shape=[pltpu.HBM((2,...  16.5 us
    pallas_call x2, Pallas kernels, gating(): pl.pallas_call(gate_kernel, grid_spec=pltpu.PrefetchScalarGridSpec(num_sc...  13 us
    pallas_call x1, Pallas kernels, project(): pl.pallas_call(project_kernel, grid=(steps,), in_specs=[pl.BlockSpec((row...  7.69 us
    pallas_call x1, Pallas kernels, mix(): pl.pallas_call(mix_kernel, grid_spec=pltpu.PrefetchScalarGridSpec(num_sca...  7.61 us
    pallas_call x1, Pallas kernels, out_share(): pl.pallas_call(share_kernel, grid=(steps,), in_specs=[pl.BlockSpec((seq,...  5.58 us
    dot_general x1, matrix products, body(): both = jnp.dot(both, pick.astype(BF), preferred_element_type=F32).astype(BF)  4.14 us
  transfers between devices with their start and end apart: 30, of which 12 were waited for; matrix products, arithmetic and copies ran while one was open for 10% of the time, Pallas kernels for 21%

profile of v4, /device:TPU:1, one launch (start us, length us, event | category | flops | bytes accessed | tf_op | source)
XLA Modules:
  0.0 176.2 jit_solution(1246068252324951806)
XLA Ops:
  13.6 2.6 %collective-permute-start.1 = (bf16[8,3456]{1,0:T(8,128)(2,1)S(1)}, bf16[8,3456]{1,0:T(8,128)(2,1)S(1)}, u32[]{:S(2)}, u32[]{:S(2)}) collective-permute-start(bf16[8,3456]{1,0:T(8,128)(2,1)S(1)} %get-tuple-element.48), channel_id=1, source_target_pairs={{0,4},{1,5},{2,6},{3,7},{4,0},{5,1},{6,2},{7,3},{8,12},{9,13},{10,... | collective-permute-start | bytes 165896 | tf_op jit(solution)/shard_map/ppermute | solution.py:377
  16.9 2.7 %collective-permute-start.5 = (bf16[8,3456]{1,0:T(8,128)(2,1)S(1)}, bf16[8,3456]{1,0:T(8,128)(2,1)S(1)}, u32[]{:S(2)}, u32[]{:S(2)}) collective-permute-start(bf16[8,3456]{1,0:T(8,128)(2,1)S(1)} %get-tuple-element.47), channel_id=1, source_target_pairs={{0,1},{1,0},{2,3},{3,2},{4,5},{5,4},{6,7},{7,6},{8,9},{9,8},{10,11... | collective-permute-start | bytes 165896 | tf_op jit(solution)/shard_map/ppermute | solution.py:377
  19.6 3.8 %collective-permute-start.9 = (bf16[8,3456]{1,0:T(8,128)(2,1)S(1)}, bf16[8,3456]{1,0:T(8,128)(2,1)S(1)}, u32[]{:S(2)}, u32[]{:S(2)}) collective-permute-start(bf16[8,3456]{1,0:T(8,128)(2,1)S(1)} %get-tuple-element.46), channel_id=1, source_target_pairs={{0,32},{1,33},{2,34},{3,35},{4,36},{5,37},{6,38},{7,39},{8,40},{9,... | collective-permute-start | bytes 165896 | tf_op jit(solution)/shard_map/ppermute | solution.py:377
  25.1 3.2 %collective-permute-done.2 = bf16[16,3456]{1,0:T(8,128)(2,1)S(1)} collective-permute-done((bf16[16,3456]{1,0:T(8,128)(2,1)S(1)}, bf16[16,3456]{1,0:T(8,128)(2,1)S(1)}, u32[]{:S(2)}, u32[]{:S(2)}) %collective-permute-start.2) | collective-permute-done | bytes 110624 | tf_op jit(solution)/shard_map/ppermute | solution.py:377
  29.5 5.2 %collective-permute-done.3 = bf16[32,3456]{1,0:T(8,128)(2,1)S(1)} collective-permute-done((bf16[32,3456]{1,0:T(8,128)(2,1)S(1)}, bf16[32,3456]{1,0:T(8,128)(2,1)S(1)}, u32[]{:S(2)}, u32[]{:S(2)}) %collective-permute-start.3) | collective-permute-done | bytes 221216 | tf_op jit(solution)/shard_map/ppermute | solution.py:377
  36.0 6.8 %collective-permute-done.4 = bf16[64,3456]{1,0:T(8,128)(2,1)S(1)} collective-permute-done((bf16[64,3456]{1,0:T(8,128)(2,1)S(1)}, bf16[64,3456]{1,0:T(8,128)(2,1)S(1)}, u32[]{:S(2)}, u32[]{:S(2)}) %collective-permute-start.4) | collective-permute-done | bytes 442400 | tf_op jit(solution)/shard_map/ppermute | solution.py:377
  49.0 3.3 %collective-permute-start.13 = (bf16[392,1536]{1,0:T(8,128)(2,1)}, bf16[392,1536]{1,0:T(8,128)(2,1)}, u32[]{:S(2)}, u32[]{:S(2)}) collective-permute-start(bf16[392,1536]{1,0:T(8,128)(2,1)} %pad_maximum_fusion.1), channel_id=1, source_target_pairs={{0,16},{1,17},{2,18},{3,19},{4,20},{5,21},{6,22},{7,23},{8,24},{9,... | collective-permute-start | bytes 3612680 | tf_op jit(solution)/shard_map/ppermute | solution.py:377
  53.5 2.0 %collective-permute-start.18 = (bf16[128,1920]{1,0:T(8,128)(2,1)S(1)}, bf16[128,1920]{1,0:T(8,128)(2,1)S(1)}, u32[]{:S(2)}, u32[]{:S(2)}) collective-permute-start(bf16[128,1920]{1,0:T(8,128)(2,1)S(1)} %slice.115), channel_id=1, source_target_pairs={{0,4},{1,5},{2,6},{3,7},{4,0},{5,1},{6,2},{7,3},{8,12},{9,13},{10,... | collective-permute-start | bytes 1474568 | tf_op jit(solution)/shard_map/ppermute | solution.py:377
  55.5 6.3 %collective-permute-done.14 = bf16[128,1920]{1,0:T(8,128)(2,1)S(1)} collective-permute-done((bf16[128,1920]{1,0:T(8,128)(2,1)S(1)}, bf16[128,1920]{1,0:T(8,128)(2,1)S(1)}, u32[]{:S(2)}, u32[]{:S(2)}) %collective-permute-start.14) | collective-permute-done | bytes 491552 | tf_op jit(solution)/shard_map/ppermute | solution.py:377
  63.8 2.3 %collective-permute-start.17 = (bf16[256,1920]{1,0:T(8,128)(2,1)}, bf16[256,1920]{1,0:T(8,128)(2,1)}, u32[]{:S(2)}, u32[]{:S(2)}) collective-permute-start(bf16[256,1920]{1,0:T(8,128)(2,1)} %pad_maximum_fusion.3.refs_2_), channel_id=1, source_target_pairs={{0,4},{1,5},{2,6},{3,7},{4,0},{5,1},{6,2},{7,3},{8,12},{9,13},{10,... | collective-permute-start | bytes 2949128 | tf_op jit(solution)/shard_map/ppermute | solution.py:377
  67.1 2.4 %collective-permute-start.19 = (bf16[256,1920]{1,0:T(8,128)(2,1)}, bf16[256,1920]{1,0:T(8,128)(2,1)}, u32[]{:S(2)}, u32[]{:S(2)}) collective-permute-start(bf16[256,1920]{1,0:T(8,128)(2,1)} %pad_maximum_fusion.4.refs_4_), channel_id=1, source_target_pairs={{0,1},{1,0},{2,3},{3,2},{4,5},{5,4},{6,7},{7,6},{8,9},{9,8},{10,11... | collective-permute-start | bytes 2949128 | tf_op jit(solution)/shard_map/ppermute | solution.py:377
  72.4 4.1 %fusion.2.tokens_ref = bf16[768,1536]{1,0:T(8,128)(2,1)S(1)} fusion(s32[1536]{0:T(1024)S(1)} %pad_add_fusion, bf16[384,1536]{1,0:T(8,128)(2,1)S(1)} %slice.112, bf16[384,1536]{1,0:T(8,128)(2,1)S(1)} %copy-done.8), kind=kOutput, calls=%fused_computation.3 | convolution fusion | flops 3632136192 | bytes 4724736 | tf_op jit(solution)/shard_map/dot_general | solution.py:475
  77.5 10.5 %collective-permute-done.17.refs_3_ = bf16[256,1920]{1,0:T(8,128)(2,1)} collective-permute-done((bf16[256,1920]{1,0:T(8,128)(2,1)}, bf16[256,1920]{1,0:T(8,128)(2,1)}, u32[]{:S(2)}, u32[]{:S(2)}) %collective-permute-start.17) | collective-permute-done | bytes 983072 | tf_op jit(solution)/shard_map/ppermute | solution.py:377
  88.0 6.5 %collective-permute-done.19.refs_5_ = bf16[256,1920]{1,0:T(8,128)(2,1)} collective-permute-done((bf16[256,1920]{1,0:T(8,128)(2,1)}, bf16[256,1920]{1,0:T(8,128)(2,1)}, u32[]{:S(2)}, u32[]{:S(2)}) %collective-permute-start.19) | collective-permute-done | bytes 983072 | tf_op jit(solution)/shard_map/ppermute | solution.py:377
  94.8 7.7 %project.1.input_ref.side_ref = bf16[768,1920]{1,0:T(8,128)(2,1)S(1)} custom-call(bf16[768,1536]{1,0:T(8,128)(2,1)S(1)} %fusion.2.tokens_ref, bf16[256,1920]{1,0:T(8,128)(2,1)S(1)} %pad_maximum_fusion.2.refs_0_, bf16[256,1920]{1,0:T(8,128)(2,1)} %collective-permute-done.15.refs_1_, bf16[256,1920]{1,0:T(8,128)(2,1)} %pad_maximum_fusion.3.refs_2_, ...), custom_call_target="tpu_custom_call" | custom-call | flops 4529848320 | bytes 10485760 | tf_op jit(solution)/shard_map/project/pallas_call | solution.py:215
  104.7 2.5 %collective-permute-start.24 = (bf16[256,1536]{1,0:T(8,128)(2,1)S(1)}, bf16[256,1536]{1,0:T(8,128)(2,1)S(1)}, u32[]{:S(2)}, u32[]{:S(2)}) collective-permute-start(bf16[256,1536]{1,0:T(8,128)(2,1)S(1)} %pad_maximum_fusion.9.refs_2_), channel_id=1, source_target_pairs={{0,4},{1,5},{2,6},{3,7},{4,0},{5,1},{6,2},{7,3},{8,12},{9,13},{10,... | collective-permute-start | bytes 2359304 | tf_op jit(solution)/shard_map/ppermute | solution.py:377
  107.1 2.1 %collective-permute-start.25 = (bf16[256,1536]{1,0:T(8,128)(2,1)S(1)}, bf16[256,1536]{1,0:T(8,128)(2,1)S(1)}, u32[]{:S(2)}, u32[]{:S(2)}) collective-permute-start(bf16[256,1536]{1,0:T(8,128)(2,1)S(1)} %pad_maximum_fusion.10.refs_4_), channel_id=1, source_target_pairs={{0,1},{1,0},{2,3},{3,2},{4,5},{5,4},{6,7},{7,6},{8,9},{9,8},{10,11... | collective-permute-start | bytes 2359304 | tf_op jit(solution)/shard_map/ppermute | solution.py:377
  112.5 16.5 %scan.1 = (f32[2,384,1536]{2,1,0:T(8,128)}, f32[2,1536,128]{2,1,0:T(8,128)}) custom-call(s32[3]{0:T(128)S(1)} %pad_add_fusion.1.meta_ref, bf16[768,1920]{1,0:T(8,128)(2,1)S(1)} %project.1.input_ref.side_ref, bf16[768,1920]{1,0:T(8,128)(2,1)S(1)} %project.1.input_ref.side_ref, f32[4,3328]{1,0:T(4,128)S(1)} %copy-done.2, f32[4,3328]{1,0:T(4,128)S(1)} %copy-done.2, ...), custom_call_target="tpu_custom_call" | custom-call | flops 1509949440 | bytes 9437184 | tf_op jit(solution)/shard_map/scan/pallas_call | solution.py:188
  130.4 6.5 %gating.3 = (bf16[384,1536]{1,0:T(8,128)(2,1)}, f32[384,128]{1,0:T(8,128)}) custom-call(s32[3]{0:T(128)S(1)} %pad_add_fusion.1.meta_ref, bf16[768,1536]{1,0:T(8,128)(2,1)S(1)} %fusion.2.tokens_ref, f32[2,384,1536]{2,1,0:T(8,128)} %get-tuple-element.33.scanned_ref, f32[1,3072]{1,0:T(1,128)S(1)} %bitcast.18, bf16[256,1536]{1,0:T(8,128)(2,1)} %copy-done.4, ...), custom_call_target="tpu_custom_call" | custom-call | flops 1811939328 | bytes 10485760 | tf_op jit(solution)/shard_map/gating/pallas_call | solution.py:254
  137.0 5.6 %out_share.1 = f32[384,1536]{1,0:T(8,128)S(1)} custom-call(bf16[384,1536]{1,0:T(8,128)(2,1)} %get-tuple-element.38.gated_ref, bf16[1536,1536]{1,0:T(8,128)(2,1)} %all-gather.2.cloned.1.call-done.weight_ref), custom_call_target="tpu_custom_call" | custom-call | flops 1811939328 | bytes 8388608 | tf_op jit(solution)/shard_map/out_share/pallas_call | solution.py:295
  142.6 5.1 %collective-permute-start.26 = (f32[384,1536]{1,0:T(8,128)S(1)}, f32[384,1536]{1,0:T(8,128)S(1)}, u32[]{:S(2)}, u32[]{:S(2)}) collective-permute-start(f32[384,1536]{1,0:T(8,128)S(1)} %out_share.1), channel_id=1, source_target_pairs={{0,16},{1,17},{2,18},{3,19},{4,20},{5,21},{6,22},{7,23},{8,24},{9,... | collective-permute-start | bytes 7077896 | tf_op jit(solution)/shard_map/ppermute | solution.py:377
  148.5 4.4 %collective-permute-done.28 = f32[1536,128]{1,0:T(8,128)S(1)} collective-permute-done((f32[1536,128]{1,0:T(8,128)S(1)}, f32[1536,128]{1,0:T(8,128)S(1)}, u32[]{:S(2)}, u32[]{:S(2)}) %collective-permute-start.28) | collective-permute-done | bytes 786464 | tf_op jit(solution)/shard_map/ppermute | solution.py:377
  154.3 6.5 %gating.2 = (bf16[384,1536]{1,0:T(8,128)(2,1)}, f32[384,128]{1,0:T(8,128)}) custom-call(s32[3]{0:T(128)S(1)} %pad_add_fusion.1.meta_ref, bf16[768,1536]{1,0:T(8,128)(2,1)S(1)} %fusion.2.tokens_ref, f32[2,384,1536]{2,1,0:T(8,128)} %get-tuple-element.33.scanned_ref, f32[1,3072]{1,0:T(1,128)S(1)} %bitcast.19, bf16[256,1536]{1,0:T(8,128)(2,1)} %copy-done.4, ...), custom_call_target="tpu_custom_call" | custom-call | flops 1811939328 | bytes 10485760 | tf_op jit(solution)/shard_map/gating/pallas_call | solution.py:254
  161.7 7.6 %mix.1 = bf16[384,1536]{1,0:T(8,128)(2,1)} custom-call(s32[3]{0:T(128)S(1)} %pad_add_fusion.1.meta_ref, bf16[384,1536]{1,0:T(8,128)(2,1)} %get-tuple-element.37.mine_ref, bf16[1536,1536]{1,0:T(8,128)(2,1)} %all-gather.2.cloned.1.call-done.weight_ref, f32[384,1536]{1,0:T(8,128)S(1)} %collective-permute-done.26.share_ref, f32[384,128]{1,0:T(8,128)S(1)} %copy-done, ...), custom_call_target="tpu_custom_call" | custom-call | flops 1811939328 | bytes 8388608 | tf_op jit(solution)/shard_map/mix/pallas_call | solution.py:337
  (149 shorter events, 31.5 us)
Async XLA Ops:
  7.2 129.8 %all-gather.2.cloned.1.call-start = ((), (), s32[]{:S(2)}) async-start(), calls=%async_computation | async-start | bytes 4792320 | tf_op jit(solution)/shard_map/all_gather | solution.py:452
  13.6 9.8 %collective-permute-start.1 = (bf16[8,3456]{1,0:T(8,128)(2,1)S(1)}, bf16[8,3456]{1,0:T(8,128)(2,1)S(1)}, u32[]{:S(2)}, u32[]{:S(2)}) collective-permute-start(bf16[8,3456]{1,0:T(8,128)(2,1)S(1)} %get-tuple-element.48), channel_id=1, source_target_pairs={{0,4},{1,5},{2,6},{3,7},{4,0},{5,1},{6,2},{7,3},{8,12},{9,13},{10,... | collective-permute-start | bytes 165896 | tf_op jit(solution)/shard_map/ppermute | solution.py:377
  16.9 6.6 %collective-permute-start.5 = (bf16[8,3456]{1,0:T(8,128)(2,1)S(1)}, bf16[8,3456]{1,0:T(8,128)(2,1)S(1)}, u32[]{:S(2)}, u32[]{:S(2)}) collective-permute-start(bf16[8,3456]{1,0:T(8,128)(2,1)S(1)} %get-tuple-element.47), channel_id=1, source_target_pairs={{0,1},{1,0},{2,3},{3,2},{4,5},{5,4},{6,7},{7,6},{8,9},{9,8},{10,11... | collective-permute-start | bytes 165896 | tf_op jit(solution)/shard_map/ppermute | solution.py:377
  28.3 6.4 %collective-permute-start.3 = (bf16[32,3456]{1,0:T(8,128)(2,1)S(1)}, bf16[32,3456]{1,0:T(8,128)(2,1)S(1)}, u32[]{:S(2)}, u32[]{:S(2)}) collective-permute-start(bf16[32,3456]{1,0:T(8,128)(2,1)S(1)} %pad_maximum_fusion.14), channel_id=1, source_target_pairs={{0,32},{1,33},{2,34},{3,35},{4,36},{5,37},{6,38},{7,39},{8,40},{9,... | collective-permute-start | bytes 663560 | tf_op jit(solution)/shard_map/ppermute | solution.py:377
  28.5 6.4 %collective-permute-start.7 = (bf16[32,3456]{1,0:T(8,128)(2,1)S(1)}, bf16[32,3456]{1,0:T(8,128)(2,1)S(1)}, u32[]{:S(2)}, u32[]{:S(2)}) collective-permute-start(bf16[32,3456]{1,0:T(8,128)(2,1)S(1)} %pad_maximum_fusion.15), channel_id=1, source_target_pairs={{0,12},{1,13},{2,14},{3,15},{4,8},{5,9},{6,10},{7,11},{8,4},{9,5},... | collective-permute-start | bytes 663560 | tf_op jit(solution)/shard_map/ppermute | solution.py:377
  29.4 5.6 %collective-permute-start.11 = (bf16[32,3456]{1,0:T(8,128)(2,1)S(1)}, bf16[32,3456]{1,0:T(8,128)(2,1)S(1)}, u32[]{:S(2)}, u32[]{:S(2)}) collective-permute-start(bf16[32,3456]{1,0:T(8,128)(2,1)S(1)} %pad_maximum_fusion.16), channel_id=1, source_target_pairs={{0,3},{1,2},{2,1},{3,0},{4,7},{5,6},{6,5},{7,4},{8,11},{9,10},{10,... | collective-permute-start | bytes 663560 | tf_op jit(solution)/shard_map/ppermute | solution.py:377
  34.7 8.0 %collective-permute-start.4 = (bf16[64,3456]{1,0:T(8,128)(2,1)S(1)}, bf16[64,3456]{1,0:T(8,128)(2,1)S(1)}, u32[]{:S(2)}, u32[]{:S(2)}) collective-permute-start(bf16[64,3456]{1,0:T(8,128)(2,1)S(1)} %pad_maximum_fusion.11), channel_id=1, source_target_pairs={{0,12},{1,13},{2,14},{3,15},{4,8},{5,9},{6,10},{7,11},{8,4},{9,5},... | collective-permute-start | bytes 1327112 | tf_op jit(solution)/shard_map/ppermute | solution.py:377
  34.9 8.0 %collective-permute-start.8 = (bf16[64,3456]{1,0:T(8,128)(2,1)S(1)}, bf16[64,3456]{1,0:T(8,128)(2,1)S(1)}, u32[]{:S(2)}, u32[]{:S(2)}) collective-permute-start(bf16[64,3456]{1,0:T(8,128)(2,1)S(1)} %pad_maximum_fusion.12), channel_id=1, source_target_pairs={{0,3},{1,2},{2,1},{3,0},{4,7},{5,6},{6,5},{7,4},{8,11},{9,10},{10,... | collective-permute-start | bytes 1327112 | tf_op jit(solution)/shard_map/ppermute | solution.py:377
  35.0 8.0 %collective-permute-start.12 = (bf16[64,3456]{1,0:T(8,128)(2,1)S(1)}, bf16[64,3456]{1,0:T(8,128)(2,1)S(1)}, u32[]{:S(2)}, u32[]{:S(2)}) collective-permute-start(bf16[64,3456]{1,0:T(8,128)(2,1)S(1)} %pad_maximum_fusion.13), channel_id=1, source_target_pairs={{0,96},{1,97},{2,98},{3,99},{4,100},{5,101},{6,102},{7,103},{8,104... | collective-permute-start | bytes 1327112 | tf_op jit(solution)/shard_map/ppermute | solution.py:377
  49.0 22.0 %collective-permute-start.13 = (bf16[392,1536]{1,0:T(8,128)(2,1)}, bf16[392,1536]{1,0:T(8,128)(2,1)}, u32[]{:S(2)}, u32[]{:S(2)}) collective-permute-start(bf16[392,1536]{1,0:T(8,128)(2,1)} %pad_maximum_fusion.1), channel_id=1, source_target_pairs={{0,16},{1,17},{2,18},{3,19},{4,20},{5,21},{6,22},{7,23},{8,24},{9,... | collective-permute-start | bytes 3612680 | tf_op jit(solution)/shard_map/ppermute | solution.py:377
  52.4 9.4 %collective-permute-start.14 = (bf16[128,1920]{1,0:T(8,128)(2,1)S(1)}, bf16[128,1920]{1,0:T(8,128)(2,1)S(1)}, u32[]{:S(2)}, u32[]{:S(2)}) collective-permute-start(bf16[128,1920]{1,0:T(8,128)(2,1)S(1)} %slice.113), channel_id=1, source_target_pairs={{0,3},{1,2},{2,1},{3,0},{4,7},{5,6},{6,5},{7,4},{8,11},{9,10},{10,... | collective-permute-start | bytes 1474568 | tf_op jit(solution)/shard_map/ppermute | solution.py:377
  52.6 10.0 %collective-permute-start.16 = (bf16[128,1920]{1,0:T(8,128)(2,1)S(1)}, bf16[128,1920]{1,0:T(8,128)(2,1)S(1)}, u32[]{:S(2)}, u32[]{:S(2)}) collective-permute-start(bf16[128,1920]{1,0:T(8,128)(2,1)S(1)} %slice.114), channel_id=1, source_target_pairs={{0,96},{1,97},{2,98},{3,99},{4,100},{5,101},{6,102},{7,103},{8,104... | collective-permute-start | bytes 1474568 | tf_op jit(solution)/shard_map/ppermute | solution.py:377
  53.5 12.5 %collective-permute-start.18 = (bf16[128,1920]{1,0:T(8,128)(2,1)S(1)}, bf16[128,1920]{1,0:T(8,128)(2,1)S(1)}, u32[]{:S(2)}, u32[]{:S(2)}) collective-permute-start(bf16[128,1920]{1,0:T(8,128)(2,1)S(1)} %slice.115), channel_id=1, source_target_pairs={{0,4},{1,5},{2,6},{3,7},{4,0},{5,1},{6,2},{7,3},{8,12},{9,13},{10,... | collective-permute-start | bytes 1474568 | tf_op jit(solution)/shard_map/ppermute | solution.py:377
  61.9 15.6 %collective-permute-start.15 = (bf16[256,1920]{1,0:T(8,128)(2,1)S(1)}, bf16[256,1920]{1,0:T(8,128)(2,1)}, u32[]{:S(2)}, u32[]{:S(2)}) collective-permute-start(bf16[256,1920]{1,0:T(8,128)(2,1)S(1)} %pad_maximum_fusion.2.refs_0_), channel_id=1, source_target_pairs={{0,96},{1,97},{2,98},{3,99},{4,100},{5,101},{6,102},{7,103},{8,104... | collective-permute-start | bytes 2949128 | tf_op jit(solution)/shard_map/ppermute | solution.py:377
  63.8 24.2 %collective-permute-start.17 = (bf16[256,1920]{1,0:T(8,128)(2,1)}, bf16[256,1920]{1,0:T(8,128)(2,1)}, u32[]{:S(2)}, u32[]{:S(2)}) collective-permute-start(bf16[256,1920]{1,0:T(8,128)(2,1)} %pad_maximum_fusion.3.refs_2_), channel_id=1, source_target_pairs={{0,4},{1,5},{2,6},{3,7},{4,0},{5,1},{6,2},{7,3},{8,12},{9,13},{10,... | collective-permute-start | bytes 2949128 | tf_op jit(solution)/shard_map/ppermute | solution.py:377
  67.1 27.4 %collective-permute-start.19 = (bf16[256,1920]{1,0:T(8,128)(2,1)}, bf16[256,1920]{1,0:T(8,128)(2,1)}, u32[]{:S(2)}, u32[]{:S(2)}) collective-permute-start(bf16[256,1920]{1,0:T(8,128)(2,1)} %pad_maximum_fusion.4.refs_4_), channel_id=1, source_target_pairs={{0,1},{1,0},{2,3},{3,2},{4,5},{5,4},{6,7},{7,6},{8,9},{9,8},{10,11... | collective-permute-start | bytes 2949128 | tf_op jit(solution)/shard_map/ppermute | solution.py:377
  94.5 8.0 %collective-permute-start.20 = (bf16[128,1536]{1,0:T(8,128)(2,1)S(1)}, bf16[128,1536]{1,0:T(8,128)(2,1)S(1)}, u32[]{:S(2)}, u32[]{:S(2)}) collective-permute-start(bf16[128,1536]{1,0:T(8,128)(2,1)S(1)} %slice.116), channel_id=1, source_target_pairs={{0,3},{1,2},{2,1},{3,0},{4,7},{5,6},{6,5},{7,4},{8,11},{9,10},{10,... | collective-permute-start | bytes 1179656 | tf_op jit(solution)/shard_map/ppermute | solution.py:377
  94.7 7.9 %collective-permute-start.21 = (bf16[128,1536]{1,0:T(8,128)(2,1)S(1)}, bf16[128,1536]{1,0:T(8,128)(2,1)S(1)}, u32[]{:S(2)}, u32[]{:S(2)}) collective-permute-start(bf16[128,1536]{1,0:T(8,128)(2,1)S(1)} %slice.117), channel_id=1, source_target_pairs={{0,96},{1,97},{2,98},{3,99},{4,100},{5,101},{6,102},{7,103},{8,104... | collective-permute-start | bytes 1179656 | tf_op jit(solution)/shard_map/ppermute | solution.py:377
  94.7 8.1 %collective-permute-start.22 = (bf16[128,1536]{1,0:T(8,128)(2,1)S(1)}, bf16[128,1536]{1,0:T(8,128)(2,1)S(1)}, u32[]{:S(2)}, u32[]{:S(2)}) collective-permute-start(bf16[128,1536]{1,0:T(8,128)(2,1)S(1)} %slice.118), channel_id=1, source_target_pairs={{0,4},{1,5},{2,6},{3,7},{4,0},{5,1},{6,2},{7,3},{8,12},{9,13},{10,... | collective-permute-start | bytes 1179656 | tf_op jit(solution)/shard_map/ppermute | solution.py:377
  102.9 26.1 %collective-permute-start.23 = (bf16[256,1536]{1,0:T(8,128)(2,1)S(1)}, bf16[256,1536]{1,0:T(8,128)(2,1)S(1)}, u32[]{:S(2)}, u32[]{:S(2)}) collective-permute-start(bf16[256,1536]{1,0:T(8,128)(2,1)S(1)} %pad_maximum_fusion.8.refs_0_), channel_id=1, source_target_pairs={{0,96},{1,97},{2,98},{3,99},{4,100},{5,101},{6,102},{7,103},{8,104... | collective-permute-start | bytes 2359304 | tf_op jit(solution)/shard_map/ppermute | solution.py:377
  104.7 24.4 %collective-permute-start.24 = (bf16[256,1536]{1,0:T(8,128)(2,1)S(1)}, bf16[256,1536]{1,0:T(8,128)(2,1)S(1)}, u32[]{:S(2)}, u32[]{:S(2)}) collective-permute-start(bf16[256,1536]{1,0:T(8,128)(2,1)S(1)} %pad_maximum_fusion.9.refs_2_), channel_id=1, source_target_pairs={{0,4},{1,5},{2,6},{3,7},{4,0},{5,1},{6,2},{7,3},{8,12},{9,13},{10,... | collective-permute-start | bytes 2359304 | tf_op jit(solution)/shard_map/ppermute | solution.py:377
  107.1 21.9 %collective-permute-start.25 = (bf16[256,1536]{1,0:T(8,128)(2,1)S(1)}, bf16[256,1536]{1,0:T(8,128)(2,1)S(1)}, u32[]{:S(2)}, u32[]{:S(2)}) collective-permute-start(bf16[256,1536]{1,0:T(8,128)(2,1)S(1)} %pad_maximum_fusion.10.refs_4_), channel_id=1, source_target_pairs={{0,1},{1,0},{2,3},{3,2},{4,5},{5,4},{6,7},{7,6},{8,9},{9,8},{10,11... | collective-permute-start | bytes 2359304 | tf_op jit(solution)/shard_map/ppermute | solution.py:377
  142.6 18.2 %collective-permute-start.26 = (f32[384,1536]{1,0:T(8,128)S(1)}, f32[384,1536]{1,0:T(8,128)S(1)}, u32[]{:S(2)}, u32[]{:S(2)}) collective-permute-start(f32[384,1536]{1,0:T(8,128)S(1)} %out_share.1), channel_id=1, source_target_pairs={{0,16},{1,17},{2,18},{3,19},{4,20},{5,21},{6,22},{7,23},{8,24},{9,... | collective-permute-start | bytes 7077896 | tf_op jit(solution)/shard_map/ppermute | solution.py:377
  148.0 12.8 %collective-permute-start.27 = (f32[384,128]{1,0:T(8,128)S(1)}, f32[384,128]{1,0:T(8,128)S(1)}, u32[]{:S(2)}, u32[]{:S(2)}) collective-permute-start(f32[384,128]{1,0:T(8,128)S(1)} %copy-done.19), channel_id=1, source_target_pairs={{0,16},{1,17},{2,18},{3,19},{4,20},{5,21},{6,22},{7,23},{8,24},{9,... | collective-permute-start | bytes 589832 | tf_op jit(solution)/shard_map/ppermute | solution.py:377
  (27 other events, 215.9 us)
Sparse Core Ops, SparseCore 0:
  23.5 71.2 all-gather.1

commit v5 on v4

--- a/solution.py
+++ b/solution.py
@@ -11,10 +11,6 @@
 EPSILON = 1e-05
 BF = jnp.bfloat16
 F32 = jnp.float32
-
-
-def in_hbm(value):
-    return pltpu.with_memory_space_constraint(value, pltpu.HBM)
 
 
 def silu(v):
@@ -189,8 +185,8 @@
         scan_kernel,
         grid_spec=grid_spec,
         out_shape=[
-            pltpu.HBM((2, seq, half), F32),
-            pltpu.HBM((2, half, state_dim), F32),
+            jax.ShapeDtypeStruct((2, seq, half), F32),
+            jax.ShapeDtypeStruct((2, half, state_dim), F32),
         ],
         compiler_params=pltpu.CompilerParams(
             dimension_semantics=("arbitrary", "arbitrary"), vmem_limit_bytes=24 << 20
@@ -268,8 +264,8 @@
             ],
         ),
         out_shape=[
-            pltpu.HBM((seq, half), BF),
-            pltpu.HBM((seq, LANES), F32),
+            jax.ShapeDtypeStruct((seq, half), BF),
+            jax.ShapeDtypeStruct((seq, LANES), F32),
         ],
         compiler_params=pltpu.CompilerParams(
             dimension_semantics=("arbitrary",), vmem_limit_bytes=24 << 20
@@ -278,76 +274,102 @@
             flops=2 * seq * model * half, transcendentals=seq * half, bytes_accessed=10 << 20
         ),
         name="gating",
-    )(meta, tokens, in_hbm(scanned), gain, *map(in_hbm, pieces))
-
-
-def share_kernel(gated_ref, weight_ref, out_ref):
-    out_ref[...] = lax.dot_general(
-        gated_ref[...], weight_ref[...], (((1,), (1,)), ((), ())), preferred_element_type=F32
-    )
-
-
-def out_share(gated, weight):
+    )(meta, tokens, scanned, gain, *pieces)
+
+
+def place_rows(places_ref, gated_ref, pieces, out_ref):
+    step = pl.program_id(0)
+    weight = jnp.concatenate([piece[...] for piece in pieces], axis=0)
+    total = lax.dot_general(
+        weight, gated_ref[...], (((1,), (1,)), ((), ())), preferred_element_type=F32
+    )
+    each = pieces[0].shape[0] // BLOCK_ROWS
+    steps = pl.num_programs(0)
+    for index in range(len(pieces)):
+        for block in range(each):
+            at = (index * each + block) * BLOCK_ROWS
+            place = places_ref[(index * steps + step) * each + block]
+            out_ref[pl.ds(pl.multiple_of(place, BLOCK_ROWS), BLOCK_ROWS), :] = total[
+                at : at + BLOCK_ROWS
+            ]
+
+
+def share_kernel(places_ref, gated_ref, *refs):
+    place_rows(places_ref, gated_ref, refs[:-1], refs[-1])
+
+
+def out_share(places, gated, pieces):
     seq, half = gated.shape
-    model = weight.shape[0]
+    rows = pieces[0].shape[0]
+    model = rows * len(pieces)
     steps = 4
-    tile = model // steps
     return pl.pallas_call(
         share_kernel,
-        grid=(steps,),
-        in_specs=[
-            pl.BlockSpec((seq, half), lambda n: (0, 0)),
-            pl.BlockSpec((tile, half), lambda n: (n, 0)),
-        ],
-        out_specs=pl.BlockSpec((seq, tile), lambda n: (0, n)),
-        out_shape=jax.ShapeDtypeStruct((seq, model), F32),
+        grid_spec=pltpu.PrefetchScalarGridSpec(
+            num_scalar_prefetch=1,
+            grid=(steps,),
+            in_specs=[pl.BlockSpec((seq, half), lambda n, p: (0, 0))]
+            + [pl.BlockSpec((rows // steps, half), lambda n, p: (n, 1)) for _ in pieces],
+            out_specs=pl.BlockSpec((model, seq), lambda n, p: (0, 0)),
+        ),
+        out_shape=jax.ShapeDtypeStruct((model, seq), F32),
         compiler_params=pltpu.CompilerParams(
-            dimension_semantics=("arbitrary",), vmem_limit_bytes=24 << 20
+            dimension_semantics=("arbitrary",), vmem_limit_bytes=20 << 20
         ),
         cost_estimate=pl.CostEstimate(
             flops=2 * seq * half * model, transcendentals=0, bytes_accessed=8 << 20
         ),
         name="out_share",
-    )(in_hbm(gated), in_hbm(weight))
-
-
-def mix_kernel(meta_ref, mine_ref, weight_ref, share_ref, sq_mine, sq_other, pick_ref, out_ref):
-    seq = mine_ref.shape[0]
-    inner = 2 * mine_ref.shape[1]
-    total = share_ref[...] + lax.dot_general(
-        mine_ref[...], weight_ref[...], (((1,), (1,)), ((), ())), preferred_element_type=F32
-    )
-    mean = jnp.sum(sq_mine[...] + sq_other[...], axis=1, keepdims=True) / inner
-    live = lax.broadcasted_iota(jnp.int32, (seq, 1), 0) < meta_ref[1]
-    scale = jnp.where(live, lax.rsqrt(mean + EPSILON), 0.0)
-    short = (total * scale).astype(BF)
-    out_ref[...] = jnp.dot(short, pick_ref[...], preferred_element_type=F32).astype(BF)
-
-
-def mix(meta, mine, weight, share, sq_mine, sq_other):
+    )(places, gated, *pieces)
+
+
+def mix_kernel(meta_ref, places_ref, mine_ref, share_ref, sq_mine, sq_other, pick_ref, *refs):
+    pieces, out_ref, total_scr = refs[:-2], refs[-2], refs[-1]
+    place_rows(places_ref, mine_ref, pieces, total_scr)
+
+    @pl.when(pl.program_id(0) == pl.num_programs(0) - 1)
+    def _():
+        seq = mine_ref.shape[0]
+        inner = 2 * mine_ref.shape[1]
+        squares = jnp.transpose(sq_mine[...] + sq_other[...])
+        mean = jnp.sum(squares, axis=0, keepdims=True) / inner
+        live = lax.broadcasted_iota(jnp.int32, (1, seq), 1) < meta_ref[1]
+        scale = jnp.where(live, lax.rsqrt(mean + EPSILON), 0.0)
+        tile = pick_ref.shape[0]
+        for at in range(0, out_ref.shape[1], tile):
+            rows = slice(at, at + tile)
+            short = ((total_scr[rows] + share_ref[rows]) * scale).astype(BF)
+            out_ref[:, rows] = lax.dot_general(
+                short, pick_ref[...], (((0,), (0,)), ((), ())), preferred_element_type=F32
+            ).astype(BF)
+
+
+def mix(meta, places, mine, share, sq_mine, sq_other, pieces):
     seq, half = mine.shape
-    model = weight.shape[0]
+    rows = pieces[0].shape[0]
+    model = rows * len(pieces)
     steps = 4
-    tile = model // steps
+    tile = model // 4
     column = jnp.arange(tile, dtype=jnp.int32)
     chip, rest = column // (2 * SHARD_ROWS), column % (2 * SHARD_ROWS)
-    place = rest // SHARD_ROWS * (tile // 2) + chip * SHARD_ROWS + rest % SHARD_ROWS
-    pick = (place[:, None] == column[None]).astype(BF)
-    fixed = lambda n, m: (0, 0)
+    target = rest // SHARD_ROWS * (tile // 2) + chip * SHARD_ROWS + rest % SHARD_ROWS
+    pick = (target[:, None] == column[None]).astype(BF)
+    fixed = lambda n, m, p: (0, 0)
     return pl.pallas_call(
         mix_kernel,
         grid_spec=pltpu.PrefetchScalarGridSpec(
-            num_scalar_prefetch=1,
+            num_scalar_prefetch=2,
             grid=(steps,),
             in_specs=[
                 pl.BlockSpec((seq, half), fixed),
-                pl.BlockSpec((tile, half), lambda n, m: (n, 0)),
-                pl.BlockSpec((seq, tile), lambda n, m: (0, n)),
+                pl.BlockSpec((model, seq), fixed),
                 pl.BlockSpec((seq, LANES), fixed),
                 pl.BlockSpec((seq, LANES), fixed),
                 pl.BlockSpec((tile, tile), fixed),
-            ],
-            out_specs=pl.BlockSpec((seq, tile), lambda n, m: (0, n)),
+            ]
+            + [pl.BlockSpec((rows // steps, half), lambda n, m, p: (n, 1)) for _ in pieces],
+            out_specs=pl.BlockSpec((seq, model), fixed),
+            scratch_shapes=[pltpu.VMEM((model, seq), F32)],
         ),
         out_shape=jax.ShapeDtypeStruct((seq, model), BF),
         compiler_params=pltpu.CompilerParams(
@@ -357,7 +379,7 @@
             flops=2 * seq * half * model, transcendentals=0, bytes_accessed=8 << 20
         ),
         name="mix",
-    )(meta, in_hbm(mine), in_hbm(weight), share, sq_mine, sq_other, pick)
+    )(meta, places, mine, share, sq_mine, sq_other, pick, *pieces)
 
 
 EVERYONE = ("req", "unit")
@@ -365,7 +387,7 @@
 CORE = 16
 SHARD_ROWS = 12
 COLOURS = 3
-SAME_CORE = [[d for d in range(DEVICES) if d // CORE % 2 == core] for core in range(2)]
+BLOCK_ROWS = 8
 LINKS = (1 << 2, 1, 1 << 5, 3 << 2, 3, 3 << 5)
 
 
@@ -393,23 +415,31 @@
     ]
 
 
-def row_sources(me, core):
-    sources = []
-    block = jnp.arange(64, dtype=jnp.int32)
-    row = jnp.arange(8, dtype=jnp.int32)
-    for colour in range(COLOURS):
-        masks = []
-        for side in range(2):
-            mask = jnp.zeros_like(block)
-            for step in range(6):
-                mask = mask ^ (((block >> step) & 1) * link_of(colour, side, step))
-            masks.append(mask)
-        chip = (me ^ jnp.where(core == 0, masks[0], masks[1])) & ~CORE
-        local = colour * 8 + row
-        upper = (local >= SHARD_ROWS).astype(jnp.int32)
-        device = chip[:, None] + CORE * upper[None]
-        sources.append((device * SHARD_ROWS + (local - SHARD_ROWS * upper)[None]).reshape(-1))
-    return jnp.concatenate(sources)
+def gathered_chip(me, core, colour, block):
+    mask = jnp.zeros_like(block)
+    for step in range(6):
+        link = jnp.zeros_like(block)
+        for c in range(COLOURS):
+            here = jnp.where(core == 0, link_of(c, 0, step), link_of(c, 1, step))
+            link = jnp.where(colour == c, here, link)
+        mask = mask ^ (((block >> step) & 1) * link)
+    return (me ^ mask) & ~CORE
+
+
+def row_sources(me, core, model):
+    row = jnp.arange(model, dtype=jnp.int32)
+    colour, block = row // (model // COLOURS), row // BLOCK_ROWS % 64
+    local = colour * BLOCK_ROWS + row % BLOCK_ROWS
+    upper = (local >= SHARD_ROWS).astype(jnp.int32)
+    device = gathered_chip(me, core, colour, block) + CORE * upper
+    return device * SHARD_ROWS + local - SHARD_ROWS * upper
+
+
+def row_places(me, core):
+    index = jnp.arange(COLOURS * 64, dtype=jnp.int32)
+    chip = gathered_chip(me, core, index // 64, index % 64)
+    chip = (chip >> 5) * CORE + (chip & (CORE - 1))
+    return chip * 2 * SHARD_ROWS + index // 64 * BLOCK_ROWS
 
 
 def body(
@@ -439,58 +469,59 @@
     spare = LANES - head_count
 
     cut = half + width + LANES
-    side = jnp.pad(jnp.concatenate([state_proj, step_proj], axis=1), ((0, 0), (0, spare)))
+    length = lax.dynamic_slice_in_dim(lengths, unit_id, 1, 0)
+    coded = jnp.stack([length // 16, length % 16], axis=1).astype(F32)
+    coded = jnp.pad(coded, ((0, SHARD_ROWS - 1), (0, spare - 2)))
+    side = jnp.concatenate([state_proj, step_proj, coded], axis=1)
     low = [input_proj[:, :half], side, gate_proj[:, :half], out_proj[:, :half]]
     high = [input_proj[:, half:], side, gate_proj[:, half:], out_proj[:, half:]]
     low = jnp.concatenate(low, axis=1).astype(BF)
     high = jnp.concatenate(high, axis=1).astype(BF)
     received = swap(jnp.where(first_core, high, low))
+    code = received[0, cut - spare : cut - spare + 2].astype(jnp.int32)
+    meta = jnp.stack([core, length[0], code[0] * 16 + code[1]])
+
     kept = jnp.where(first_core, low, high)
     pair = jnp.concatenate(
         [jnp.where(first_core, kept, received), jnp.where(first_core, received, kept)], axis=0
     )
-    out_weight = lax.all_gather(
-        pair[:, cut + half :], EVERYONE, axis=0, tiled=True, axis_index_groups=SAME_CORE
-    )
-    pair = pair[:, : cut + half]
     held = [pair[8 * c : 8 * c + 8] for c in range(COLOURS)]
-    for step in range(3):
+    for step in range(4):
+        if step == 3:
+            held, unit_id = lax.optimization_barrier((held, unit_id))
         held = joined(held, moved_over(held, step))
-    moved, unit_id = lax.optimization_barrier((moved_over(held, 3), unit_id))
-    held = joined(held, moved)
-    early, late = [h[:, :cut] for h in held], [h[:, cut:] for h in held]
-    early = joined(early, moved_over(early, 4))
+    moved = moved_over(held, 4)
+
+    own = lax.dynamic_index_in_dim(tokens, unit_id, 0, keepdims=False)
+    both = jnp.concatenate([own, swap(own)], axis=0)
+    pick = jnp.arange(model_dim, dtype=jnp.int32)[:, None] == row_sources(me, core, model_dim)[None]
+    both = jnp.dot(both, pick.astype(BF), preferred_element_type=F32).astype(BF)
+    small = (meta, row_places(me, core), jnp.pad(step_bias, (0, spare)), jnp.pad(log_rate, (0, spare)))
+    moved, both, small = lax.optimization_barrier((moved, both, small))
+    meta, places, bias, log_rate = small
+
+    early = joined([h[:, :cut] for h in held], [m[:, :cut] for m in moved])
+    late = joined([h[:, cut:] for h in held], [m[:, cut:] for m in moved])
     moved, late = lax.optimization_barrier((moved_over(early, 5), late))
-    early = [piece for both in zip(early, moved) for piece in both]
-    late = joined(late, moved_over(late, 4))
-    own = lax.dynamic_index_in_dim(tokens, unit_id, 0, keepdims=False)
-    length = lax.dynamic_slice_in_dim(lengths, unit_id, 1, 0)
-    coded = jnp.stack([length // 16, length % 16], axis=1).astype(BF)
-    coded = jnp.pad(coded, ((0, 7), (0, model_dim - 2)))
-    other = swap(jnp.concatenate([own, coded], axis=0))
-    code = other[seq_len, :2].astype(jnp.int32)
-    meta = jnp.stack([core, length[0], code[0] * 16 + code[1]])
-    both = jnp.concatenate([own, other[:seq_len]], axis=0)
-    pick = jnp.arange(model_dim, dtype=jnp.int32)[:, None] == row_sources(me, core)[None]
-    both = jnp.dot(both, pick.astype(BF), preferred_element_type=F32).astype(BF)
-
-    projected, late = lax.optimization_barrier((project(both, early), late))
+    early = [piece for two in zip(early, moved) for piece in two]
     late = [piece for two in zip(late, moved_over(late, 5)) for piece in two]
+
+    projected = project(both, early)
     scanned, state = scan(
         meta,
         projected,
         conv_weight,
-        jnp.pad(step_bias, (0, spare))[None],
-        jnp.pad(log_rate, (0, spare))[None],
+        bias[None],
+        log_rate[None],
         skip_gain,
         width,
     )
     state_other = swap(state[1])
     gain = norm_gain[None]
     sent, square_sent = gating(1, meta, both, scanned, gain, late)
-    share, square_other = swap(out_share(sent, out_weight)), swap(square_sent)
+    share, square_other = swap(out_share(places, sent, late)), swap(square_sent)
     mine, square = gating(0, meta, both, scanned, gain, late)
-    mixed = mix(meta, mine, out_weight, share, square, square_other)
+    mixed = mix(meta, places, mine, share, square, square_other, late)
     state = jnp.concatenate(
         [jnp.where(first_core, state[0], state_other), jnp.where(first_core, state_other, state[0])]
     )

time: 179 us -> 142 us (0.79); the launches traced: 176 us -> 142 us
  between operations: 18.5 us -> 5.05 us
  waiting for transfers between devices: 45.2 us -> 35.9 us
  Pallas kernels: 50.4 us -> 41.5 us
  other arithmetic: 12.2 us -> 8.92 us
  starting transfers between devices: 36.8 us -> 39.9 us
  local copies, waits for them, and re-layouts: 8.95 us -> 6.38 us
    ppermute x29 -> x26, waiting for transfers between devices: 45.2 us -> 35.9 us  [hop(): lax.ppermute(value, EVERYONE, [(d, d ^ mask_of(d // CORE % 2)) for d in r...]
    pallas_call x2, Pallas kernels: 13 us -> 8.27 us  [gating(): pl.pallas_call(gate_kernel, grid_spec=pltpu.PrefetchScalarGridSpec(num_sc...]
    ppermute x29 -> x26, starting transfers between devices: 36.8 us -> 39.9 us  [hop(): lax.ppermute(value, EVERYONE, [(d, d ^ mask_of(d // CORE % 2)) for d in r...]
    pallas_call x2, Pallas kernels: 22.1 us -> 20 us  [the longest x1 15.9 us: scan(): pl.pallas_call(scan_kernel, grid_spec=grid_spec, out_shape=[jax.ShapeDtyp...]
    concatenate x3 -> x0, other arithmetic: 1.85 us -> none  [the longest x1 1.2 us: body(): other = swap(jnp.concatenate([own, coded], axis=0))]
    unnamed x42 -> x16, local copies, waits for them, and re-layouts: 3.01 us -> 1.16 us
  transfers between devices with their start and end apart: 30 -> 26, of which waited for: 12 -> 11; matrix products, arithmetic and copies ran while one was open for 10% -> 8% of each run, Pallas kernels for 21% -> 19%
where the time goes in v5:
time: 142 us
  Pallas kernels  41.5 us (29%)
  starting transfers between devices  39.9 us (28%)
  waiting for transfers between devices  35.9 us (25%)
  other arithmetic  8.92 us (6%)
  local copies, waits for them, and re-layouts  6.38 us (4%)
  between operations  5.05 us (4%)
  matrix products  4.13 us (3%)
    ppermute x26, starting transfers between devices, hop(): lax.ppermute(value, EVERYONE, [(d, d ^ mask_of(d // CORE % 2)) for d in r...  39.9 us
    ppermute x26, waiting for transfers between devices, hop(): lax.ppermute(value, EVERYONE, [(d, d ^ mask_of(d // CORE % 2)) for d in r...  35.9 us
    pallas_call x1, Pallas kernels, scan(): pl.pallas_call(scan_kernel, grid_spec=grid_spec, out_shape=[jax.ShapeDtyp...  15.9 us
    pallas_call x2, Pallas kernels, gating(): pl.pallas_call(gate_kernel, grid_spec=pltpu.PrefetchScalarGridSpec(num_sc...  8.27 us
    pallas_call x1, Pallas kernels, project(): pl.pallas_call(project_kernel, grid=(steps,), in_specs=[pl.BlockSpec((row...  6.81 us
    pallas_call x1, Pallas kernels, mix(): pl.pallas_call(mix_kernel, grid_spec=pltpu.PrefetchScalarGridSpec(num_sca...  6.39 us
    another operation x5, other arithmetic  4.24 us
    pallas_call x1, Pallas kernels, out_share(): pl.pallas_call(share_kernel, grid_spec=pltpu.PrefetchScalarGridSpec(num_s...  4.15 us
  transfers between devices with their start and end apart: 26, of which 11 were waited for; matrix products, arithmetic and copies ran while one was open for 8% of the time, Pallas kernels for 19%

profile of v5, /device:TPU:1, one launch (start us, length us, event | category | flops | bytes accessed | tf_op | source)
XLA Modules:
  0.0 141.8 jit_solution(8416015278147748106)
XLA Ops:
  11.8 2.6 %collective-permute-start.1 = (bf16[8,4992]{1,0:T(8,128)(2,1)S(1)}, bf16[8,4992]{1,0:T(8,128)(2,1)S(1)}, u32[]{:S(2)}, u32[]{:S(2)}) collective-permute-start(bf16[8,4992]{1,0:T(8,128)(2,1)S(1)} %get-tuple-element.56), channel_id=1, source_target_pairs={{0,4},{1,5},{2,6},{3,7},{4,0},{5,1},{6,2},{7,3},{8,12},{9,13},{10,... | collective-permute-start | bytes 239624 | tf_op jit(solution)/shard_map/ppermute | solution.py:399
  14.4 2.7 %collective-permute-start.4 = (bf16[8,4992]{1,0:T(8,128)(2,1)S(1)}, bf16[8,4992]{1,0:T(8,128)(2,1)S(1)}, u32[]{:S(2)}, u32[]{:S(2)}) collective-permute-start(bf16[8,4992]{1,0:T(8,128)(2,1)S(1)} %get-tuple-element.55), channel_id=1, source_target_pairs={{0,1},{1,0},{2,3},{3,2},{4,5},{5,4},{6,7},{7,6},{8,9},{9,8},{10,11... | collective-permute-start | bytes 239624 | tf_op jit(solution)/shard_map/ppermute | solution.py:399
  17.1 3.8 %collective-permute-start.7 = (bf16[8,4992]{1,0:T(8,128)(2,1)S(1)}, bf16[8,4992]{1,0:T(8,128)(2,1)S(1)}, u32[]{:S(2)}, u32[]{:S(2)}) collective-permute-start(bf16[8,4992]{1,0:T(8,128)(2,1)S(1)} %get-tuple-element.54), channel_id=1, source_target_pairs={{0,32},{1,33},{2,34},{3,35},{4,36},{5,37},{6,38},{7,39},{8,40},{9,... | collective-permute-start | bytes 239624 | tf_op jit(solution)/shard_map/ppermute | solution.py:399
  21.0 2.1 %collective-permute-start.5 = (bf16[16,4992]{1,0:T(8,128)(2,1)S(1)}, bf16[16,4992]{1,0:T(8,128)(2,1)S(1)}, u32[]{:S(2)}, u32[]{:S(2)}) collective-permute-start(bf16[16,4992]{1,0:T(8,128)(2,1)S(1)} %pad_maximum_fusion.17), channel_id=1, source_target_pairs={{0,32},{1,33},{2,34},{3,35},{4,36},{5,37},{6,38},{7,39},{8,40},{9,... | collective-permute-start | bytes 479240 | tf_op jit(solution)/shard_map/ppermute | solution.py:399
  23.5 3.1 %collective-permute-done.2 = bf16[16,4992]{1,0:T(8,128)(2,1)S(1)} collective-permute-done((bf16[16,4992]{1,0:T(8,128)(2,1)S(1)}, bf16[16,4992]{1,0:T(8,128)(2,1)S(1)}, u32[]{:S(2)}, u32[]{:S(2)}) %collective-permute-start.2) | collective-permute-done | bytes 159776 | tf_op jit(solution)/shard_map/ppermute | solution.py:399
  27.7 6.3 %collective-permute-done.3 = bf16[32,4992]{1,0:T(8,128)(2,1)S(1)} collective-permute-done((bf16[32,4992]{1,0:T(8,128)(2,1)S(1)}, bf16[32,4992]{1,0:T(8,128)(2,1)S(1)}, u32[]{:S(2)}, u32[]{:S(2)}) %collective-permute-start.3) | collective-permute-done | bytes 319520 | tf_op jit(solution)/shard_map/ppermute | solution.py:399
  36.3 8.3 %collective-permute-start.16 = (bf16[384,1536]{1,0:T(8,128)(2,1)S(1)}, bf16[384,1536]{1,0:T(8,128)(2,1)S(1)}, u32[]{:S(2)}, u32[]{:S(2)}) collective-permute-start(bf16[384,1536]{1,0:T(8,128)(2,1)S(1)} %dynamic-slice_bitcast_fusion), channel_id=1, source_target_pairs={{0,16},{1,17},{2,18},{3,19},{4,20},{5,21},{6,22},{7,23},{8,24},{9,... | collective-permute-start | bytes 3538952 | tf_op jit(solution)/shard_map/ppermute | solution.py:399
  51.0 4.1 %fusion.2.tokens_ref = bf16[768,1536]{1,0:T(8,128)(2,1)S(1)} fusion(s32[1536]{0:T(1024)S(1)} %select_subtract_fusion, bf16[384,1536]{1,0:T(8,128)(2,1)S(1)} %collective-permute-done.16, bf16[384,1536]{1,0:T(8,128)(2,1)S(1)} %dynamic-slice_bitcast_fusion), kind=kOutput, calls=%fused_computation.3 | convolution fusion | flops 3632136192 | bytes 4724736 | tf_op jit(solution)/shard_map/dot_general | solution.py:498
  55.1 6.1 %collective-permute-done.11 = bf16[128,4992]{1,0:T(8,128)(2,1)S(1)} collective-permute-done((bf16[128,4992]{1,0:T(8,128)(2,1)S(1)}, bf16[128,4992]{1,0:T(8,128)(2,1)S(1)}, u32[]{:S(2)}, u32[]{:S(2)}) %collective-permute-start.11) | collective-permute-done | bytes 1277984 | tf_op jit(solution)/shard_map/ppermute | solution.py:399
  62.5 1.9 %collective-permute-done.15 = bf16[128,4992]{1,0:T(8,128)(2,1)S(1)} collective-permute-done((bf16[128,4992]{1,0:T(8,128)(2,1)S(1)}, bf16[128,4992]{1,0:T(8,128)(2,1)S(1)}, u32[]{:S(2)}, u32[]{:S(2)}) %collective-permute-start.15) | collective-permute-done | bytes 1277984 | tf_op jit(solution)/shard_map/ppermute | solution.py:399
  67.0 1.5 %collective-permute-start.18 = (bf16[256,1920]{1,0:T(8,128)(2,1)S(1)}, bf16[256,1920]{1,0:T(8,128)(2,1)S(1)}, u32[]{:S(2)}, u32[]{:S(2)}) collective-permute-start(bf16[256,1920]{1,0:T(8,128)(2,1)S(1)} %pad_maximum_fusion.8.refs_2_), channel_id=1, source_target_pairs={{0,4},{1,5},{2,6},{3,7},{4,0},{5,1},{6,2},{7,3},{8,12},{9,13},{10,... | collective-permute-start | bytes 2949128 | tf_op jit(solution)/shard_map/ppermute | solution.py:399
  68.6 2.4 %collective-permute-start.19 = (bf16[256,1920]{1,0:T(8,128)(2,1)S(1)}, bf16[256,1920]{1,0:T(8,128)(2,1)S(1)}, u32[]{:S(2)}, u32[]{:S(2)}) collective-permute-start(bf16[256,1920]{1,0:T(8,128)(2,1)S(1)} %pad_maximum_fusion.9.refs_4_), channel_id=1, source_target_pairs={{0,1},{1,0},{2,3},{3,2},{4,5},{5,4},{6,7},{7,6},{8,9},{9,8},{10,11... | collective-permute-start | bytes 2949128 | tf_op jit(solution)/shard_map/ppermute | solution.py:399
  72.4 6.8 %collective-permute-done.17.refs_1_ = bf16[256,1920]{1,0:T(8,128)(2,1)S(1)} collective-permute-done((bf16[256,1920]{1,0:T(8,128)(2,1)S(1)}, bf16[256,1920]{1,0:T(8,128)(2,1)S(1)}, u32[]{:S(2)}, u32[]{:S(2)}) %collective-permute-start.17) | collective-permute-done | bytes 983072 | tf_op jit(solution)/shard_map/ppermute | solution.py:399
  79.2 2.3 %collective-permute-done.18.refs_3_ = bf16[256,1920]{1,0:T(8,128)(2,1)S(1)} collective-permute-done((bf16[256,1920]{1,0:T(8,128)(2,1)S(1)}, bf16[256,1920]{1,0:T(8,128)(2,1)S(1)}, u32[]{:S(2)}, u32[]{:S(2)}) %collective-permute-start.18) | collective-permute-done | bytes 983072 | tf_op jit(solution)/shard_map/ppermute | solution.py:399
  81.6 1.6 %collective-permute-done.19.refs_5_ = bf16[256,1920]{1,0:T(8,128)(2,1)S(1)} collective-permute-done((bf16[256,1920]{1,0:T(8,128)(2,1)S(1)}, bf16[256,1920]{1,0:T(8,128)(2,1)S(1)}, u32[]{:S(2)}, u32[]{:S(2)}) %collective-permute-start.19) | collective-permute-done | bytes 983072 | tf_op jit(solution)/shard_map/ppermute | solution.py:399
  84.7 2.0 %collective-permute-start.22 = (bf16[256,3072]{1,0:T(8,128)(2,1)S(1)}, bf16[256,3072]{1,0:T(8,128)(2,1)S(1)}, u32[]{:S(2)}, u32[]{:S(2)}) collective-permute-start(bf16[256,3072]{1,0:T(8,128)(2,1)S(1)} %pad_maximum_fusion.2.refs_4_), channel_id=1, source_target_pairs={{0,1},{1,0},{2,3},{3,2},{4,5},{5,4},{6,7},{7,6},{8,9},{9,8},{10,11... | collective-permute-start | bytes 4718600 | tf_op jit(solution)/shard_map/ppermute | solution.py:399
  86.7 6.8 %project.1.input_ref.side_ref = bf16[768,1920]{1,0:T(8,128)(2,1)S(1)} custom-call(bf16[768,1536]{1,0:T(8,128)(2,1)S(1)} %fusion.2.tokens_ref, bf16[256,1920]{1,0:T(8,128)(2,1)S(1)} %pad_maximum_fusion.7.refs_0_, bf16[256,1920]{1,0:T(8,128)(2,1)S(1)} %collective-permute-done.17.refs_1_, bf16[256,1920]{1,0:T(8,128)(2,1)S(1)} %pad_maximum_fusion.8.refs_2_, ...), custom_call_target="tpu_custom_call" | custom-call | flops 4529848320 | bytes 10485760 | tf_op jit(solution)/shard_map/project/pallas_call | solution.py:211
  93.5 15.9 %scan.1 = (f32[2,384,1536]{2,1,0:T(8,128)S(1)}, f32[2,1536,128]{2,1,0:T(8,128)S(1)}) custom-call(s32[3]{0:T(128)S(1)} %pad_add_fusion.meta_ref, bf16[768,1920]{1,0:T(8,128)(2,1)S(1)} %project.1.input_ref.side_ref, bf16[768,1920]{1,0:T(8,128)(2,1)S(1)} %project.1.input_ref.side_ref, f32[4,3328]{1,0:T(4,128)S(1)} %copy-done.1, f32[4,3328]{1,0:T(4,128)S(1)} %copy-done.1, ...), custom_call_target="tpu_custom_call" | custom-call | flops 1509949440 | bytes 9437184 | tf_op jit(solution)/shard_map/scan/pallas_call | solution.py:184
  109.4 4.1 %gating.3 = (bf16[384,1536]{1,0:T(8,128)(2,1)S(1)}, f32[384,128]{1,0:T(8,128)S(1)}) custom-call(s32[3]{0:T(128)S(1)} %pad_add_fusion.meta_ref, bf16[768,1536]{1,0:T(8,128)(2,1)S(1)} %fusion.2.tokens_ref, f32[2,384,1536]{2,1,0:T(8,128)S(1)} %get-tuple-element.41.scanned_ref, f32[1,3072]{1,0:T(1,128)S(1)} %bitcast.16, ...), custom_call_target="tpu_custom_call" | custom-call | flops 1811939328 | bytes 10485760 | tf_op jit(solution)/shard_map/gating/pallas_call | solution.py:250
  113.6 4.2 %out_share.1 = f32[1536,384]{1,0:T(8,128)S(1)} custom-call(s32[192]{0:T(256)S(1)} %multiply_add_fusion.places_ref, bf16[384,1536]{1,0:T(8,128)(2,1)S(1)} %get-tuple-element.46.gated_ref, bf16[256,3072]{1,0:T(8,128)(2,1)S(1)} %pad_maximum_fusion.refs_0_, bf16[256,3072]{1,0:T(8,128)(2,1)S(1)} %collective-permute-done.20.refs_1_, ...), custom_call_target="tpu_custom_call" | custom-call | flops 1811939328 | bytes 8388608 | tf_op jit(solution)/shard_map/out_share/pallas_call | solution.py:306
  117.7 6.4 %collective-permute-start.23 = (f32[1536,384]{1,0:T(8,128)S(1)}, f32[1536,384]{1,0:T(8,128)S(1)}, u32[]{:S(2)}, u32[]{:S(2)}) collective-permute-start(f32[1536,384]{1,0:T(8,128)S(1)} %out_share.1), channel_id=1, source_target_pairs={{0,16},{1,17},{2,18},{3,19},{4,20},{5,21},{6,22},{7,23},{8,24},{9,... | collective-permute-start | bytes 7077896 | tf_op jit(solution)/shard_map/ppermute | solution.py:399
  124.5 5.0 %collective-permute-done.25 = f32[1536,128]{1,0:T(8,128)S(1)} collective-permute-done((f32[1536,128]{1,0:T(8,128)S(1)}, f32[1536,128]{1,0:T(8,128)S(1)}, u32[]{:S(2)}, u32[]{:S(2)}) %collective-permute-start.25) | collective-permute-done | bytes 786464 | tf_op jit(solution)/shard_map/ppermute | solution.py:399
  131.2 4.1 %gating.2 = (bf16[384,1536]{1,0:T(8,128)(2,1)S(1)}, f32[384,128]{1,0:T(8,128)S(1)}) custom-call(s32[3]{0:T(128)S(1)} %pad_add_fusion.meta_ref, bf16[768,1536]{1,0:T(8,128)(2,1)S(1)} %fusion.2.tokens_ref, f32[2,384,1536]{2,1,0:T(8,128)S(1)} %get-tuple-element.41.scanned_ref, f32[1,3072]{1,0:T(1,128)S(1)} %bitcast.17, ...), custom_call_target="tpu_custom_call" | custom-call | flops 1811939328 | bytes 10485760 | tf_op jit(solution)/shard_map/gating/pallas_call | solution.py:250
  135.4 6.4 %mix.1 = bf16[384,1536]{1,0:T(8,128)(2,1)} custom-call(s32[3]{0:T(128)S(1)} %pad_add_fusion.meta_ref, s32[192]{0:T(256)S(1)} %multiply_add_fusion.places_ref, bf16[384,1536]{1,0:T(8,128)(2,1)S(1)} %get-tuple-element.45.mine_ref, f32[1536,384]{1,0:T(8,128)S(1)} %collective-permute-done.23.share_ref, f32[384,128]{1,0:T(8,128)S(1)} %get-tuple-element.47.sq_mine, ...), custom_call_target="tpu_custom_call" | custom-call | flops 1811939328 | bytes 8388608 | tf_op jit(solution)/shard_map/mix/pallas_call | solution.py:358
  (115 shorter events, 26.1 us)
Async XLA Ops:
  11.8 9.1 %collective-permute-start.1 = (bf16[8,4992]{1,0:T(8,128)(2,1)S(1)}, bf16[8,4992]{1,0:T(8,128)(2,1)S(1)}, u32[]{:S(2)}, u32[]{:S(2)}) collective-permute-start(bf16[8,4992]{1,0:T(8,128)(2,1)S(1)} %get-tuple-element.56), channel_id=1, source_target_pairs={{0,4},{1,5},{2,6},{3,7},{4,0},{5,1},{6,2},{7,3},{8,12},{9,13},{10,... | collective-permute-start | bytes 239624 | tf_op jit(solution)/shard_map/ppermute | solution.py:399
  14.4 6.6 %collective-permute-start.4 = (bf16[8,4992]{1,0:T(8,128)(2,1)S(1)}, bf16[8,4992]{1,0:T(8,128)(2,1)S(1)}, u32[]{:S(2)}, u32[]{:S(2)}) collective-permute-start(bf16[8,4992]{1,0:T(8,128)(2,1)S(1)} %get-tuple-element.55), channel_id=1, source_target_pairs={{0,1},{1,0},{2,3},{3,2},{4,5},{5,4},{6,7},{7,6},{8,9},{9,8},{10,11... | collective-permute-start | bytes 239624 | tf_op jit(solution)/shard_map/ppermute | solution.py:399
  17.1 6.0 %collective-permute-start.7 = (bf16[8,4992]{1,0:T(8,128)(2,1)S(1)}, bf16[8,4992]{1,0:T(8,128)(2,1)S(1)}, u32[]{:S(2)}, u32[]{:S(2)}) collective-permute-start(bf16[8,4992]{1,0:T(8,128)(2,1)S(1)} %get-tuple-element.54), channel_id=1, source_target_pairs={{0,32},{1,33},{2,34},{3,35},{4,36},{5,37},{6,38},{7,39},{8,40},{9,... | collective-permute-start | bytes 239624 | tf_op jit(solution)/shard_map/ppermute | solution.py:399
  20.9 5.7 %collective-permute-start.2 = (bf16[16,4992]{1,0:T(8,128)(2,1)S(1)}, bf16[16,4992]{1,0:T(8,128)(2,1)S(1)}, u32[]{:S(2)}, u32[]{:S(2)}) collective-permute-start(bf16[16,4992]{1,0:T(8,128)(2,1)S(1)} %pad_maximum_fusion.16), channel_id=1, source_target_pairs={{0,1},{1,0},{2,3},{3,2},{4,5},{5,4},{6,7},{7,6},{8,9},{9,8},{10,11... | collective-permute-start | bytes 479240 | tf_op jit(solution)/shard_map/ppermute | solution.py:399
  21.0 5.7 %collective-permute-start.5 = (bf16[16,4992]{1,0:T(8,128)(2,1)S(1)}, bf16[16,4992]{1,0:T(8,128)(2,1)S(1)}, u32[]{:S(2)}, u32[]{:S(2)}) collective-permute-start(bf16[16,4992]{1,0:T(8,128)(2,1)S(1)} %pad_maximum_fusion.17), channel_id=1, source_target_pairs={{0,32},{1,33},{2,34},{3,35},{4,36},{5,37},{6,38},{7,39},{8,40},{9,... | collective-permute-start | bytes 479240 | tf_op jit(solution)/shard_map/ppermute | solution.py:399
  26.6 7.4 %collective-permute-start.3 = (bf16[32,4992]{1,0:T(8,128)(2,1)S(1)}, bf16[32,4992]{1,0:T(8,128)(2,1)S(1)}, u32[]{:S(2)}, u32[]{:S(2)}) collective-permute-start(bf16[32,4992]{1,0:T(8,128)(2,1)S(1)} %pad_maximum_fusion.13), channel_id=1, source_target_pairs={{0,32},{1,33},{2,34},{3,35},{4,36},{5,37},{6,38},{7,39},{8,40},{9,... | collective-permute-start | bytes 958472 | tf_op jit(solution)/shard_map/ppermute | solution.py:399
  26.8 7.4 %collective-permute-start.6 = (bf16[32,4992]{1,0:T(8,128)(2,1)S(1)}, bf16[32,4992]{1,0:T(8,128)(2,1)S(1)}, u32[]{:S(2)}, u32[]{:S(2)}) collective-permute-start(bf16[32,4992]{1,0:T(8,128)(2,1)S(1)} %pad_maximum_fusion.14), channel_id=1, source_target_pairs={{0,12},{1,13},{2,14},{3,15},{4,8},{5,9},{6,10},{7,11},{8,4},{9,5},... | collective-permute-start | bytes 958472 | tf_op jit(solution)/shard_map/ppermute | solution.py:399
  27.6 6.6 %collective-permute-start.9 = (bf16[32,4992]{1,0:T(8,128)(2,1)S(1)}, bf16[32,4992]{1,0:T(8,128)(2,1)S(1)}, u32[]{:S(2)}, u32[]{:S(2)}) collective-permute-start(bf16[32,4992]{1,0:T(8,128)(2,1)S(1)} %pad_maximum_fusion.15), channel_id=1, source_target_pairs={{0,3},{1,2},{2,1},{3,0},{4,7},{5,6},{6,5},{7,4},{8,11},{9,10},{10,... | collective-permute-start | bytes 958472 | tf_op jit(solution)/shard_map/ppermute | solution.py:399
  34.3 10.4 %collective-permute-start.10 = (bf16[64,4992]{1,0:T(8,128)(2,1)S(1)}, bf16[64,4992]{1,0:T(8,128)(2,1)S(1)}, u32[]{:S(2)}, u32[]{:S(2)}) collective-permute-start(bf16[64,4992]{1,0:T(8,128)(2,1)S(1)} %pad_maximum_fusion.10), channel_id=1, source_target_pairs={{0,12},{1,13},{2,14},{3,15},{4,8},{5,9},{6,10},{7,11},{8,4},{9,5},... | collective-permute-start | bytes 1916936 | tf_op jit(solution)/shard_map/ppermute | solution.py:399
  34.8 10.1 %collective-permute-start.12 = (bf16[64,4992]{1,0:T(8,128)(2,1)S(1)}, bf16[64,4992]{1,0:T(8,128)(2,1)}, u32[]{:S(2)}, u32[]{:S(2)}) collective-permute-start(bf16[64,4992]{1,0:T(8,128)(2,1)S(1)} %pad_maximum_fusion.11), channel_id=1, source_target_pairs={{0,3},{1,2},{2,1},{3,0},{4,7},{5,6},{6,5},{7,4},{8,11},{9,10},{10,... | collective-permute-start | bytes 1916936 | tf_op jit(solution)/shard_map/ppermute | solution.py:399
  34.9 11.8 %collective-permute-start.14 = (bf16[64,4992]{1,0:T(8,128)(2,1)S(1)}, bf16[64,4992]{1,0:T(8,128)(2,1)S(1)}, u32[]{:S(2)}, u32[]{:S(2)}) collective-permute-start(bf16[64,4992]{1,0:T(8,128)(2,1)S(1)} %pad_maximum_fusion.12), channel_id=1, source_target_pairs={{0,96},{1,97},{2,98},{3,99},{4,100},{5,101},{6,102},{7,103},{8,104... | collective-permute-start | bytes 1916936 | tf_op jit(solution)/shard_map/ppermute | solution.py:399
  36.3 14.6 %collective-permute-start.16 = (bf16[384,1536]{1,0:T(8,128)(2,1)S(1)}, bf16[384,1536]{1,0:T(8,128)(2,1)S(1)}, u32[]{:S(2)}, u32[]{:S(2)}) collective-permute-start(bf16[384,1536]{1,0:T(8,128)(2,1)S(1)} %dynamic-slice_bitcast_fusion), channel_id=1, source_target_pairs={{0,16},{1,17},{2,18},{3,19},{4,20},{5,21},{6,22},{7,23},{8,24},{9,... | collective-permute-start | bytes 3538952 | tf_op jit(solution)/shard_map/ppermute | solution.py:399
  44.8 16.5 %collective-permute-start.11 = (bf16[128,4992]{1,0:T(8,128)(2,1)S(1)}, bf16[128,4992]{1,0:T(8,128)(2,1)S(1)}, u32[]{:S(2)}, u32[]{:S(2)}) collective-permute-start(bf16[128,4992]{1,0:T(8,128)(2,1)S(1)} %pad_maximum_fusion.4), channel_id=1, source_target_pairs={{0,3},{1,2},{2,1},{3,0},{4,7},{5,6},{6,5},{7,4},{8,11},{9,10},{10,... | collective-permute-start | bytes 3833864 | tf_op jit(solution)/shard_map/ppermute | solution.py:399
  46.0 16.5 %collective-permute-start.13 = (bf16[128,4992]{1,0:T(8,128)(2,1)S(1)}, bf16[128,4992]{1,0:T(8,128)(2,1)S(1)}, u32[]{:S(2)}, u32[]{:S(2)}) collective-permute-start(bf16[128,4992]{1,0:T(8,128)(2,1)S(1)} %pad_maximum_fusion.5), channel_id=1, source_target_pairs={{0,96},{1,97},{2,98},{3,99},{4,100},{5,101},{6,102},{7,103},{8,104... | collective-permute-start | bytes 3833864 | tf_op jit(solution)/shard_map/ppermute | solution.py:399
  46.7 17.7 %collective-permute-start.15 = (bf16[128,4992]{1,0:T(8,128)(2,1)S(1)}, bf16[128,4992]{1,0:T(8,128)(2,1)S(1)}, u32[]{:S(2)}, u32[]{:S(2)}) collective-permute-start(bf16[128,4992]{1,0:T(8,128)(2,1)S(1)} %pad_maximum_fusion.6), channel_id=1, source_target_pairs={{0,4},{1,5},{2,6},{3,7},{4,0},{5,1},{6,2},{7,3},{8,12},{9,13},{10,... | collective-permute-start | bytes 3833864 | tf_op jit(solution)/shard_map/ppermute | solution.py:399
  65.9 13.3 %collective-permute-start.17 = (bf16[256,1920]{1,0:T(8,128)(2,1)S(1)}, bf16[256,1920]{1,0:T(8,128)(2,1)S(1)}, u32[]{:S(2)}, u32[]{:S(2)}) collective-permute-start(bf16[256,1920]{1,0:T(8,128)(2,1)S(1)} %pad_maximum_fusion.7.refs_0_), channel_id=1, source_target_pairs={{0,96},{1,97},{2,98},{3,99},{4,100},{5,101},{6,102},{7,103},{8,104... | collective-permute-start | bytes 2949128 | tf_op jit(solution)/shard_map/ppermute | solution.py:399
  67.0 14.5 %collective-permute-start.18 = (bf16[256,1920]{1,0:T(8,128)(2,1)S(1)}, bf16[256,1920]{1,0:T(8,128)(2,1)S(1)}, u32[]{:S(2)}, u32[]{:S(2)}) collective-permute-start(bf16[256,1920]{1,0:T(8,128)(2,1)S(1)} %pad_maximum_fusion.8.refs_2_), channel_id=1, source_target_pairs={{0,4},{1,5},{2,6},{3,7},{4,0},{5,1},{6,2},{7,3},{8,12},{9,13},{10,... | collective-permute-start | bytes 2949128 | tf_op jit(solution)/shard_map/ppermute | solution.py:399
  68.6 14.5 %collective-permute-start.19 = (bf16[256,1920]{1,0:T(8,128)(2,1)S(1)}, bf16[256,1920]{1,0:T(8,128)(2,1)S(1)}, u32[]{:S(2)}, u32[]{:S(2)}) collective-permute-start(bf16[256,1920]{1,0:T(8,128)(2,1)S(1)} %pad_maximum_fusion.9.refs_4_), channel_id=1, source_target_pairs={{0,1},{1,0},{2,3},{3,2},{4,5},{5,4},{6,7},{7,6},{8,9},{9,8},{10,11... | collective-permute-start | bytes 2949128 | tf_op jit(solution)/shard_map/ppermute | solution.py:399
  83.2 26.2 %collective-permute-start.20 = (bf16[256,3072]{1,0:T(8,128)(2,1)S(1)}, bf16[256,3072]{1,0:T(8,128)(2,1)S(1)}, u32[]{:S(2)}, u32[]{:S(2)}) collective-permute-start(bf16[256,3072]{1,0:T(8,128)(2,1)S(1)} %pad_maximum_fusion.refs_0_), channel_id=1, source_target_pairs={{0,96},{1,97},{2,98},{3,99},{4,100},{5,101},{6,102},{7,103},{8,104... | collective-permute-start | bytes 4718600 | tf_op jit(solution)/shard_map/ppermute | solution.py:399
  83.4 26.0 %collective-permute-start.21 = (bf16[256,3072]{1,0:T(8,128)(2,1)S(1)}, bf16[256,3072]{1,0:T(8,128)(2,1)S(1)}, u32[]{:S(2)}, u32[]{:S(2)}) collective-permute-start(bf16[256,3072]{1,0:T(8,128)(2,1)S(1)} %pad_maximum_fusion.1.refs_2_), channel_id=1, source_target_pairs={{0,4},{1,5},{2,6},{3,7},{4,0},{5,1},{6,2},{7,3},{8,12},{9,13},{10,... | collective-permute-start | bytes 4718600 | tf_op jit(solution)/shard_map/ppermute | solution.py:399
  84.7 24.8 %collective-permute-start.22 = (bf16[256,3072]{1,0:T(8,128)(2,1)S(1)}, bf16[256,3072]{1,0:T(8,128)(2,1)S(1)}, u32[]{:S(2)}, u32[]{:S(2)}) collective-permute-start(bf16[256,3072]{1,0:T(8,128)(2,1)S(1)} %pad_maximum_fusion.2.refs_4_), channel_id=1, source_target_pairs={{0,1},{1,0},{2,3},{3,2},{4,5},{5,4},{6,7},{7,6},{8,9},{9,8},{10,11... | collective-permute-start | bytes 4718600 | tf_op jit(solution)/shard_map/ppermute | solution.py:399
  117.7 17.6 %collective-permute-start.23 = (f32[1536,384]{1,0:T(8,128)S(1)}, f32[1536,384]{1,0:T(8,128)S(1)}, u32[]{:S(2)}, u32[]{:S(2)}) collective-permute-start(f32[1536,384]{1,0:T(8,128)S(1)} %out_share.1), channel_id=1, source_target_pairs={{0,16},{1,17},{2,18},{3,19},{4,20},{5,21},{6,22},{7,23},{8,24},{9,... | collective-permute-start | bytes 7077896 | tf_op jit(solution)/shard_map/ppermute | solution.py:399
  124.2 5.2 %collective-permute-start.25 = (f32[1536,128]{1,0:T(8,128)S(1)}, f32[1536,128]{1,0:T(8,128)S(1)}, u32[]{:S(2)}, u32[]{:S(2)}) collective-permute-start(f32[1536,128]{1,0:T(8,128)S(1)} %slice_bitcast_fusion), channel_id=1, source_target_pairs={{0,16},{1,17},{2,18},{3,19},{4,20},{5,21},{6,22},{7,23},{8,24},{9,... | collective-permute-start | bytes 2359304 | tf_op jit(solution)/shard_map/ppermute | solution.py:399
  129.5 5.8 %collective-permute-start.24 = (f32[384,128]{1,0:T(8,128)S(1)}, f32[384,128]{1,0:T(8,128)S(1)}, u32[]{:S(2)}, u32[]{:S(2)}) collective-permute-start(f32[384,128]{1,0:T(8,128)S(1)} %get-tuple-element.48), channel_id=1, source_target_pairs={{0,16},{1,17},{2,18},{3,19},{4,20},{5,21},{6,22},{7,23},{8,24},{9,... | collective-permute-start | bytes 589832 | tf_op jit(solution)/shard_map/ppermute | solution.py:399
  (16 other events, 87.0 us)

commit v6 on v5

--- a/solution.py
+++ b/solution.py
@@ -1,3 +1,5 @@
+import functools
+
 import jax
 import jax.numpy as jnp
 from jax import lax
@@ -19,16 +21,20 @@
 
 
 def causal_conv(values, taps):
-    rows = lax.broadcasted_iota(jnp.int32, values.shape, 0)
+    rows = lax.broadcasted_iota(jnp.int32, (BLOCK_ROWS, values.shape[1]), 0)
     count = taps.shape[0]
     total = values * taps[count - 1 : count]
     for back in range(1, count):
-        moved = jnp.where(rows >= back, pltpu.roll(values, back, 0), 0.0)
+        moved = pltpu.roll(values, back, 0)
+        moved = jnp.concatenate(
+            [jnp.where(rows >= back, moved[:BLOCK_ROWS], 0.0), moved[BLOCK_ROWS:]], axis=0
+        )
         total = total + moved * taps[count - 1 - back : count - back]
     return silu(total)
 
 
 def scan_kernel(
+    which,
     meta_ref,
     input_ref,
     side_ref,
@@ -46,14 +52,13 @@
     c_scr,
     cb_scr,
 ):
-    which = pl.program_id(0)
-    step = pl.program_id(1)
+    step = pl.program_id(0)
     seq = input_ref.shape[0]
     state_dim = side_taps_ref.shape[1] // 2
     groups = decay_col.shape[0]
     blocks = seq // SPAN
     position = lax.broadcasted_iota(jnp.int32, (seq, LANES), 0)
-    group_here = meta_ref[0] * pl.num_programs(1) + step
+    group_here = meta_ref[0] * pl.num_programs(0) + step
 
     @pl.when(step == 0)
     def _():
@@ -68,10 +73,11 @@
             cb_scr[block] = lax.dot_general(
                 c_short[at], b_short[at], (((1,), (1,)), ((), ())), preferred_element_type=F32
             )
-        raw = side[:, 2 * state_dim :] + bias_ref[...]
+        spare = jnp.zeros((1, LANES - bias_ref.shape[1]), F32)
+        raw = side[:, 2 * state_dim :] + jnp.concatenate([bias_ref[...], spare], axis=1)
         live = (position < meta_ref[1 + which]).astype(F32)
         delta = (jnp.maximum(raw, 0.0) + jnp.log1p(jnp.exp(-jnp.abs(raw)))) * live
-        total = delta * -jnp.exp(log_rate_ref[...])
+        total = delta * -jnp.exp(jnp.concatenate([log_rate_ref[...], spare], axis=1))
         within = position % SPAN
         reach = 1
         while reach < SPAN:
@@ -145,7 +151,7 @@
         state_ref[cols, :] = state
 
 
-def scan(meta, projected, conv_weight, bias, log_rate, skip, width):
+def scan(which, meta, projected, conv_weight, bias, log_rate, skip, width):
     rows, total = projected.shape
     seq = rows // 2
     state_dim = width // 2
@@ -153,24 +159,24 @@
     inner = 2 * half
     cols = HEADS_STEP * LANES // 2
     groups = half // cols
-    taps = conv_weight.shape[0]
-    here = lambda r, g, m: (0, m[0] * groups + g)
-    fixed = lambda r, g, m: (0, 0)
+    taps, heads = conv_weight.shape[0], bias.shape[1]
+    here = lambda g, m: (0, m[0] * groups + g)
+    fixed = lambda g, m: (0, 0)
     grid_spec = pltpu.PrefetchScalarGridSpec(
         num_scalar_prefetch=1,
-        grid=(2, groups),
+        grid=(groups,),
         in_specs=[
-            pl.BlockSpec((seq, cols), lambda r, g, m: (r, g)),
-            pl.BlockSpec((seq, width + LANES), lambda r, g, m: (r, half // (width + LANES))),
+            pl.BlockSpec((seq, cols), lambda g, m: (which, g)),
+            pl.BlockSpec((seq, width + LANES), lambda g, m: (which, half // (width + LANES))),
             pl.BlockSpec((taps, cols), here),
-            pl.BlockSpec((taps, width), lambda r, g, m: (0, inner // width)),
-            pl.BlockSpec((1, LANES), fixed),
-            pl.BlockSpec((1, LANES), fixed),
+            pl.BlockSpec((taps, width), lambda g, m: (0, inner // width)),
+            pl.BlockSpec((1, heads), fixed),
+            pl.BlockSpec((1, heads), fixed),
             pl.BlockSpec(memory_space=pltpu.SMEM),
         ],
         out_specs=[
-            pl.BlockSpec((None, seq, cols), lambda r, g, m: (r, 0, g)),
-            pl.BlockSpec((None, cols, state_dim), lambda r, g, m: (r, g, 0)),
+            pl.BlockSpec((seq, cols), lambda g, m: (0, g)),
+            pl.BlockSpec((cols, state_dim), lambda g, m: (g, 0)),
         ],
         scratch_shapes=[
             pltpu.VMEM((2 * groups, seq, HEADS_STEP), F32),
@@ -182,20 +188,55 @@
         ],
     )
     return pl.pallas_call(
-        scan_kernel,
+        functools.partial(scan_kernel, which),
         grid_spec=grid_spec,
         out_shape=[
-            jax.ShapeDtypeStruct((2, seq, half), F32),
-            jax.ShapeDtypeStruct((2, half, state_dim), F32),
+            jax.ShapeDtypeStruct((seq, half), F32),
+            jax.ShapeDtypeStruct((half, state_dim), F32),
         ],
         compiler_params=pltpu.CompilerParams(
-            dimension_semantics=("arbitrary", "arbitrary"), vmem_limit_bytes=24 << 20
+            dimension_semantics=("arbitrary",), vmem_limit_bytes=24 << 20
         ),
         cost_estimate=pl.CostEstimate(
-            flops=2 * inner * seq * 640, transcendentals=inner * seq * 6, bytes_accessed=9 << 20
+            flops=inner * seq * 640, transcendentals=inner * seq * 3, bytes_accessed=5 << 20
         ),
         name="scan",
     )(meta, projected, projected, conv_weight, conv_weight, bias, log_rate, skip)
+
+
+def shards_kernel(
+    meta_ref, lengths_ref, input_ref, state_ref, step_ref, gate_ref, out_ref, kept_ref, sent_ref
+):
+    rows, half = input_ref.shape[0], input_ref.shape[1] // 2
+    width, heads = state_ref.shape[1], step_ref.shape[1]
+    length = lengths_ref[meta_ref[1]]
+    row = lax.broadcasted_iota(jnp.int32, (rows, LANES), 0)
+    lane = lax.broadcasted_iota(jnp.int32, (rows, LANES), 1)
+    coded = jnp.where(lane == heads, length >> 4, jnp.where(lane == heads + 1, length & 15, 0))
+    coded = jnp.where(row == 0, coded, 0).astype(F32).astype(BF)
+    for ref, core in ((kept_ref, meta_ref[0]), (sent_ref, 1 - meta_ref[0])):
+        at = pl.ds(pl.multiple_of(core * half, half), half)
+        ref[:, :half] = input_ref[:, at].astype(BF)
+        ref[:, half : half + width] = state_ref[...].astype(BF)
+        ref[:, half + width : half + width + LANES] = coded
+        ref[:, half + width : half + width + heads] = step_ref[...].astype(BF)
+        start = half + width + LANES
+        ref[:, start : start + half] = gate_ref[:, at].astype(BF)
+        ref[:, start + half :] = out_ref[:, at].astype(BF)
+
+
+def shards(meta, lengths, inputs, state, step, gate, out):
+    rows, inner = inputs.shape
+    total = 3 * (inner // 2) + state.shape[1] + LANES
+    scalars = pl.BlockSpec(memory_space=pltpu.SMEM)
+    whole = pl.BlockSpec(memory_space=pltpu.VMEM)
+    return pl.pallas_call(
+        shards_kernel,
+        in_specs=[scalars] * 2 + [whole] * 5,
+        out_specs=[whole] * 2,
+        out_shape=[jax.ShapeDtypeStruct((rows, total), BF)] * 2,
+        name="shards",
+    )(meta, lengths, inputs, state, step, gate, out)
 
 
 def project_kernel(tokens_ref, *refs):
@@ -242,7 +283,7 @@
 
 
 def gating(which, meta, tokens, scanned, gain, pieces):
-    _, seq, half = scanned.shape
+    seq, half = scanned.shape
     model = tokens.shape[1]
     depth = pieces[0].shape[0]
     steps = 3
@@ -254,7 +295,7 @@
             grid=(steps,),
             in_specs=[
                 pl.BlockSpec((seq, model), lambda n, m: (which, 0)),
-                pl.BlockSpec((None, seq, tile), lambda n, m: (which, 0, n)),
+                pl.BlockSpec((seq, tile), lambda n, m: (0, n)),
                 pl.BlockSpec((1, tile), lambda n, m: (0, m[0] * steps + n)),
             ]
             + [pl.BlockSpec((depth, tile), lambda n, m: (0, n)) for _ in pieces],
@@ -469,61 +510,54 @@
     spare = LANES - head_count
 
     cut = half + width + LANES
-    length = lax.dynamic_slice_in_dim(lengths, unit_id, 1, 0)
-    coded = jnp.stack([length // 16, length % 16], axis=1).astype(F32)
-    coded = jnp.pad(coded, ((0, SHARD_ROWS - 1), (0, spare - 2)))
-    side = jnp.concatenate([state_proj, step_proj, coded], axis=1)
-    low = [input_proj[:, :half], side, gate_proj[:, :half], out_proj[:, :half]]
-    high = [input_proj[:, half:], side, gate_proj[:, half:], out_proj[:, half:]]
-    low = jnp.concatenate(low, axis=1).astype(BF)
-    high = jnp.concatenate(high, axis=1).astype(BF)
-    received = swap(jnp.where(first_core, high, low))
-    code = received[0, cut - spare : cut - spare + 2].astype(jnp.int32)
-    meta = jnp.stack([core, length[0], code[0] * 16 + code[1]])
-
-    kept = jnp.where(first_core, low, high)
+    kept, sent = shards(
+        jnp.stack([core, unit_id]), lengths, input_proj, state_proj, step_proj, gate_proj, out_proj
+    )
+    received = swap(sent)
     pair = jnp.concatenate(
         [jnp.where(first_core, kept, received), jnp.where(first_core, received, kept)], axis=0
     )
     held = [pair[8 * c : 8 * c + 8] for c in range(COLOURS)]
     for step in range(4):
         if step == 3:
-            held, unit_id = lax.optimization_barrier((held, unit_id))
+            held, unit_id, kept, received = lax.optimization_barrier((held, unit_id, kept, received))
         held = joined(held, moved_over(held, step))
-    moved = moved_over(held, 4)
+    early, late = [h[:, :cut] for h in held], [h[:, cut:] for h in held]
+    early = joined(early, moved_over(early, 4))
+    moved = moved_over(early, 5)
 
     own = lax.dynamic_index_in_dim(tokens, unit_id, 0, keepdims=False)
     both = jnp.concatenate([own, swap(own)], axis=0)
     pick = jnp.arange(model_dim, dtype=jnp.int32)[:, None] == row_sources(me, core, model_dim)[None]
     both = jnp.dot(both, pick.astype(BF), preferred_element_type=F32).astype(BF)
-    small = (meta, row_places(me, core), jnp.pad(step_bias, (0, spare)), jnp.pad(log_rate, (0, spare)))
-    moved, both, small = lax.optimization_barrier((moved, both, small))
-    meta, places, bias, log_rate = small
-
-    early = joined([h[:, :cut] for h in held], [m[:, :cut] for m in moved])
-    late = joined([h[:, cut:] for h in held], [m[:, cut:] for m in moved])
-    moved, late = lax.optimization_barrier((moved_over(early, 5), late))
+    codes = cut - spare
+    codes = [part[0, codes : codes + 2].astype(jnp.int32) for part in (kept, received)]
+    meta = jnp.stack([core] + [code[0] * 16 + code[1] for code in codes])
+    small = (meta, row_places(me, core))
+    moved[0], both, small = lax.optimization_barrier((moved[0], both, small))
+    meta, places = small
+    for c in range(COLOURS):
+        moved[c], late[c] = lax.optimization_barrier((moved[c], late[c]))
     early = [piece for two in zip(early, moved) for piece in two]
+
+    late = joined(late, moved_over(late, 4))
+    projected, late = lax.optimization_barrier((project(both, early), late))
     late = [piece for two in zip(late, moved_over(late, 5)) for piece in two]
 
-    projected = project(both, early)
-    scanned, state = scan(
-        meta,
-        projected,
-        conv_weight,
-        bias[None],
-        log_rate[None],
-        skip_gain,
-        width,
-    )
-    state_other = swap(state[1])
+    inputs = (meta, projected, conv_weight, step_bias[None], log_rate[None], skip_gain, width)
+    scanned_other, state_sent = scan(1, *inputs)
+    state_other = swap(state_sent)
+    scanned, state = scan(0, *inputs)
+    scanned_other, scanned, state_other = lax.optimization_barrier(
+        (scanned_other, scanned, state_other)
+    )
     gain = norm_gain[None]
-    sent, square_sent = gating(1, meta, both, scanned, gain, late)
+    sent, square_sent = gating(1, meta, both, scanned_other, gain, late)
     share, square_other = swap(out_share(places, sent, late)), swap(square_sent)
     mine, square = gating(0, meta, both, scanned, gain, late)
     mixed = mix(meta, places, mine, share, square, square_other, late)
     state = jnp.concatenate(
-        [jnp.where(first_core, state[0], state_other), jnp.where(first_core, state_other, state[0])]
+        [jnp.where(first_core, state, state_other), jnp.where(first_core, state_other, state)]
     )
     return (mixed[None], state.reshape(1, head_count, head_dim, width // 2))
 

time: 142 us -> 141 us (level)
  starting transfers between devices: 39.9 us -> 44.4 us
  other arithmetic: 8.92 us -> 5 us
  local copies, waits for them, and re-layouts: 6.38 us -> 2.86 us
  Pallas kernels: 41.5 us -> 44.7 us
    ppermute x26 -> x29, starting transfers between devices: 39.9 us -> 44.4 us  [hop(): lax.ppermute(value, EVERYONE, [(d, d ^ mask_of(d // CORE % 2)) for d in r...]
    another operation x6 -> x2, other arithmetic: 4.96 us -> 0.63 us  [the longest x1 0.56 us: body(): jnp.stack([core, unit_id])]
    pallas_call x1 -> x3, Pallas kernels: 15.9 us -> 19 us  [the longest x2 17.1 us: scan(): pl.pallas_call(functools.partial(scan_kernel, which), grid_spec=grid_spec...]
    ppermute x26 -> x29, waiting for transfers between devices: 35.9 us -> 36.4 us  [hop(): lax.ppermute(value, EVERYONE, [(d, d ^ mask_of(d // CORE % 2)) for d in r...]
  transfers between devices with their start and end apart: 26 -> 29, of which waited for: 11 -> 13; matrix products, arithmetic and copies ran while one was open for 8% -> 7% of each run, Pallas kernels for 19% -> 20%
where the time goes in v6:
time: 141 us
  Pallas kernels  44.7 us (32%)
  starting transfers between devices  44.4 us (31%)
  waiting for transfers between devices  36.4 us (26%)
  other arithmetic  5 us (4%)
  matrix products  4.14 us (3%)
  between operations  3.67 us (3%)
  local copies, waits for them, and re-layouts  2.86 us (2%)
    ppermute x29, starting transfers between devices, hop(): lax.ppermute(value, EVERYONE, [(d, d ^ mask_of(d // CORE % 2)) for d in r...  44.4 us
    ppermute x29, waiting for transfers between devices, hop(): lax.ppermute(value, EVERYONE, [(d, d ^ mask_of(d // CORE % 2)) for d in r...  36.4 us
    pallas_call x2, Pallas kernels, scan(): pl.pallas_call(functools.partial(scan_kernel, which), grid_spec=grid_spec...  17.1 us
    pallas_call x2, Pallas kernels, gating(): pl.pallas_call(gate_kernel, grid_spec=pltpu.PrefetchScalarGridSpec(num_sc...  8.29 us
    pallas_call x1, Pallas kernels, project(): pl.pallas_call(project_kernel, grid=(steps,), in_specs=[pl.BlockSpec((row...  6.81 us
    pallas_call x1, Pallas kernels, mix(): pl.pallas_call(mix_kernel, grid_spec=pltpu.PrefetchScalarGridSpec(num_sca...  6.4 us
    pallas_call x1, Pallas kernels, out_share(): pl.pallas_call(share_kernel, grid_spec=pltpu.PrefetchScalarGridSpec(num_s...  4.16 us
    dot_general x1, matrix products, body(): both = jnp.dot(both, pick.astype(BF), preferred_element_type=F32).astype(BF)  4.14 us
  transfers between devices with their start and end apart: 29, of which 13 were waited for; matrix products, arithmetic and copies ran while one was open for 7% of the time, Pallas kernels for 20%

profile of v6, /device:TPU:1, one launch (start us, length us, event | category | flops | bytes accessed | tf_op | source)
XLA Modules:
  0.0 141.2 jit_solution(5027812949928126040)
XLA Ops:
  6.8 2.6 %collective-permute-start.1 = (bf16[8,4992]{1,0:T(8,128)(2,1)S(1)}, bf16[8,4992]{1,0:T(8,128)(2,1)S(1)}, u32[]{:S(2)}, u32[]{:S(2)}) collective-permute-start(bf16[8,4992]{1,0:T(8,128)(2,1)S(1)} %get-tuple-element.74), channel_id=1, source_target_pairs={{0,4},{1,5},{2,6},{3,7},{4,0},{5,1},{6,2},{7,3},{8,12},{9,13},{10,... | collective-permute-start | bytes 239624 | tf_op jit(solution)/shard_map/ppermute | solution.py:440
  9.5 2.8 %collective-permute-start.4 = (bf16[8,4992]{1,0:T(8,128)(2,1)S(1)}, bf16[8,4992]{1,0:T(8,128)(2,1)S(1)}, u32[]{:S(2)}, u32[]{:S(2)}) collective-permute-start(bf16[8,4992]{1,0:T(8,128)(2,1)S(1)} %get-tuple-element.73), channel_id=1, source_target_pairs={{0,1},{1,0},{2,3},{3,2},{4,5},{5,4},{6,7},{7,6},{8,9},{9,8},{10,11... | collective-permute-start | bytes 239624 | tf_op jit(solution)/shard_map/ppermute | solution.py:440
  12.3 3.8 %collective-permute-start.7 = (bf16[8,4992]{1,0:T(8,128)(2,1)S(1)}, bf16[8,4992]{1,0:T(8,128)(2,1)S(1)}, u32[]{:S(2)}, u32[]{:S(2)}) collective-permute-start(bf16[8,4992]{1,0:T(8,128)(2,1)S(1)} %get-tuple-element.72), channel_id=1, source_target_pairs={{0,32},{1,33},{2,34},{3,35},{4,36},{5,37},{6,38},{7,39},{8,40},{9,... | collective-permute-start | bytes 239624 | tf_op jit(solution)/shard_map/ppermute | solution.py:440
  18.5 3.1 %collective-permute-done.2 = bf16[16,4992]{1,0:T(8,128)(2,1)S(1)} collective-permute-done((bf16[16,4992]{1,0:T(8,128)(2,1)S(1)}, bf16[16,4992]{1,0:T(8,128)(2,1)S(1)}, u32[]{:S(2)}, u32[]{:S(2)}) %collective-permute-start.2) | collective-permute-done | bytes 159776 | tf_op jit(solution)/shard_map/ppermute | solution.py:440
  22.9 6.2 %collective-permute-done.3 = bf16[32,4992]{1,0:T(8,128)(2,1)S(1)} collective-permute-done((bf16[32,4992]{1,0:T(8,128)(2,1)S(1)}, bf16[32,4992]{1,0:T(8,128)(2,1)S(1)}, u32[]{:S(2)}, u32[]{:S(2)}) %collective-permute-start.3) | collective-permute-done | bytes 319520 | tf_op jit(solution)/shard_map/ppermute | solution.py:440
  31.1 3.6 %collective-permute-start.13 = (bf16[384,1536]{1,0:T(8,128)(2,1)S(1)}, bf16[384,1536]{1,0:T(8,128)(2,1)S(1)}, u32[]{:S(2)}, u32[]{:S(2)}) collective-permute-start(bf16[384,1536]{1,0:T(8,128)(2,1)S(1)} %dynamic-slice_bitcast_fusion), channel_id=1, source_target_pairs={{0,16},{1,17},{2,18},{3,19},{4,20},{5,21},{6,22},{7,23},{8,24},{9,... | collective-permute-start | bytes 3538952 | tf_op jit(solution)/shard_map/ppermute | solution.py:440
  41.5 6.0 %collective-permute-done.14 = bf16[64,4992]{1,0:T(8,128)(2,1)S(1)} collective-permute-done((bf16[64,4992]{1,0:T(8,128)(2,1)S(1)}, bf16[64,4992]{1,0:T(8,128)(2,1)S(1)}, u32[]{:S(2)}, u32[]{:S(2)}) %collective-permute-start.14) | collective-permute-done | bytes 639008 | tf_op jit(solution)/shard_map/ppermute | solution.py:440
  49.6 3.3 %collective-permute-done.11 = bf16[128,1920]{1,0:T(8,128)(2,1)S(1)} collective-permute-done((bf16[128,1920]{1,0:T(8,128)(2,1)S(1)}, bf16[128,1920]{1,0:T(8,128)(2,1)S(1)}, u32[]{:S(2)}, u32[]{:S(2)}) %collective-permute-start.11) | collective-permute-done | bytes 491552 | tf_op jit(solution)/shard_map/ppermute | solution.py:440
  53.4 2.3 %collective-permute-done.15 = bf16[128,1920]{1,0:T(8,128)(2,1)S(1)} collective-permute-done((bf16[128,1920]{1,0:T(8,128)(2,1)S(1)}, bf16[128,1920]{1,0:T(8,128)(2,1)S(1)}, u32[]{:S(2)}, u32[]{:S(2)}) %collective-permute-start.15) | collective-permute-done | bytes 491552 | tf_op jit(solution)/shard_map/ppermute | solution.py:440
  57.8 2.0 %collective-permute-start.19 = (bf16[256,1920]{1,0:T(8,128)(2,1)S(1)}, bf16[256,1920]{1,0:T(8,128)(2,1)S(1)}, u32[]{:S(2)}, u32[]{:S(2)}) collective-permute-start(bf16[256,1920]{1,0:T(8,128)(2,1)S(1)} %pad_maximum_fusion.9.refs_4_), channel_id=1, source_target_pairs={{0,1},{1,0},{2,3},{3,2},{4,5},{5,4},{6,7},{7,6},{8,9},{9,8},{10,11... | collective-permute-start | bytes 2949128 | tf_op jit(solution)/shard_map/ppermute | solution.py:440
  59.8 4.1 %fusion.2.tokens_ref = bf16[768,1536]{1,0:T(8,128)(2,1)S(1)} fusion(s32[1536]{0:T(1024)S(1)} %select_subtract_fusion, bf16[384,1536]{1,0:T(8,128)(2,1)S(1)} %collective-permute-done.13, bf16[384,1536]{1,0:T(8,128)(2,1)S(1)} %dynamic-slice_bitcast_fusion), kind=kOutput, calls=%fused_computation.3 | convolution fusion | flops 3632136192 | bytes 4724736 | tf_op jit(solution)/shard_map/dot_general | solution.py:532
  63.9 2.4 %collective-permute-done.12.refs_1_ = bf16[256,1920]{1,0:T(8,128)(2,1)S(1)} collective-permute-done((bf16[256,1920]{1,0:T(8,128)(2,1)S(1)}, bf16[256,1920]{1,0:T(8,128)(2,1)S(1)}, u32[]{:S(2)}, u32[]{:S(2)}) %collective-permute-start.12) | collective-permute-done | bytes 983072 | tf_op jit(solution)/shard_map/ppermute | solution.py:440
  66.4 3.6 %collective-permute-done.16.refs_3_ = bf16[256,1920]{1,0:T(8,128)(2,1)S(1)} collective-permute-done((bf16[256,1920]{1,0:T(8,128)(2,1)S(1)}, bf16[256,1920]{1,0:T(8,128)(2,1)S(1)}, u32[]{:S(2)}, u32[]{:S(2)}) %collective-permute-start.16) | collective-permute-done | bytes 983072 | tf_op jit(solution)/shard_map/ppermute | solution.py:440
  73.3 6.8 %project.1.input_ref.side_ref = bf16[768,1920]{1,0:T(8,128)(2,1)S(1)} custom-call(bf16[768,1536]{1,0:T(8,128)(2,1)S(1)} %fusion.2.tokens_ref, bf16[256,1920]{1,0:T(8,128)(2,1)S(1)} %pad_maximum_fusion.7.refs_0_, bf16[256,1920]{1,0:T(8,128)(2,1)S(1)} %collective-permute-done.12.refs_1_, bf16[256,1920]{1,0:T(8,128)(2,1)S(1)} %pad_maximum_fusion.8.refs_2_, ...), custom_call_target="tpu_custom_call" | custom-call | flops 4529848320 | bytes 10485760 | tf_op jit(solution)/shard_map/project/pallas_call | solution.py:252
  80.2 3.7 %collective-permute-done.20 = bf16[128,3072]{1,0:T(8,128)(2,1)S(1)} collective-permute-done((bf16[128,3072]{1,0:T(8,128)(2,1)S(1)}, bf16[128,3072]{1,0:T(8,128)(2,1)S(1)}, u32[]{:S(2)}, u32[]{:S(2)}) %collective-permute-start.20) | collective-permute-done | bytes 786464 | tf_op jit(solution)/shard_map/ppermute | solution.py:440
  86.8 2.0 %collective-permute-start.26 = (bf16[256,3072]{1,0:T(8,128)(2,1)S(1)}, bf16[256,3072]{1,0:T(8,128)(2,1)S(1)}, u32[]{:S(2)}, u32[]{:S(2)}) collective-permute-start(bf16[256,3072]{1,0:T(8,128)(2,1)S(1)} %pad_maximum_fusion.2.refs_4_), channel_id=1, source_target_pairs={{0,1},{1,0},{2,3},{3,2},{4,5},{5,4},{6,7},{7,6},{8,9},{9,8},{10,11... | collective-permute-start | bytes 4718600 | tf_op jit(solution)/shard_map/ppermute | solution.py:440
  88.8 8.5 %scan.2 = (f32[384,1536]{1,0:T(8,128)S(1)}, f32[1536,128]{1,0:T(8,128)S(1)}) custom-call(s32[3]{0:T(128)S(1)} %pad_add_fusion.1.meta_ref, bf16[768,1920]{1,0:T(8,128)(2,1)S(1)} %project.1.input_ref.side_ref, bf16[768,1920]{1,0:T(8,128)(2,1)S(1)} %project.1.input_ref.side_ref, f32[4,3328]{1,0:T(4,128)S(1)} %copy-done.1, f32[4,3328]{1,0:T(4,128)S(1)} %copy-done.1, ...), custom_call_target="tpu_custom_call" | custom-call | flops 754974720 | bytes 5242880 | tf_op jit(solution)/shard_map/scan/pallas_call | solution.py:190
  97.3 11.6 %collective-permute-start.23 = (f32[1536,128]{1,0:T(8,128)S(1)}, f32[1536,128]{1,0:T(8,128)S(1)}, u32[]{:S(2)}, u32[]{:S(2)}) collective-permute-start(f32[1536,128]{1,0:T(8,128)S(1)} %get-tuple-element.56), channel_id=1, source_target_pairs={{0,16},{1,17},{2,18},{3,19},{4,20},{5,21},{6,22},{7,23},{8,24},{9,... | collective-permute-start | bytes 2359304 | tf_op jit(solution)/shard_map/ppermute | solution.py:440
  108.9 8.5 %scan.3 = (f32[384,1536]{1,0:T(8,128)S(1)}, f32[1536,128]{1,0:T(8,128)S(1)}) custom-call(s32[3]{0:T(128)S(1)} %pad_add_fusion.1.meta_ref, bf16[768,1920]{1,0:T(8,128)(2,1)S(1)} %project.1.input_ref.side_ref, bf16[768,1920]{1,0:T(8,128)(2,1)S(1)} %project.1.input_ref.side_ref, f32[4,3328]{1,0:T(4,128)S(1)} %copy-done.1, f32[4,3328]{1,0:T(4,128)S(1)} %copy-done.1, ...), custom_call_target="tpu_custom_call" | custom-call | flops 754974720 | bytes 5242880 | tf_op jit(solution)/shard_map/scan/pallas_call | solution.py:190
  117.5 4.1 %gating.3 = (bf16[384,1536]{1,0:T(8,128)(2,1)S(1)}, f32[384,128]{1,0:T(8,128)S(1)}) custom-call(s32[3]{0:T(128)S(1)} %pad_add_fusion.1.meta_ref, bf16[768,1536]{1,0:T(8,128)(2,1)S(1)} %fusion.2.tokens_ref, f32[384,1536]{1,0:T(8,128)S(1)} %get-tuple-element.62.scanned_ref, f32[1,3072]{1,0:T(1,128)S(1)} %bitcast.11, ...), custom_call_target="tpu_custom_call" | custom-call | flops 1811939328 | bytes 10485760 | tf_op jit(solution)/shard_map/gating/pallas_call | solution.py:291
  121.6 4.2 %out_share.1 = f32[1536,384]{1,0:T(8,128)S(1)} custom-call(s32[192]{0:T(256)S(1)} %multiply_add_fusion.places_ref, bf16[384,1536]{1,0:T(8,128)(2,1)S(1)} %get-tuple-element.63.gated_ref, bf16[256,3072]{1,0:T(8,128)(2,1)S(1)} %pad_maximum_fusion.refs_0_, bf16[256,3072]{1,0:T(8,128)(2,1)S(1)} %collective-permute-done.24.refs_1_, ...), custom_call_target="tpu_custom_call" | custom-call | flops 1811939328 | bytes 8388608 | tf_op jit(solution)/shard_map/out_share/pallas_call | solution.py:347
  125.8 3.2 %collective-permute-start.27 = (f32[1536,384]{1,0:T(8,128)S(1)}, f32[1536,384]{1,0:T(8,128)S(1)}, u32[]{:S(2)}, u32[]{:S(2)}) collective-permute-start(f32[1536,384]{1,0:T(8,128)S(1)} %out_share.1), channel_id=1, source_target_pairs={{0,16},{1,17},{2,18},{3,19},{4,20},{5,21},{6,22},{7,23},{8,24},{9,... | collective-permute-start | bytes 7077896 | tf_op jit(solution)/shard_map/ppermute | solution.py:440
  130.6 4.1 %gating.2 = (bf16[384,1536]{1,0:T(8,128)(2,1)S(1)}, f32[384,128]{1,0:T(8,128)S(1)}) custom-call(s32[3]{0:T(128)S(1)} %pad_add_fusion.1.meta_ref, bf16[768,1536]{1,0:T(8,128)(2,1)S(1)} %fusion.2.tokens_ref, f32[384,1536]{1,0:T(8,128)S(1)} %get-tuple-element.57.scanned_ref, f32[1,3072]{1,0:T(1,128)S(1)} %bitcast.12, ...), custom_call_target="tpu_custom_call" | custom-call | flops 1811939328 | bytes 10485760 | tf_op jit(solution)/shard_map/gating/pallas_call | solution.py:291
  134.8 6.4 %mix.1 = bf16[384,1536]{1,0:T(8,128)(2,1)} custom-call(s32[3]{0:T(128)S(1)} %pad_add_fusion.1.meta_ref, s32[192]{0:T(256)S(1)} %multiply_add_fusion.places_ref, bf16[384,1536]{1,0:T(8,128)(2,1)S(1)} %get-tuple-element.61.mine_ref, f32[1536,384]{1,0:T(8,128)S(1)} %collective-permute-done.27.share_ref, f32[384,128]{1,0:T(8,128)S(1)} %get-tuple-element.64.sq_mine, ...), custom_call_target="tpu_custom_call" | custom-call | flops 1811939328 | bytes 8388608 | tf_op jit(solution)/shard_map/mix/pallas_call | solution.py:399
  (91 shorter events, 28.5 us)
Async XLA Ops:
  6.8 9.2 %collective-permute-start.1 = (bf16[8,4992]{1,0:T(8,128)(2,1)S(1)}, bf16[8,4992]{1,0:T(8,128)(2,1)S(1)}, u32[]{:S(2)}, u32[]{:S(2)}) collective-permute-start(bf16[8,4992]{1,0:T(8,128)(2,1)S(1)} %get-tuple-element.74), channel_id=1, source_target_pairs={{0,4},{1,5},{2,6},{3,7},{4,0},{5,1},{6,2},{7,3},{8,12},{9,13},{10,... | collective-permute-start | bytes 239624 | tf_op jit(solution)/shard_map/ppermute | solution.py:440
  9.5 6.8 %collective-permute-start.4 = (bf16[8,4992]{1,0:T(8,128)(2,1)S(1)}, bf16[8,4992]{1,0:T(8,128)(2,1)S(1)}, u32[]{:S(2)}, u32[]{:S(2)}) collective-permute-start(bf16[8,4992]{1,0:T(8,128)(2,1)S(1)} %get-tuple-element.73), channel_id=1, source_target_pairs={{0,1},{1,0},{2,3},{3,2},{4,5},{5,4},{6,7},{7,6},{8,9},{9,8},{10,11... | collective-permute-start | bytes 239624 | tf_op jit(solution)/shard_map/ppermute | solution.py:440
  12.3 5.9 %collective-permute-start.7 = (bf16[8,4992]{1,0:T(8,128)(2,1)S(1)}, bf16[8,4992]{1,0:T(8,128)(2,1)S(1)}, u32[]{:S(2)}, u32[]{:S(2)}) collective-permute-start(bf16[8,4992]{1,0:T(8,128)(2,1)S(1)} %get-tuple-element.72), channel_id=1, source_target_pairs={{0,32},{1,33},{2,34},{3,35},{4,36},{5,37},{6,38},{7,39},{8,40},{9,... | collective-permute-start | bytes 239624 | tf_op jit(solution)/shard_map/ppermute | solution.py:440
  21.7 7.4 %collective-permute-start.3 = (bf16[32,4992]{1,0:T(8,128)(2,1)S(1)}, bf16[32,4992]{1,0:T(8,128)(2,1)S(1)}, u32[]{:S(2)}, u32[]{:S(2)}) collective-permute-start(bf16[32,4992]{1,0:T(8,128)(2,1)S(1)} %pad_maximum_fusion.13), channel_id=1, source_target_pairs={{0,32},{1,33},{2,34},{3,35},{4,36},{5,37},{6,38},{7,39},{8,40},{9,... | collective-permute-start | bytes 958472 | tf_op jit(solution)/shard_map/ppermute | solution.py:440
  21.8 7.3 %collective-permute-start.6 = (bf16[32,4992]{1,0:T(8,128)(2,1)S(1)}, bf16[32,4992]{1,0:T(8,128)(2,1)S(1)}, u32[]{:S(2)}, u32[]{:S(2)}) collective-permute-start(bf16[32,4992]{1,0:T(8,128)(2,1)S(1)} %pad_maximum_fusion.14), channel_id=1, source_target_pairs={{0,12},{1,13},{2,14},{3,15},{4,8},{5,9},{6,10},{7,11},{8,4},{9,5},... | collective-permute-start | bytes 958472 | tf_op jit(solution)/shard_map/ppermute | solution.py:440
  22.7 6.5 %collective-permute-start.9 = (bf16[32,4992]{1,0:T(8,128)(2,1)S(1)}, bf16[32,4992]{1,0:T(8,128)(2,1)S(1)}, u32[]{:S(2)}, u32[]{:S(2)}) collective-permute-start(bf16[32,4992]{1,0:T(8,128)(2,1)S(1)} %pad_maximum_fusion.15), channel_id=1, source_target_pairs={{0,3},{1,2},{2,1},{3,0},{4,7},{5,6},{6,5},{7,4},{8,11},{9,10},{10,... | collective-permute-start | bytes 958472 | tf_op jit(solution)/shard_map/ppermute | solution.py:440
  29.3 10.6 %collective-permute-start.10 = (bf16[64,4992]{1,0:T(8,128)(2,1)S(1)}, bf16[64,4992]{1,0:T(8,128)(2,1)S(1)}, u32[]{:S(2)}, u32[]{:S(2)}) collective-permute-start(bf16[64,4992]{1,0:T(8,128)(2,1)S(1)} %pad_maximum_fusion.10), channel_id=1, source_target_pairs={{0,12},{1,13},{2,14},{3,15},{4,8},{5,9},{6,10},{7,11},{8,4},{9,5},... | collective-permute-start | bytes 1916936 | tf_op jit(solution)/shard_map/ppermute | solution.py:440
  31.1 28.7 %collective-permute-start.13 = (bf16[384,1536]{1,0:T(8,128)(2,1)S(1)}, bf16[384,1536]{1,0:T(8,128)(2,1)S(1)}, u32[]{:S(2)}, u32[]{:S(2)}) collective-permute-start(bf16[384,1536]{1,0:T(8,128)(2,1)S(1)} %dynamic-slice_bitcast_fusion), channel_id=1, source_target_pairs={{0,16},{1,17},{2,18},{3,19},{4,20},{5,21},{6,22},{7,23},{8,24},{9,... | collective-permute-start | bytes 3538952 | tf_op jit(solution)/shard_map/ppermute | solution.py:440
  37.9 9.6 %collective-permute-start.14 = (bf16[64,4992]{1,0:T(8,128)(2,1)S(1)}, bf16[64,4992]{1,0:T(8,128)(2,1)S(1)}, u32[]{:S(2)}, u32[]{:S(2)}) collective-permute-start(bf16[64,4992]{1,0:T(8,128)(2,1)S(1)} %pad_maximum_fusion.11), channel_id=1, source_target_pairs={{0,3},{1,2},{2,1},{3,0},{4,7},{5,6},{6,5},{7,4},{8,11},{9,10},{10,... | collective-permute-start | bytes 1916936 | tf_op jit(solution)/shard_map/ppermute | solution.py:440
  38.0 10.2 %collective-permute-start.17 = (bf16[64,4992]{1,0:T(8,128)(2,1)S(1)}, bf16[64,4992]{1,0:T(8,128)(2,1)S(1)}, u32[]{:S(2)}, u32[]{:S(2)}) collective-permute-start(bf16[64,4992]{1,0:T(8,128)(2,1)S(1)} %pad_maximum_fusion.12), channel_id=1, source_target_pairs={{0,96},{1,97},{2,98},{3,99},{4,100},{5,101},{6,102},{7,103},{8,104... | collective-permute-start | bytes 1916936 | tf_op jit(solution)/shard_map/ppermute | solution.py:440
  40.0 12.8 %collective-permute-start.11 = (bf16[128,1920]{1,0:T(8,128)(2,1)S(1)}, bf16[128,1920]{1,0:T(8,128)(2,1)S(1)}, u32[]{:S(2)}, u32[]{:S(2)}) collective-permute-start(bf16[128,1920]{1,0:T(8,128)(2,1)S(1)} %slice.66), channel_id=1, source_target_pairs={{0,3},{1,2},{2,1},{3,0},{4,7},{5,6},{6,5},{7,4},{8,11},{9,10},{10,... | collective-permute-start | bytes 1474568 | tf_op jit(solution)/shard_map/ppermute | solution.py:440
  47.7 8.1 %collective-permute-start.15 = (bf16[128,1920]{1,0:T(8,128)(2,1)S(1)}, bf16[128,1920]{1,0:T(8,128)(2,1)S(1)}, u32[]{:S(2)}, u32[]{:S(2)}) collective-permute-start(bf16[128,1920]{1,0:T(8,128)(2,1)S(1)} %slice.68), channel_id=1, source_target_pairs={{0,96},{1,97},{2,98},{3,99},{4,100},{5,101},{6,102},{7,103},{8,104... | collective-permute-start | bytes 1474568 | tf_op jit(solution)/shard_map/ppermute | solution.py:440
  48.4 9.3 %collective-permute-start.18 = (bf16[128,1920]{1,0:T(8,128)(2,1)S(1)}, bf16[128,1920]{1,0:T(8,128)(2,1)S(1)}, u32[]{:S(2)}, u32[]{:S(2)}) collective-permute-start(bf16[128,1920]{1,0:T(8,128)(2,1)S(1)} %slice.70), channel_id=1, source_target_pairs={{0,4},{1,5},{2,6},{3,7},{4,0},{5,1},{6,2},{7,3},{8,12},{9,13},{10,... | collective-permute-start | bytes 1474568 | tf_op jit(solution)/shard_map/ppermute | solution.py:440
  52.9 13.4 %collective-permute-start.12 = (bf16[256,1920]{1,0:T(8,128)(2,1)S(1)}, bf16[256,1920]{1,0:T(8,128)(2,1)S(1)}, u32[]{:S(2)}, u32[]{:S(2)}) collective-permute-start(bf16[256,1920]{1,0:T(8,128)(2,1)S(1)} %pad_maximum_fusion.7.refs_0_), channel_id=1, source_target_pairs={{0,96},{1,97},{2,98},{3,99},{4,100},{5,101},{6,102},{7,103},{8,104... | collective-permute-start | bytes 2949128 | tf_op jit(solution)/shard_map/ppermute | solution.py:440
  55.8 14.2 %collective-permute-start.16 = (bf16[256,1920]{1,0:T(8,128)(2,1)S(1)}, bf16[256,1920]{1,0:T(8,128)(2,1)S(1)}, u32[]{:S(2)}, u32[]{:S(2)}) collective-permute-start(bf16[256,1920]{1,0:T(8,128)(2,1)S(1)} %pad_maximum_fusion.8.refs_2_), channel_id=1, source_target_pairs={{0,4},{1,5},{2,6},{3,7},{4,0},{5,1},{6,2},{7,3},{8,12},{9,13},{10,... | collective-permute-start | bytes 2949128 | tf_op jit(solution)/shard_map/ppermute | solution.py:440
  57.8 14.2 %collective-permute-start.19 = (bf16[256,1920]{1,0:T(8,128)(2,1)S(1)}, bf16[256,1920]{1,0:T(8,128)(2,1)S(1)}, u32[]{:S(2)}, u32[]{:S(2)}) collective-permute-start(bf16[256,1920]{1,0:T(8,128)(2,1)S(1)} %pad_maximum_fusion.9.refs_4_), channel_id=1, source_target_pairs={{0,1},{1,0},{2,3},{3,2},{4,5},{5,4},{6,7},{7,6},{8,9},{9,8},{10,11... | collective-permute-start | bytes 2949128 | tf_op jit(solution)/shard_map/ppermute | solution.py:440
  66.3 17.5 %collective-permute-start.20 = (bf16[128,3072]{1,0:T(8,128)(2,1)S(1)}, bf16[128,3072]{1,0:T(8,128)(2,1)S(1)}, u32[]{:S(2)}, u32[]{:S(2)}) collective-permute-start(bf16[128,3072]{1,0:T(8,128)(2,1)S(1)} %slice.67), channel_id=1, source_target_pairs={{0,3},{1,2},{2,1},{3,0},{4,7},{5,6},{6,5},{7,4},{8,11},{9,10},{10,... | collective-permute-start | bytes 2359304 | tf_op jit(solution)/shard_map/ppermute | solution.py:440
  72.0 11.9 %collective-permute-start.21 = (bf16[128,3072]{1,0:T(8,128)(2,1)S(1)}, bf16[128,3072]{1,0:T(8,128)(2,1)S(1)}, u32[]{:S(2)}, u32[]{:S(2)}) collective-permute-start(bf16[128,3072]{1,0:T(8,128)(2,1)S(1)} %slice.69), channel_id=1, source_target_pairs={{0,96},{1,97},{2,98},{3,99},{4,100},{5,101},{6,102},{7,103},{8,104... | collective-permute-start | bytes 2359304 | tf_op jit(solution)/shard_map/ppermute | solution.py:440
  72.7 12.1 %collective-permute-start.22 = (bf16[128,3072]{1,0:T(8,128)(2,1)S(1)}, bf16[128,3072]{1,0:T(8,128)(2,1)S(1)}, u32[]{:S(2)}, u32[]{:S(2)}) collective-permute-start(bf16[128,3072]{1,0:T(8,128)(2,1)S(1)} %slice.71), channel_id=1, source_target_pairs={{0,4},{1,5},{2,6},{3,7},{4,0},{5,1},{6,2},{7,3},{8,12},{9,13},{10,... | collective-permute-start | bytes 2359304 | tf_op jit(solution)/shard_map/ppermute | solution.py:440
  84.9 32.6 %collective-permute-start.24 = (bf16[256,3072]{1,0:T(8,128)(2,1)S(1)}, bf16[256,3072]{1,0:T(8,128)(2,1)S(1)}, u32[]{:S(2)}, u32[]{:S(2)}) collective-permute-start(bf16[256,3072]{1,0:T(8,128)(2,1)S(1)} %pad_maximum_fusion.refs_0_), channel_id=1, source_target_pairs={{0,96},{1,97},{2,98},{3,99},{4,100},{5,101},{6,102},{7,103},{8,104... | collective-permute-start | bytes 4718600 | tf_op jit(solution)/shard_map/ppermute | solution.py:440
  85.7 31.7 %collective-permute-start.25 = (bf16[256,3072]{1,0:T(8,128)(2,1)S(1)}, bf16[256,3072]{1,0:T(8,128)(2,1)S(1)}, u32[]{:S(2)}, u32[]{:S(2)}) collective-permute-start(bf16[256,3072]{1,0:T(8,128)(2,1)S(1)} %pad_maximum_fusion.1.refs_2_), channel_id=1, source_target_pairs={{0,4},{1,5},{2,6},{3,7},{4,0},{5,1},{6,2},{7,3},{8,12},{9,13},{10,... | collective-permute-start | bytes 4718600 | tf_op jit(solution)/shard_map/ppermute | solution.py:440
  86.8 30.7 %collective-permute-start.26 = (bf16[256,3072]{1,0:T(8,128)(2,1)S(1)}, bf16[256,3072]{1,0:T(8,128)(2,1)S(1)}, u32[]{:S(2)}, u32[]{:S(2)}) collective-permute-start(bf16[256,3072]{1,0:T(8,128)(2,1)S(1)} %pad_maximum_fusion.2.refs_4_), channel_id=1, source_target_pairs={{0,1},{1,0},{2,3},{3,2},{4,5},{5,4},{6,7},{7,6},{8,9},{9,8},{10,11... | collective-permute-start | bytes 4718600 | tf_op jit(solution)/shard_map/ppermute | solution.py:440
  97.3 20.1 %collective-permute-start.23 = (f32[1536,128]{1,0:T(8,128)S(1)}, f32[1536,128]{1,0:T(8,128)S(1)}, u32[]{:S(2)}, u32[]{:S(2)}) collective-permute-start(f32[1536,128]{1,0:T(8,128)S(1)} %get-tuple-element.56), channel_id=1, source_target_pairs={{0,16},{1,17},{2,18},{3,19},{4,20},{5,21},{6,22},{7,23},{8,24},{9,... | collective-permute-start | bytes 2359304 | tf_op jit(solution)/shard_map/ppermute | solution.py:440
  125.8 9.0 %collective-permute-start.27 = (f32[1536,384]{1,0:T(8,128)S(1)}, f32[1536,384]{1,0:T(8,128)S(1)}, u32[]{:S(2)}, u32[]{:S(2)}) collective-permute-start(f32[1536,384]{1,0:T(8,128)S(1)} %out_share.1), channel_id=1, source_target_pairs={{0,16},{1,17},{2,18},{3,19},{4,20},{5,21},{6,22},{7,23},{8,24},{9,... | collective-permute-start | bytes 7077896 | tf_op jit(solution)/shard_map/ppermute | solution.py:440
  (10 other events, 62.6 us)

commit v7 on v6

--- a/solution.py
+++ b/solution.py
@@ -9,10 +9,16 @@
 
 SPAN = 128
 LANES = 128
+HEADS = 48
 HEADS_STEP = 8
 EPSILON = 1e-05
 BF = jnp.bfloat16
 F32 = jnp.float32
+
+
+def length_of(shard_ref, heads):
+    coded = shard_ref[:1].astype(F32)
+    return 16.0 * coded[:, heads : heads + 1] + coded[:, heads + 1 : heads + 2]
 
 
 def silu(v):
@@ -34,8 +40,8 @@
 
 
 def scan_kernel(
-    which,
     meta_ref,
+    shard_ref,
     input_ref,
     side_ref,
     taps_ref,
@@ -75,7 +81,7 @@
             )
         spare = jnp.zeros((1, LANES - bias_ref.shape[1]), F32)
         raw = side[:, 2 * state_dim :] + jnp.concatenate([bias_ref[...], spare], axis=1)
-        live = (position < meta_ref[1 + which]).astype(F32)
+        live = (position.astype(F32) < length_of(shard_ref, bias_ref.shape[1])).astype(F32)
         delta = (jnp.maximum(raw, 0.0) + jnp.log1p(jnp.exp(-jnp.abs(raw)))) * live
         total = delta * -jnp.exp(jnp.concatenate([log_rate_ref[...], spare], axis=1))
         within = position % SPAN
@@ -151,7 +157,7 @@
         state_ref[cols, :] = state
 
 
-def scan(which, meta, projected, conv_weight, bias, log_rate, skip, width):
+def scan(which, meta, shard, projected, conv_weight, bias, log_rate, skip, width):
     rows, total = projected.shape
     seq = rows // 2
     state_dim = width // 2
@@ -166,6 +172,7 @@
         num_scalar_prefetch=1,
         grid=(groups,),
         in_specs=[
+            pl.BlockSpec((shard.shape[0], LANES), lambda g, m: (0, total // LANES - 1)),
             pl.BlockSpec((seq, cols), lambda g, m: (which, g)),
             pl.BlockSpec((seq, width + LANES), lambda g, m: (which, half // (width + LANES))),
             pl.BlockSpec((taps, cols), here),
@@ -188,7 +195,7 @@
         ],
     )
     return pl.pallas_call(
-        functools.partial(scan_kernel, which),
+        scan_kernel,
         grid_spec=grid_spec,
         out_shape=[
             jax.ShapeDtypeStruct((seq, half), F32),
@@ -201,7 +208,7 @@
             flops=inner * seq * 640, transcendentals=inner * seq * 3, bytes_accessed=5 << 20
         ),
         name="scan",
-    )(meta, projected, projected, conv_weight, conv_weight, bias, log_rate, skip)
+    )(meta, shard, projected, projected, conv_weight, conv_weight, bias, log_rate, skip)
 
 
 def shards_kernel(
@@ -266,161 +273,101 @@
     )(tokens, *pieces)
 
 
-def gate_kernel(meta_ref, tokens_ref, scanned_ref, gain_ref, *refs):
-    gated_ref, square_ref = refs[-2:]
-    weight = jnp.concatenate([piece[...] for piece in refs[:-2]], axis=0)
-    gate = jnp.dot(tokens_ref[...], weight, preferred_element_type=F32).astype(BF)
-    gated = scanned_ref[...] * silu(gate.astype(F32))
-    gated_ref[...] = (gated * gain_ref[...]).astype(BF)
-
-    @pl.when(pl.program_id(0) == 0)
-    def _():
-        square_ref[...] = jnp.zeros_like(square_ref)
-
-    square = gated * gated
-    for at in range(0, square.shape[1], LANES):
-        square_ref[...] += square[:, at : at + LANES]
-
-
-def gating(which, meta, tokens, scanned, gain, pieces):
+def share_kernel(which, meta_ref, places_ref, tokens_ref, scanned_ref, gain_ref, *refs):
+    pieces, (share_ref, square_ref, gated_scr) = refs[:-3], refs[-3:]
+    seq, half = scanned_ref.shape
+    rows = slice(which * seq, (which + 1) * seq)
+    tile = half // 3
+    square_ref[...] = jnp.zeros_like(square_ref)
+    for at in range(0, half, tile):
+        cols = slice(at, at + tile)
+        weight = jnp.concatenate([piece[:, cols] for piece in pieces], axis=0)
+        gate = jnp.dot(tokens_ref[rows], weight, preferred_element_type=F32).astype(BF)
+        gated = scanned_ref[:, cols] * silu(gate.astype(F32))
+        gain_at = pl.multiple_of(meta_ref[0] * half + at, LANES)
+        gated_scr[:, cols] = (gated * gain_ref[:, pl.ds(gain_at, tile)]).astype(BF)
+        square = gated * gated
+        for lane in range(0, tile, LANES):
+            square_ref[...] += square[:, lane : lane + LANES]
+    steps = 4
+    depth = pieces[0].shape[0] // steps
+    each = depth // BLOCK_ROWS
+    for step in range(steps):
+        weight = jnp.concatenate(
+            [piece[step * depth : (step + 1) * depth, half:] for piece in pieces], axis=0
+        )
+        total = lax.dot_general(
+            weight, gated_scr[...], (((1,), (1,)), ((), ())), preferred_element_type=F32
+        )
+        for index in range(len(pieces)):
+            for block in range(each):
+                at = (index * each + block) * BLOCK_ROWS
+                place = places_ref[(index * steps + step) * each + block]
+                share_ref[pl.ds(pl.multiple_of(place, BLOCK_ROWS), BLOCK_ROWS), :] = total[
+                    at : at + BLOCK_ROWS
+                ]
+
+
+def out_share(which, meta, places, tokens, scanned, gain, pieces):
     seq, half = scanned.shape
     model = tokens.shape[1]
-    depth = pieces[0].shape[0]
-    steps = 3
-    tile = half // steps
+    scalars = pl.BlockSpec(memory_space=pltpu.SMEM)
+    whole = pl.BlockSpec(memory_space=pltpu.VMEM)
     return pl.pallas_call(
-        gate_kernel,
-        grid_spec=pltpu.PrefetchScalarGridSpec(
-            num_scalar_prefetch=1,
-            grid=(steps,),
-            in_specs=[
-                pl.BlockSpec((seq, model), lambda n, m: (which, 0)),
-                pl.BlockSpec((seq, tile), lambda n, m: (0, n)),
-                pl.BlockSpec((1, tile), lambda n, m: (0, m[0] * steps + n)),
-            ]
-            + [pl.BlockSpec((depth, tile), lambda n, m: (0, n)) for _ in pieces],
-            out_specs=[
-                pl.BlockSpec((seq, tile), lambda n, m: (0, n)),
-                pl.BlockSpec((seq, LANES), lambda n, m: (0, 0)),
-            ],
-        ),
+        functools.partial(share_kernel, which),
+        in_specs=[scalars] * 2 + [whole] * (3 + len(pieces)),
+        out_specs=[whole] * 2,
         out_shape=[
-            jax.ShapeDtypeStruct((seq, half), BF),
+            jax.ShapeDtypeStruct((model, seq), F32),
             jax.ShapeDtypeStruct((seq, LANES), F32),
         ],
-        compiler_params=pltpu.CompilerParams(
-            dimension_semantics=("arbitrary",), vmem_limit_bytes=24 << 20
-        ),
+        scratch_shapes=[pltpu.VMEM((seq, half), BF)],
+        compiler_params=pltpu.CompilerParams(vmem_limit_bytes=16 << 20),
         cost_estimate=pl.CostEstimate(
-            flops=2 * seq * model * half, transcendentals=seq * half, bytes_accessed=10 << 20
-        ),
-        name="gating",
-    )(meta, tokens, scanned, gain, *pieces)
-
-
-def place_rows(places_ref, gated_ref, pieces, out_ref):
-    step = pl.program_id(0)
-    weight = jnp.concatenate([piece[...] for piece in pieces], axis=0)
-    total = lax.dot_general(
-        weight, gated_ref[...], (((1,), (1,)), ((), ())), preferred_element_type=F32
-    )
-    each = pieces[0].shape[0] // BLOCK_ROWS
-    steps = pl.num_programs(0)
-    for index in range(len(pieces)):
-        for block in range(each):
-            at = (index * each + block) * BLOCK_ROWS
-            place = places_ref[(index * steps + step) * each + block]
-            out_ref[pl.ds(pl.multiple_of(place, BLOCK_ROWS), BLOCK_ROWS), :] = total[
-                at : at + BLOCK_ROWS
-            ]
-
-
-def share_kernel(places_ref, gated_ref, *refs):
-    place_rows(places_ref, gated_ref, refs[:-1], refs[-1])
-
-
-def out_share(places, gated, pieces):
-    seq, half = gated.shape
-    rows = pieces[0].shape[0]
-    model = rows * len(pieces)
-    steps = 4
-    return pl.pallas_call(
-        share_kernel,
-        grid_spec=pltpu.PrefetchScalarGridSpec(
-            num_scalar_prefetch=1,
-            grid=(steps,),
-            in_specs=[pl.BlockSpec((seq, half), lambda n, p: (0, 0))]
-            + [pl.BlockSpec((rows // steps, half), lambda n, p: (n, 1)) for _ in pieces],
-            out_specs=pl.BlockSpec((model, seq), lambda n, p: (0, 0)),
-        ),
-        out_shape=jax.ShapeDtypeStruct((model, seq), F32),
-        compiler_params=pltpu.CompilerParams(
-            dimension_semantics=("arbitrary",), vmem_limit_bytes=20 << 20
-        ),
-        cost_estimate=pl.CostEstimate(
-            flops=2 * seq * half * model, transcendentals=0, bytes_accessed=8 << 20
+            flops=4 * seq * half * model, transcendentals=seq * half, bytes_accessed=16 << 20
         ),
         name="out_share",
-    )(places, gated, *pieces)
-
-
-def mix_kernel(meta_ref, places_ref, mine_ref, share_ref, sq_mine, sq_other, pick_ref, *refs):
-    pieces, out_ref, total_scr = refs[:-2], refs[-2], refs[-1]
-    place_rows(places_ref, mine_ref, pieces, total_scr)
-
-    @pl.when(pl.program_id(0) == pl.num_programs(0) - 1)
-    def _():
-        seq = mine_ref.shape[0]
-        inner = 2 * mine_ref.shape[1]
-        squares = jnp.transpose(sq_mine[...] + sq_other[...])
-        mean = jnp.sum(squares, axis=0, keepdims=True) / inner
-        live = lax.broadcasted_iota(jnp.int32, (1, seq), 1) < meta_ref[1]
-        scale = jnp.where(live, lax.rsqrt(mean + EPSILON), 0.0)
-        tile = pick_ref.shape[0]
-        for at in range(0, out_ref.shape[1], tile):
-            rows = slice(at, at + tile)
-            short = ((total_scr[rows] + share_ref[rows]) * scale).astype(BF)
-            out_ref[:, rows] = lax.dot_general(
-                short, pick_ref[...], (((0,), (0,)), ((), ())), preferred_element_type=F32
-            ).astype(BF)
-
-
-def mix(meta, places, mine, share, sq_mine, sq_other, pieces):
-    seq, half = mine.shape
-    rows = pieces[0].shape[0]
-    model = rows * len(pieces)
-    steps = 4
+    )(meta, places, tokens, scanned, gain, *pieces)
+
+
+def mix_kernel(shard_ref, mine_ref, other_ref, sq_mine, sq_other, pick_ref, out_ref):
+    seq, model = out_ref.shape
+    inner = 2 * model
+    squares = jnp.transpose(sq_mine[...] + sq_other[...])
+    mean = jnp.sum(squares, axis=0, keepdims=True) / inner
+    live = lax.broadcasted_iota(jnp.int32, (1, seq), 1).astype(F32) < length_of(shard_ref, HEADS)
+    scale = jnp.where(live, lax.rsqrt(mean + EPSILON), 0.0)
+    tile = pick_ref.shape[0]
+    for at in range(0, model, tile):
+        rows = slice(at, at + tile)
+        short = ((mine_ref[rows] + other_ref[rows]) * scale).astype(BF)
+        out_ref[:, rows] = lax.dot_general(
+            short, pick_ref[...], (((0,), (0,)), ((), ())), preferred_element_type=F32
+        ).astype(BF)
+
+
+def mix(shard, cut, mine, other, sq_mine, sq_other):
+    model, seq = mine.shape
     tile = model // 4
     column = jnp.arange(tile, dtype=jnp.int32)
     chip, rest = column // (2 * SHARD_ROWS), column % (2 * SHARD_ROWS)
     target = rest // SHARD_ROWS * (tile // 2) + chip * SHARD_ROWS + rest % SHARD_ROWS
     pick = (target[:, None] == column[None]).astype(BF)
-    fixed = lambda n, m, p: (0, 0)
+    whole = pl.BlockSpec(memory_space=pltpu.VMEM)
+    fixed = lambda i: (0, 0)
     return pl.pallas_call(
         mix_kernel,
-        grid_spec=pltpu.PrefetchScalarGridSpec(
-            num_scalar_prefetch=2,
-            grid=(steps,),
-            in_specs=[
-                pl.BlockSpec((seq, half), fixed),
-                pl.BlockSpec((model, seq), fixed),
-                pl.BlockSpec((seq, LANES), fixed),
-                pl.BlockSpec((seq, LANES), fixed),
-                pl.BlockSpec((tile, tile), fixed),
-            ]
-            + [pl.BlockSpec((rows // steps, half), lambda n, m, p: (n, 1)) for _ in pieces],
-            out_specs=pl.BlockSpec((seq, model), fixed),
-            scratch_shapes=[pltpu.VMEM((model, seq), F32)],
-        ),
+        grid=(1,),
+        in_specs=[pl.BlockSpec((shard.shape[0], LANES), lambda i: (0, cut // LANES - 1))]
+        + [whole] * 5,
+        out_specs=whole,
         out_shape=jax.ShapeDtypeStruct((seq, model), BF),
-        compiler_params=pltpu.CompilerParams(
-            dimension_semantics=("arbitrary",), vmem_limit_bytes=24 << 20
-        ),
+        compiler_params=pltpu.CompilerParams(vmem_limit_bytes=16 << 20),
         cost_estimate=pl.CostEstimate(
-            flops=2 * seq * half * model, transcendentals=0, bytes_accessed=8 << 20
+            flops=2 * seq * tile * model, transcendentals=0, bytes_accessed=8 << 20
         ),
         name="mix",
-    )(meta, places, mine, share, sq_mine, sq_other, pick, *pieces)
+    )(shard, mine, other, sq_mine, sq_other, pick)
 
 
 EVERYONE = ("req", "unit")
@@ -433,7 +380,7 @@
 
 
 def link_of(colour, core, step):
-    return LINKS[(colour + 3 * core + step) % 6]
+    return LINKS[(colour + 3 * core - step) % 6]
 
 
 def hop(value, mask_of):
@@ -507,11 +454,11 @@
     head_dim = inner_dim // head_count
     width = state_proj.shape[1]
     half = inner_dim // 2
-    spare = LANES - head_count
 
     cut = half + width + LANES
+    meta = jnp.stack([core, unit_id])
     kept, sent = shards(
-        jnp.stack([core, unit_id]), lengths, input_proj, state_proj, step_proj, gate_proj, out_proj
+        meta, lengths, input_proj, state_proj, step_proj, gate_proj, out_proj
     )
     received = swap(sent)
     pair = jnp.concatenate(
@@ -519,43 +466,36 @@
     )
     held = [pair[8 * c : 8 * c + 8] for c in range(COLOURS)]
     for step in range(4):
-        if step == 3:
-            held, unit_id, kept, received = lax.optimization_barrier((held, unit_id, kept, received))
         held = joined(held, moved_over(held, step))
-    early, late = [h[:, :cut] for h in held], [h[:, cut:] for h in held]
-    early = joined(early, moved_over(early, 4))
-    moved = moved_over(early, 5)
+    held[2], unit_id = lax.optimization_barrier((held[2], unit_id))
+    moved = moved_over(held, 4)
 
     own = lax.dynamic_index_in_dim(tokens, unit_id, 0, keepdims=False)
     both = jnp.concatenate([own, swap(own)], axis=0)
     pick = jnp.arange(model_dim, dtype=jnp.int32)[:, None] == row_sources(me, core, model_dim)[None]
     both = jnp.dot(both, pick.astype(BF), preferred_element_type=F32).astype(BF)
-    codes = cut - spare
-    codes = [part[0, codes : codes + 2].astype(jnp.int32) for part in (kept, received)]
-    meta = jnp.stack([core] + [code[0] * 16 + code[1] for code in codes])
-    small = (meta, row_places(me, core))
-    moved[0], both, small = lax.optimization_barrier((moved[0], both, small))
-    meta, places = small
+    moved[0], both, places = lax.optimization_barrier((moved[0], both, row_places(me, core)))
+    early = joined([h[:, :cut] for h in held], [m[:, :cut] for m in moved])
+    late = joined([h[:, cut:] for h in held], [m[:, cut:] for m in moved])
+    moved = moved_over(early, 5)
     for c in range(COLOURS):
         moved[c], late[c] = lax.optimization_barrier((moved[c], late[c]))
     early = [piece for two in zip(early, moved) for piece in two]
-
-    late = joined(late, moved_over(late, 4))
-    projected, late = lax.optimization_barrier((project(both, early), late))
     late = [piece for two in zip(late, moved_over(late, 5)) for piece in two]
 
-    inputs = (meta, projected, conv_weight, step_bias[None], log_rate[None], skip_gain, width)
-    scanned_other, state_sent = scan(1, *inputs)
+    projected = project(both, early)
+    inputs = (projected, conv_weight, step_bias[None], log_rate[None], skip_gain, width)
+    scanned_other, state_sent = scan(1, meta, received, *inputs)
     state_other = swap(state_sent)
-    scanned, state = scan(0, *inputs)
+    scanned, state = scan(0, meta, kept, *inputs)
     scanned_other, scanned, state_other = lax.optimization_barrier(
         (scanned_other, scanned, state_other)
     )
-    gain = norm_gain[None]
-    sent, square_sent = gating(1, meta, both, scanned_other, gain, late)
-    share, square_other = swap(out_share(places, sent, late)), swap(square_sent)
-    mine, square = gating(0, meta, both, scanned, gain, late)
-    mixed = mix(meta, places, mine, share, square, square_other, late)
+    shared = (meta, places, both)
+    sent, square_sent = out_share(1, *shared, scanned_other, norm_gain[None], late)
+    other, square_other = swap(sent), swap(square_sent)
+    mine, square = out_share(0, *shared, scanned, norm_gain[None], late)
+    mixed = mix(kept, cut, mine, other, square, square_other)
     state = jnp.concatenate(
         [jnp.where(first_core, state, state_other), jnp.where(first_core, state_other, state)]
     )

time: 141 us -> 127 us (0.901)
  starting transfers between devices: 44.4 us -> 25.3 us
  local copies, waits for them, and re-layouts: 2.86 us -> 11.6 us
  Pallas kernels: 44.7 us -> 38.5 us
  between operations: 3.67 us -> 1.16 us
  other arithmetic: 5 us -> 7.44 us
  matrix products: 4.14 us -> 5.79 us
    ppermute x29 -> x26, starting transfers between devices: 44.4 us -> 25.3 us  [hop(): lax.ppermute(value, EVERYONE, [(d, d ^ mask_of(d // CORE % 2)) for d in r...]
    slice x8 -> x12, local copies, waits for them, and re-layouts: 1.48 us -> 9.22 us  [the longest x6 4.88 us: body(): late = joined([h[:, cut:] for h in held], [m[:, cut:] for m in moved])]
    pallas_call x6 -> x5, Pallas kernels: 35.9 us -> 29.7 us  [the longest x2 17.2 us: scan(): pl.pallas_call(scan_kernel, grid_spec=grid_spec, out_shape=[jax.ShapeDtyp...]
    concatenate x18, other arithmetic: 1.07 us -> 4.29 us  [joined(): jnp.concatenate([h, m], axis=0)]
    dot_general x1, matrix products: 4.14 us -> 5.79 us  [body(): both = jnp.dot(both, pick.astype(BF), preferred_element_type=F32).astype(BF)]
    ppermute x29 -> x26, waiting for transfers between devices: 36.4 us -> 36.9 us  [hop(): lax.ppermute(value, EVERYONE, [(d, d ^ mask_of(d // CORE % 2)) for d in r...]
  transfers between devices with their start and end apart: 29 -> 26, of which waited for: 13 -> 9; matrix products, arithmetic and copies ran while one was open for 7% -> 18% of each run, Pallas kernels for 20% -> 23%
where the time goes in v7:
time: 127 us
  Pallas kernels  38.5 us (30%)
  waiting for transfers between devices  36.9 us (29%)
  starting transfers between devices  25.3 us (20%)
  local copies, waits for them, and re-layouts  11.6 us (9%)
  other arithmetic  7.44 us (6%)
  matrix products  5.79 us (5%)
    ppermute x26, waiting for transfers between devices, hop(): lax.ppermute(value, EVERYONE, [(d, d ^ mask_of(d // CORE % 2)) for d in r...  36.9 us
    ppermute x26, starting transfers between devices, hop(): lax.ppermute(value, EVERYONE, [(d, d ^ mask_of(d // CORE % 2)) for d in r...  25.3 us
    pallas_call x2, Pallas kernels, scan(): pl.pallas_call(scan_kernel, grid_spec=grid_spec, out_shape=[jax.ShapeDtyp...  17.2 us
    pallas_call x2, Pallas kernels, out_share(): pl.pallas_call(functools.partial(share_kernel, which), in_specs=[scalars]...  10.2 us
    pallas_call x1, Pallas kernels, project(): pl.pallas_call(project_kernel, grid=(steps,), in_specs=[pl.BlockSpec((row...  6.82 us
    dot_general x1, matrix products, body(): both = jnp.dot(both, pick.astype(BF), preferred_element_type=F32).astype(BF)  5.79 us
    slice x6, local copies, waits for them, and re-layouts, body(): late = joined([h[:, cut:] for h in held], [m[:, cut:] for m in moved])  4.88 us
    slice x6, local copies, waits for them, and re-layouts, body(): early = joined([h[:, :cut] for h in held], [m[:, :cut] for m in moved])  4.34 us
  transfers between devices with their start and end apart: 26, of which 9 were waited for; matrix products, arithmetic and copies ran while one was open for 18% of the time, Pallas kernels for 23%

profile of v7, /device:TPU:1, one launch (start us, length us, event | category | flops | bytes accessed | tf_op | source)
XLA Modules:
  0.0 126.7 jit_solution(16054543519517743667)
XLA Ops:
  1.3 1.9 %shards.1 = (bf16[12,4992]{1,0:T(8,128)(2,1)}, bf16[12,4992]{1,0:T(8,128)(2,1)}) custom-call(s32[2]{0:T(128)} %pad_add_fusion.meta_ref, s32[16]{0:T(128)} %lengths_ref.1, f32[12,3072]{1,0:T(8,128)} %input_ref.1, f32[12,256]{1,0:T(8,128)} %state_ref.1, f32[12,48]{1,0:T(8,128)} %step_ref.1, f32[12,3072]{1,0:T(8,128)} %gate_ref.1, f32[12,3072]{1,0:T(8,128)} %out_ref.1), custom_call_target="tpu_custom_call" | custom-call | tf_op jit(solution)/shard_map/shards/pallas_call | solution.py:240
  3.2 1.4 %collective-permute-start = (bf16[12,4992]{1,0:T(8,128)(2,1)}, bf16[12,4992]{1,0:T(8,128)(2,1)S(1)}, u32[]{:S(2)}, u32[]{:S(2)}) collective-permute-start(bf16[12,4992]{1,0:T(8,128)(2,1)} %get-tuple-element.27), channel_id=1, source_target_pairs={{0,16},{1,17},{2,18},{3,19},{4,20},{5,21},{6,22},{7,23},{8,24},{9,... | collective-permute-start | bytes 359432 | tf_op jit(solution)/shard_map/ppermute | solution.py:387
  6.9 3.9 %collective-permute-start.6 = (bf16[8,4992]{1,0:T(8,128)(2,1)S(1)}, bf16[8,4992]{1,0:T(8,128)(2,1)S(1)}, u32[]{:S(2)}, u32[]{:S(2)}) collective-permute-start(bf16[8,4992]{1,0:T(8,128)(2,1)S(1)} %get-tuple-element.56), channel_id=1, source_target_pairs={{0,32},{1,33},{2,34},{3,35},{4,36},{5,37},{6,38},{7,39},{8,40},{9,... | collective-permute-start | bytes 239624 | tf_op jit(solution)/shard_map/ppermute | solution.py:387
  10.8 2.7 %collective-permute-start.12 = (bf16[8,4992]{1,0:T(8,128)(2,1)S(1)}, bf16[8,4992]{1,0:T(8,128)(2,1)S(1)}, u32[]{:S(2)}, u32[]{:S(2)}) collective-permute-start(bf16[8,4992]{1,0:T(8,128)(2,1)S(1)} %get-tuple-element.54), channel_id=1, source_target_pairs={{0,1},{1,0},{2,3},{3,2},{4,5},{5,4},{6,7},{7,6},{8,9},{9,8},{10,11... | collective-permute-start | bytes 239624 | tf_op jit(solution)/shard_map/ppermute | solution.py:387
  13.5 2.5 %collective-permute-start.1 = (bf16[8,4992]{1,0:T(8,128)(2,1)S(1)}, bf16[8,4992]{1,0:T(8,128)(2,1)S(1)}, u32[]{:S(2)}, u32[]{:S(2)}) collective-permute-start(bf16[8,4992]{1,0:T(8,128)(2,1)S(1)} %get-tuple-element.55), channel_id=1, source_target_pairs={{0,4},{1,5},{2,6},{3,7},{4,0},{5,1},{6,2},{7,3},{8,12},{9,13},{10,... | collective-permute-start | bytes 239624 | tf_op jit(solution)/shard_map/ppermute | solution.py:387
  16.1 1.9 %collective-permute-start.13 = (bf16[16,4992]{1,0:T(8,128)(2,1)S(1)}, bf16[16,4992]{1,0:T(8,128)(2,1)S(1)}, u32[]{:S(2)}, u32[]{:S(2)}) collective-permute-start(bf16[16,4992]{1,0:T(8,128)(2,1)S(1)} %pad_maximum_fusion.18), channel_id=1, source_target_pairs={{0,4},{1,5},{2,6},{3,7},{4,0},{5,1},{6,2},{7,3},{8,12},{9,13},{10,... | collective-permute-start | bytes 479240 | tf_op jit(solution)/shard_map/ppermute | solution.py:387
  18.1 3.6 %collective-permute-done.7 = bf16[16,4992]{1,0:T(8,128)(2,1)S(1)} collective-permute-done((bf16[16,4992]{1,0:T(8,128)(2,1)S(1)}, bf16[16,4992]{1,0:T(8,128)(2,1)S(1)}, u32[]{:S(2)}, u32[]{:S(2)}) %collective-permute-start.7) | collective-permute-done | bytes 159776 | tf_op jit(solution)/shard_map/ppermute | solution.py:387
  22.6 6.5 %collective-permute-done.8 = bf16[32,4992]{1,0:T(8,128)(2,1)S(1)} collective-permute-done((bf16[32,4992]{1,0:T(8,128)(2,1)S(1)}, bf16[32,4992]{1,0:T(8,128)(2,1)S(1)}, u32[]{:S(2)}, u32[]{:S(2)}) %collective-permute-start.8) | collective-permute-done | bytes 319520 | tf_op jit(solution)/shard_map/ppermute | solution.py:387
  29.6 9.3 %collective-permute-done.9 = bf16[64,4992]{1,0:T(8,128)(2,1)S(1)} collective-permute-done((bf16[64,4992]{1,0:T(8,128)(2,1)S(1)}, bf16[64,4992]{1,0:T(8,128)(2,1)S(1)}, u32[]{:S(2)}, u32[]{:S(2)}) %collective-permute-start.9) | collective-permute-done | bytes 639008 | tf_op jit(solution)/shard_map/ppermute | solution.py:387
  39.2 2.4 %dynamic-slice_bitcast_fusion = bf16[384,1536]{1,0:T(8,128)(2,1)} fusion(bf16[16,384,1536]{2,1,0:T(8,128)(2,1)} %param.12, s32[]{:T(128)S(6)} %select_n.465), kind=kLoop, calls=%fused_computation.14 | loop fusion | bytes 2359300 | tf_op jit(solution)/shard_map/jit(dynamic_index_in_dim)/squeeze | solution.py:473
  42.8 2.2 %pad_maximum_fusion.4 = bf16[128,4992]{1,0:T(8,128)(2,1)} fusion(bf16[64,4992]{1,0:T(8,128)(2,1)} %collective-permute-done.4, bf16[64,4992]{1,0:T(8,128)(2,1)S(1)} %pad_maximum_fusion.10), kind=kLoop, calls=%fused_computation.11 | loop fusion | flops 2555904 | bytes 2555904 | tf_op jit(solution)/shard_map/concatenate | solution.py:402
  45.0 2.6 %collective-permute-start.5 = (bf16[128,4992]{1,0:T(8,128)(2,1)}, bf16[128,4992]{1,0:T(8,128)(2,1)}, u32[]{:S(2)}, u32[]{:S(2)}) collective-permute-start(bf16[128,4992]{1,0:T(8,128)(2,1)} %pad_maximum_fusion.4), channel_id=1, source_target_pairs={{0,32},{1,33},{2,34},{3,35},{4,36},{5,37},{6,38},{7,39},{8,40},{9,... | collective-permute-start | bytes 3833864 | tf_op jit(solution)/shard_map/ppermute | solution.py:387
  52.6 5.8 %fusion.2.tokens_ref = bf16[768,1536]{1,0:T(8,128)(2,1)S(1)} fusion(s32[1536]{0:T(1024)S(1)} %select_subtract_fusion, bf16[384,1536]{1,0:T(8,128)(2,1)} %collective-permute-done.10, bf16[384,1536]{1,0:T(8,128)(2,1)} %dynamic-slice_bitcast_fusion), kind=kOutput, calls=%fused_computation.3 | convolution fusion | flops 3632136192 | bytes 4724736 | tf_op jit(solution)/shard_map/dot_general | solution.py:476
  58.4 4.5 %collective-permute-done.5 = bf16[128,4992]{1,0:T(8,128)(2,1)} collective-permute-done((bf16[128,4992]{1,0:T(8,128)(2,1)}, bf16[128,4992]{1,0:T(8,128)(2,1)}, u32[]{:S(2)}, u32[]{:S(2)}) %collective-permute-start.5) | collective-permute-done | bytes 1277984 | tf_op jit(solution)/shard_map/ppermute | solution.py:387
  68.4 2.8 %collective-permute-start.17 = (bf16[256,1920]{1,0:T(8,128)(2,1)S(1)}, bf16[256,1920]{1,0:T(8,128)(2,1)S(1)}, u32[]{:S(2)}, u32[]{:S(2)}) collective-permute-start(bf16[256,1920]{1,0:T(8,128)(2,1)S(1)} %pad_maximum_fusion.8.refs_2_), channel_id=1, source_target_pairs={{0,32},{1,33},{2,34},{3,35},{4,36},{5,37},{6,38},{7,39},{8,40},{9,... | collective-permute-start | bytes 2949128 | tf_op jit(solution)/shard_map/ppermute | solution.py:387
  74.1 5.6 %collective-permute-done.19.refs_5_ = bf16[256,1920]{1,0:T(8,128)(2,1)S(1)} collective-permute-done((bf16[256,1920]{1,0:T(8,128)(2,1)S(1)}, bf16[256,1920]{1,0:T(8,128)(2,1)S(1)}, u32[]{:S(2)}, u32[]{:S(2)}) %collective-permute-start.19) | collective-permute-done | bytes 983072 | tf_op jit(solution)/shard_map/ppermute | solution.py:387
  79.7 3.0 %collective-permute-done.17.refs_3_ = bf16[256,1920]{1,0:T(8,128)(2,1)S(1)} collective-permute-done((bf16[256,1920]{1,0:T(8,128)(2,1)S(1)}, bf16[256,1920]{1,0:T(8,128)(2,1)S(1)}, u32[]{:S(2)}, u32[]{:S(2)}) %collective-permute-start.17) | collective-permute-done | bytes 983072 | tf_op jit(solution)/shard_map/ppermute | solution.py:387
  82.6 2.8 %collective-permute-done.11.refs_1_ = bf16[256,1920]{1,0:T(8,128)(2,1)S(1)} collective-permute-done((bf16[256,1920]{1,0:T(8,128)(2,1)S(1)}, bf16[256,1920]{1,0:T(8,128)(2,1)S(1)}, u32[]{:S(2)}, u32[]{:S(2)}) %collective-permute-start.11) | collective-permute-done | bytes 983072 | tf_op jit(solution)/shard_map/ppermute | solution.py:387
  86.9 6.8 %project.1.input_ref.side_ref = bf16[768,1920]{1,0:T(8,128)(2,1)S(1)} custom-call(bf16[768,1536]{1,0:T(8,128)(2,1)S(1)} %fusion.2.tokens_ref, bf16[256,1920]{1,0:T(8,128)(2,1)S(1)} %pad_maximum_fusion.7.refs_0_, bf16[256,1920]{1,0:T(8,128)(2,1)S(1)} %collective-permute-done.11.refs_1_, bf16[256,1920]{1,0:T(8,128)(2,1)S(1)} %pad_maximum_fusion.8.refs_2_, ...), custom_call_target="tpu_custom_call" | custom-call | flops 4529848320 | bytes 10485760 | tf_op jit(solution)/shard_map/project/pallas_call | solution.py:259
  93.8 8.6 %scan.2 = (f32[384,1536]{1,0:T(8,128)S(1)}, f32[1536,128]{1,0:T(8,128)S(1)}) custom-call(s32[2]{0:T(128)S(1)} %copy-done.2, bf16[12,4992]{1,0:T(8,128)(2,1)S(1)} %collective-permute-done.shard_ref, bf16[768,1920]{1,0:T(8,128)(2,1)S(1)} %project.1.input_ref.side_ref, bf16[768,1920]{1,0:T(8,128)(2,1)S(1)} %project.1.input_ref.side_ref, ...), custom_call_target="tpu_custom_call" | custom-call | flops 754974720 | bytes 5242880 | tf_op jit(solution)/shard_map/scan/pallas_call | solution.py:197
  103.4 8.6 %scan.3 = (f32[384,1536]{1,0:T(8,128)S(1)}, f32[1536,128]{1,0:T(8,128)S(1)}) custom-call(s32[2]{0:T(128)S(1)} %copy-done.2, bf16[12,4992]{1,0:T(8,128)(2,1)S(1)} %copy-done, bf16[768,1920]{1,0:T(8,128)(2,1)S(1)} %project.1.input_ref.side_ref, bf16[768,1920]{1,0:T(8,128)(2,1)S(1)} %project.1.input_ref.side_ref, f32[4,3328]{1,0:T(4,128)S(1)} %copy-done.3, ...), custom_call_target="tpu_custom_call" | custom-call | flops 754974720 | bytes 5242880 | tf_op jit(solution)/shard_map/scan/pallas_call | solution.py:197
  112.1 5.1 %out_share.3 = (f32[1536,384]{1,0:T(8,128)S(1)}, f32[384,128]{1,0:T(8,128)S(1)}) custom-call(s32[2]{0:T(128)S(1)} %copy-done.2, s32[192]{0:T(256)S(1)} %multiply_add_fusion.places_ref, bf16[768,1536]{1,0:T(8,128)(2,1)S(1)} %fusion.2.tokens_ref, f32[384,1536]{1,0:T(8,128)S(1)} %get-tuple-element.44.scanned_ref, f32[1,3072]{1,0:T(1,128)S(1)} %bitcast.9, ...), custom_call_target="tpu_custom_call" | custom-call | flops 3623878656 | bytes 16777216 | tf_op jit(solution)/shard_map/out_share/pallas_call | solution.py:316
  119.3 5.1 %out_share.2 = (f32[1536,384]{1,0:T(8,128)S(1)}, f32[384,128]{1,0:T(8,128)S(1)}) custom-call(s32[2]{0:T(128)S(1)} %copy-done.2, s32[192]{0:T(256)S(1)} %multiply_add_fusion.places_ref, bf16[768,1536]{1,0:T(8,128)(2,1)S(1)} %fusion.2.tokens_ref, f32[384,1536]{1,0:T(8,128)S(1)} %get-tuple-element.39.scanned_ref, f32[1,3072]{1,0:T(1,128)S(1)} %bitcast.10, ...), custom_call_target="tpu_custom_call" | custom-call | flops 3623878656 | bytes 16777216 | tf_op jit(solution)/shard_map/out_share/pallas_call | solution.py:316
  124.5 2.2 %mix.1 = bf16[384,1536]{1,0:T(8,128)(2,1)} custom-call(bf16[12,4992]{1,0:T(8,128)(2,1)S(1)} %copy-done, f32[1536,384]{1,0:T(8,128)S(1)} %get-tuple-element.43.mine_ref, f32[1536,384]{1,0:T(8,128)S(1)} %collective-permute-done.24.other_ref, f32[384,128]{1,0:T(8,128)S(1)} %get-tuple-element.46.sq_mine, f32[384,128]{1,0:T(8,128)S(1)} %collective-permute-done.25.sq_other, ...), custom_call_target="tpu_custom_call" | custom-call | flops 452984832 | bytes 8388608 | tf_op jit(solution)/shard_map/mix/pallas_call | solution.py:358
  (90 shorter events, 23.6 us)
Async XLA Ops:
  6.9 9.1 %collective-permute-start.6 = (bf16[8,4992]{1,0:T(8,128)(2,1)S(1)}, bf16[8,4992]{1,0:T(8,128)(2,1)S(1)}, u32[]{:S(2)}, u32[]{:S(2)}) collective-permute-start(bf16[8,4992]{1,0:T(8,128)(2,1)S(1)} %get-tuple-element.56), channel_id=1, source_target_pairs={{0,32},{1,33},{2,34},{3,35},{4,36},{5,37},{6,38},{7,39},{8,40},{9,... | collective-permute-start | bytes 239624 | tf_op jit(solution)/shard_map/ppermute | solution.py:387
  10.8 5.3 %collective-permute-start.12 = (bf16[8,4992]{1,0:T(8,128)(2,1)S(1)}, bf16[8,4992]{1,0:T(8,128)(2,1)S(1)}, u32[]{:S(2)}, u32[]{:S(2)}) collective-permute-start(bf16[8,4992]{1,0:T(8,128)(2,1)S(1)} %get-tuple-element.54), channel_id=1, source_target_pairs={{0,1},{1,0},{2,3},{3,2},{4,5},{5,4},{6,7},{7,6},{8,9},{9,8},{10,11... | collective-permute-start | bytes 239624 | tf_op jit(solution)/shard_map/ppermute | solution.py:387
  16.0 5.7 %collective-permute-start.7 = (bf16[16,4992]{1,0:T(8,128)(2,1)S(1)}, bf16[16,4992]{1,0:T(8,128)(2,1)S(1)}, u32[]{:S(2)}, u32[]{:S(2)}) collective-permute-start(bf16[16,4992]{1,0:T(8,128)(2,1)S(1)} %pad_maximum_fusion.17), channel_id=1, source_target_pairs={{0,1},{1,0},{2,3},{3,2},{4,5},{5,4},{6,7},{7,6},{8,9},{9,8},{10,11... | collective-permute-start | bytes 479240 | tf_op jit(solution)/shard_map/ppermute | solution.py:387
  16.1 5.7 %collective-permute-start.13 = (bf16[16,4992]{1,0:T(8,128)(2,1)S(1)}, bf16[16,4992]{1,0:T(8,128)(2,1)S(1)}, u32[]{:S(2)}, u32[]{:S(2)}) collective-permute-start(bf16[16,4992]{1,0:T(8,128)(2,1)S(1)} %pad_maximum_fusion.18), channel_id=1, source_target_pairs={{0,4},{1,5},{2,6},{3,7},{4,0},{5,1},{6,2},{7,3},{8,12},{9,13},{10,... | collective-permute-start | bytes 479240 | tf_op jit(solution)/shard_map/ppermute | solution.py:387
  18.0 4.5 %collective-permute-start.2 = (bf16[16,4992]{1,0:T(8,128)(2,1)S(1)}, bf16[16,4992]{1,0:T(8,128)(2,1)S(1)}, u32[]{:S(2)}, u32[]{:S(2)}) collective-permute-start(bf16[16,4992]{1,0:T(8,128)(2,1)S(1)} %pad_maximum_fusion.16), channel_id=1, source_target_pairs={{0,96},{1,97},{2,98},{3,99},{4,100},{5,101},{6,102},{7,103},{8,104... | collective-permute-start | bytes 479240 | tf_op jit(solution)/shard_map/ppermute | solution.py:387
  21.8 7.4 %collective-permute-start.8 = (bf16[32,4992]{1,0:T(8,128)(2,1)S(1)}, bf16[32,4992]{1,0:T(8,128)(2,1)S(1)}, u32[]{:S(2)}, u32[]{:S(2)}) collective-permute-start(bf16[32,4992]{1,0:T(8,128)(2,1)S(1)} %pad_maximum_fusion.14), channel_id=1, source_target_pairs={{0,4},{1,5},{2,6},{3,7},{4,0},{5,1},{6,2},{7,3},{8,12},{9,13},{10,... | collective-permute-start | bytes 958472 | tf_op jit(solution)/shard_map/ppermute | solution.py:387
  21.9 7.4 %collective-permute-start.14 = (bf16[32,4992]{1,0:T(8,128)(2,1)S(1)}, bf16[32,4992]{1,0:T(8,128)(2,1)S(1)}, u32[]{:S(2)}, u32[]{:S(2)}) collective-permute-start(bf16[32,4992]{1,0:T(8,128)(2,1)S(1)} %pad_maximum_fusion.15), channel_id=1, source_target_pairs={{0,96},{1,97},{2,98},{3,99},{4,100},{5,101},{6,102},{7,103},{8,104... | collective-permute-start | bytes 958472 | tf_op jit(solution)/shard_map/ppermute | solution.py:387
  22.5 6.9 %collective-permute-start.3 = (bf16[32,4992]{1,0:T(8,128)(2,1)S(1)}, bf16[32,4992]{1,0:T(8,128)(2,1)S(1)}, u32[]{:S(2)}, u32[]{:S(2)}) collective-permute-start(bf16[32,4992]{1,0:T(8,128)(2,1)S(1)} %pad_maximum_fusion.13), channel_id=1, source_target_pairs={{0,3},{1,2},{2,1},{3,0},{4,7},{5,6},{6,5},{7,4},{8,11},{9,10},{10,... | collective-permute-start | bytes 958472 | tf_op jit(solution)/shard_map/ppermute | solution.py:387
  29.2 9.7 %collective-permute-start.9 = (bf16[64,4992]{1,0:T(8,128)(2,1)S(1)}, bf16[64,4992]{1,0:T(8,128)(2,1)S(1)}, u32[]{:S(2)}, u32[]{:S(2)}) collective-permute-start(bf16[64,4992]{1,0:T(8,128)(2,1)S(1)} %pad_maximum_fusion.11), channel_id=1, source_target_pairs={{0,96},{1,97},{2,98},{3,99},{4,100},{5,101},{6,102},{7,103},{8,104... | collective-permute-start | bytes 1916936 | tf_op jit(solution)/shard_map/ppermute | solution.py:387
  29.4 18.2 %collective-permute-start.15 = (bf16[64,4992]{1,0:T(8,128)(2,1)S(1)}, bf16[64,4992]{1,0:T(8,128)(2,1)}, u32[]{:S(2)}, u32[]{:S(2)}) collective-permute-start(bf16[64,4992]{1,0:T(8,128)(2,1)S(1)} %pad_maximum_fusion.12), channel_id=1, source_target_pairs={{0,3},{1,2},{2,1},{3,0},{4,7},{5,6},{6,5},{7,4},{8,11},{9,10},{10,... | collective-permute-start | bytes 1916936 | tf_op jit(solution)/shard_map/ppermute | solution.py:387
  29.6 13.2 %collective-permute-start.4 = (bf16[64,4992]{1,0:T(8,128)(2,1)S(1)}, bf16[64,4992]{1,0:T(8,128)(2,1)}, u32[]{:S(2)}, u32[]{:S(2)}) collective-permute-start(bf16[64,4992]{1,0:T(8,128)(2,1)S(1)} %pad_maximum_fusion.10), channel_id=1, source_target_pairs={{0,12},{1,13},{2,14},{3,15},{4,8},{5,9},{6,10},{7,11},{8,4},{9,5},... | collective-permute-start | bytes 1916936 | tf_op jit(solution)/shard_map/ppermute | solution.py:387
  39.1 26.1 %collective-permute-start.18 = (bf16[128,4992]{1,0:T(8,128)(2,1)S(1)}, bf16[128,4992]{1,0:T(8,128)(2,1)}, u32[]{:S(2)}, u32[]{:S(2)}) collective-permute-start(bf16[128,4992]{1,0:T(8,128)(2,1)S(1)} %pad_maximum_fusion.5), channel_id=1, source_target_pairs={{0,3},{1,2},{2,1},{3,0},{4,7},{5,6},{6,5},{7,4},{8,11},{9,10},{10,... | collective-permute-start | bytes 3833864 | tf_op jit(solution)/shard_map/ppermute | solution.py:387
  41.5 11.0 %collective-permute-start.10 = (bf16[384,1536]{1,0:T(8,128)(2,1)}, bf16[384,1536]{1,0:T(8,128)(2,1)}, u32[]{:S(2)}, u32[]{:S(2)}) collective-permute-start(bf16[384,1536]{1,0:T(8,128)(2,1)} %dynamic-slice_bitcast_fusion), channel_id=1, source_target_pairs={{0,16},{1,17},{2,18},{3,19},{4,20},{5,21},{6,22},{7,23},{8,24},{9,... | collective-permute-start | bytes 3538952 | tf_op jit(solution)/shard_map/ppermute | solution.py:387
  45.0 17.9 %collective-permute-start.5 = (bf16[128,4992]{1,0:T(8,128)(2,1)}, bf16[128,4992]{1,0:T(8,128)(2,1)}, u32[]{:S(2)}, u32[]{:S(2)}) collective-permute-start(bf16[128,4992]{1,0:T(8,128)(2,1)} %pad_maximum_fusion.4), channel_id=1, source_target_pairs={{0,32},{1,33},{2,34},{3,35},{4,36},{5,37},{6,38},{7,39},{8,40},{9,... | collective-permute-start | bytes 3833864 | tf_op jit(solution)/shard_map/ppermute | solution.py:387
  48.7 18.5 %collective-permute-start.16 = (bf16[128,4992]{1,0:T(8,128)(2,1)S(1)}, bf16[128,4992]{1,0:T(8,128)(2,1)}, u32[]{:S(2)}, u32[]{:S(2)}) collective-permute-start(bf16[128,4992]{1,0:T(8,128)(2,1)S(1)} %pad_maximum_fusion.6), channel_id=1, source_target_pairs={{0,12},{1,13},{2,14},{3,15},{4,8},{5,9},{6,10},{7,11},{8,4},{9,5},... | collective-permute-start | bytes 3833864 | tf_op jit(solution)/shard_map/ppermute | solution.py:387
  66.3 13.3 %collective-permute-start.19 = (bf16[256,1920]{1,0:T(8,128)(2,1)S(1)}, bf16[256,1920]{1,0:T(8,128)(2,1)S(1)}, u32[]{:S(2)}, u32[]{:S(2)}) collective-permute-start(bf16[256,1920]{1,0:T(8,128)(2,1)S(1)} %pad_maximum_fusion.9.refs_4_), channel_id=1, source_target_pairs={{0,12},{1,13},{2,14},{3,15},{4,8},{5,9},{6,10},{7,11},{8,4},{9,5},... | collective-permute-start | bytes 2949128 | tf_op jit(solution)/shard_map/ppermute | solution.py:387
  68.4 14.2 %collective-permute-start.17 = (bf16[256,1920]{1,0:T(8,128)(2,1)S(1)}, bf16[256,1920]{1,0:T(8,128)(2,1)S(1)}, u32[]{:S(2)}, u32[]{:S(2)}) collective-permute-start(bf16[256,1920]{1,0:T(8,128)(2,1)S(1)} %pad_maximum_fusion.8.refs_2_), channel_id=1, source_target_pairs={{0,32},{1,33},{2,34},{3,35},{4,36},{5,37},{6,38},{7,39},{8,40},{9,... | collective-permute-start | bytes 2949128 | tf_op jit(solution)/shard_map/ppermute | solution.py:387
  71.2 14.2 %collective-permute-start.11 = (bf16[256,1920]{1,0:T(8,128)(2,1)S(1)}, bf16[256,1920]{1,0:T(8,128)(2,1)S(1)}, u32[]{:S(2)}, u32[]{:S(2)}) collective-permute-start(bf16[256,1920]{1,0:T(8,128)(2,1)S(1)} %pad_maximum_fusion.7.refs_0_), channel_id=1, source_target_pairs={{0,1},{1,0},{2,3},{3,2},{4,5},{5,4},{6,7},{7,6},{8,9},{9,8},{10,11... | collective-permute-start | bytes 2949128 | tf_op jit(solution)/shard_map/ppermute | solution.py:387
  85.4 26.6 %collective-permute-start.23 = (bf16[256,3072]{1,0:T(8,128)(2,1)S(1)}, bf16[256,3072]{1,0:T(8,128)(2,1)S(1)}, u32[]{:S(2)}, u32[]{:S(2)}) collective-permute-start(bf16[256,3072]{1,0:T(8,128)(2,1)S(1)} %pad_maximum_fusion.2.refs_4_), channel_id=1, source_target_pairs={{0,12},{1,13},{2,14},{3,15},{4,8},{5,9},{6,10},{7,11},{8,4},{9,5},... | collective-permute-start | bytes 4718600 | tf_op jit(solution)/shard_map/ppermute | solution.py:387
  86.0 26.1 %collective-permute-start.22 = (bf16[256,3072]{1,0:T(8,128)(2,1)S(1)}, bf16[256,3072]{1,0:T(8,128)(2,1)S(1)}, u32[]{:S(2)}, u32[]{:S(2)}) collective-permute-start(bf16[256,3072]{1,0:T(8,128)(2,1)S(1)} %pad_maximum_fusion.1.refs_2_), channel_id=1, source_target_pairs={{0,32},{1,33},{2,34},{3,35},{4,36},{5,37},{6,38},{7,39},{8,40},{9,... | collective-permute-start | bytes 4718600 | tf_op jit(solution)/shard_map/ppermute | solution.py:387
  86.1 26.0 %collective-permute-start.21 = (bf16[256,3072]{1,0:T(8,128)(2,1)S(1)}, bf16[256,3072]{1,0:T(8,128)(2,1)S(1)}, u32[]{:S(2)}, u32[]{:S(2)}) collective-permute-start(bf16[256,3072]{1,0:T(8,128)(2,1)S(1)} %pad_maximum_fusion.refs_0_), channel_id=1, source_target_pairs={{0,1},{1,0},{2,3},{3,2},{4,5},{5,4},{6,7},{7,6},{8,9},{9,8},{10,11... | collective-permute-start | bytes 4718600 | tf_op jit(solution)/shard_map/ppermute | solution.py:387
  102.4 9.6 %collective-permute-start.20 = (f32[1536,128]{1,0:T(8,128)S(1)}, f32[1536,128]{1,0:T(8,128)S(1)}, u32[]{:S(2)}, u32[]{:S(2)}) collective-permute-start(f32[1536,128]{1,0:T(8,128)S(1)} %get-tuple-element.38), channel_id=1, source_target_pairs={{0,16},{1,17},{2,18},{3,19},{4,20},{5,21},{6,22},{7,23},{8,24},{9,... | collective-permute-start | bytes 2359304 | tf_op jit(solution)/shard_map/ppermute | solution.py:387
  117.2 7.2 %collective-permute-start.24 = (f32[1536,384]{1,0:T(8,128)S(1)}, f32[1536,384]{1,0:T(8,128)S(1)}, u32[]{:S(2)}, u32[]{:S(2)}) collective-permute-start(f32[1536,384]{1,0:T(8,128)S(1)} %get-tuple-element.45), channel_id=1, source_target_pairs={{0,16},{1,17},{2,18},{3,19},{4,20},{5,21},{6,22},{7,23},{8,24},{9,... | collective-permute-start | bytes 7077896 | tf_op jit(solution)/shard_map/ppermute | solution.py:387
  118.9 5.6 %collective-permute-start.25 = (f32[384,128]{1,0:T(8,128)S(1)}, f32[384,128]{1,0:T(8,128)S(1)}, u32[]{:S(2)}, u32[]{:S(2)}) collective-permute-start(f32[384,128]{1,0:T(8,128)S(1)} %get-tuple-element.47), channel_id=1, source_target_pairs={{0,16},{1,17},{2,18},{3,19},{4,20},{5,21},{6,22},{7,23},{8,24},{9,... | collective-permute-start | bytes 589832 | tf_op jit(solution)/shard_map/ppermute | solution.py:387
  (9 other events, 125.0 us)

commit v8 on v7

--- a/solution.py
+++ b/solution.py
@@ -242,35 +242,75 @@
         in_specs=[scalars] * 2 + [whole] * 5,
         out_specs=[whole] * 2,
         out_shape=[jax.ShapeDtypeStruct((rows, total), BF)] * 2,
+        compiler_params=pltpu.CompilerParams(vmem_limit_bytes=6 << 20),
         name="shards",
     )(meta, lengths, inputs, state, step, gate, out)
 
 
-def project_kernel(tokens_ref, *refs):
-    weight = jnp.concatenate([piece[...] for piece in refs[:-1]], axis=0)
-    refs[-1][...] = jnp.dot(tokens_ref[...], weight, preferred_element_type=F32).astype(BF)
-
-
-def project(tokens, pieces):
+def join_kernel(held_ref, moved_ref, *outs):
+    rows, start = held_ref.shape[0], 0
+    for out_ref in outs:
+        cols = slice(start, start + out_ref.shape[1])
+        out_ref[:rows] = held_ref[:, cols]
+        out_ref[rows:] = moved_ref[:, cols]
+        start += out_ref.shape[1]
+
+
+def join(held, moved, *widths):
+    rows, total = held.shape
+    whole = pl.BlockSpec(memory_space=pltpu.VMEM)
+    return pl.pallas_call(
+        join_kernel,
+        in_specs=[whole] * 2,
+        out_specs=[whole] * len(widths),
+        out_shape=[jax.ShapeDtypeStruct((2 * rows, width), BF) for width in widths],
+        compiler_params=pltpu.CompilerParams(vmem_limit_bytes=6 << 20),
+        cost_estimate=pl.CostEstimate(
+            flops=0, transcendentals=0, bytes_accessed=8 * rows * total
+        ),
+        name="join",
+    )(held, moved)
+
+
+def project_kernel(first, tokens_ref, *refs):
+    begin_ref, pieces, out_ref = refs[0], refs[:-1], refs[-1]
+    if not first:
+        pieces = pieces[1:]
+    depth, total = pieces[0].shape
+    tokens = jnp.concatenate(
+        [
+            tokens_ref[:, at : at + depth]
+            for at in range(0 if first else depth, tokens_ref.shape[1], 2 * depth)
+        ],
+        axis=1,
+    )
+    tile = total // 5
+    for at in range(0, total, tile):
+        cols = slice(at, at + tile)
+        weight = jnp.concatenate([piece[:, cols] for piece in pieces], axis=0)
+        part = jnp.dot(tokens, weight, preferred_element_type=F32)
+        if not first:
+            part = part + begin_ref[:, cols]
+        out_ref[:, cols] = part.astype(out_ref.dtype)
+
+
+def project(tokens, pieces, begun=None):
     rows, model = tokens.shape
     depth, total = pieces[0].shape
-    steps = 3
-    tile = total // steps
+    first = begun is None
+    whole = pl.BlockSpec(memory_space=pltpu.VMEM)
+    begun = () if first else (begun,)
     return pl.pallas_call(
-        project_kernel,
-        grid=(steps,),
-        in_specs=[pl.BlockSpec((rows, model), lambda n: (0, 0))]
-        + [pl.BlockSpec((depth, tile), lambda n: (0, n)) for _ in pieces],
-        out_specs=pl.BlockSpec((rows, tile), lambda n: (0, n)),
-        out_shape=jax.ShapeDtypeStruct((rows, total), BF),
-        compiler_params=pltpu.CompilerParams(
-            dimension_semantics=("arbitrary",), vmem_limit_bytes=24 << 20
-        ),
+        functools.partial(project_kernel, first),
+        in_specs=[whole] * (1 + len(begun) + len(pieces)),
+        out_specs=whole,
+        out_shape=jax.ShapeDtypeStruct((rows, total), F32 if first else BF),
+        compiler_params=pltpu.CompilerParams(vmem_limit_bytes=16 << 20),
         cost_estimate=pl.CostEstimate(
-            flops=2 * rows * model * total, transcendentals=0, bytes_accessed=10 << 20
+            flops=rows * model * total, transcendentals=0, bytes_accessed=10 << 20
         ),
         name="project",
-    )(tokens, *pieces)
+    )(tokens, *begun, *pieces)
 
 
 def share_kernel(which, meta_ref, places_ref, tokens_ref, scanned_ref, gain_ref, *refs):
@@ -460,14 +500,15 @@
     kept, sent = shards(
         meta, lengths, input_proj, state_proj, step_proj, gate_proj, out_proj
     )
+    sent, unit_id = lax.optimization_barrier((sent, unit_id))
     received = swap(sent)
     pair = jnp.concatenate(
         [jnp.where(first_core, kept, received), jnp.where(first_core, received, kept)], axis=0
     )
     held = [pair[8 * c : 8 * c + 8] for c in range(COLOURS)]
-    for step in range(4):
+    for step in range(3):
         held = joined(held, moved_over(held, step))
-    held[2], unit_id = lax.optimization_barrier((held[2], unit_id))
+    held = [join(h, m, cut + 2 * half)[0] for h, m in zip(held, moved_over(held, 3))]
     moved = moved_over(held, 4)
 
     own = lax.dynamic_index_in_dim(tokens, unit_id, 0, keepdims=False)
@@ -475,15 +516,16 @@
     pick = jnp.arange(model_dim, dtype=jnp.int32)[:, None] == row_sources(me, core, model_dim)[None]
     both = jnp.dot(both, pick.astype(BF), preferred_element_type=F32).astype(BF)
     moved[0], both, places = lax.optimization_barrier((moved[0], both, row_places(me, core)))
-    early = joined([h[:, :cut] for h in held], [m[:, :cut] for m in moved])
-    late = joined([h[:, cut:] for h in held], [m[:, cut:] for m in moved])
+    early, late = zip(*[join(h, m, cut, 2 * half) for h, m in zip(held, moved)])
+    late = list(late)
     moved = moved_over(early, 5)
+    begun = project(both, early)
+    moved[0], begun = lax.optimization_barrier((moved[0], begun))
     for c in range(COLOURS):
         moved[c], late[c] = lax.optimization_barrier((moved[c], late[c]))
-    early = [piece for two in zip(early, moved) for piece in two]
     late = [piece for two in zip(late, moved_over(late, 5)) for piece in two]
 
-    projected = project(both, early)
+    projected = project(both, moved, begun)
     inputs = (projected, conv_weight, step_bias[None], log_rate[None], skip_gain, width)
     scanned_other, state_sent = scan(1, meta, received, *inputs)
     state_other = swap(state_sent)

time: 127 us -> 120 us (0.945)
  other arithmetic: 7.44 us -> 2.11 us
  waiting for transfers between devices: 36.9 us -> 32.3 us
  local copies, waits for them, and re-layouts: 11.6 us -> 7.23 us
  Pallas kernels: 38.5 us -> 42.8 us
  starting transfers between devices: 25.3 us -> 28.7 us
    slice x12 -> x0, local copies, waits for them, and re-layouts: 9.22 us -> none  [the longest x6 4.88 us: body(): late = joined([h[:, cut:] for h in held], [m[:, cut:] for m in moved])]
    pallas_call x1 -> x8, Pallas kernels: 6.82 us -> 12.6 us  [the longest x2 6.49 us: project(): pl.pallas_call(functools.partial(project_kernel, first), in_specs=[whole]...]
    unnamed x14 -> x22, local copies, waits for them, and re-layouts: 0.04 us -> 4.87 us
    ppermute x26, waiting for transfers between devices: 36.9 us -> 32.3 us  [hop(): lax.ppermute(value, EVERYONE, [(d, d ^ mask_of(d // CORE % 2)) for d in r...]
    concatenate x18 -> x9, other arithmetic: 4.29 us -> 0.3 us  [joined(): jnp.concatenate([h, m], axis=0)]
    ppermute x26, starting transfers between devices: 25.3 us -> 28.7 us  [hop(): lax.ppermute(value, EVERYONE, [(d, d ^ mask_of(d // CORE % 2)) for d in r...]
    pallas_call x1, Pallas kernels: 1.91 us -> 0.58 us  [shards(): pl.pallas_call(shards_kernel, in_specs=[scalars] * 2 + [whole] * 5, out_s...]
  transfers between devices with their start and end apart: 26 -> 26, of which waited for: 9 -> 9; matrix products, arithmetic and copies ran while one was open for 18% -> 8% of each run, Pallas kernels for 23% -> 29%
where the time goes in v8:
time: 120 us
  Pallas kernels  42.8 us (36%)
  waiting for transfers between devices  32.3 us (27%)
  starting transfers between devices  28.7 us (24%)
  local copies, waits for them, and re-layouts  7.23 us (6%)
  matrix products  5.79 us (5%)
  other arithmetic  2.11 us (2%)
    ppermute x26, waiting for transfers between devices, hop(): lax.ppermute(value, EVERYONE, [(d, d ^ mask_of(d // CORE % 2)) for d in r...  32.3 us
    ppermute x26, starting transfers between devices, hop(): lax.ppermute(value, EVERYONE, [(d, d ^ mask_of(d // CORE % 2)) for d in r...  28.7 us
    pallas_call x2, Pallas kernels, scan(): pl.pallas_call(scan_kernel, grid_spec=grid_spec, out_shape=[jax.ShapeDtyp...  17.1 us
    pallas_call x2, Pallas kernels, out_share(): pl.pallas_call(functools.partial(share_kernel, which), in_specs=[scalars]...  10.2 us
    pallas_call x2, Pallas kernels, project(): pl.pallas_call(functools.partial(project_kernel, first), in_specs=[whole]...  6.49 us
    pallas_call x6, Pallas kernels, join(): pl.pallas_call(join_kernel, in_specs=[whole] * 2, out_specs=[whole] * len...  6.11 us
    dot_general x1, matrix products, body(): both = jnp.dot(both, pick.astype(BF), preferred_element_type=F32).astype(BF)  5.79 us
    unnamed x22, local copies, waits for them, and re-layouts  4.87 us
  transfers between devices with their start and end apart: 26, of which 9 were waited for; matrix products, arithmetic and copies ran while one was open for 8% of the time, Pallas kernels for 29%

profile of v8, /device:TPU:1, one launch (start us, length us, event | category | flops | bytes accessed | tf_op | source)
XLA Modules:
  0.0 119.9 jit_solution(8181594859553056929)
XLA Ops:
  8.8 3.9 %collective-permute-start.13 = (bf16[8,4992]{1,0:T(8,128)(2,1)S(1)}, bf16[8,4992]{1,0:T(8,128)(2,1)S(1)}, u32[]{:S(2)}, u32[]{:S(2)}) collective-permute-start(bf16[8,4992]{1,0:T(8,128)(2,1)S(1)} %get-tuple-element.70), channel_id=1, source_target_pairs={{0,32},{1,33},{2,34},{3,35},{4,36},{5,37},{6,38},{7,39},{8,40},{9,... | collective-permute-start | bytes 239624 | tf_op jit(solution)/shard_map/ppermute | solution.py:427
  12.7 2.7 %collective-permute-start.8 = (bf16[8,4992]{1,0:T(8,128)(2,1)S(1)}, bf16[8,4992]{1,0:T(8,128)(2,1)S(1)}, u32[]{:S(2)}, u32[]{:S(2)}) collective-permute-start(bf16[8,4992]{1,0:T(8,128)(2,1)S(1)} %get-tuple-element.71), channel_id=1, source_target_pairs={{0,1},{1,0},{2,3},{3,2},{4,5},{5,4},{6,7},{7,6},{8,9},{9,8},{10,11... | collective-permute-start | bytes 239624 | tf_op jit(solution)/shard_map/ppermute | solution.py:427
  15.5 2.5 %collective-permute-start.1 = (bf16[8,4992]{1,0:T(8,128)(2,1)S(1)}, bf16[8,4992]{1,0:T(8,128)(2,1)S(1)}, u32[]{:S(2)}, u32[]{:S(2)}) collective-permute-start(bf16[8,4992]{1,0:T(8,128)(2,1)S(1)} %get-tuple-element.72), channel_id=1, source_target_pairs={{0,4},{1,5},{2,6},{3,7},{4,0},{5,1},{6,2},{7,3},{8,12},{9,13},{10,... | collective-permute-start | bytes 239624 | tf_op jit(solution)/shard_map/ppermute | solution.py:427
  18.1 1.9 %collective-permute-start.9 = (bf16[16,4992]{1,0:T(8,128)(2,1)S(1)}, bf16[16,4992]{1,0:T(8,128)(2,1)S(1)}, u32[]{:S(2)}, u32[]{:S(2)}) collective-permute-start(bf16[16,4992]{1,0:T(8,128)(2,1)S(1)} %pad_maximum_fusion.8), channel_id=1, source_target_pairs={{0,4},{1,5},{2,6},{3,7},{4,0},{5,1},{6,2},{7,3},{8,12},{9,13},{10,... | collective-permute-start | bytes 479240 | tf_op jit(solution)/shard_map/ppermute | solution.py:427
  20.1 3.6 %collective-permute-done.14 = bf16[16,4992]{1,0:T(8,128)(2,1)S(1)} collective-permute-done((bf16[16,4992]{1,0:T(8,128)(2,1)S(1)}, bf16[16,4992]{1,0:T(8,128)(2,1)S(1)}, u32[]{:S(2)}, u32[]{:S(2)}) %collective-permute-start.14) | collective-permute-done | bytes 159776 | tf_op jit(solution)/shard_map/ppermute | solution.py:427
  24.6 6.5 %collective-permute-done.15 = bf16[32,4992]{1,0:T(8,128)(2,1)S(1)} collective-permute-done((bf16[32,4992]{1,0:T(8,128)(2,1)S(1)}, bf16[32,4992]{1,0:T(8,128)(2,1)S(1)}, u32[]{:S(2)}, u32[]{:S(2)}) %collective-permute-start.15) | collective-permute-done | bytes 319520 | tf_op jit(solution)/shard_map/ppermute | solution.py:427
  31.6 2.4 %dynamic-slice_bitcast_fusion = bf16[384,1536]{1,0:T(8,128)(2,1)} fusion(bf16[16,384,1536]{2,1,0:T(8,128)(2,1)} %param.12, s32[]{:T(128)S(6)} %select_n.464), kind=kLoop, calls=%fused_computation.8 | loop fusion | bytes 2359300 | tf_op jit(solution)/shard_map/jit(dynamic_index_in_dim)/squeeze | solution.py:514
  34.0 4.8 %collective-permute-start.6 = (bf16[384,1536]{1,0:T(8,128)(2,1)}, bf16[384,1536]{1,0:T(8,128)(2,1)}, u32[]{:S(2)}, u32[]{:S(2)}) collective-permute-start(bf16[384,1536]{1,0:T(8,128)(2,1)} %dynamic-slice_bitcast_fusion), channel_id=1, source_target_pairs={{0,16},{1,17},{2,18},{3,19},{4,20},{5,21},{6,22},{7,23},{8,24},{9,... | collective-permute-start | bytes 3538952 | tf_op jit(solution)/shard_map/ppermute | solution.py:427
  38.8 2.0 %collective-permute-done.16.moved_ref = bf16[64,4992]{1,0:T(8,128)(2,1)S(1)} collective-permute-done((bf16[64,4992]{1,0:T(8,128)(2,1)S(1)}, bf16[64,4992]{1,0:T(8,128)(2,1)S(1)}, u32[]{:S(2)}, u32[]{:S(2)}) %collective-permute-start.16) | collective-permute-done | bytes 639008 | tf_op jit(solution)/shard_map/ppermute | solution.py:427
  43.3 5.8 %fusion.2.tokens_ref = bf16[768,1536]{1,0:T(8,128)(2,1)S(1)} fusion(s32[1536]{0:T(1024)S(1)} %select_subtract_fusion, bf16[384,1536]{1,0:T(8,128)(2,1)} %collective-permute-done.6, bf16[384,1536]{1,0:T(8,128)(2,1)} %dynamic-slice_bitcast_fusion), kind=kOutput, calls=%fused_computation.3 | convolution fusion | flops 3632136192 | bytes 4724736 | tf_op jit(solution)/shard_map/dot_general | solution.py:517
  49.1 9.6 %collective-permute-done.17.moved_ref = bf16[128,4992]{1,0:T(8,128)(2,1)} collective-permute-done((bf16[128,4992]{1,0:T(8,128)(2,1)}, bf16[128,4992]{1,0:T(8,128)(2,1)}, u32[]{:S(2)}, u32[]{:S(2)}) %collective-permute-start.17) | collective-permute-done | bytes 1277984 | tf_op jit(solution)/shard_map/ppermute | solution.py:427
  58.7 1.9 %join.11 = (bf16[256,1920]{1,0:T(8,128)(2,1)S(1)}, bf16[256,3072]{1,0:T(8,128)(2,1)S(1)}) custom-call(bf16[128,4992]{1,0:T(8,128)(2,1)} %join.10.held_ref, bf16[128,4992]{1,0:T(8,128)(2,1)} %collective-permute-done.17.moved_ref), custom_call_target="tpu_custom_call" | custom-call | bytes 5111808 | tf_op jit(solution)/shard_map/join/pallas_call | solution.py:262
  63.7 1.8 %collective-permute-start.7 = (bf16[256,1920]{1,0:T(8,128)(2,1)S(1)}, bf16[256,1920]{1,0:T(8,128)(2,1)S(1)}, u32[]{:S(2)}, u32[]{:S(2)}) collective-permute-start(bf16[256,1920]{1,0:T(8,128)(2,1)S(1)} %get-tuple-element.41.refs_0_), channel_id=1, source_target_pairs={{0,1},{1,0},{2,3},{3,2},{4,5},{5,4},{6,7},{7,6},{8,9},{9,8},{10,11... | collective-permute-start | bytes 2949128 | tf_op jit(solution)/shard_map/ppermute | solution.py:427
  65.5 3.2 %project.2.refs_0_ = f32[768,1920]{1,0:T(8,128)S(1)} custom-call(bf16[768,1536]{1,0:T(8,128)(2,1)S(1)} %fusion.2.tokens_ref, bf16[256,1920]{1,0:T(8,128)(2,1)S(1)} %get-tuple-element.41.refs_0_, bf16[256,1920]{1,0:T(8,128)(2,1)S(1)} %get-tuple-element.42.refs_1_, bf16[256,1920]{1,0:T(8,128)(2,1)S(1)} %get-tuple-element.43.refs_2_), custom_call_target="tpu_custom_call" | custom-call | flops 2264924160 | bytes 10485760 | tf_op jit(solution)/shard_map/project/pallas_call | solution.py:303
  68.7 5.2 %collective-permute-done.19.refs_3_ = bf16[256,1920]{1,0:T(8,128)(2,1)S(1)} collective-permute-done((bf16[256,1920]{1,0:T(8,128)(2,1)S(1)}, bf16[256,1920]{1,0:T(8,128)(2,1)S(1)}, u32[]{:S(2)}, u32[]{:S(2)}) %collective-permute-start.19) | collective-permute-done | bytes 983072 | tf_op jit(solution)/shard_map/ppermute | solution.py:427
  73.9 2.8 %collective-permute-done.18.refs_2_ = bf16[256,1920]{1,0:T(8,128)(2,1)S(1)} collective-permute-done((bf16[256,1920]{1,0:T(8,128)(2,1)S(1)}, bf16[256,1920]{1,0:T(8,128)(2,1)S(1)}, u32[]{:S(2)}, u32[]{:S(2)}) %collective-permute-start.18) | collective-permute-done | bytes 983072 | tf_op jit(solution)/shard_map/ppermute | solution.py:427
  79.5 2.7 %collective-permute-start.22 = (bf16[256,3072]{1,0:T(8,128)(2,1)S(1)}, bf16[256,3072]{1,0:T(8,128)(2,1)S(1)}, u32[]{:S(2)}, u32[]{:S(2)}) collective-permute-start(bf16[256,3072]{1,0:T(8,128)(2,1)S(1)} %get-tuple-element.57.refs_2_), channel_id=1, source_target_pairs={{0,32},{1,33},{2,34},{3,35},{4,36},{5,37},{6,38},{7,39},{8,40},{9,... | collective-permute-start | bytes 4718600 | tf_op jit(solution)/shard_map/ppermute | solution.py:427
  82.1 3.3 %project.3.input_ref.side_ref = bf16[768,1920]{1,0:T(8,128)(2,1)S(1)} custom-call(bf16[768,1536]{1,0:T(8,128)(2,1)S(1)} %fusion.2.tokens_ref, f32[768,1920]{1,0:T(8,128)S(1)} %project.2.refs_0_, bf16[256,1920]{1,0:T(8,128)(2,1)S(1)} %collective-permute-done.7.refs_1_, bf16[256,1920]{1,0:T(8,128)(2,1)S(1)} %collective-permute-done.18.refs_2_, ...), custom_call_target="tpu_custom_call" | custom-call | flops 2264924160 | bytes 10485760 | tf_op jit(solution)/shard_map/project/pallas_call | solution.py:303
  85.4 8.5 %scan.2 = (f32[384,1536]{1,0:T(8,128)S(1)}, f32[1536,128]{1,0:T(8,128)S(1)}) custom-call(s32[2]{0:T(128)S(1)} %pad_add_fusion.meta_ref, bf16[12,4992]{1,0:T(8,128)(2,1)S(1)} %collective-permute-done.shard_ref, bf16[768,1920]{1,0:T(8,128)(2,1)S(1)} %project.3.input_ref.side_ref, bf16[768,1920]{1,0:T(8,128)(2,1)S(1)} %project.3.input_ref.side_ref, ...), custom_call_target="tpu_custom_call" | custom-call | flops 754974720 | bytes 5242880 | tf_op jit(solution)/shard_map/scan/pallas_call | solution.py:197
  94.0 2.4 %collective-permute-start.20 = (f32[1536,128]{1,0:T(8,128)S(1)}, f32[1536,128]{1,0:T(8,128)S(1)}, u32[]{:S(2)}, u32[]{:S(2)}) collective-permute-start(f32[1536,128]{1,0:T(8,128)S(1)} %get-tuple-element.54), channel_id=1, source_target_pairs={{0,16},{1,17},{2,18},{3,19},{4,20},{5,21},{6,22},{7,23},{8,24},{9,... | collective-permute-start | bytes 2359304 | tf_op jit(solution)/shard_map/ppermute | solution.py:427
  96.4 8.5 %scan.3 = (f32[384,1536]{1,0:T(8,128)S(1)}, f32[1536,128]{1,0:T(8,128)S(1)}) custom-call(s32[2]{0:T(128)S(1)} %pad_add_fusion.meta_ref, bf16[12,4992]{1,0:T(8,128)(2,1)S(1)} %get-tuple-element.34.shard_ref, bf16[768,1920]{1,0:T(8,128)(2,1)S(1)} %project.3.input_ref.side_ref, bf16[768,1920]{1,0:T(8,128)(2,1)S(1)} %project.3.input_ref.side_ref, ...), custom_call_target="tpu_custom_call" | custom-call | flops 754974720 | bytes 5242880 | tf_op jit(solution)/shard_map/scan/pallas_call | solution.py:197
  105.0 5.1 %out_share.3 = (f32[1536,384]{1,0:T(8,128)S(1)}, f32[384,128]{1,0:T(8,128)S(1)}) custom-call(s32[2]{0:T(128)S(1)} %pad_add_fusion.meta_ref, s32[192]{0:T(256)S(1)} %multiply_add_fusion.places_ref, bf16[768,1536]{1,0:T(8,128)(2,1)S(1)} %fusion.2.tokens_ref, f32[384,1536]{1,0:T(8,128)S(1)} %get-tuple-element.60.scanned_ref, f32[1,3072]{1,0:T(1,128)S(1)} %bitcast.9, ...), custom_call_target="tpu_custom_call" | custom-call | flops 3623878656 | bytes 16777216 | tf_op jit(solution)/shard_map/out_share/pallas_call | solution.py:356
  112.5 5.1 %out_share.2 = (f32[1536,384]{1,0:T(8,128)S(1)}, f32[384,128]{1,0:T(8,128)S(1)}) custom-call(s32[2]{0:T(128)S(1)} %pad_add_fusion.meta_ref, s32[192]{0:T(256)S(1)} %multiply_add_fusion.places_ref, bf16[768,1536]{1,0:T(8,128)(2,1)S(1)} %fusion.2.tokens_ref, f32[384,1536]{1,0:T(8,128)S(1)} %get-tuple-element.55.scanned_ref, f32[1,3072]{1,0:T(1,128)S(1)} %bitcast.10, ...), custom_call_target="tpu_custom_call" | custom-call | flops 3623878656 | bytes 16777216 | tf_op jit(solution)/shard_map/out_share/pallas_call | solution.py:356
  117.7 2.3 %mix.1 = bf16[384,1536]{1,0:T(8,128)(2,1)} custom-call(bf16[12,4992]{1,0:T(8,128)(2,1)S(1)} %get-tuple-element.34.shard_ref, f32[1536,384]{1,0:T(8,128)S(1)} %get-tuple-element.59.mine_ref, f32[1536,384]{1,0:T(8,128)S(1)} %collective-permute-done.24.other_ref, f32[384,128]{1,0:T(8,128)S(1)} %get-tuple-element.62.sq_mine, ...), custom_call_target="tpu_custom_call" | custom-call | flops 452984832 | bytes 8388608 | tf_op jit(solution)/shard_map/mix/pallas_call | solution.py:398
  (84 shorter events, 20.5 us)
Async XLA Ops:
  8.8 9.1 %collective-permute-start.13 = (bf16[8,4992]{1,0:T(8,128)(2,1)S(1)}, bf16[8,4992]{1,0:T(8,128)(2,1)S(1)}, u32[]{:S(2)}, u32[]{:S(2)}) collective-permute-start(bf16[8,4992]{1,0:T(8,128)(2,1)S(1)} %get-tuple-element.70), channel_id=1, source_target_pairs={{0,32},{1,33},{2,34},{3,35},{4,36},{5,37},{6,38},{7,39},{8,40},{9,... | collective-permute-start | bytes 239624 | tf_op jit(solution)/shard_map/ppermute | solution.py:427
  12.7 5.3 %collective-permute-start.8 = (bf16[8,4992]{1,0:T(8,128)(2,1)S(1)}, bf16[8,4992]{1,0:T(8,128)(2,1)S(1)}, u32[]{:S(2)}, u32[]{:S(2)}) collective-permute-start(bf16[8,4992]{1,0:T(8,128)(2,1)S(1)} %get-tuple-element.71), channel_id=1, source_target_pairs={{0,1},{1,0},{2,3},{3,2},{4,5},{5,4},{6,7},{7,6},{8,9},{9,8},{10,11... | collective-permute-start | bytes 239624 | tf_op jit(solution)/shard_map/ppermute | solution.py:427
  18.0 5.7 %collective-permute-start.14 = (bf16[16,4992]{1,0:T(8,128)(2,1)S(1)}, bf16[16,4992]{1,0:T(8,128)(2,1)S(1)}, u32[]{:S(2)}, u32[]{:S(2)}) collective-permute-start(bf16[16,4992]{1,0:T(8,128)(2,1)S(1)} %pad_maximum_fusion.9), channel_id=1, source_target_pairs={{0,1},{1,0},{2,3},{3,2},{4,5},{5,4},{6,7},{7,6},{8,9},{9,8},{10,11... | collective-permute-start | bytes 479240 | tf_op jit(solution)/shard_map/ppermute | solution.py:427
  18.1 5.7 %collective-permute-start.9 = (bf16[16,4992]{1,0:T(8,128)(2,1)S(1)}, bf16[16,4992]{1,0:T(8,128)(2,1)S(1)}, u32[]{:S(2)}, u32[]{:S(2)}) collective-permute-start(bf16[16,4992]{1,0:T(8,128)(2,1)S(1)} %pad_maximum_fusion.8), channel_id=1, source_target_pairs={{0,4},{1,5},{2,6},{3,7},{4,0},{5,1},{6,2},{7,3},{8,12},{9,13},{10,... | collective-permute-start | bytes 479240 | tf_op jit(solution)/shard_map/ppermute | solution.py:427
  20.0 4.5 %collective-permute-start.2 = (bf16[16,4992]{1,0:T(8,128)(2,1)S(1)}, bf16[16,4992]{1,0:T(8,128)(2,1)S(1)}, u32[]{:S(2)}, u32[]{:S(2)}) collective-permute-start(bf16[16,4992]{1,0:T(8,128)(2,1)S(1)} %pad_maximum_fusion.7), channel_id=1, source_target_pairs={{0,96},{1,97},{2,98},{3,99},{4,100},{5,101},{6,102},{7,103},{8,104... | collective-permute-start | bytes 479240 | tf_op jit(solution)/shard_map/ppermute | solution.py:427
  23.7 7.4 %collective-permute-start.15 = (bf16[32,4992]{1,0:T(8,128)(2,1)S(1)}, bf16[32,4992]{1,0:T(8,128)(2,1)S(1)}, u32[]{:S(2)}, u32[]{:S(2)}) collective-permute-start(bf16[32,4992]{1,0:T(8,128)(2,1)S(1)} %pad_maximum_fusion.6), channel_id=1, source_target_pairs={{0,4},{1,5},{2,6},{3,7},{4,0},{5,1},{6,2},{7,3},{8,12},{9,13},{10,... | collective-permute-start | bytes 958472 | tf_op jit(solution)/shard_map/ppermute | solution.py:427
  23.8 7.4 %collective-permute-start.10 = (bf16[32,4992]{1,0:T(8,128)(2,1)S(1)}, bf16[32,4992]{1,0:T(8,128)(2,1)S(1)}, u32[]{:S(2)}, u32[]{:S(2)}) collective-permute-start(bf16[32,4992]{1,0:T(8,128)(2,1)S(1)} %pad_maximum_fusion.5), channel_id=1, source_target_pairs={{0,96},{1,97},{2,98},{3,99},{4,100},{5,101},{6,102},{7,103},{8,104... | collective-permute-start | bytes 958472 | tf_op jit(solution)/shard_map/ppermute | solution.py:427
  24.5 6.9 %collective-permute-start.3 = (bf16[32,4992]{1,0:T(8,128)(2,1)S(1)}, bf16[32,4992]{1,0:T(8,128)(2,1)S(1)}, u32[]{:S(2)}, u32[]{:S(2)}) collective-permute-start(bf16[32,4992]{1,0:T(8,128)(2,1)S(1)} %pad_maximum_fusion.4), channel_id=1, source_target_pairs={{0,3},{1,2},{2,1},{3,0},{4,7},{5,6},{6,5},{7,4},{8,11},{9,10},{10,... | collective-permute-start | bytes 958472 | tf_op jit(solution)/shard_map/ppermute | solution.py:427
  31.2 9.6 %collective-permute-start.16 = (bf16[64,4992]{1,0:T(8,128)(2,1)S(1)}, bf16[64,4992]{1,0:T(8,128)(2,1)S(1)}, u32[]{:S(2)}, u32[]{:S(2)}) collective-permute-start(bf16[64,4992]{1,0:T(8,128)(2,1)S(1)} %pad_maximum_fusion.3.held_ref), channel_id=1, source_target_pairs={{0,96},{1,97},{2,98},{3,99},{4,100},{5,101},{6,102},{7,103},{8,104... | collective-permute-start | bytes 1916936 | tf_op jit(solution)/shard_map/ppermute | solution.py:427
  31.3 10.6 %collective-permute-start.11 = (bf16[64,4992]{1,0:T(8,128)(2,1)S(1)}, bf16[64,4992]{1,0:T(8,128)(2,1)S(1)}, u32[]{:S(2)}, u32[]{:S(2)}) collective-permute-start(bf16[64,4992]{1,0:T(8,128)(2,1)S(1)} %pad_maximum_fusion.2.held_ref), channel_id=1, source_target_pairs={{0,3},{1,2},{2,1},{3,0},{4,7},{5,6},{6,5},{7,4},{8,11},{9,10},{10,... | collective-permute-start | bytes 1916936 | tf_op jit(solution)/shard_map/ppermute | solution.py:427
  31.5 10.6 %collective-permute-start.4 = (bf16[64,4992]{1,0:T(8,128)(2,1)S(1)}, bf16[64,4992]{1,0:T(8,128)(2,1)S(1)}, u32[]{:S(2)}, u32[]{:S(2)}) collective-permute-start(bf16[64,4992]{1,0:T(8,128)(2,1)S(1)} %pad_maximum_fusion.1.held_ref), channel_id=1, source_target_pairs={{0,12},{1,13},{2,14},{3,15},{4,8},{5,9},{6,10},{7,11},{8,4},{9,5},... | collective-permute-start | bytes 1916936 | tf_op jit(solution)/shard_map/ppermute | solution.py:427
  34.0 9.3 %collective-permute-start.6 = (bf16[384,1536]{1,0:T(8,128)(2,1)}, bf16[384,1536]{1,0:T(8,128)(2,1)}, u32[]{:S(2)}, u32[]{:S(2)}) collective-permute-start(bf16[384,1536]{1,0:T(8,128)(2,1)} %dynamic-slice_bitcast_fusion), channel_id=1, source_target_pairs={{0,16},{1,17},{2,18},{3,19},{4,20},{5,21},{6,22},{7,23},{8,24},{9,... | collective-permute-start | bytes 3538952 | tf_op jit(solution)/shard_map/ppermute | solution.py:427
  42.0 16.7 %collective-permute-start.17 = (bf16[128,4992]{1,0:T(8,128)(2,1)}, bf16[128,4992]{1,0:T(8,128)(2,1)}, u32[]{:S(2)}, u32[]{:S(2)}) collective-permute-start(bf16[128,4992]{1,0:T(8,128)(2,1)} %join.10.held_ref), channel_id=1, source_target_pairs={{0,3},{1,2},{2,1},{3,0},{4,7},{5,6},{6,5},{7,4},{8,11},{9,10},{10,... | collective-permute-start | bytes 3833864 | tf_op jit(solution)/shard_map/ppermute | solution.py:427
  42.0 18.6 %collective-permute-start.12 = (bf16[128,4992]{1,0:T(8,128)(2,1)S(1)}, bf16[128,4992]{1,0:T(8,128)(2,1)}, u32[]{:S(2)}, u32[]{:S(2)}) collective-permute-start(bf16[128,4992]{1,0:T(8,128)(2,1)S(1)} %join.8.held_ref), channel_id=1, source_target_pairs={{0,12},{1,13},{2,14},{3,15},{4,8},{5,9},{6,10},{7,11},{8,4},{9,5},... | collective-permute-start | bytes 3833864 | tf_op jit(solution)/shard_map/ppermute | solution.py:427
  42.2 20.0 %collective-permute-start.5 = (bf16[128,4992]{1,0:T(8,128)(2,1)S(1)}, bf16[128,4992]{1,0:T(8,128)(2,1)}, u32[]{:S(2)}, u32[]{:S(2)}) collective-permute-start(bf16[128,4992]{1,0:T(8,128)(2,1)S(1)} %join.6.held_ref), channel_id=1, source_target_pairs={{0,32},{1,33},{2,34},{3,35},{4,36},{5,37},{6,38},{7,39},{8,40},{9,... | collective-permute-start | bytes 3833864 | tf_op jit(solution)/shard_map/ppermute | solution.py:427
  60.5 13.3 %collective-permute-start.19 = (bf16[256,1920]{1,0:T(8,128)(2,1)S(1)}, bf16[256,1920]{1,0:T(8,128)(2,1)S(1)}, u32[]{:S(2)}, u32[]{:S(2)}) collective-permute-start(bf16[256,1920]{1,0:T(8,128)(2,1)S(1)} %get-tuple-element.43.refs_2_), channel_id=1, source_target_pairs={{0,12},{1,13},{2,14},{3,15},{4,8},{5,9},{6,10},{7,11},{8,4},{9,5},... | collective-permute-start | bytes 2949128 | tf_op jit(solution)/shard_map/ppermute | solution.py:427
  62.1 14.5 %collective-permute-start.18 = (bf16[256,1920]{1,0:T(8,128)(2,1)S(1)}, bf16[256,1920]{1,0:T(8,128)(2,1)S(1)}, u32[]{:S(2)}, u32[]{:S(2)}) collective-permute-start(bf16[256,1920]{1,0:T(8,128)(2,1)S(1)} %get-tuple-element.42.refs_1_), channel_id=1, source_target_pairs={{0,32},{1,33},{2,34},{3,35},{4,36},{5,37},{6,38},{7,39},{8,40},{9,... | collective-permute-start | bytes 2949128 | tf_op jit(solution)/shard_map/ppermute | solution.py:427
  63.7 14.2 %collective-permute-start.7 = (bf16[256,1920]{1,0:T(8,128)(2,1)S(1)}, bf16[256,1920]{1,0:T(8,128)(2,1)S(1)}, u32[]{:S(2)}, u32[]{:S(2)}) collective-permute-start(bf16[256,1920]{1,0:T(8,128)(2,1)S(1)} %get-tuple-element.41.refs_0_), channel_id=1, source_target_pairs={{0,1},{1,0},{2,3},{3,2},{4,5},{5,4},{6,7},{7,6},{8,9},{9,8},{10,11... | collective-permute-start | bytes 2949128 | tf_op jit(solution)/shard_map/ppermute | solution.py:427
  77.9 27.0 %collective-permute-start.23 = (bf16[256,3072]{1,0:T(8,128)(2,1)S(1)}, bf16[256,3072]{1,0:T(8,128)(2,1)S(1)}, u32[]{:S(2)}, u32[]{:S(2)}) collective-permute-start(bf16[256,3072]{1,0:T(8,128)(2,1)S(1)} %get-tuple-element.58.refs_4_), channel_id=1, source_target_pairs={{0,12},{1,13},{2,14},{3,15},{4,8},{5,9},{6,10},{7,11},{8,4},{9,5},... | collective-permute-start | bytes 4718600 | tf_op jit(solution)/shard_map/ppermute | solution.py:427
  79.5 25.5 %collective-permute-start.22 = (bf16[256,3072]{1,0:T(8,128)(2,1)S(1)}, bf16[256,3072]{1,0:T(8,128)(2,1)S(1)}, u32[]{:S(2)}, u32[]{:S(2)}) collective-permute-start(bf16[256,3072]{1,0:T(8,128)(2,1)S(1)} %get-tuple-element.57.refs_2_), channel_id=1, source_target_pairs={{0,32},{1,33},{2,34},{3,35},{4,36},{5,37},{6,38},{7,39},{8,40},{9,... | collective-permute-start | bytes 4718600 | tf_op jit(solution)/shard_map/ppermute | solution.py:427
  82.1 22.9 %collective-permute-start.21 = (bf16[256,3072]{1,0:T(8,128)(2,1)S(1)}, bf16[256,3072]{1,0:T(8,128)(2,1)S(1)}, u32[]{:S(2)}, u32[]{:S(2)}) collective-permute-start(bf16[256,3072]{1,0:T(8,128)(2,1)S(1)} %get-tuple-element.56.refs_0_), channel_id=1, source_target_pairs={{0,1},{1,0},{2,3},{3,2},{4,5},{5,4},{6,7},{7,6},{8,9},{9,8},{10,11... | collective-permute-start | bytes 4718600 | tf_op jit(solution)/shard_map/ppermute | solution.py:427
  94.0 10.9 %collective-permute-start.20 = (f32[1536,128]{1,0:T(8,128)S(1)}, f32[1536,128]{1,0:T(8,128)S(1)}, u32[]{:S(2)}, u32[]{:S(2)}) collective-permute-start(f32[1536,128]{1,0:T(8,128)S(1)} %get-tuple-element.54), channel_id=1, source_target_pairs={{0,16},{1,17},{2,18},{3,19},{4,20},{5,21},{6,22},{7,23},{8,24},{9,... | collective-permute-start | bytes 2359304 | tf_op jit(solution)/shard_map/ppermute | solution.py:427
  110.1 7.5 %collective-permute-start.24 = (f32[1536,384]{1,0:T(8,128)S(1)}, f32[1536,384]{1,0:T(8,128)S(1)}, u32[]{:S(2)}, u32[]{:S(2)}) collective-permute-start(f32[1536,384]{1,0:T(8,128)S(1)} %get-tuple-element.61), channel_id=1, source_target_pairs={{0,16},{1,17},{2,18},{3,19},{4,20},{5,21},{6,22},{7,23},{8,24},{9,... | collective-permute-start | bytes 7077896 | tf_op jit(solution)/shard_map/ppermute | solution.py:427
  112.0 5.6 %collective-permute-start.25 = (f32[384,128]{1,0:T(8,128)S(1)}, f32[384,128]{1,0:T(8,128)S(1)}, u32[]{:S(2)}, u32[]{:S(2)}) collective-permute-start(f32[384,128]{1,0:T(8,128)S(1)} %get-tuple-element.63), channel_id=1, source_target_pairs={{0,16},{1,17},{2,18},{3,19},{4,20},{5,21},{6,22},{7,23},{8,24},{9,... | collective-permute-start | bytes 589832 | tf_op jit(solution)/shard_map/ppermute | solution.py:427
  (13 other events, 52.8 us)

commit v9 on v8

--- a/solution.py
+++ b/solution.py
@@ -12,12 +12,13 @@
 HEADS = 48
 HEADS_STEP = 8
 EPSILON = 1e-05
+LOG2E = 1.4426950408889634
 BF = jnp.bfloat16
 F32 = jnp.float32
 
 
-def length_of(shard_ref, heads):
-    coded = shard_ref[:1].astype(F32)
+def length_of(shard_ref, heads, start=0):
+    coded = shard_ref[:1, start : start + LANES].astype(F32)
     return 16.0 * coded[:, heads : heads + 1] + coded[:, heads + 1 : heads + 2]
 
 
@@ -40,175 +41,161 @@
 
 
 def scan_kernel(
+    which,
     meta_ref,
     shard_ref,
-    input_ref,
-    side_ref,
+    projected_ref,
     taps_ref,
-    side_taps_ref,
     bias_ref,
     log_rate_ref,
     skip_ref,
     scanned_ref,
     state_ref,
     decay_col,
-    delta_col,
+    delta_row,
     decay_row,
     b_scr,
     c_scr,
     cb_scr,
 ):
-    step = pl.program_id(0)
-    seq = input_ref.shape[0]
-    state_dim = side_taps_ref.shape[1] // 2
+    seq, half = scanned_ref.shape
+    state_dim = state_ref.shape[1]
     groups = decay_col.shape[0]
+    group_cols = HEADS_STEP * LANES // 2
     blocks = seq // SPAN
+    every = slice(which * seq, (which + 1) * seq)
     position = lax.broadcasted_iota(jnp.int32, (seq, LANES), 0)
-    group_here = meta_ref[0] * pl.num_programs(0) + step
-
-    @pl.when(step == 0)
-    def _():
-        side = side_ref[...].astype(F32)
-        conv = causal_conv(side[:, : 2 * state_dim], side_taps_ref[...])
-        b_short = conv[:, :state_dim].astype(BF)
-        c_short = conv[:, state_dim:].astype(BF)
-        b_scr[...] = b_short
-        c_scr[...] = c_short
-        for block in range(blocks):
-            at = slice(block * SPAN, (block + 1) * SPAN)
-            cb_scr[block] = lax.dot_general(
-                c_short[at], b_short[at], (((1,), (1,)), ((), ())), preferred_element_type=F32
-            )
-        spare = jnp.zeros((1, LANES - bias_ref.shape[1]), F32)
-        raw = side[:, 2 * state_dim :] + jnp.concatenate([bias_ref[...], spare], axis=1)
-        live = (position.astype(F32) < length_of(shard_ref, bias_ref.shape[1])).astype(F32)
-        delta = (jnp.maximum(raw, 0.0) + jnp.log1p(jnp.exp(-jnp.abs(raw)))) * live
-        total = delta * -jnp.exp(jnp.concatenate([log_rate_ref[...], spare], axis=1))
-        within = position % SPAN
-        reach = 1
-        while reach < SPAN:
-            total = total + jnp.where(within >= reach, pltpu.roll(total, reach, 0), 0.0)
-            reach *= 2
-        turned = jnp.transpose(total)
-        for group in range(groups):
-            at = slice(group * HEADS_STEP, (group + 1) * HEADS_STEP)
-            decay_col[group] = total[:, at]
-            delta_col[group] = delta[:, at]
-            decay_row[group] = turned[at]
-
-    decays = decay_col[group_here]
-    deltas = delta_col[group_here]
-    rows_of = decay_row[group_here]
     lower = lax.broadcasted_iota(jnp.int32, (SPAN, SPAN), 0) >= lax.broadcasted_iota(
         jnp.int32, (SPAN, SPAN), 1
     )
+    side = projected_ref[every, half:].astype(F32)
+    conv = causal_conv(side[:, : 2 * state_dim], taps_ref[:, 2 * half :])
+    b_short = conv[:, :state_dim].astype(BF)
+    c_short = conv[:, state_dim:].astype(BF)
+    b_scr[...] = b_short
+    c_scr[...] = c_short
+    for block in range(blocks):
+        at = slice(block * SPAN, (block + 1) * SPAN)
+        cb_scr[block] = lax.dot_general(
+            c_short[at], b_short[at], (((1,), (1,)), ((), ())), preferred_element_type=F32
+        )
+        cb_scr[block] = jnp.where(lower, cb_scr[block], 0.0)
+    spare = jnp.zeros((1, LANES - bias_ref.shape[1]), F32)
+    raw = side[:, 2 * state_dim :] + jnp.concatenate([bias_ref[...], spare], axis=1)
+    live = (position.astype(F32) < length_of(
+            shard_ref, bias_ref.shape[1], half + 2 * state_dim
+        )).astype(F32)
+    delta = (jnp.maximum(raw, 0.0) + jnp.log1p(jnp.exp(-jnp.abs(raw)))) * live
+    total = delta * (-LOG2E * jnp.exp(jnp.concatenate([log_rate_ref[...], spare], axis=1)))
+    within = position % SPAN
+    reach = 1
+    while reach < SPAN:
+        total = total + jnp.where(within >= reach, pltpu.roll(total, reach, 0), 0.0)
+        reach *= 2
+    turned = jnp.transpose(total)
+    turned_delta = jnp.transpose(delta)
+    for group in range(groups):
+        at = slice(group * HEADS_STEP, (group + 1) * HEADS_STEP)
+        decay_col[group] = total[:, at]
+        delta_row[group] = turned_delta[at]
+        decay_row[group] = turned[at]
+
     left = lax.broadcasted_iota(jnp.int32, (SPAN, LANES), 1) < LANES // 2
     top = lax.broadcasted_iota(jnp.int32, (LANES, state_dim), 0) < LANES // 2
-    for pair in range(HEADS_STEP // 2):
-        cols = slice(pair * LANES, (pair + 1) * LANES)
-        one, two = 2 * pair, 2 * pair + 1
-        x_conv = causal_conv(input_ref[:, cols].astype(F32), taps_ref[:, cols])
-        head = group_here * HEADS_STEP + one
-        skip = jnp.where(left[:1], skip_ref[head], skip_ref[head + 1])
-        state = jnp.zeros((LANES, state_dim), F32)
-        for block in range(blocks):
-            at = slice(block * SPAN, (block + 1) * SPAN)
-            x_here = x_conv[at]
-            cb = cb_scr[block]
-            d_one, d_two = decays[at, one : one + 1], decays[at, two : two + 1]
-            mix_one = cb * jnp.exp(
-                jnp.where(lower, d_one - rows_of[one : one + 1, at], -jnp.inf)
+
+    def group(step, carry):
+        group_here = meta_ref[0] * (groups // 2) + step
+        decays = decay_col[group_here]
+        delta_of = delta_row[group_here]
+        rows_of = decay_row[group_here]
+        weight_of = delta_of * jnp.exp2(
+            jnp.concatenate(
+                [
+                    rows_of[:, end - 1 : end] - rows_of[:, end - SPAN : end]
+                    for end in range(SPAN, seq + 1, SPAN)
+                ],
+                axis=1,
             )
-            mix_two = cb * jnp.exp(
-                jnp.where(lower, d_two - rows_of[two : two + 1, at], -jnp.inf)
-            )
-            decay = jnp.where(left, d_one, d_two)
-            x_step = x_here * jnp.where(
-                left, deltas[at, one : one + 1], deltas[at, two : two + 1]
-            )
-            short = x_step.astype(BF)
-            zero = jnp.zeros_like(short)
-            mixing = jnp.concatenate([mix_one.astype(BF), mix_two.astype(BF)], axis=1)
-            spread = jnp.concatenate(
-                [jnp.where(left, short, zero), jnp.where(left, zero, short)], axis=0
-            )
-            out = jnp.dot(mixing, spread, preferred_element_type=F32)
-            if block:
-                out = out + jnp.exp(decay) * lax.dot_general(
-                    c_scr[at],
-                    state.astype(BF),
-                    (((1,), (1,)), ((), ())),
-                    preferred_element_type=F32,
+        )
+        for pair in range(HEADS_STEP // 2):
+            here = pl.ds(pl.multiple_of(step * group_cols + pair * LANES, LANES), LANES)
+            taps_at = pl.multiple_of(meta_ref[0] * half + step * group_cols + pair * LANES, LANES)
+            taps_at = pl.ds(taps_at, LANES)
+            one, two = 2 * pair, 2 * pair + 1
+            x_conv = causal_conv(projected_ref[every, here].astype(F32), taps_ref[:, taps_at])
+            head = group_here * HEADS_STEP + one
+            skip = jnp.where(left[:1], skip_ref[head], skip_ref[head + 1])
+            state = jnp.zeros((LANES, state_dim), F32)
+            for block in range(blocks):
+                at = slice(block * SPAN, (block + 1) * SPAN)
+                x_here = x_conv[at]
+                cb = cb_scr[block]
+                d_one, d_two = decays[at, one : one + 1], decays[at, two : two + 1]
+                mix_one = cb * jnp.exp2(jnp.minimum(d_one - rows_of[one : one + 1, at], 0.0)) * delta_of[one : one + 1, at]
+                mix_two = cb * jnp.exp2(jnp.minimum(d_two - rows_of[two : two + 1, at], 0.0)) * delta_of[two : two + 1, at]
+                decay = jnp.where(left, d_one, d_two)
+                short = x_here.astype(BF)
+                zero = jnp.zeros_like(short)
+                mixing = jnp.concatenate([mix_one.astype(BF), mix_two.astype(BF)], axis=1)
+                spread = jnp.concatenate(
+                    [jnp.where(left, short, zero), jnp.where(left, zero, short)], axis=0
                 )
-            ending = decay[SPAN - 1 : SPAN]
-            weighted = (x_step * jnp.exp(ending - decay)).astype(BF)
-            fresh = lax.dot_general(
-                weighted, b_scr[at], (((0,), (0,)), ((), ())), preferred_element_type=F32
-            )
-            if block:
-                fade = jnp.where(
-                    top,
-                    jnp.exp(d_one[SPAN - 1 : SPAN]),
-                    jnp.exp(d_two[SPAN - 1 : SPAN]),
+                out = jnp.dot(mixing, spread, preferred_element_type=F32)
+                if block:
+                    out = out + jnp.exp2(decay) * lax.dot_general(
+                        c_scr[at],
+                        state.astype(BF),
+                        (((1,), (1,)), ((), ())),
+                        preferred_element_type=F32,
+                    )
+                weighted = jnp.transpose(short).astype(F32) * jnp.where(
+                    top, weight_of[one : one + 1, at], weight_of[two : two + 1, at]
                 )
-                fresh = fade * state + fresh
-            state = fresh
-            scanned_ref[at, cols] = out + skip * x_here
-        state_ref[cols, :] = state
+                fresh = jnp.dot(weighted.astype(BF), b_scr[at], preferred_element_type=F32)
+                if block:
+                    fade = jnp.where(
+                        top,
+                        jnp.exp2(d_one[SPAN - 1 : SPAN]),
+                        jnp.exp2(d_two[SPAN - 1 : SPAN]),
+                    )
+                    fresh = fade * state + fresh
+                state = fresh
+                scanned_ref[at, here] = out + skip * x_here
+            state_ref[here, :] = state
+        return carry
+
+    lax.fori_loop(0, groups // 2, group, 0)
 
 
 def scan(which, meta, shard, projected, conv_weight, bias, log_rate, skip, width):
-    rows, total = projected.shape
-    seq = rows // 2
+    seq, total = projected.shape[0] // 2, projected.shape[1]
     state_dim = width // 2
     half = total - width - LANES
-    inner = 2 * half
-    cols = HEADS_STEP * LANES // 2
-    groups = half // cols
-    taps, heads = conv_weight.shape[0], bias.shape[1]
-    here = lambda g, m: (0, m[0] * groups + g)
-    fixed = lambda g, m: (0, 0)
-    grid_spec = pltpu.PrefetchScalarGridSpec(
-        num_scalar_prefetch=1,
-        grid=(groups,),
-        in_specs=[
-            pl.BlockSpec((shard.shape[0], LANES), lambda g, m: (0, total // LANES - 1)),
-            pl.BlockSpec((seq, cols), lambda g, m: (which, g)),
-            pl.BlockSpec((seq, width + LANES), lambda g, m: (which, half // (width + LANES))),
-            pl.BlockSpec((taps, cols), here),
-            pl.BlockSpec((taps, width), lambda g, m: (0, inner // width)),
-            pl.BlockSpec((1, heads), fixed),
-            pl.BlockSpec((1, heads), fixed),
-            pl.BlockSpec(memory_space=pltpu.SMEM),
-        ],
-        out_specs=[
-            pl.BlockSpec((seq, cols), lambda g, m: (0, g)),
-            pl.BlockSpec((cols, state_dim), lambda g, m: (g, 0)),
+    groups = 2 * half // (HEADS_STEP * LANES // 2)
+    scalars = pl.BlockSpec(memory_space=pltpu.SMEM)
+    whole = pl.BlockSpec(memory_space=pltpu.VMEM)
+    return pl.pallas_call(
+        functools.partial(scan_kernel, which),
+        in_specs=[scalars] + [whole] * 5 + [scalars],
+        out_specs=[whole] * 2,
+        out_shape=[
+            jax.ShapeDtypeStruct((seq, half), F32),
+            jax.ShapeDtypeStruct((half, state_dim), F32),
         ],
         scratch_shapes=[
-            pltpu.VMEM((2 * groups, seq, HEADS_STEP), F32),
-            pltpu.VMEM((2 * groups, seq, HEADS_STEP), F32),
-            pltpu.VMEM((2 * groups, HEADS_STEP, seq), F32),
+            pltpu.VMEM((groups, seq, HEADS_STEP), F32),
+            pltpu.VMEM((groups, HEADS_STEP, seq), F32),
+            pltpu.VMEM((groups, HEADS_STEP, seq), F32),
             pltpu.VMEM((seq, state_dim), BF),
             pltpu.VMEM((seq, state_dim), BF),
             pltpu.VMEM((seq // SPAN, SPAN, SPAN), F32),
         ],
-    )
-    return pl.pallas_call(
-        scan_kernel,
-        grid_spec=grid_spec,
-        out_shape=[
-            jax.ShapeDtypeStruct((seq, half), F32),
-            jax.ShapeDtypeStruct((half, state_dim), F32),
-        ],
-        compiler_params=pltpu.CompilerParams(
-            dimension_semantics=("arbitrary",), vmem_limit_bytes=24 << 20
-        ),
+        compiler_params=pltpu.CompilerParams(vmem_limit_bytes=16 << 20),
         cost_estimate=pl.CostEstimate(
-            flops=inner * seq * 640, transcendentals=inner * seq * 3, bytes_accessed=5 << 20
+            flops=2 * half * seq * 640, transcendentals=half * seq * 6, bytes_accessed=5 << 20
         ),
         name="scan",
-    )(meta, shard, projected, projected, conv_weight, conv_weight, bias, log_rate, skip)
+    )(meta, shard, projected, conv_weight, bias, log_rate, skip)
 
 
 def shards_kernel(
@@ -242,7 +229,6 @@
         in_specs=[scalars] * 2 + [whole] * 5,
         out_specs=[whole] * 2,
         out_shape=[jax.ShapeDtypeStruct((rows, total), BF)] * 2,
-        compiler_params=pltpu.CompilerParams(vmem_limit_bytes=6 << 20),
         name="shards",
     )(meta, lengths, inputs, state, step, gate, out)
 

time: 120 us -> 117 us (0.975)
  local copies, waits for them, and re-layouts: 7.23 us -> 2.4 us
  Pallas kernels: 42.8 us -> 39.3 us
  waiting for transfers between devices: 32.3 us -> 35 us
  starting transfers between devices: 28.7 us -> 30.2 us
  other arithmetic: 2.11 us -> 3.51 us
    pallas_call x2, Pallas kernels: 17.1 us -> 12.2 us  [scan(): pl.pallas_call(functools.partial(scan_kernel, which), in_specs=[scalars]...]
    unnamed x22 -> x14, local copies, waits for them, and re-layouts: 4.87 us -> 0.03 us
    ppermute x26, waiting for transfers between devices: 32.3 us -> 35 us  [hop(): lax.ppermute(value, EVERYONE, [(d, d ^ mask_of(d // CORE % 2)) for d in r...]
    ppermute x26, starting transfers between devices: 28.7 us -> 30.2 us  [hop(): lax.ppermute(value, EVERYONE, [(d, d ^ mask_of(d // CORE % 2)) for d in r...]
    pallas_call x1, Pallas kernels: 0.58 us -> 1.91 us  [shards(): pl.pallas_call(shards_kernel, in_specs=[scalars] * 2 + [whole] * 5, out_s...]
  transfers between devices with their start and end apart: 26 -> 26, of which waited for: 9 -> 11; matrix products, arithmetic and copies ran while one was open for 8% -> 9% of each run, Pallas kernels for 29% -> 26%
where the time goes in v9:
time: 117 us
  Pallas kernels  39.3 us (34%)
  waiting for transfers between devices  35 us (30%)
  starting transfers between devices  30.2 us (26%)
  matrix products  5.78 us (5%)
  other arithmetic  3.51 us (3%)
  local copies, waits for them, and re-layouts  2.4 us (2%)
    ppermute x26, waiting for transfers between devices, hop(): lax.ppermute(value, EVERYONE, [(d, d ^ mask_of(d // CORE % 2)) for d in r...  35 us
    ppermute x26, starting transfers between devices, hop(): lax.ppermute(value, EVERYONE, [(d, d ^ mask_of(d // CORE % 2)) for d in r...  30.2 us
    pallas_call x2, Pallas kernels, scan(): pl.pallas_call(functools.partial(scan_kernel, which), in_specs=[scalars]...  12.2 us
    pallas_call x2, Pallas kernels, out_share(): pl.pallas_call(functools.partial(share_kernel, which), in_specs=[scalars]...  10.3 us
    pallas_call x2, Pallas kernels, project(): pl.pallas_call(functools.partial(project_kernel, first), in_specs=[whole]...  6.49 us
    pallas_call x6, Pallas kernels, join(): pl.pallas_call(join_kernel, in_specs=[whole] * 2, out_specs=[whole] * len...  6.11 us
    dot_general x1, matrix products, body(): both = jnp.dot(both, pick.astype(BF), preferred_element_type=F32).astype(BF)  5.78 us
    squeeze x1, local copies, waits for them, and re-layouts, body(): own = lax.dynamic_index_in_dim(tokens, unit_id, 0, keepdims=False)  2.37 us
  transfers between devices with their start and end apart: 26, of which 11 were waited for; matrix products, arithmetic and copies ran while one was open for 9% of the time, Pallas kernels for 26%

profile of v9, /device:TPU:1, one launch (start us, length us, event | category | flops | bytes accessed | tf_op | source)
XLA Modules:
  0.0 117.2 jit_solution(958508731542334951)
XLA Ops:
  1.3 1.9 %shards.1 = (bf16[12,4992]{1,0:T(8,128)(2,1)}, bf16[12,4992]{1,0:T(8,128)(2,1)}) custom-call(s32[2]{0:T(128)} %pad_add_fusion.meta_ref, s32[16]{0:T(128)} %lengths_ref.1, f32[12,3072]{1,0:T(8,128)} %input_ref.1, f32[12,256]{1,0:T(8,128)} %state_ref.1, f32[12,48]{1,0:T(8,128)} %step_ref.1, f32[12,3072]{1,0:T(8,128)} %gate_ref.1, f32[12,3072]{1,0:T(8,128)} %out_ref.1), custom_call_target="tpu_custom_call" | custom-call | tf_op jit(solution)/shard_map/shards/pallas_call | solution.py:227
  6.9 3.9 %collective-permute-start.13 = (bf16[8,4992]{1,0:T(8,128)(2,1)S(1)}, bf16[8,4992]{1,0:T(8,128)(2,1)S(1)}, u32[]{:S(2)}, u32[]{:S(2)}) collective-permute-start(bf16[8,4992]{1,0:T(8,128)(2,1)S(1)} %get-tuple-element.70), channel_id=1, source_target_pairs={{0,32},{1,33},{2,34},{3,35},{4,36},{5,37},{6,38},{7,39},{8,40},{9,... | collective-permute-start | bytes 239624 | tf_op jit(solution)/shard_map/ppermute | solution.py:413
  10.8 2.7 %collective-permute-start.8 = (bf16[8,4992]{1,0:T(8,128)(2,1)S(1)}, bf16[8,4992]{1,0:T(8,128)(2,1)S(1)}, u32[]{:S(2)}, u32[]{:S(2)}) collective-permute-start(bf16[8,4992]{1,0:T(8,128)(2,1)S(1)} %get-tuple-element.71), channel_id=1, source_target_pairs={{0,1},{1,0},{2,3},{3,2},{4,5},{5,4},{6,7},{7,6},{8,9},{9,8},{10,11... | collective-permute-start | bytes 239624 | tf_op jit(solution)/shard_map/ppermute | solution.py:413
  13.6 2.5 %collective-permute-start.1 = (bf16[8,4992]{1,0:T(8,128)(2,1)S(1)}, bf16[8,4992]{1,0:T(8,128)(2,1)S(1)}, u32[]{:S(2)}, u32[]{:S(2)}) collective-permute-start(bf16[8,4992]{1,0:T(8,128)(2,1)S(1)} %get-tuple-element.72), channel_id=1, source_target_pairs={{0,4},{1,5},{2,6},{3,7},{4,0},{5,1},{6,2},{7,3},{8,12},{9,13},{10,... | collective-permute-start | bytes 239624 | tf_op jit(solution)/shard_map/ppermute | solution.py:413
  18.2 3.6 %collective-permute-done.14 = bf16[16,4992]{1,0:T(8,128)(2,1)S(1)} collective-permute-done((bf16[16,4992]{1,0:T(8,128)(2,1)S(1)}, bf16[16,4992]{1,0:T(8,128)(2,1)S(1)}, u32[]{:S(2)}, u32[]{:S(2)}) %collective-permute-start.14) | collective-permute-done | bytes 159776 | tf_op jit(solution)/shard_map/ppermute | solution.py:413
  22.7 6.5 %collective-permute-done.15 = bf16[32,4992]{1,0:T(8,128)(2,1)S(1)} collective-permute-done((bf16[32,4992]{1,0:T(8,128)(2,1)S(1)}, bf16[32,4992]{1,0:T(8,128)(2,1)S(1)}, u32[]{:S(2)}, u32[]{:S(2)}) %collective-permute-start.15) | collective-permute-done | bytes 319520 | tf_op jit(solution)/shard_map/ppermute | solution.py:413
  29.7 2.4 %dynamic-slice_bitcast_fusion = bf16[384,1536]{1,0:T(8,128)(2,1)} fusion(bf16[16,384,1536]{2,1,0:T(8,128)(2,1)} %param.12, s32[]{:T(128)S(6)} %select_n.464), kind=kLoop, calls=%fused_computation.8 | loop fusion | bytes 2359300 | tf_op jit(solution)/shard_map/jit(dynamic_index_in_dim)/squeeze | solution.py:500
  32.1 4.8 %collective-permute-start.6 = (bf16[384,1536]{1,0:T(8,128)(2,1)}, bf16[384,1536]{1,0:T(8,128)(2,1)}, u32[]{:S(2)}, u32[]{:S(2)}) collective-permute-start(bf16[384,1536]{1,0:T(8,128)(2,1)} %dynamic-slice_bitcast_fusion), channel_id=1, source_target_pairs={{0,16},{1,17},{2,18},{3,19},{4,20},{5,21},{6,22},{7,23},{8,24},{9,... | collective-permute-start | bytes 3538952 | tf_op jit(solution)/shard_map/ppermute | solution.py:413
  36.9 2.0 %collective-permute-done.16.moved_ref = bf16[64,4992]{1,0:T(8,128)(2,1)S(1)} collective-permute-done((bf16[64,4992]{1,0:T(8,128)(2,1)S(1)}, bf16[64,4992]{1,0:T(8,128)(2,1)S(1)}, u32[]{:S(2)}, u32[]{:S(2)}) %collective-permute-start.16) | collective-permute-done | bytes 639008 | tf_op jit(solution)/shard_map/ppermute | solution.py:413
  41.4 5.8 %fusion.2.tokens_ref = bf16[768,1536]{1,0:T(8,128)(2,1)S(1)} fusion(s32[1536]{0:T(1024)S(1)} %select_subtract_fusion, bf16[384,1536]{1,0:T(8,128)(2,1)} %collective-permute-done.6, bf16[384,1536]{1,0:T(8,128)(2,1)} %dynamic-slice_bitcast_fusion), kind=kOutput, calls=%fused_computation.3 | convolution fusion | flops 3632136192 | bytes 4724736 | tf_op jit(solution)/shard_map/dot_general | solution.py:503
  47.2 9.6 %collective-permute-done.17.moved_ref = bf16[128,4992]{1,0:T(8,128)(2,1)} collective-permute-done((bf16[128,4992]{1,0:T(8,128)(2,1)}, bf16[128,4992]{1,0:T(8,128)(2,1)}, u32[]{:S(2)}, u32[]{:S(2)}) %collective-permute-start.17) | collective-permute-done | bytes 1277984 | tf_op jit(solution)/shard_map/ppermute | solution.py:413
  63.6 3.2 %project.2.refs_0_ = f32[768,1920]{1,0:T(8,128)S(1)} custom-call(bf16[768,1536]{1,0:T(8,128)(2,1)S(1)} %fusion.2.tokens_ref, bf16[256,1920]{1,0:T(8,128)(2,1)S(1)} %get-tuple-element.41.refs_0_, bf16[256,1920]{1,0:T(8,128)(2,1)S(1)} %get-tuple-element.42.refs_1_, bf16[256,1920]{1,0:T(8,128)(2,1)S(1)} %get-tuple-element.43.refs_2_), custom_call_target="tpu_custom_call" | custom-call | flops 2264924160 | bytes 10485760 | tf_op jit(solution)/shard_map/project/pallas_call | solution.py:289
  66.8 5.2 %collective-permute-done.19.refs_3_ = bf16[256,1920]{1,0:T(8,128)(2,1)S(1)} collective-permute-done((bf16[256,1920]{1,0:T(8,128)(2,1)S(1)}, bf16[256,1920]{1,0:T(8,128)(2,1)S(1)}, u32[]{:S(2)}, u32[]{:S(2)}) %collective-permute-start.19) | collective-permute-done | bytes 983072 | tf_op jit(solution)/shard_map/ppermute | solution.py:413
  72.0 2.8 %collective-permute-done.18.refs_2_ = bf16[256,1920]{1,0:T(8,128)(2,1)S(1)} collective-permute-done((bf16[256,1920]{1,0:T(8,128)(2,1)S(1)}, bf16[256,1920]{1,0:T(8,128)(2,1)S(1)}, u32[]{:S(2)}, u32[]{:S(2)}) %collective-permute-start.18) | collective-permute-done | bytes 983072 | tf_op jit(solution)/shard_map/ppermute | solution.py:413
  77.6 2.7 %collective-permute-start.22 = (bf16[256,3072]{1,0:T(8,128)(2,1)S(1)}, bf16[256,3072]{1,0:T(8,128)(2,1)S(1)}, u32[]{:S(2)}, u32[]{:S(2)}) collective-permute-start(bf16[256,3072]{1,0:T(8,128)(2,1)S(1)} %get-tuple-element.57.refs_2_), channel_id=1, source_target_pairs={{0,32},{1,33},{2,34},{3,35},{4,36},{5,37},{6,38},{7,39},{8,40},{9,... | collective-permute-start | bytes 4718600 | tf_op jit(solution)/shard_map/ppermute | solution.py:413
  80.2 3.3 %project.3.projected_ref = bf16[768,1920]{1,0:T(8,128)(2,1)S(1)} custom-call(bf16[768,1536]{1,0:T(8,128)(2,1)S(1)} %fusion.2.tokens_ref, f32[768,1920]{1,0:T(8,128)S(1)} %project.2.refs_0_, bf16[256,1920]{1,0:T(8,128)(2,1)S(1)} %collective-permute-done.7.refs_1_, bf16[256,1920]{1,0:T(8,128)(2,1)S(1)} %collective-permute-done.18.refs_2_, ...), custom_call_target="tpu_custom_call" | custom-call | flops 2264924160 | bytes 10485760 | tf_op jit(solution)/shard_map/project/pallas_call | solution.py:289
  83.6 6.1 %scan.2 = (f32[384,1536]{1,0:T(8,128)S(1)}, f32[1536,128]{1,0:T(8,128)S(1)}) custom-call(s32[2]{0:T(128)S(1)} %copy-done.2, bf16[12,4992]{1,0:T(8,128)(2,1)S(1)} %collective-permute-done.shard_ref, bf16[768,1920]{1,0:T(8,128)(2,1)S(1)} %project.3.projected_ref, f32[4,3328]{1,0:T(4,128)S(1)} %copy-done.3, f32[1,48]{1,0:T(1,128)S(1)} %bitcast.11, ...), custom_call_target="tpu_custom_call" | custom-call | flops 754974720 | bytes 5242880 | tf_op jit(solution)/shard_map/scan/pallas_call | solution.py:177
  89.7 2.4 %collective-permute-start.20 = (f32[1536,128]{1,0:T(8,128)S(1)}, f32[1536,128]{1,0:T(8,128)S(1)}, u32[]{:S(2)}, u32[]{:S(2)}) collective-permute-start(f32[1536,128]{1,0:T(8,128)S(1)} %get-tuple-element.54), channel_id=1, source_target_pairs={{0,16},{1,17},{2,18},{3,19},{4,20},{5,21},{6,22},{7,23},{8,24},{9,... | collective-permute-start | bytes 2359304 | tf_op jit(solution)/shard_map/ppermute | solution.py:413
  92.1 6.1 %scan.3 = (f32[384,1536]{1,0:T(8,128)S(1)}, f32[1536,128]{1,0:T(8,128)S(1)}) custom-call(s32[2]{0:T(128)S(1)} %copy-done.2, bf16[12,4992]{1,0:T(8,128)(2,1)S(1)} %copy-done, bf16[768,1920]{1,0:T(8,128)(2,1)S(1)} %project.3.projected_ref, f32[4,3328]{1,0:T(4,128)S(1)} %copy-done.3, f32[1,48]{1,0:T(1,128)S(1)} %bitcast.12, f32[1,48]{1,0:T(1,128)S(1)} %bitcast.14, ...), custom_call_target="tpu_custom_call" | custom-call | flops 754974720 | bytes 5242880 | tf_op jit(solution)/shard_map/scan/pallas_call | solution.py:177
  98.4 2.4 %collective-permute-done.21.refs_1_ = bf16[256,3072]{1,0:T(8,128)(2,1)S(1)} collective-permute-done((bf16[256,3072]{1,0:T(8,128)(2,1)S(1)}, bf16[256,3072]{1,0:T(8,128)(2,1)S(1)}, u32[]{:S(2)}, u32[]{:S(2)}) %collective-permute-start.21) | collective-permute-done | bytes 1572896 | tf_op jit(solution)/shard_map/ppermute | solution.py:413
  100.7 5.1 %out_share.3 = (f32[1536,384]{1,0:T(8,128)S(1)}, f32[384,128]{1,0:T(8,128)S(1)}) custom-call(s32[2]{0:T(128)S(1)} %copy-done.2, s32[192]{0:T(256)S(1)} %multiply_add_fusion.places_ref, bf16[768,1536]{1,0:T(8,128)(2,1)S(1)} %fusion.2.tokens_ref, f32[384,1536]{1,0:T(8,128)S(1)} %get-tuple-element.60.scanned_ref, f32[1,3072]{1,0:T(1,128)S(1)} %bitcast.9, ...), custom_call_target="tpu_custom_call" | custom-call | flops 3623878656 | bytes 16777216 | tf_op jit(solution)/shard_map/out_share/pallas_call | solution.py:342
  105.9 2.3 %collective-permute-start.24 = (f32[1536,384]{1,0:T(8,128)S(1)}, f32[1536,384]{1,0:T(8,128)S(1)}, u32[]{:S(2)}, u32[]{:S(2)}) collective-permute-start(f32[1536,384]{1,0:T(8,128)S(1)} %get-tuple-element.61), channel_id=1, source_target_pairs={{0,16},{1,17},{2,18},{3,19},{4,20},{5,21},{6,22},{7,23},{8,24},{9,... | collective-permute-start | bytes 7077896 | tf_op jit(solution)/shard_map/ppermute | solution.py:413
  109.7 5.1 %out_share.2 = (f32[1536,384]{1,0:T(8,128)S(1)}, f32[384,128]{1,0:T(8,128)S(1)}) custom-call(s32[2]{0:T(128)S(1)} %copy-done.2, s32[192]{0:T(256)S(1)} %multiply_add_fusion.places_ref, bf16[768,1536]{1,0:T(8,128)(2,1)S(1)} %fusion.2.tokens_ref, f32[384,1536]{1,0:T(8,128)S(1)} %get-tuple-element.55.scanned_ref, f32[1,3072]{1,0:T(1,128)S(1)} %bitcast.10, ...), custom_call_target="tpu_custom_call" | custom-call | flops 3623878656 | bytes 16777216 | tf_op jit(solution)/shard_map/out_share/pallas_call | solution.py:342
  114.9 2.3 %mix.1 = bf16[384,1536]{1,0:T(8,128)(2,1)} custom-call(bf16[12,4992]{1,0:T(8,128)(2,1)S(1)} %copy-done, f32[1536,384]{1,0:T(8,128)S(1)} %get-tuple-element.59.mine_ref, f32[1536,384]{1,0:T(8,128)S(1)} %collective-permute-done.24.other_ref, f32[384,128]{1,0:T(8,128)S(1)} %get-tuple-element.62.sq_mine, f32[384,128]{1,0:T(8,128)S(1)} %collective-permute-done.25.sq_other, ...), custom_call_target="tpu_custom_call" | custom-call | flops 452984832 | bytes 8388608 | tf_op jit(solution)/shard_map/mix/pallas_call | solution.py:384
  (76 shorter events, 21.4 us)
Async XLA Ops:
  6.9 9.1 %collective-permute-start.13 = (bf16[8,4992]{1,0:T(8,128)(2,1)S(1)}, bf16[8,4992]{1,0:T(8,128)(2,1)S(1)}, u32[]{:S(2)}, u32[]{:S(2)}) collective-permute-start(bf16[8,4992]{1,0:T(8,128)(2,1)S(1)} %get-tuple-element.70), channel_id=1, source_target_pairs={{0,32},{1,33},{2,34},{3,35},{4,36},{5,37},{6,38},{7,39},{8,40},{9,... | collective-permute-start | bytes 239624 | tf_op jit(solution)/shard_map/ppermute | solution.py:413
  10.8 5.3 %collective-permute-start.8 = (bf16[8,4992]{1,0:T(8,128)(2,1)S(1)}, bf16[8,4992]{1,0:T(8,128)(2,1)S(1)}, u32[]{:S(2)}, u32[]{:S(2)}) collective-permute-start(bf16[8,4992]{1,0:T(8,128)(2,1)S(1)} %get-tuple-element.71), channel_id=1, source_target_pairs={{0,1},{1,0},{2,3},{3,2},{4,5},{5,4},{6,7},{7,6},{8,9},{9,8},{10,11... | collective-permute-start | bytes 239624 | tf_op jit(solution)/shard_map/ppermute | solution.py:413
  16.1 5.7 %collective-permute-start.14 = (bf16[16,4992]{1,0:T(8,128)(2,1)S(1)}, bf16[16,4992]{1,0:T(8,128)(2,1)S(1)}, u32[]{:S(2)}, u32[]{:S(2)}) collective-permute-start(bf16[16,4992]{1,0:T(8,128)(2,1)S(1)} %pad_maximum_fusion.9), channel_id=1, source_target_pairs={{0,1},{1,0},{2,3},{3,2},{4,5},{5,4},{6,7},{7,6},{8,9},{9,8},{10,11... | collective-permute-start | bytes 479240 | tf_op jit(solution)/shard_map/ppermute | solution.py:413
  16.2 5.7 %collective-permute-start.9 = (bf16[16,4992]{1,0:T(8,128)(2,1)S(1)}, bf16[16,4992]{1,0:T(8,128)(2,1)S(1)}, u32[]{:S(2)}, u32[]{:S(2)}) collective-permute-start(bf16[16,4992]{1,0:T(8,128)(2,1)S(1)} %pad_maximum_fusion.8), channel_id=1, source_target_pairs={{0,4},{1,5},{2,6},{3,7},{4,0},{5,1},{6,2},{7,3},{8,12},{9,13},{10,... | collective-permute-start | bytes 479240 | tf_op jit(solution)/shard_map/ppermute | solution.py:413
  18.1 4.5 %collective-permute-start.2 = (bf16[16,4992]{1,0:T(8,128)(2,1)S(1)}, bf16[16,4992]{1,0:T(8,128)(2,1)S(1)}, u32[]{:S(2)}, u32[]{:S(2)}) collective-permute-start(bf16[16,4992]{1,0:T(8,128)(2,1)S(1)} %pad_maximum_fusion.7), channel_id=1, source_target_pairs={{0,96},{1,97},{2,98},{3,99},{4,100},{5,101},{6,102},{7,103},{8,104... | collective-permute-start | bytes 479240 | tf_op jit(solution)/shard_map/ppermute | solution.py:413
  21.8 7.4 %collective-permute-start.15 = (bf16[32,4992]{1,0:T(8,128)(2,1)S(1)}, bf16[32,4992]{1,0:T(8,128)(2,1)S(1)}, u32[]{:S(2)}, u32[]{:S(2)}) collective-permute-start(bf16[32,4992]{1,0:T(8,128)(2,1)S(1)} %pad_maximum_fusion.6), channel_id=1, source_target_pairs={{0,4},{1,5},{2,6},{3,7},{4,0},{5,1},{6,2},{7,3},{8,12},{9,13},{10,... | collective-permute-start | bytes 958472 | tf_op jit(solution)/shard_map/ppermute | solution.py:413
  21.9 7.4 %collective-permute-start.10 = (bf16[32,4992]{1,0:T(8,128)(2,1)S(1)}, bf16[32,4992]{1,0:T(8,128)(2,1)S(1)}, u32[]{:S(2)}, u32[]{:S(2)}) collective-permute-start(bf16[32,4992]{1,0:T(8,128)(2,1)S(1)} %pad_maximum_fusion.5), channel_id=1, source_target_pairs={{0,96},{1,97},{2,98},{3,99},{4,100},{5,101},{6,102},{7,103},{8,104... | collective-permute-start | bytes 958472 | tf_op jit(solution)/shard_map/ppermute | solution.py:413
  22.6 6.9 %collective-permute-start.3 = (bf16[32,4992]{1,0:T(8,128)(2,1)S(1)}, bf16[32,4992]{1,0:T(8,128)(2,1)S(1)}, u32[]{:S(2)}, u32[]{:S(2)}) collective-permute-start(bf16[32,4992]{1,0:T(8,128)(2,1)S(1)} %pad_maximum_fusion.4), channel_id=1, source_target_pairs={{0,3},{1,2},{2,1},{3,0},{4,7},{5,6},{6,5},{7,4},{8,11},{9,10},{10,... | collective-permute-start | bytes 958472 | tf_op jit(solution)/shard_map/ppermute | solution.py:413
  29.3 9.6 %collective-permute-start.16 = (bf16[64,4992]{1,0:T(8,128)(2,1)S(1)}, bf16[64,4992]{1,0:T(8,128)(2,1)S(1)}, u32[]{:S(2)}, u32[]{:S(2)}) collective-permute-start(bf16[64,4992]{1,0:T(8,128)(2,1)S(1)} %pad_maximum_fusion.3.held_ref), channel_id=1, source_target_pairs={{0,96},{1,97},{2,98},{3,99},{4,100},{5,101},{6,102},{7,103},{8,104... | collective-permute-start | bytes 1916936 | tf_op jit(solution)/shard_map/ppermute | solution.py:413
  29.4 10.6 %collective-permute-start.11 = (bf16[64,4992]{1,0:T(8,128)(2,1)S(1)}, bf16[64,4992]{1,0:T(8,128)(2,1)S(1)}, u32[]{:S(2)}, u32[]{:S(2)}) collective-permute-start(bf16[64,4992]{1,0:T(8,128)(2,1)S(1)} %pad_maximum_fusion.2.held_ref), channel_id=1, source_target_pairs={{0,3},{1,2},{2,1},{3,0},{4,7},{5,6},{6,5},{7,4},{8,11},{9,10},{10,... | collective-permute-start | bytes 1916936 | tf_op jit(solution)/shard_map/ppermute | solution.py:413
  29.6 10.6 %collective-permute-start.4 = (bf16[64,4992]{1,0:T(8,128)(2,1)S(1)}, bf16[64,4992]{1,0:T(8,128)(2,1)S(1)}, u32[]{:S(2)}, u32[]{:S(2)}) collective-permute-start(bf16[64,4992]{1,0:T(8,128)(2,1)S(1)} %pad_maximum_fusion.1.held_ref), channel_id=1, source_target_pairs={{0,12},{1,13},{2,14},{3,15},{4,8},{5,9},{6,10},{7,11},{8,4},{9,5},... | collective-permute-start | bytes 1916936 | tf_op jit(solution)/shard_map/ppermute | solution.py:413
  32.1 9.3 %collective-permute-start.6 = (bf16[384,1536]{1,0:T(8,128)(2,1)}, bf16[384,1536]{1,0:T(8,128)(2,1)}, u32[]{:S(2)}, u32[]{:S(2)}) collective-permute-start(bf16[384,1536]{1,0:T(8,128)(2,1)} %dynamic-slice_bitcast_fusion), channel_id=1, source_target_pairs={{0,16},{1,17},{2,18},{3,19},{4,20},{5,21},{6,22},{7,23},{8,24},{9,... | collective-permute-start | bytes 3538952 | tf_op jit(solution)/shard_map/ppermute | solution.py:413
  40.1 16.7 %collective-permute-start.17 = (bf16[128,4992]{1,0:T(8,128)(2,1)}, bf16[128,4992]{1,0:T(8,128)(2,1)}, u32[]{:S(2)}, u32[]{:S(2)}) collective-permute-start(bf16[128,4992]{1,0:T(8,128)(2,1)} %join.10.held_ref), channel_id=1, source_target_pairs={{0,3},{1,2},{2,1},{3,0},{4,7},{5,6},{6,5},{7,4},{8,11},{9,10},{10,... | collective-permute-start | bytes 3833864 | tf_op jit(solution)/shard_map/ppermute | solution.py:413
  40.1 18.6 %collective-permute-start.12 = (bf16[128,4992]{1,0:T(8,128)(2,1)S(1)}, bf16[128,4992]{1,0:T(8,128)(2,1)}, u32[]{:S(2)}, u32[]{:S(2)}) collective-permute-start(bf16[128,4992]{1,0:T(8,128)(2,1)S(1)} %join.8.held_ref), channel_id=1, source_target_pairs={{0,12},{1,13},{2,14},{3,15},{4,8},{5,9},{6,10},{7,11},{8,4},{9,5},... | collective-permute-start | bytes 3833864 | tf_op jit(solution)/shard_map/ppermute | solution.py:413
  40.3 20.0 %collective-permute-start.5 = (bf16[128,4992]{1,0:T(8,128)(2,1)S(1)}, bf16[128,4992]{1,0:T(8,128)(2,1)}, u32[]{:S(2)}, u32[]{:S(2)}) collective-permute-start(bf16[128,4992]{1,0:T(8,128)(2,1)S(1)} %join.6.held_ref), channel_id=1, source_target_pairs={{0,32},{1,33},{2,34},{3,35},{4,36},{5,37},{6,38},{7,39},{8,40},{9,... | collective-permute-start | bytes 3833864 | tf_op jit(solution)/shard_map/ppermute | solution.py:413
  58.6 13.3 %collective-permute-start.19 = (bf16[256,1920]{1,0:T(8,128)(2,1)S(1)}, bf16[256,1920]{1,0:T(8,128)(2,1)S(1)}, u32[]{:S(2)}, u32[]{:S(2)}) collective-permute-start(bf16[256,1920]{1,0:T(8,128)(2,1)S(1)} %get-tuple-element.43.refs_2_), channel_id=1, source_target_pairs={{0,12},{1,13},{2,14},{3,15},{4,8},{5,9},{6,10},{7,11},{8,4},{9,5},... | collective-permute-start | bytes 2949128 | tf_op jit(solution)/shard_map/ppermute | solution.py:413
  60.2 14.5 %collective-permute-start.18 = (bf16[256,1920]{1,0:T(8,128)(2,1)S(1)}, bf16[256,1920]{1,0:T(8,128)(2,1)S(1)}, u32[]{:S(2)}, u32[]{:S(2)}) collective-permute-start(bf16[256,1920]{1,0:T(8,128)(2,1)S(1)} %get-tuple-element.42.refs_1_), channel_id=1, source_target_pairs={{0,32},{1,33},{2,34},{3,35},{4,36},{5,37},{6,38},{7,39},{8,40},{9,... | collective-permute-start | bytes 2949128 | tf_op jit(solution)/shard_map/ppermute | solution.py:413
  61.8 14.2 %collective-permute-start.7 = (bf16[256,1920]{1,0:T(8,128)(2,1)S(1)}, bf16[256,1920]{1,0:T(8,128)(2,1)S(1)}, u32[]{:S(2)}, u32[]{:S(2)}) collective-permute-start(bf16[256,1920]{1,0:T(8,128)(2,1)S(1)} %get-tuple-element.41.refs_0_), channel_id=1, source_target_pairs={{0,1},{1,0},{2,3},{3,2},{4,5},{5,4},{6,7},{7,6},{8,9},{9,8},{10,11... | collective-permute-start | bytes 2949128 | tf_op jit(solution)/shard_map/ppermute | solution.py:413
  76.1 22.2 %collective-permute-start.23 = (bf16[256,3072]{1,0:T(8,128)(2,1)S(1)}, bf16[256,3072]{1,0:T(8,128)(2,1)S(1)}, u32[]{:S(2)}, u32[]{:S(2)}) collective-permute-start(bf16[256,3072]{1,0:T(8,128)(2,1)S(1)} %get-tuple-element.58.refs_4_), channel_id=1, source_target_pairs={{0,12},{1,13},{2,14},{3,15},{4,8},{5,9},{6,10},{7,11},{8,4},{9,5},... | collective-permute-start | bytes 4718600 | tf_op jit(solution)/shard_map/ppermute | solution.py:413
  77.6 20.8 %collective-permute-start.22 = (bf16[256,3072]{1,0:T(8,128)(2,1)S(1)}, bf16[256,3072]{1,0:T(8,128)(2,1)S(1)}, u32[]{:S(2)}, u32[]{:S(2)}) collective-permute-start(bf16[256,3072]{1,0:T(8,128)(2,1)S(1)} %get-tuple-element.57.refs_2_), channel_id=1, source_target_pairs={{0,32},{1,33},{2,34},{3,35},{4,36},{5,37},{6,38},{7,39},{8,40},{9,... | collective-permute-start | bytes 4718600 | tf_op jit(solution)/shard_map/ppermute | solution.py:413
  80.2 20.5 %collective-permute-start.21 = (bf16[256,3072]{1,0:T(8,128)(2,1)S(1)}, bf16[256,3072]{1,0:T(8,128)(2,1)S(1)}, u32[]{:S(2)}, u32[]{:S(2)}) collective-permute-start(bf16[256,3072]{1,0:T(8,128)(2,1)S(1)} %get-tuple-element.56.refs_0_), channel_id=1, source_target_pairs={{0,1},{1,0},{2,3},{3,2},{4,5},{5,4},{6,7},{7,6},{8,9},{9,8},{10,11... | collective-permute-start | bytes 4718600 | tf_op jit(solution)/shard_map/ppermute | solution.py:413
  89.7 8.5 %collective-permute-start.20 = (f32[1536,128]{1,0:T(8,128)S(1)}, f32[1536,128]{1,0:T(8,128)S(1)}, u32[]{:S(2)}, u32[]{:S(2)}) collective-permute-start(f32[1536,128]{1,0:T(8,128)S(1)} %get-tuple-element.54), channel_id=1, source_target_pairs={{0,16},{1,17},{2,18},{3,19},{4,20},{5,21},{6,22},{7,23},{8,24},{9,... | collective-permute-start | bytes 2359304 | tf_op jit(solution)/shard_map/ppermute | solution.py:413
  105.9 9.0 %collective-permute-start.24 = (f32[1536,384]{1,0:T(8,128)S(1)}, f32[1536,384]{1,0:T(8,128)S(1)}, u32[]{:S(2)}, u32[]{:S(2)}) collective-permute-start(f32[1536,384]{1,0:T(8,128)S(1)} %get-tuple-element.61), channel_id=1, source_target_pairs={{0,16},{1,17},{2,18},{3,19},{4,20},{5,21},{6,22},{7,23},{8,24},{9,... | collective-permute-start | bytes 7077896 | tf_op jit(solution)/shard_map/ppermute | solution.py:413
  109.7 5.2 %collective-permute-start.25 = (f32[384,128]{1,0:T(8,128)S(1)}, f32[384,128]{1,0:T(8,128)S(1)}, u32[]{:S(2)}, u32[]{:S(2)}) collective-permute-start(f32[384,128]{1,0:T(8,128)S(1)} %get-tuple-element.63), channel_id=1, source_target_pairs={{0,16},{1,17},{2,18},{3,19},{4,20},{5,21},{6,22},{7,23},{8,24},{9,... | collective-permute-start | bytes 589832 | tf_op jit(solution)/shard_map/ppermute | solution.py:413
  (9 other events, 64.2 us)

commit v10 on v9

--- a/solution.py
+++ b/solution.py
@@ -233,26 +233,23 @@
     )(meta, lengths, inputs, state, step, gate, out)
 
 
-def join_kernel(held_ref, moved_ref, *outs):
-    rows, start = held_ref.shape[0], 0
-    for out_ref in outs:
-        cols = slice(start, start + out_ref.shape[1])
-        out_ref[:rows] = held_ref[:, cols]
-        out_ref[rows:] = moved_ref[:, cols]
-        start += out_ref.shape[1]
-
-
-def join(held, moved, *widths):
-    rows, total = held.shape
+def join_kernel(start, held_ref, moved_ref, out_ref):
+    rows, cols = held_ref.shape[0], slice(start, start + out_ref.shape[1])
+    out_ref[:rows] = held_ref[:, cols]
+    out_ref[rows:] = moved_ref[:, cols]
+
+
+def join(held, moved, start, stop):
+    rows, width = held.shape[0], stop - start
     whole = pl.BlockSpec(memory_space=pltpu.VMEM)
     return pl.pallas_call(
-        join_kernel,
+        functools.partial(join_kernel, start),
         in_specs=[whole] * 2,
-        out_specs=[whole] * len(widths),
-        out_shape=[jax.ShapeDtypeStruct((2 * rows, width), BF) for width in widths],
+        out_specs=whole,
+        out_shape=jax.ShapeDtypeStruct((2 * rows, width), BF),
         compiler_params=pltpu.CompilerParams(vmem_limit_bytes=6 << 20),
         cost_estimate=pl.CostEstimate(
-            flops=0, transcendentals=0, bytes_accessed=8 * rows * total
+            flops=0, transcendentals=0, bytes_accessed=8 * rows * width
         ),
         name="join",
     )(held, moved)
@@ -356,7 +353,27 @@
     )(meta, places, tokens, scanned, gain, *pieces)
 
 
-def mix_kernel(shard_ref, mine_ref, other_ref, sq_mine, sq_other, pick_ref, out_ref):
+def mix_kernel(
+    meta_ref,
+    shard_ref,
+    mine_ref,
+    other_ref,
+    sq_mine,
+    sq_other,
+    pick_ref,
+    state_ref,
+    state_other_ref,
+    out_ref,
+    state_out_ref,
+    sems,
+):
+    core, half = meta_ref[0], state_ref.shape[0]
+    copies = []
+    for index, source in enumerate((state_ref, state_other_ref)):
+        place = (core if index == 0 else 1 - core) * half
+        place = pl.ds(pl.multiple_of(place, half), half)
+        copies.append(pltpu.make_async_copy(source, state_out_ref.at[place], sems.at[index]))
+        copies[-1].start()
     seq, model = out_ref.shape
     inner = 2 * model
     squares = jnp.transpose(sq_mine[...] + sq_other[...])
@@ -370,9 +387,11 @@
         out_ref[:, rows] = lax.dot_general(
             short, pick_ref[...], (((0,), (0,)), ((), ())), preferred_element_type=F32
         ).astype(BF)
-
-
-def mix(shard, cut, mine, other, sq_mine, sq_other):
+    for copy in copies:
+        copy.wait()
+
+
+def mix(meta, shard, cut, mine, other, sq_mine, sq_other, state, state_other):
     model, seq = mine.shape
     tile = model // 4
     column = jnp.arange(tile, dtype=jnp.int32)
@@ -380,20 +399,28 @@
     target = rest // SHARD_ROWS * (tile // 2) + chip * SHARD_ROWS + rest % SHARD_ROWS
     pick = (target[:, None] == column[None]).astype(BF)
     whole = pl.BlockSpec(memory_space=pltpu.VMEM)
-    fixed = lambda i: (0, 0)
+    anywhere = pl.BlockSpec(memory_space=pl.ANY)
     return pl.pallas_call(
         mix_kernel,
         grid=(1,),
-        in_specs=[pl.BlockSpec((shard.shape[0], LANES), lambda i: (0, cut // LANES - 1))]
-        + [whole] * 5,
-        out_specs=whole,
-        out_shape=jax.ShapeDtypeStruct((seq, model), BF),
+        in_specs=[
+            pl.BlockSpec(memory_space=pltpu.SMEM),
+            pl.BlockSpec((shard.shape[0], LANES), lambda i: (0, cut // LANES - 1)),
+        ]
+        + [whole] * 5
+        + [anywhere] * 2,
+        out_specs=[whole, anywhere],
+        out_shape=[
+            jax.ShapeDtypeStruct((seq, model), BF),
+            jax.ShapeDtypeStruct((2 * state.shape[0], state.shape[1]), F32),
+        ],
+        scratch_shapes=[pltpu.SemaphoreType.DMA((2,))],
         compiler_params=pltpu.CompilerParams(vmem_limit_bytes=16 << 20),
         cost_estimate=pl.CostEstimate(
             flops=2 * seq * tile * model, transcendentals=0, bytes_accessed=8 << 20
         ),
         name="mix",
-    )(shard, mine, other, sq_mine, sq_other, pick)
+    )(meta, shard, mine, other, sq_mine, sq_other, pick, state, state_other)
 
 
 EVERYONE = ("req", "unit")
@@ -487,28 +514,26 @@
         meta, lengths, input_proj, state_proj, step_proj, gate_proj, out_proj
     )
     sent, unit_id = lax.optimization_barrier((sent, unit_id))
-    received = swap(sent)
+    own = lax.dynamic_index_in_dim(tokens, unit_id, 0, keepdims=False)
+    received, own = lax.optimization_barrier((swap(sent), own))
     pair = jnp.concatenate(
         [jnp.where(first_core, kept, received), jnp.where(first_core, received, kept)], axis=0
     )
     held = [pair[8 * c : 8 * c + 8] for c in range(COLOURS)]
     for step in range(3):
         held = joined(held, moved_over(held, step))
-    held = [join(h, m, cut + 2 * half)[0] for h, m in zip(held, moved_over(held, 3))]
+    held = [join(h, m, 0, cut + 2 * half) for h, m in zip(held, moved_over(held, 3))]
     moved = moved_over(held, 4)
 
-    own = lax.dynamic_index_in_dim(tokens, unit_id, 0, keepdims=False)
     both = jnp.concatenate([own, swap(own)], axis=0)
     pick = jnp.arange(model_dim, dtype=jnp.int32)[:, None] == row_sources(me, core, model_dim)[None]
     both = jnp.dot(both, pick.astype(BF), preferred_element_type=F32).astype(BF)
     moved[0], both, places = lax.optimization_barrier((moved[0], both, row_places(me, core)))
-    early, late = zip(*[join(h, m, cut, 2 * half) for h, m in zip(held, moved)])
-    late = list(late)
+    early = [join(h, m, 0, cut) for h, m in zip(held, moved)]
+    early[2], held, rest = lax.optimization_barrier((early[2], held, moved))
+    late = [join(h, m, cut, cut + 2 * half) for h, m in zip(held, rest)]
     moved = moved_over(early, 5)
-    begun = project(both, early)
-    moved[0], begun = lax.optimization_barrier((moved[0], begun))
-    for c in range(COLOURS):
-        moved[c], late[c] = lax.optimization_barrier((moved[c], late[c]))
+    late[2], begun = lax.optimization_barrier((late[2], project(both, early)))
     late = [piece for two in zip(late, moved_over(late, 5)) for piece in two]
 
     projected = project(both, moved, begun)
@@ -523,9 +548,8 @@
     sent, square_sent = out_share(1, *shared, scanned_other, norm_gain[None], late)
     other, square_other = swap(sent), swap(square_sent)
     mine, square = out_share(0, *shared, scanned, norm_gain[None], late)
-    mixed = mix(kept, cut, mine, other, square, square_other)
-    state = jnp.concatenate(
-        [jnp.where(first_core, state, state_other), jnp.where(first_core, state_other, state)]
+    mixed, state = mix(
+        meta, kept, cut, mine, other, square, square_other, state, state_other
     )
     return (mixed[None], state.reshape(1, head_count, head_dim, width // 2))
 

time: 117 us -> 117 us (level); the launches traced: 117 us -> 116 us
  starting transfers between devices: 30.2 us -> 39 us
  waiting for transfers between devices: 35 us -> 27.6 us
  Pallas kernels: 39.3 us -> 37.7 us
  other arithmetic: 3.51 us -> 2.06 us
    ppermute x26, starting transfers between devices: 30.2 us -> 39 us  [hop(): lax.ppermute(value, EVERYONE, [(d, d ^ mask_of(d // CORE % 2)) for d in r...]
    ppermute x26, waiting for transfers between devices: 35 us -> 27.6 us  [hop(): lax.ppermute(value, EVERYONE, [(d, d ^ mask_of(d // CORE % 2)) for d in r...]
    pallas_call x7 -> x10, Pallas kernels: 8.39 us -> 6.79 us  [the longest x1 3.66 us: mix(): pl.pallas_call(mix_kernel, grid=(1,), in_specs=[pl.BlockSpec(memory_space...]
    concatenate x1, other arithmetic: 1.25 us -> 0.06 us  [body(): jnp.concatenate([jnp.where(first_core, kept, received), jnp.where(first_c...]
  transfers between devices with their start and end apart: 26 -> 26, of which waited for: 11 -> 11; matrix products, arithmetic and copies ran while one was open for 9% -> 8% of each run, Pallas kernels for 26% -> 23%
where the time goes in v10:
time: 117 us; the launch traced here: 116 us
  starting transfers between devices  39 us (33%)
  Pallas kernels  37.7 us (32%)
  waiting for transfers between devices  27.6 us (24%)
  matrix products  5.78 us (5%)
  local copies, waits for them, and re-layouts  2.4 us (2%)
  other arithmetic  2.06 us (2%)
  between operations  1.17 us (1%)
    ppermute x26, starting transfers between devices, hop(): lax.ppermute(value, EVERYONE, [(d, d ^ mask_of(d // CORE % 2)) for d in r...  39 us
    ppermute x26, waiting for transfers between devices, hop(): lax.ppermute(value, EVERYONE, [(d, d ^ mask_of(d // CORE % 2)) for d in r...  27.6 us
    pallas_call x2, Pallas kernels, scan(): pl.pallas_call(functools.partial(scan_kernel, which), in_specs=[scalars]...  12.3 us
    pallas_call x2, Pallas kernels, out_share(): pl.pallas_call(functools.partial(share_kernel, which), in_specs=[scalars]...  10.3 us
    pallas_call x2, Pallas kernels, project(): pl.pallas_call(functools.partial(project_kernel, first), in_specs=[whole]...  6.42 us
    dot_general x1, matrix products, body(): both = jnp.dot(both, pick.astype(BF), preferred_element_type=F32).astype(BF)  5.78 us
    pallas_call x1, Pallas kernels, mix(): pl.pallas_call(mix_kernel, grid=(1,), in_specs=[pl.BlockSpec(memory_space...  3.66 us
    pallas_call x9, Pallas kernels, join(): pl.pallas_call(functools.partial(join_kernel, start), in_specs=[whole] *...  3.13 us
  transfers between devices with their start and end apart: 26, of which 11 were waited for; matrix products, arithmetic and copies ran while one was open for 8% of the time, Pallas kernels for 23%

profile of v10, /device:TPU:1, one launch (start us, length us, event | category | flops | bytes accessed | tf_op | source)
XLA Modules:
  0.0 115.7 jit_solution(1787590263946224839)
XLA Ops:
  1.3 1.9 %shards.1 = (bf16[12,4992]{1,0:T(8,128)(2,1)}, bf16[12,4992]{1,0:T(8,128)(2,1)}) custom-call(s32[2]{0:T(128)} %pad_add_fusion.meta_ref, s32[16]{0:T(128)} %lengths_ref.1, f32[12,3072]{1,0:T(8,128)} %input_ref.1, f32[12,256]{1,0:T(8,128)} %state_ref.1, f32[12,48]{1,0:T(8,128)} %step_ref.1, f32[12,3072]{1,0:T(8,128)} %gate_ref.1, f32[12,3072]{1,0:T(8,128)} %out_ref.1), custom_call_target="tpu_custom_call" | custom-call | tf_op jit(solution)/shard_map/shards/pallas_call | solution.py:227
  4.7 2.4 %dynamic-slice_bitcast_fusion = bf16[384,1536]{1,0:T(8,128)(2,1)} fusion(bf16[16,384,1536]{2,1,0:T(8,128)(2,1)} %param.12, s32[]{:T(128)S(6)} %select_n.451), kind=kLoop, calls=%fused_computation.7 | loop fusion | bytes 2359300 | tf_op jit(solution)/shard_map/jit(dynamic_index_in_dim)/squeeze | solution.py:517
  7.1 2.6 %collective-permute-start.1 = (bf16[8,4992]{1,0:T(8,128)(2,1)S(1)}, bf16[8,4992]{1,0:T(8,128)(2,1)S(1)}, u32[]{:S(2)}, u32[]{:S(2)}) collective-permute-start(bf16[8,4992]{1,0:T(8,128)(2,1)S(1)} %get-tuple-element.67), channel_id=1, source_target_pairs={{0,4},{1,5},{2,6},{3,7},{4,0},{5,1},{6,2},{7,3},{8,12},{9,13},{10,... | collective-permute-start | bytes 239624 | tf_op jit(solution)/shard_map/ppermute | solution.py:440
  9.8 3.8 %collective-permute-start.7 = (bf16[8,4992]{1,0:T(8,128)(2,1)S(1)}, bf16[8,4992]{1,0:T(8,128)(2,1)S(1)}, u32[]{:S(2)}, u32[]{:S(2)}) collective-permute-start(bf16[8,4992]{1,0:T(8,128)(2,1)S(1)} %get-tuple-element.68), channel_id=1, source_target_pairs={{0,32},{1,33},{2,34},{3,35},{4,36},{5,37},{6,38},{7,39},{8,40},{9,... | collective-permute-start | bytes 239624 | tf_op jit(solution)/shard_map/ppermute | solution.py:440
  13.5 2.7 %collective-permute-start.12 = (bf16[8,4992]{1,0:T(8,128)(2,1)S(1)}, bf16[8,4992]{1,0:T(8,128)(2,1)S(1)}, u32[]{:S(2)}, u32[]{:S(2)}) collective-permute-start(bf16[8,4992]{1,0:T(8,128)(2,1)S(1)} %get-tuple-element.66), channel_id=1, source_target_pairs={{0,1},{1,0},{2,3},{3,2},{4,5},{5,4},{6,7},{7,6},{8,9},{9,8},{10,11... | collective-permute-start | bytes 239624 | tf_op jit(solution)/shard_map/ppermute | solution.py:440
  24.4 2.7 %collective-permute-done.3 = bf16[32,4992]{1,0:T(8,128)(2,1)S(1)} collective-permute-done((bf16[32,4992]{1,0:T(8,128)(2,1)S(1)}, bf16[32,4992]{1,0:T(8,128)(2,1)S(1)}, u32[]{:S(2)}, u32[]{:S(2)}) %collective-permute-start.3) | collective-permute-done | bytes 319520 | tf_op jit(solution)/shard_map/ppermute | solution.py:440
  27.2 2.1 %collective-permute-done.9 = bf16[32,4992]{1,0:T(8,128)(2,1)S(1)} collective-permute-done((bf16[32,4992]{1,0:T(8,128)(2,1)S(1)}, bf16[32,4992]{1,0:T(8,128)(2,1)S(1)}, u32[]{:S(2)}, u32[]{:S(2)}) %collective-permute-start.9) | collective-permute-done | bytes 319520 | tf_op jit(solution)/shard_map/ppermute | solution.py:440
  31.4 5.4 %collective-permute-done.4.moved_ref = bf16[64,4992]{1,0:T(8,128)(2,1)S(1)} collective-permute-done((bf16[64,4992]{1,0:T(8,128)(2,1)S(1)}, bf16[64,4992]{1,0:T(8,128)(2,1)S(1)}, u32[]{:S(2)}, u32[]{:S(2)}) %collective-permute-start.4) | collective-permute-done | bytes 639008 | tf_op jit(solution)/shard_map/ppermute | solution.py:440
  36.9 2.1 %collective-permute-start.5 = (bf16[128,4992]{1,0:T(8,128)(2,1)S(1)}, bf16[128,4992]{1,0:T(8,128)(2,1)S(1)}, u32[]{:S(2)}, u32[]{:S(2)}) collective-permute-start(bf16[128,4992]{1,0:T(8,128)(2,1)S(1)} %join.9.held_ref), channel_id=1, source_target_pairs={{0,32},{1,33},{2,34},{3,35},{4,36},{5,37},{6,38},{7,39},{8,40},{9,... | collective-permute-start | bytes 3833864 | tf_op jit(solution)/shard_map/ppermute | solution.py:440
  43.0 5.8 %fusion.2.tokens_ref = bf16[768,1536]{1,0:T(8,128)(2,1)S(1)} fusion(s32[1536]{0:T(1024)S(1)} %select_subtract_fusion, bf16[384,1536]{1,0:T(8,128)(2,1)} %collective-permute-done.6, bf16[384,1536]{1,0:T(8,128)(2,1)} %dynamic-slice_bitcast_fusion), kind=kOutput, calls=%fused_computation.3 | convolution fusion | flops 3632136192 | bytes 4724736 | tf_op jit(solution)/shard_map/dot_general | solution.py:530
  48.8 6.6 %collective-permute-done.5.moved_ref = bf16[128,4992]{1,0:T(8,128)(2,1)S(1)} collective-permute-done((bf16[128,4992]{1,0:T(8,128)(2,1)S(1)}, bf16[128,4992]{1,0:T(8,128)(2,1)S(1)}, u32[]{:S(2)}, u32[]{:S(2)}) %collective-permute-start.5) | collective-permute-done | bytes 1277984 | tf_op jit(solution)/shard_map/ppermute | solution.py:440
  55.5 2.8 %collective-permute-start.17 = (bf16[256,1920]{1,0:T(8,128)(2,1)S(1)}, bf16[256,1920]{1,0:T(8,128)(2,1)S(1)}, u32[]{:S(2)}, u32[]{:S(2)}) collective-permute-start(bf16[256,1920]{1,0:T(8,128)(2,1)S(1)} %join.14.refs_0_), channel_id=1, source_target_pairs={{0,1},{1,0},{2,3},{3,2},{4,5},{5,4},{6,7},{7,6},{8,9},{9,8},{10,11... | collective-permute-start | bytes 2949128 | tf_op jit(solution)/shard_map/ppermute | solution.py:440
  59.2 2.3 %collective-permute-start.18 = (bf16[256,1920]{1,0:T(8,128)(2,1)S(1)}, bf16[256,1920]{1,0:T(8,128)(2,1)S(1)}, u32[]{:S(2)}, u32[]{:S(2)}) collective-permute-start(bf16[256,1920]{1,0:T(8,128)(2,1)S(1)} %join.15.refs_1_), channel_id=1, source_target_pairs={{0,32},{1,33},{2,34},{3,35},{4,36},{5,37},{6,38},{7,39},{8,40},{9,... | collective-permute-start | bytes 2949128 | tf_op jit(solution)/shard_map/ppermute | solution.py:440
  61.6 3.2 %project.2.refs_0_ = f32[768,1920]{1,0:T(8,128)S(1)} custom-call(bf16[768,1536]{1,0:T(8,128)(2,1)S(1)} %fusion.2.tokens_ref, bf16[256,1920]{1,0:T(8,128)(2,1)S(1)} %join.14.refs_0_, bf16[256,1920]{1,0:T(8,128)(2,1)S(1)} %join.15.refs_1_, bf16[256,1920]{1,0:T(8,128)(2,1)S(1)} %join.11.refs_2_), custom_call_target="tpu_custom_call" | custom-call | flops 2264924160 | bytes 10485760 | tf_op jit(solution)/shard_map/project/pallas_call | solution.py:286
  64.9 2.1 %collective-permute-start.21 = (bf16[256,3072]{1,0:T(8,128)(2,1)S(1)}, bf16[256,3072]{1,0:T(8,128)(2,1)S(1)}, u32[]{:S(2)}, u32[]{:S(2)}) collective-permute-start(bf16[256,3072]{1,0:T(8,128)(2,1)S(1)} %join.16.refs_0_), channel_id=1, source_target_pairs={{0,1},{1,0},{2,3},{3,2},{4,5},{5,4},{6,7},{7,6},{8,9},{9,8},{10,11... | collective-permute-start | bytes 4718600 | tf_op jit(solution)/shard_map/ppermute | solution.py:440
  68.2 5.8 %collective-permute-done.17.refs_1_ = bf16[256,1920]{1,0:T(8,128)(2,1)S(1)} collective-permute-done((bf16[256,1920]{1,0:T(8,128)(2,1)S(1)}, bf16[256,1920]{1,0:T(8,128)(2,1)S(1)}, u32[]{:S(2)}, u32[]{:S(2)}) %collective-permute-start.17) | collective-permute-done | bytes 983072 | tf_op jit(solution)/shard_map/ppermute | solution.py:440
  74.0 2.0 %collective-permute-start.23 = (bf16[256,3072]{1,0:T(8,128)(2,1)S(1)}, bf16[256,3072]{1,0:T(8,128)(2,1)S(1)}, u32[]{:S(2)}, u32[]{:S(2)}) collective-permute-start(bf16[256,3072]{1,0:T(8,128)(2,1)S(1)} %join.13.refs_4_), channel_id=1, source_target_pairs={{0,12},{1,13},{2,14},{3,15},{4,8},{5,9},{6,10},{7,11},{8,4},{9,5},... | collective-permute-start | bytes 4718600 | tf_op jit(solution)/shard_map/ppermute | solution.py:440
  76.1 3.2 %project.3.projected_ref = bf16[768,1920]{1,0:T(8,128)(2,1)S(1)} custom-call(bf16[768,1536]{1,0:T(8,128)(2,1)S(1)} %fusion.2.tokens_ref, f32[768,1920]{1,0:T(8,128)S(1)} %project.2.refs_0_, bf16[256,1920]{1,0:T(8,128)(2,1)S(1)} %collective-permute-done.17.refs_1_, bf16[256,1920]{1,0:T(8,128)(2,1)S(1)} %collective-permute-done.18.refs_2_, ...), custom_call_target="tpu_custom_call" | custom-call | flops 2264924160 | bytes 10485760 | tf_op jit(solution)/shard_map/project/pallas_call | solution.py:286
  79.3 6.2 %scan.2 = (f32[384,1536]{1,0:T(8,128)S(1)}, f32[1536,128]{1,0:T(8,128)S(1)}) custom-call(s32[2]{0:T(128)S(1)} %copy-done.2, bf16[12,4992]{1,0:T(8,128)(2,1)S(1)} %collective-permute-done.shard_ref, bf16[768,1920]{1,0:T(8,128)(2,1)S(1)} %project.3.projected_ref, f32[4,3328]{1,0:T(4,128)S(1)} %copy-done.3, f32[1,48]{1,0:T(1,128)S(1)} %bitcast.11, ...), custom_call_target="tpu_custom_call" | custom-call | flops 754974720 | bytes 5242880 | tf_op jit(solution)/shard_map/scan/pallas_call | solution.py:177
  85.5 8.1 %collective-permute-start.20 = (f32[1536,128]{1,0:T(8,128)S(1)}, f32[1536,128]{1,0:T(8,128)S(1)}, u32[]{:S(2)}, u32[]{:S(2)}) collective-permute-start(f32[1536,128]{1,0:T(8,128)S(1)} %get-tuple-element.48), channel_id=1, source_target_pairs={{0,16},{1,17},{2,18},{3,19},{4,20},{5,21},{6,22},{7,23},{8,24},{9,... | collective-permute-start | bytes 2359304 | tf_op jit(solution)/shard_map/ppermute | solution.py:440
  93.7 6.2 %scan.3 = (f32[384,1536]{1,0:T(8,128)S(1)}, f32[1536,128]{1,0:T(8,128)S(1)}) custom-call(s32[2]{0:T(128)S(1)} %copy-done.2, bf16[12,4992]{1,0:T(8,128)(2,1)S(1)} %copy-done, bf16[768,1920]{1,0:T(8,128)(2,1)S(1)} %project.3.projected_ref, f32[4,3328]{1,0:T(4,128)S(1)} %copy-done.3, f32[1,48]{1,0:T(1,128)S(1)} %bitcast.12, f32[1,48]{1,0:T(1,128)S(1)} %bitcast.14, ...), custom_call_target="tpu_custom_call" | custom-call | flops 754974720 | bytes 5242880 | tf_op jit(solution)/shard_map/scan/pallas_call | solution.py:177
  99.9 5.1 %out_share.3 = (f32[1536,384]{1,0:T(8,128)S(1)}, f32[384,128]{1,0:T(8,128)S(1)}) custom-call(s32[2]{0:T(128)S(1)} %copy-done.2, s32[192]{0:T(256)S(1)} %multiply_add_fusion.places_ref, bf16[768,1536]{1,0:T(8,128)(2,1)S(1)} %fusion.2.tokens_ref, f32[384,1536]{1,0:T(8,128)S(1)} %get-tuple-element.56.scanned_ref, f32[1,3072]{1,0:T(1,128)S(1)} %bitcast.9, ...), custom_call_target="tpu_custom_call" | custom-call | flops 3623878656 | bytes 16777216 | tf_op jit(solution)/shard_map/out_share/pallas_call | solution.py:339
  106.7 5.1 %out_share.2 = (f32[1536,384]{1,0:T(8,128)S(1)}, f32[384,128]{1,0:T(8,128)S(1)}) custom-call(s32[2]{0:T(128)S(1)} %copy-done.2, s32[192]{0:T(256)S(1)} %multiply_add_fusion.places_ref, bf16[768,1536]{1,0:T(8,128)(2,1)S(1)} %fusion.2.tokens_ref, f32[384,1536]{1,0:T(8,128)S(1)} %get-tuple-element.49.scanned_ref, f32[1,3072]{1,0:T(1,128)S(1)} %bitcast.10, ...), custom_call_target="tpu_custom_call" | custom-call | flops 3623878656 | bytes 16777216 | tf_op jit(solution)/shard_map/out_share/pallas_call | solution.py:339
  111.8 3.7 %mix.1 = (bf16[384,1536]{1,0:T(8,128)(2,1)}, f32[3072,128]{1,0:T(8,128)}) custom-call(s32[2]{0:T(128)S(1)} %copy-done.2, bf16[12,4992]{1,0:T(8,128)(2,1)S(1)} %copy-done, f32[1536,384]{1,0:T(8,128)S(1)} %get-tuple-element.55.mine_ref, f32[1536,384]{1,0:T(8,128)S(1)} %collective-permute-done.24.other_ref, f32[384,128]{1,0:T(8,128)S(1)} %get-tuple-element.58.sq_mine, ...), custom_call_target="tpu_custom_call" | custom-call | flops 452984832 | bytes 8388608 | tf_op jit(solution)/shard_map/mix/pallas_call | solution.py:403
  (77 shorter events, 20.6 us)
Async XLA Ops:
  7.1 9.1 %collective-permute-start.1 = (bf16[8,4992]{1,0:T(8,128)(2,1)S(1)}, bf16[8,4992]{1,0:T(8,128)(2,1)S(1)}, u32[]{:S(2)}, u32[]{:S(2)}) collective-permute-start(bf16[8,4992]{1,0:T(8,128)(2,1)S(1)} %get-tuple-element.67), channel_id=1, source_target_pairs={{0,4},{1,5},{2,6},{3,7},{4,0},{5,1},{6,2},{7,3},{8,12},{9,13},{10,... | collective-permute-start | bytes 239624 | tf_op jit(solution)/shard_map/ppermute | solution.py:440
  9.8 33.3 %collective-permute-start.6 = (bf16[384,1536]{1,0:T(8,128)(2,1)}, bf16[384,1536]{1,0:T(8,128)(2,1)}, u32[]{:S(2)}, u32[]{:S(2)}) collective-permute-start(bf16[384,1536]{1,0:T(8,128)(2,1)} %dynamic-slice_bitcast_fusion), channel_id=1, source_target_pairs={{0,16},{1,17},{2,18},{3,19},{4,20},{5,21},{6,22},{7,23},{8,24},{9,... | collective-permute-start | bytes 3538952 | tf_op jit(solution)/shard_map/ppermute | solution.py:440
  9.8 6.6 %collective-permute-start.7 = (bf16[8,4992]{1,0:T(8,128)(2,1)S(1)}, bf16[8,4992]{1,0:T(8,128)(2,1)S(1)}, u32[]{:S(2)}, u32[]{:S(2)}) collective-permute-start(bf16[8,4992]{1,0:T(8,128)(2,1)S(1)} %get-tuple-element.68), channel_id=1, source_target_pairs={{0,32},{1,33},{2,34},{3,35},{4,36},{5,37},{6,38},{7,39},{8,40},{9,... | collective-permute-start | bytes 239624 | tf_op jit(solution)/shard_map/ppermute | solution.py:440
  13.5 4.8 %collective-permute-start.12 = (bf16[8,4992]{1,0:T(8,128)(2,1)S(1)}, bf16[8,4992]{1,0:T(8,128)(2,1)S(1)}, u32[]{:S(2)}, u32[]{:S(2)}) collective-permute-start(bf16[8,4992]{1,0:T(8,128)(2,1)S(1)} %get-tuple-element.66), channel_id=1, source_target_pairs={{0,1},{1,0},{2,3},{3,2},{4,5},{5,4},{6,7},{7,6},{8,9},{9,8},{10,11... | collective-permute-start | bytes 239624 | tf_op jit(solution)/shard_map/ppermute | solution.py:440
  16.4 5.4 %collective-permute-start.8 = (bf16[16,4992]{1,0:T(8,128)(2,1)S(1)}, bf16[16,4992]{1,0:T(8,128)(2,1)S(1)}, u32[]{:S(2)}, u32[]{:S(2)}) collective-permute-start(bf16[16,4992]{1,0:T(8,128)(2,1)S(1)} %pad_maximum_fusion.7), channel_id=1, source_target_pairs={{0,1},{1,0},{2,3},{3,2},{4,5},{5,4},{6,7},{7,6},{8,9},{9,8},{10,11... | collective-permute-start | bytes 479240 | tf_op jit(solution)/shard_map/ppermute | solution.py:440
  18.4 5.4 %collective-permute-start.13 = (bf16[16,4992]{1,0:T(8,128)(2,1)S(1)}, bf16[16,4992]{1,0:T(8,128)(2,1)S(1)}, u32[]{:S(2)}, u32[]{:S(2)}) collective-permute-start(bf16[16,4992]{1,0:T(8,128)(2,1)S(1)} %pad_maximum_fusion.8), channel_id=1, source_target_pairs={{0,4},{1,5},{2,6},{3,7},{4,0},{5,1},{6,2},{7,3},{8,12},{9,13},{10,... | collective-permute-start | bytes 479240 | tf_op jit(solution)/shard_map/ppermute | solution.py:440
  20.8 6.2 %collective-permute-start.3 = (bf16[32,4992]{1,0:T(8,128)(2,1)S(1)}, bf16[32,4992]{1,0:T(8,128)(2,1)S(1)}, u32[]{:S(2)}, u32[]{:S(2)}) collective-permute-start(bf16[32,4992]{1,0:T(8,128)(2,1)S(1)} %pad_maximum_fusion.3), channel_id=1, source_target_pairs={{0,3},{1,2},{2,1},{3,0},{4,7},{5,6},{6,5},{7,4},{8,11},{9,10},{10,... | collective-permute-start | bytes 958472 | tf_op jit(solution)/shard_map/ppermute | solution.py:440
  21.9 7.4 %collective-permute-start.9 = (bf16[32,4992]{1,0:T(8,128)(2,1)S(1)}, bf16[32,4992]{1,0:T(8,128)(2,1)S(1)}, u32[]{:S(2)}, u32[]{:S(2)}) collective-permute-start(bf16[32,4992]{1,0:T(8,128)(2,1)S(1)} %pad_maximum_fusion.4), channel_id=1, source_target_pairs={{0,4},{1,5},{2,6},{3,7},{4,0},{5,1},{6,2},{7,3},{8,12},{9,13},{10,... | collective-permute-start | bytes 958472 | tf_op jit(solution)/shard_map/ppermute | solution.py:440
  23.8 6.7 %collective-permute-start.14 = (bf16[32,4992]{1,0:T(8,128)(2,1)S(1)}, bf16[32,4992]{1,0:T(8,128)(2,1)S(1)}, u32[]{:S(2)}, u32[]{:S(2)}) collective-permute-start(bf16[32,4992]{1,0:T(8,128)(2,1)S(1)} %pad_maximum_fusion.5), channel_id=1, source_target_pairs={{0,96},{1,97},{2,98},{3,99},{4,100},{5,101},{6,102},{7,103},{8,104... | collective-permute-start | bytes 958472 | tf_op jit(solution)/shard_map/ppermute | solution.py:440
  27.1 9.7 %collective-permute-start.4 = (bf16[64,4992]{1,0:T(8,128)(2,1)S(1)}, bf16[64,4992]{1,0:T(8,128)(2,1)S(1)}, u32[]{:S(2)}, u32[]{:S(2)}) collective-permute-start(bf16[64,4992]{1,0:T(8,128)(2,1)S(1)} %pad_maximum_fusion.held_ref), channel_id=1, source_target_pairs={{0,12},{1,13},{2,14},{3,15},{4,8},{5,9},{6,10},{7,11},{8,4},{9,5},... | collective-permute-start | bytes 1916936 | tf_op jit(solution)/shard_map/ppermute | solution.py:440
  29.3 9.8 %collective-permute-start.10 = (bf16[64,4992]{1,0:T(8,128)(2,1)S(1)}, bf16[64,4992]{1,0:T(8,128)(2,1)}, u32[]{:S(2)}, u32[]{:S(2)}) collective-permute-start(bf16[64,4992]{1,0:T(8,128)(2,1)S(1)} %pad_maximum_fusion.1.held_ref), channel_id=1, source_target_pairs={{0,96},{1,97},{2,98},{3,99},{4,100},{5,101},{6,102},{7,103},{8,104... | collective-permute-start | bytes 1916936 | tf_op jit(solution)/shard_map/ppermute | solution.py:440
  31.4 9.9 %collective-permute-start.15 = (bf16[64,4992]{1,0:T(8,128)(2,1)}, bf16[64,4992]{1,0:T(8,128)(2,1)}, u32[]{:S(2)}, u32[]{:S(2)}) collective-permute-start(bf16[64,4992]{1,0:T(8,128)(2,1)} %pad_maximum_fusion.2.held_ref), channel_id=1, source_target_pairs={{0,3},{1,2},{2,1},{3,0},{4,7},{5,6},{6,5},{7,4},{8,11},{9,10},{10,... | collective-permute-start | bytes 1916936 | tf_op jit(solution)/shard_map/ppermute | solution.py:440
  36.9 18.5 %collective-permute-start.5 = (bf16[128,4992]{1,0:T(8,128)(2,1)S(1)}, bf16[128,4992]{1,0:T(8,128)(2,1)S(1)}, u32[]{:S(2)}, u32[]{:S(2)}) collective-permute-start(bf16[128,4992]{1,0:T(8,128)(2,1)S(1)} %join.9.held_ref), channel_id=1, source_target_pairs={{0,32},{1,33},{2,34},{3,35},{4,36},{5,37},{6,38},{7,39},{8,40},{9,... | collective-permute-start | bytes 3833864 | tf_op jit(solution)/shard_map/ppermute | solution.py:440
  40.3 18.0 %collective-permute-start.11 = (bf16[128,4992]{1,0:T(8,128)(2,1)S(1)}, bf16[128,4992]{1,0:T(8,128)(2,1)S(1)}, u32[]{:S(2)}, u32[]{:S(2)}) collective-permute-start(bf16[128,4992]{1,0:T(8,128)(2,1)S(1)} %join.10.held_ref), channel_id=1, source_target_pairs={{0,3},{1,2},{2,1},{3,0},{4,7},{5,6},{6,5},{7,4},{8,11},{9,10},{10,... | collective-permute-start | bytes 3833864 | tf_op jit(solution)/shard_map/ppermute | solution.py:440
  42.7 16.5 %collective-permute-start.16 = (bf16[128,4992]{1,0:T(8,128)(2,1)S(1)}, bf16[128,4992]{1,0:T(8,128)(2,1)S(1)}, u32[]{:S(2)}, u32[]{:S(2)}) collective-permute-start(bf16[128,4992]{1,0:T(8,128)(2,1)S(1)} %join.12.held_ref), channel_id=1, source_target_pairs={{0,12},{1,13},{2,14},{3,15},{4,8},{5,9},{6,10},{7,11},{8,4},{9,5},... | collective-permute-start | bytes 3833864 | tf_op jit(solution)/shard_map/ppermute | solution.py:440
  55.5 18.6 %collective-permute-start.17 = (bf16[256,1920]{1,0:T(8,128)(2,1)S(1)}, bf16[256,1920]{1,0:T(8,128)(2,1)S(1)}, u32[]{:S(2)}, u32[]{:S(2)}) collective-permute-start(bf16[256,1920]{1,0:T(8,128)(2,1)S(1)} %join.14.refs_0_), channel_id=1, source_target_pairs={{0,1},{1,0},{2,3},{3,2},{4,5},{5,4},{6,7},{7,6},{8,9},{9,8},{10,11... | collective-permute-start | bytes 2949128 | tf_op jit(solution)/shard_map/ppermute | solution.py:440
  59.2 16.9 %collective-permute-start.18 = (bf16[256,1920]{1,0:T(8,128)(2,1)S(1)}, bf16[256,1920]{1,0:T(8,128)(2,1)S(1)}, u32[]{:S(2)}, u32[]{:S(2)}) collective-permute-start(bf16[256,1920]{1,0:T(8,128)(2,1)S(1)} %join.15.refs_1_), channel_id=1, source_target_pairs={{0,32},{1,33},{2,34},{3,35},{4,36},{5,37},{6,38},{7,39},{8,40},{9,... | collective-permute-start | bytes 2949128 | tf_op jit(solution)/shard_map/ppermute | solution.py:440
  61.5 14.6 %collective-permute-start.19 = (bf16[256,1920]{1,0:T(8,128)(2,1)S(1)}, bf16[256,1920]{1,0:T(8,128)(2,1)S(1)}, u32[]{:S(2)}, u32[]{:S(2)}) collective-permute-start(bf16[256,1920]{1,0:T(8,128)(2,1)S(1)} %join.11.refs_2_), channel_id=1, source_target_pairs={{0,12},{1,13},{2,14},{3,15},{4,8},{5,9},{6,10},{7,11},{8,4},{9,5},... | collective-permute-start | bytes 2949128 | tf_op jit(solution)/shard_map/ppermute | solution.py:440
  64.9 34.9 %collective-permute-start.21 = (bf16[256,3072]{1,0:T(8,128)(2,1)S(1)}, bf16[256,3072]{1,0:T(8,128)(2,1)S(1)}, u32[]{:S(2)}, u32[]{:S(2)}) collective-permute-start(bf16[256,3072]{1,0:T(8,128)(2,1)S(1)} %join.16.refs_0_), channel_id=1, source_target_pairs={{0,1},{1,0},{2,3},{3,2},{4,5},{5,4},{6,7},{7,6},{8,9},{9,8},{10,11... | collective-permute-start | bytes 4718600 | tf_op jit(solution)/shard_map/ppermute | solution.py:440
  67.2 32.7 %collective-permute-start.22 = (bf16[256,3072]{1,0:T(8,128)(2,1)S(1)}, bf16[256,3072]{1,0:T(8,128)(2,1)S(1)}, u32[]{:S(2)}, u32[]{:S(2)}) collective-permute-start(bf16[256,3072]{1,0:T(8,128)(2,1)S(1)} %join.17.refs_2_), channel_id=1, source_target_pairs={{0,32},{1,33},{2,34},{3,35},{4,36},{5,37},{6,38},{7,39},{8,40},{9,... | collective-permute-start | bytes 4718600 | tf_op jit(solution)/shard_map/ppermute | solution.py:440
  74.0 25.8 %collective-permute-start.23 = (bf16[256,3072]{1,0:T(8,128)(2,1)S(1)}, bf16[256,3072]{1,0:T(8,128)(2,1)S(1)}, u32[]{:S(2)}, u32[]{:S(2)}) collective-permute-start(bf16[256,3072]{1,0:T(8,128)(2,1)S(1)} %join.13.refs_4_), channel_id=1, source_target_pairs={{0,12},{1,13},{2,14},{3,15},{4,8},{5,9},{6,10},{7,11},{8,4},{9,5},... | collective-permute-start | bytes 4718600 | tf_op jit(solution)/shard_map/ppermute | solution.py:440
  85.5 14.3 %collective-permute-start.20 = (f32[1536,128]{1,0:T(8,128)S(1)}, f32[1536,128]{1,0:T(8,128)S(1)}, u32[]{:S(2)}, u32[]{:S(2)}) collective-permute-start(f32[1536,128]{1,0:T(8,128)S(1)} %get-tuple-element.48), channel_id=1, source_target_pairs={{0,16},{1,17},{2,18},{3,19},{4,20},{5,21},{6,22},{7,23},{8,24},{9,... | collective-permute-start | bytes 2359304 | tf_op jit(solution)/shard_map/ppermute | solution.py:440
  105.0 6.8 %collective-permute-start.24 = (f32[1536,384]{1,0:T(8,128)S(1)}, f32[1536,384]{1,0:T(8,128)S(1)}, u32[]{:S(2)}, u32[]{:S(2)}) collective-permute-start(f32[1536,384]{1,0:T(8,128)S(1)} %get-tuple-element.57), channel_id=1, source_target_pairs={{0,16},{1,17},{2,18},{3,19},{4,20},{5,21},{6,22},{7,23},{8,24},{9,... | collective-permute-start | bytes 7077896 | tf_op jit(solution)/shard_map/ppermute | solution.py:440
  106.4 5.4 %collective-permute-start.25 = (f32[384,128]{1,0:T(8,128)S(1)}, f32[384,128]{1,0:T(8,128)S(1)}, u32[]{:S(2)}, u32[]{:S(2)}) collective-permute-start(f32[384,128]{1,0:T(8,128)S(1)} %get-tuple-element.59), channel_id=1, source_target_pairs={{0,16},{1,17},{2,18},{3,19},{4,20},{5,21},{6,22},{7,23},{8,24},{9,... | collective-permute-start | bytes 589832 | tf_op jit(solution)/shard_map/ppermute | solution.py:440
  (9 other events, 87.3 us)

commit v11 on v9

--- a/solution.py
+++ b/solution.py
@@ -233,26 +233,23 @@
     )(meta, lengths, inputs, state, step, gate, out)
 
 
-def join_kernel(held_ref, moved_ref, *outs):
-    rows, start = held_ref.shape[0], 0
-    for out_ref in outs:
-        cols = slice(start, start + out_ref.shape[1])
-        out_ref[:rows] = held_ref[:, cols]
-        out_ref[rows:] = moved_ref[:, cols]
-        start += out_ref.shape[1]
-
-
-def join(held, moved, *widths):
-    rows, total = held.shape
+def join_kernel(start, held_ref, moved_ref, out_ref):
+    rows, cols = held_ref.shape[0], slice(start, start + out_ref.shape[1])
+    out_ref[:rows] = held_ref[:, cols]
+    out_ref[rows:] = moved_ref[:, cols]
+
+
+def join(held, moved, start, stop):
+    rows, width = held.shape[0], stop - start
     whole = pl.BlockSpec(memory_space=pltpu.VMEM)
     return pl.pallas_call(
-        join_kernel,
+        functools.partial(join_kernel, start),
         in_specs=[whole] * 2,
-        out_specs=[whole] * len(widths),
-        out_shape=[jax.ShapeDtypeStruct((2 * rows, width), BF) for width in widths],
+        out_specs=whole,
+        out_shape=jax.ShapeDtypeStruct((2 * rows, width), BF),
         compiler_params=pltpu.CompilerParams(vmem_limit_bytes=6 << 20),
         cost_estimate=pl.CostEstimate(
-            flops=0, transcendentals=0, bytes_accessed=8 * rows * total
+            flops=0, transcendentals=0, bytes_accessed=8 * rows * width
         ),
         name="join",
     )(held, moved)
@@ -299,8 +296,22 @@
     )(tokens, *begun, *pieces)
 
 
-def share_kernel(which, meta_ref, places_ref, tokens_ref, scanned_ref, gain_ref, *refs):
-    pieces, (share_ref, square_ref, gated_scr) = refs[:-3], refs[-3:]
+def share_kernel(which, count, meta_ref, places_ref, tokens_ref, scanned_ref, gain_ref, *refs):
+    pieces, states, (share_ref, square_ref, *rest) = refs[:count], (), refs[count:]
+    copies = []
+    if which == 0:
+        states, (share_ref, square_ref, state_out_ref, gated_scr, sems) = (
+            refs[count : count + 2],
+            refs[count + 2 :],
+        )
+        core, rows_half = meta_ref[0], states[0].shape[0]
+        for index, source in enumerate(states):
+            place = (core if index == 0 else 1 - core) * rows_half
+            place = pl.ds(pl.multiple_of(place, rows_half), rows_half)
+            copies.append(pltpu.make_async_copy(source, state_out_ref.at[place], sems.at[index]))
+            copies[-1].start()
+    else:
+        (gated_scr,) = rest
     seq, half = scanned_ref.shape
     rows = slice(which * seq, (which + 1) * seq)
     tile = half // 3
@@ -332,28 +343,34 @@
                 share_ref[pl.ds(pl.multiple_of(place, BLOCK_ROWS), BLOCK_ROWS), :] = total[
                     at : at + BLOCK_ROWS
                 ]
-
-
-def out_share(which, meta, places, tokens, scanned, gain, pieces):
+    for copy in copies:
+        copy.wait()
+
+
+def out_share(which, meta, places, tokens, scanned, gain, pieces, states=()):
     seq, half = scanned.shape
     model = tokens.shape[1]
     scalars = pl.BlockSpec(memory_space=pltpu.SMEM)
     whole = pl.BlockSpec(memory_space=pltpu.VMEM)
+    anywhere = pl.BlockSpec(memory_space=pl.ANY)
+    joined_state = [jax.ShapeDtypeStruct((2 * x.shape[0], x.shape[1]), F32) for x in states[:1]]
     return pl.pallas_call(
-        functools.partial(share_kernel, which),
-        in_specs=[scalars] * 2 + [whole] * (3 + len(pieces)),
-        out_specs=[whole] * 2,
+        functools.partial(share_kernel, which, len(pieces)),
+        in_specs=[scalars] * 2 + [whole] * (3 + len(pieces)) + [anywhere] * len(states),
+        out_specs=[whole] * 2 + [anywhere] * len(joined_state),
         out_shape=[
             jax.ShapeDtypeStruct((model, seq), F32),
             jax.ShapeDtypeStruct((seq, LANES), F32),
-        ],
-        scratch_shapes=[pltpu.VMEM((seq, half), BF)],
+        ]
+        + joined_state,
+        scratch_shapes=[pltpu.VMEM((seq, half), BF)]
+        + [pltpu.SemaphoreType.DMA((2,))] * len(joined_state),
         compiler_params=pltpu.CompilerParams(vmem_limit_bytes=16 << 20),
         cost_estimate=pl.CostEstimate(
             flops=4 * seq * half * model, transcendentals=seq * half, bytes_accessed=16 << 20
         ),
         name="out_share",
-    )(meta, places, tokens, scanned, gain, *pieces)
+    )(meta, places, tokens, scanned, gain, *pieces, *states)
 
 
 def mix_kernel(shard_ref, mine_ref, other_ref, sq_mine, sq_other, pick_ref, out_ref):
@@ -380,7 +397,6 @@
     target = rest // SHARD_ROWS * (tile // 2) + chip * SHARD_ROWS + rest % SHARD_ROWS
     pick = (target[:, None] == column[None]).astype(BF)
     whole = pl.BlockSpec(memory_space=pltpu.VMEM)
-    fixed = lambda i: (0, 0)
     return pl.pallas_call(
         mix_kernel,
         grid=(1,),
@@ -494,7 +510,7 @@
     held = [pair[8 * c : 8 * c + 8] for c in range(COLOURS)]
     for step in range(3):
         held = joined(held, moved_over(held, step))
-    held = [join(h, m, cut + 2 * half)[0] for h, m in zip(held, moved_over(held, 3))]
+    held = [join(h, m, 0, cut + 2 * half) for h, m in zip(held, moved_over(held, 3))]
     moved = moved_over(held, 4)
 
     own = lax.dynamic_index_in_dim(tokens, unit_id, 0, keepdims=False)
@@ -502,13 +518,11 @@
     pick = jnp.arange(model_dim, dtype=jnp.int32)[:, None] == row_sources(me, core, model_dim)[None]
     both = jnp.dot(both, pick.astype(BF), preferred_element_type=F32).astype(BF)
     moved[0], both, places = lax.optimization_barrier((moved[0], both, row_places(me, core)))
-    early, late = zip(*[join(h, m, cut, 2 * half) for h, m in zip(held, moved)])
-    late = list(late)
+    early = [join(h, m, 0, cut) for h, m in zip(held, moved)]
+    early[2], held = lax.optimization_barrier((early[2], held))
+    late = [join(h, m, cut, cut + 2 * half) for h, m in zip(held, moved)]
     moved = moved_over(early, 5)
-    begun = project(both, early)
-    moved[0], begun = lax.optimization_barrier((moved[0], begun))
-    for c in range(COLOURS):
-        moved[c], late[c] = lax.optimization_barrier((moved[c], late[c]))
+    late[2], begun = lax.optimization_barrier((late[2], project(both, early)))
     late = [piece for two in zip(late, moved_over(late, 5)) for piece in two]
 
     projected = project(both, moved, begun)
@@ -522,11 +536,10 @@
     shared = (meta, places, both)
     sent, square_sent = out_share(1, *shared, scanned_other, norm_gain[None], late)
     other, square_other = swap(sent), swap(square_sent)
-    mine, square = out_share(0, *shared, scanned, norm_gain[None], late)
+    mine, square, state = out_share(
+        0, *shared, scanned, norm_gain[None], late, (state, state_other)
+    )
     mixed = mix(kept, cut, mine, other, square, square_other)
-    state = jnp.concatenate(
-        [jnp.where(first_core, state, state_other), jnp.where(first_core, state_other, state)]
-    )
     return (mixed[None], state.reshape(1, head_count, head_dim, width // 2))
 
 

time: 117 us -> 123 us (1.051)
  starting transfers between devices: 30.2 us -> 42.3 us
  waiting for transfers between devices: 35 us -> 30.2 us
  Pallas kernels: 39.3 us -> 37.4 us
    ppermute x26, starting transfers between devices: 30.2 us -> 42.3 us  [hop(): lax.ppermute(value, EVERYONE, [(d, d ^ mask_of(d // CORE % 2)) for d in r...]
    ppermute x26, waiting for transfers between devices: 35 us -> 30.2 us  [hop(): lax.ppermute(value, EVERYONE, [(d, d ^ mask_of(d // CORE % 2)) for d in r...]
    pallas_call x8 -> x11, Pallas kernels: 16.4 us -> 14.5 us  [the longest x2 11.3 us: out_share(): pl.pallas_call(functools.partial(share_kernel, which, len(pieces)), in_sp...]
  transfers between devices with their start and end apart: 26 -> 26, of which waited for: 11 -> 12; matrix products, arithmetic and copies ran while one was open for 9% -> 8% of each run, Pallas kernels for 26% -> 23%
where the time goes in v11:
time: 123 us; the launch traced here: 122 us
  starting transfers between devices  42.3 us (34%)
  Pallas kernels  37.4 us (30%)
  waiting for transfers between devices  30.2 us (25%)
  matrix products  5.79 us (5%)
  other arithmetic  2.88 us (2%)
  local copies, waits for them, and re-layouts  2.4 us (2%)
    ppermute x26, starting transfers between devices, hop(): lax.ppermute(value, EVERYONE, [(d, d ^ mask_of(d // CORE % 2)) for d in r...  42.3 us
    ppermute x26, waiting for transfers between devices, hop(): lax.ppermute(value, EVERYONE, [(d, d ^ mask_of(d // CORE % 2)) for d in r...  30.2 us
    pallas_call x2, Pallas kernels, scan(): pl.pallas_call(functools.partial(scan_kernel, which), in_specs=[scalars]...  12.2 us
    pallas_call x2, Pallas kernels, out_share(): pl.pallas_call(functools.partial(share_kernel, which, len(pieces)), in_sp...  11.3 us
    pallas_call x2, Pallas kernels, project(): pl.pallas_call(functools.partial(project_kernel, first), in_specs=[whole]...  6.49 us
    dot_general x1, matrix products, body(): both = jnp.dot(both, pick.astype(BF), preferred_element_type=F32).astype(BF)  5.79 us
    pallas_call x9, Pallas kernels, join(): pl.pallas_call(functools.partial(join_kernel, start), in_specs=[whole] *...  3.13 us
  transfers between devices with their start and end apart: 26, of which 12 were waited for; matrix products, arithmetic and copies ran while one was open for 8% of the time, Pallas kernels for 23%

profile of v11, /device:TPU:1, one launch (start us, length us, event | category | flops | bytes accessed | tf_op | source)
XLA Modules:
  0.0 122.0 jit_solution(10432559902692207432)
XLA Ops:
  1.3 1.9 %shards.1 = (bf16[12,4992]{1,0:T(8,128)(2,1)}, bf16[12,4992]{1,0:T(8,128)(2,1)}) custom-call(s32[2]{0:T(128)} %pad_add_fusion.meta_ref, s32[16]{0:T(128)} %lengths_ref.1, f32[12,3072]{1,0:T(8,128)} %input_ref.1, f32[12,256]{1,0:T(8,128)} %state_ref.1, f32[12,48]{1,0:T(8,128)} %step_ref.1, f32[12,3072]{1,0:T(8,128)} %gate_ref.1, f32[12,3072]{1,0:T(8,128)} %out_ref.1), custom_call_target="tpu_custom_call" | custom-call | tf_op jit(solution)/shard_map/shards/pallas_call | solution.py:227
  3.2 1.4 %collective-permute-start = (bf16[12,4992]{1,0:T(8,128)(2,1)}, bf16[12,4992]{1,0:T(8,128)(2,1)S(1)}, u32[]{:S(2)}, u32[]{:S(2)}) collective-permute-start(bf16[12,4992]{1,0:T(8,128)(2,1)} %get-tuple-element.29), channel_id=1, source_target_pairs={{0,16},{1,17},{2,18},{3,19},{4,20},{5,21},{6,22},{7,23},{8,24},{9,... | collective-permute-start | bytes 359432 | tf_op jit(solution)/shard_map/ppermute | solution.py:429
  6.8 2.6 %collective-permute-start.1 = (bf16[8,4992]{1,0:T(8,128)(2,1)S(1)}, bf16[8,4992]{1,0:T(8,128)(2,1)S(1)}, u32[]{:S(2)}, u32[]{:S(2)}) collective-permute-start(bf16[8,4992]{1,0:T(8,128)(2,1)S(1)} %get-tuple-element.55), channel_id=1, source_target_pairs={{0,4},{1,5},{2,6},{3,7},{4,0},{5,1},{6,2},{7,3},{8,12},{9,13},{10,... | collective-permute-start | bytes 239624 | tf_op jit(solution)/shard_map/ppermute | solution.py:429
  9.5 2.4 %dynamic-slice_bitcast_fusion = bf16[384,1536]{1,0:T(8,128)(2,1)} fusion(bf16[16,384,1536]{2,1,0:T(8,128)(2,1)} %param.12, s32[]{:T(128)S(6)} %select_n.452), kind=kLoop, calls=%fused_computation.7 | loop fusion | bytes 2359300 | tf_op jit(solution)/shard_map/jit(dynamic_index_in_dim)/squeeze | solution.py:516
  11.8 3.8 %collective-permute-start.7 = (bf16[8,4992]{1,0:T(8,128)(2,1)S(1)}, bf16[8,4992]{1,0:T(8,128)(2,1)S(1)}, u32[]{:S(2)}, u32[]{:S(2)}) collective-permute-start(bf16[8,4992]{1,0:T(8,128)(2,1)S(1)} %get-tuple-element.56), channel_id=1, source_target_pairs={{0,32},{1,33},{2,34},{3,35},{4,36},{5,37},{6,38},{7,39},{8,40},{9,... | collective-permute-start | bytes 239624 | tf_op jit(solution)/shard_map/ppermute | solution.py:429
  15.6 2.7 %collective-permute-start.12 = (bf16[8,4992]{1,0:T(8,128)(2,1)S(1)}, bf16[8,4992]{1,0:T(8,128)(2,1)S(1)}, u32[]{:S(2)}, u32[]{:S(2)}) collective-permute-start(bf16[8,4992]{1,0:T(8,128)(2,1)S(1)} %get-tuple-element.54), channel_id=1, source_target_pairs={{0,1},{1,0},{2,3},{3,2},{4,5},{5,4},{6,7},{7,6},{8,9},{9,8},{10,11... | collective-permute-start | bytes 239624 | tf_op jit(solution)/shard_map/ppermute | solution.py:429
  18.5 1.8 %collective-permute-start.8 = (bf16[16,4992]{1,0:T(8,128)(2,1)S(1)}, bf16[16,4992]{1,0:T(8,128)(2,1)S(1)}, u32[]{:S(2)}, u32[]{:S(2)}) collective-permute-start(bf16[16,4992]{1,0:T(8,128)(2,1)S(1)} %pad_maximum_fusion.7), channel_id=1, source_target_pairs={{0,1},{1,0},{2,3},{3,2},{4,5},{5,4},{6,7},{7,6},{8,9},{9,8},{10,11... | collective-permute-start | bytes 479240 | tf_op jit(solution)/shard_map/ppermute | solution.py:429
  26.7 2.3 %collective-permute-done.3 = bf16[32,4992]{1,0:T(8,128)(2,1)S(1)} collective-permute-done((bf16[32,4992]{1,0:T(8,128)(2,1)S(1)}, bf16[32,4992]{1,0:T(8,128)(2,1)S(1)}, u32[]{:S(2)}, u32[]{:S(2)}) %collective-permute-start.3) | collective-permute-done | bytes 319520 | tf_op jit(solution)/shard_map/ppermute | solution.py:429
  29.2 2.1 %collective-permute-done.9 = bf16[32,4992]{1,0:T(8,128)(2,1)S(1)} collective-permute-done((bf16[32,4992]{1,0:T(8,128)(2,1)S(1)}, bf16[32,4992]{1,0:T(8,128)(2,1)S(1)}, u32[]{:S(2)}, u32[]{:S(2)}) %collective-permute-start.9) | collective-permute-done | bytes 319520 | tf_op jit(solution)/shard_map/ppermute | solution.py:429
  33.5 5.4 %collective-permute-done.4.moved_ref = bf16[64,4992]{1,0:T(8,128)(2,1)S(1)} collective-permute-done((bf16[64,4992]{1,0:T(8,128)(2,1)S(1)}, bf16[64,4992]{1,0:T(8,128)(2,1)S(1)}, u32[]{:S(2)}, u32[]{:S(2)}) %collective-permute-start.4) | collective-permute-done | bytes 639008 | tf_op jit(solution)/shard_map/ppermute | solution.py:429
  39.0 1.8 %collective-permute-start.5 = (bf16[128,4992]{1,0:T(8,128)(2,1)S(1)}, bf16[128,4992]{1,0:T(8,128)(2,1)S(1)}, u32[]{:S(2)}, u32[]{:S(2)}) collective-permute-start(bf16[128,4992]{1,0:T(8,128)(2,1)S(1)} %join.9.held_ref), channel_id=1, source_target_pairs={{0,32},{1,33},{2,34},{3,35},{4,36},{5,37},{6,38},{7,39},{8,40},{9,... | collective-permute-start | bytes 3833864 | tf_op jit(solution)/shard_map/ppermute | solution.py:429
  44.9 5.8 %fusion.2.tokens_ref = bf16[768,1536]{1,0:T(8,128)(2,1)S(1)} fusion(s32[1536]{0:T(1024)S(1)} %select_subtract_fusion, bf16[384,1536]{1,0:T(8,128)(2,1)} %collective-permute-done.6, bf16[384,1536]{1,0:T(8,128)(2,1)} %dynamic-slice_bitcast_fusion), kind=kOutput, calls=%fused_computation.3 | convolution fusion | flops 3632136192 | bytes 4724736 | tf_op jit(solution)/shard_map/dot_general | solution.py:519
  50.6 6.2 %collective-permute-done.5.moved_ref = bf16[128,4992]{1,0:T(8,128)(2,1)S(1)} collective-permute-done((bf16[128,4992]{1,0:T(8,128)(2,1)S(1)}, bf16[128,4992]{1,0:T(8,128)(2,1)S(1)}, u32[]{:S(2)}, u32[]{:S(2)}) %collective-permute-start.5) | collective-permute-done | bytes 1277984 | tf_op jit(solution)/shard_map/ppermute | solution.py:429
  57.0 6.4 %collective-permute-start.17 = (bf16[256,1920]{1,0:T(8,128)(2,1)S(1)}, bf16[256,1920]{1,0:T(8,128)(2,1)S(1)}, u32[]{:S(2)}, u32[]{:S(2)}) collective-permute-start(bf16[256,1920]{1,0:T(8,128)(2,1)S(1)} %join.14.refs_0_), channel_id=1, source_target_pairs={{0,1},{1,0},{2,3},{3,2},{4,5},{5,4},{6,7},{7,6},{8,9},{9,8},{10,11... | collective-permute-start | bytes 2949128 | tf_op jit(solution)/shard_map/ppermute | solution.py:429
  63.6 3.0 %collective-permute-start.18 = (bf16[256,1920]{1,0:T(8,128)(2,1)S(1)}, bf16[256,1920]{1,0:T(8,128)(2,1)S(1)}, u32[]{:S(2)}, u32[]{:S(2)}) collective-permute-start(bf16[256,1920]{1,0:T(8,128)(2,1)S(1)} %join.15.refs_1_), channel_id=1, source_target_pairs={{0,32},{1,33},{2,34},{3,35},{4,36},{5,37},{6,38},{7,39},{8,40},{9,... | collective-permute-start | bytes 2949128 | tf_op jit(solution)/shard_map/ppermute | solution.py:429
  66.7 3.2 %project.2.refs_0_ = f32[768,1920]{1,0:T(8,128)S(1)} custom-call(bf16[768,1536]{1,0:T(8,128)(2,1)S(1)} %fusion.2.tokens_ref, bf16[256,1920]{1,0:T(8,128)(2,1)S(1)} %join.14.refs_0_, bf16[256,1920]{1,0:T(8,128)(2,1)S(1)} %join.15.refs_1_, bf16[256,1920]{1,0:T(8,128)(2,1)S(1)} %join.11.refs_2_), custom_call_target="tpu_custom_call" | custom-call | flops 2264924160 | bytes 10485760 | tf_op jit(solution)/shard_map/project/pallas_call | solution.py:286
  71.1 9.3 %collective-permute-done.17.refs_1_ = bf16[256,1920]{1,0:T(8,128)(2,1)S(1)} collective-permute-done((bf16[256,1920]{1,0:T(8,128)(2,1)S(1)}, bf16[256,1920]{1,0:T(8,128)(2,1)S(1)}, u32[]{:S(2)}, u32[]{:S(2)}) %collective-permute-start.17) | collective-permute-done | bytes 983072 | tf_op jit(solution)/shard_map/ppermute | solution.py:429
  80.3 3.3 %project.3.projected_ref = bf16[768,1920]{1,0:T(8,128)(2,1)S(1)} custom-call(bf16[768,1536]{1,0:T(8,128)(2,1)S(1)} %fusion.2.tokens_ref, f32[768,1920]{1,0:T(8,128)S(1)} %project.2.refs_0_, bf16[256,1920]{1,0:T(8,128)(2,1)S(1)} %collective-permute-done.17.refs_1_, bf16[256,1920]{1,0:T(8,128)(2,1)S(1)} %collective-permute-done.18.refs_2_, ...), custom_call_target="tpu_custom_call" | custom-call | flops 2264924160 | bytes 10485760 | tf_op jit(solution)/shard_map/project/pallas_call | solution.py:286
  83.7 6.1 %scan.2 = (f32[384,1536]{1,0:T(8,128)S(1)}, f32[1536,128]{1,0:T(8,128)S(1)}) custom-call(s32[2]{0:T(128)S(1)} %copy-done.2, bf16[12,4992]{1,0:T(8,128)(2,1)S(1)} %collective-permute-done.shard_ref, bf16[768,1920]{1,0:T(8,128)(2,1)S(1)} %project.3.projected_ref, f32[4,3328]{1,0:T(4,128)S(1)} %copy-done.3, f32[1,48]{1,0:T(1,128)S(1)} %bitcast.11, ...), custom_call_target="tpu_custom_call" | custom-call | flops 754974720 | bytes 5242880 | tf_op jit(solution)/shard_map/scan/pallas_call | solution.py:177
  89.8 10.6 %collective-permute-start.20 = (f32[1536,128]{1,0:T(8,128)S(1)}, f32[1536,128]{1,0:T(8,128)S(1)}, u32[]{:S(2)}, u32[]{:S(2)}) collective-permute-start(f32[1536,128]{1,0:T(8,128)S(1)} %get-tuple-element.39), channel_id=1, source_target_pairs={{0,16},{1,17},{2,18},{3,19},{4,20},{5,21},{6,22},{7,23},{8,24},{9,... | collective-permute-start | bytes 2359304 | tf_op jit(solution)/shard_map/ppermute | solution.py:429
  100.4 6.1 %scan.3 = (f32[384,1536]{1,0:T(8,128)S(1)}, f32[1536,128]{1,0:T(8,128)S(1)}) custom-call(s32[2]{0:T(128)S(1)} %copy-done.2, bf16[12,4992]{1,0:T(8,128)(2,1)S(1)} %copy-done, bf16[768,1920]{1,0:T(8,128)(2,1)S(1)} %project.3.projected_ref, f32[4,3328]{1,0:T(4,128)S(1)} %copy-done.3, f32[1,48]{1,0:T(1,128)S(1)} %bitcast.12, f32[1,48]{1,0:T(1,128)S(1)} %bitcast.14, ...), custom_call_target="tpu_custom_call" | custom-call | flops 754974720 | bytes 5242880 | tf_op jit(solution)/shard_map/scan/pallas_call | solution.py:177
  106.6 5.1 %out_share.3 = (f32[1536,384]{1,0:T(8,128)S(1)}, f32[384,128]{1,0:T(8,128)S(1)}) custom-call(s32[2]{0:T(128)S(1)} %copy-done.2, s32[192]{0:T(256)S(1)} %multiply_add_fusion.places_ref, bf16[768,1536]{1,0:T(8,128)(2,1)S(1)} %fusion.2.tokens_ref, f32[384,1536]{1,0:T(8,128)S(1)} %get-tuple-element.47.scanned_ref, f32[1,3072]{1,0:T(1,128)S(1)} %bitcast.9, ...), custom_call_target="tpu_custom_call" | custom-call | flops 3623878656 | bytes 16777216 | tf_op jit(solution)/shard_map/out_share/pallas_call | solution.py:357
  113.4 6.2 %out_share.2 = (f32[1536,384]{1,0:T(8,128)S(1)}, f32[384,128]{1,0:T(8,128)S(1)}, f32[3072,128]{1,0:T(8,128)}) custom-call(s32[2]{0:T(128)S(1)} %copy-done.2, s32[192]{0:T(256)S(1)} %multiply_add_fusion.places_ref, bf16[768,1536]{1,0:T(8,128)(2,1)S(1)} %fusion.2.tokens_ref, f32[384,1536]{1,0:T(8,128)S(1)} %get-tuple-element.40.scanned_ref, ...), custom_call_target="tpu_custom_call" | custom-call | flops 3623878656 | bytes 16777216 | tf_op jit(solution)/shard_map/out_share/pallas_call | solution.py:357
  119.7 2.3 %mix.1 = bf16[384,1536]{1,0:T(8,128)(2,1)} custom-call(bf16[12,4992]{1,0:T(8,128)(2,1)S(1)} %copy-done, f32[1536,384]{1,0:T(8,128)S(1)} %get-tuple-element.46.mine_ref, f32[1536,384]{1,0:T(8,128)S(1)} %collective-permute-done.24.other_ref, f32[384,128]{1,0:T(8,128)S(1)} %get-tuple-element.49.sq_mine, f32[384,128]{1,0:T(8,128)S(1)} %collective-permute-done.25.sq_other, ...), custom_call_target="tpu_custom_call" | custom-call | flops 452984832 | bytes 8388608 | tf_op jit(solution)/shard_map/mix/pallas_call | solution.py:400
  (77 shorter events, 19.0 us)
Async XLA Ops:
  6.8 11.5 %collective-permute-start.1 = (bf16[8,4992]{1,0:T(8,128)(2,1)S(1)}, bf16[8,4992]{1,0:T(8,128)(2,1)S(1)}, u32[]{:S(2)}, u32[]{:S(2)}) collective-permute-start(bf16[8,4992]{1,0:T(8,128)(2,1)S(1)} %get-tuple-element.55), channel_id=1, source_target_pairs={{0,4},{1,5},{2,6},{3,7},{4,0},{5,1},{6,2},{7,3},{8,12},{9,13},{10,... | collective-permute-start | bytes 239624 | tf_op jit(solution)/shard_map/ppermute | solution.py:429
  11.8 33.0 %collective-permute-start.6 = (bf16[384,1536]{1,0:T(8,128)(2,1)}, bf16[384,1536]{1,0:T(8,128)(2,1)}, u32[]{:S(2)}, u32[]{:S(2)}) collective-permute-start(bf16[384,1536]{1,0:T(8,128)(2,1)} %dynamic-slice_bitcast_fusion), channel_id=1, source_target_pairs={{0,16},{1,17},{2,18},{3,19},{4,20},{5,21},{6,22},{7,23},{8,24},{9,... | collective-permute-start | bytes 3538952 | tf_op jit(solution)/shard_map/ppermute | solution.py:429
  11.8 6.6 %collective-permute-start.7 = (bf16[8,4992]{1,0:T(8,128)(2,1)S(1)}, bf16[8,4992]{1,0:T(8,128)(2,1)S(1)}, u32[]{:S(2)}, u32[]{:S(2)}) collective-permute-start(bf16[8,4992]{1,0:T(8,128)(2,1)S(1)} %get-tuple-element.56), channel_id=1, source_target_pairs={{0,32},{1,33},{2,34},{3,35},{4,36},{5,37},{6,38},{7,39},{8,40},{9,... | collective-permute-start | bytes 239624 | tf_op jit(solution)/shard_map/ppermute | solution.py:429
  15.6 4.8 %collective-permute-start.12 = (bf16[8,4992]{1,0:T(8,128)(2,1)S(1)}, bf16[8,4992]{1,0:T(8,128)(2,1)S(1)}, u32[]{:S(2)}, u32[]{:S(2)}) collective-permute-start(bf16[8,4992]{1,0:T(8,128)(2,1)S(1)} %get-tuple-element.54), channel_id=1, source_target_pairs={{0,1},{1,0},{2,3},{3,2},{4,5},{5,4},{6,7},{7,6},{8,9},{9,8},{10,11... | collective-permute-start | bytes 239624 | tf_op jit(solution)/shard_map/ppermute | solution.py:429
  18.5 5.4 %collective-permute-start.8 = (bf16[16,4992]{1,0:T(8,128)(2,1)S(1)}, bf16[16,4992]{1,0:T(8,128)(2,1)S(1)}, u32[]{:S(2)}, u32[]{:S(2)}) collective-permute-start(bf16[16,4992]{1,0:T(8,128)(2,1)S(1)} %pad_maximum_fusion.7), channel_id=1, source_target_pairs={{0,1},{1,0},{2,3},{3,2},{4,5},{5,4},{6,7},{7,6},{8,9},{9,8},{10,11... | collective-permute-start | bytes 479240 | tf_op jit(solution)/shard_map/ppermute | solution.py:429
  20.5 5.4 %collective-permute-start.13 = (bf16[16,4992]{1,0:T(8,128)(2,1)S(1)}, bf16[16,4992]{1,0:T(8,128)(2,1)S(1)}, u32[]{:S(2)}, u32[]{:S(2)}) collective-permute-start(bf16[16,4992]{1,0:T(8,128)(2,1)S(1)} %pad_maximum_fusion.8), channel_id=1, source_target_pairs={{0,4},{1,5},{2,6},{3,7},{4,0},{5,1},{6,2},{7,3},{8,12},{9,13},{10,... | collective-permute-start | bytes 479240 | tf_op jit(solution)/shard_map/ppermute | solution.py:429
  22.9 6.2 %collective-permute-start.3 = (bf16[32,4992]{1,0:T(8,128)(2,1)S(1)}, bf16[32,4992]{1,0:T(8,128)(2,1)S(1)}, u32[]{:S(2)}, u32[]{:S(2)}) collective-permute-start(bf16[32,4992]{1,0:T(8,128)(2,1)S(1)} %pad_maximum_fusion.3), channel_id=1, source_target_pairs={{0,3},{1,2},{2,1},{3,0},{4,7},{5,6},{6,5},{7,4},{8,11},{9,10},{10,... | collective-permute-start | bytes 958472 | tf_op jit(solution)/shard_map/ppermute | solution.py:429
  23.9 7.4 %collective-permute-start.9 = (bf16[32,4992]{1,0:T(8,128)(2,1)S(1)}, bf16[32,4992]{1,0:T(8,128)(2,1)S(1)}, u32[]{:S(2)}, u32[]{:S(2)}) collective-permute-start(bf16[32,4992]{1,0:T(8,128)(2,1)S(1)} %pad_maximum_fusion.4), channel_id=1, source_target_pairs={{0,4},{1,5},{2,6},{3,7},{4,0},{5,1},{6,2},{7,3},{8,12},{9,13},{10,... | collective-permute-start | bytes 958472 | tf_op jit(solution)/shard_map/ppermute | solution.py:429
  25.9 6.7 %collective-permute-start.14 = (bf16[32,4992]{1,0:T(8,128)(2,1)S(1)}, bf16[32,4992]{1,0:T(8,128)(2,1)S(1)}, u32[]{:S(2)}, u32[]{:S(2)}) collective-permute-start(bf16[32,4992]{1,0:T(8,128)(2,1)S(1)} %pad_maximum_fusion.5), channel_id=1, source_target_pairs={{0,96},{1,97},{2,98},{3,99},{4,100},{5,101},{6,102},{7,103},{8,104... | collective-permute-start | bytes 958472 | tf_op jit(solution)/shard_map/ppermute | solution.py:429
  29.2 9.7 %collective-permute-start.4 = (bf16[64,4992]{1,0:T(8,128)(2,1)S(1)}, bf16[64,4992]{1,0:T(8,128)(2,1)S(1)}, u32[]{:S(2)}, u32[]{:S(2)}) collective-permute-start(bf16[64,4992]{1,0:T(8,128)(2,1)S(1)} %pad_maximum_fusion.held_ref), channel_id=1, source_target_pairs={{0,12},{1,13},{2,14},{3,15},{4,8},{5,9},{6,10},{7,11},{8,4},{9,5},... | collective-permute-start | bytes 1916936 | tf_op jit(solution)/shard_map/ppermute | solution.py:429
  31.4 9.7 %collective-permute-start.10 = (bf16[64,4992]{1,0:T(8,128)(2,1)S(1)}, bf16[64,4992]{1,0:T(8,128)(2,1)}, u32[]{:S(2)}, u32[]{:S(2)}) collective-permute-start(bf16[64,4992]{1,0:T(8,128)(2,1)S(1)} %pad_maximum_fusion.1.held_ref), channel_id=1, source_target_pairs={{0,96},{1,97},{2,98},{3,99},{4,100},{5,101},{6,102},{7,103},{8,104... | collective-permute-start | bytes 1916936 | tf_op jit(solution)/shard_map/ppermute | solution.py:429
  33.5 9.9 %collective-permute-start.15 = (bf16[64,4992]{1,0:T(8,128)(2,1)}, bf16[64,4992]{1,0:T(8,128)(2,1)}, u32[]{:S(2)}, u32[]{:S(2)}) collective-permute-start(bf16[64,4992]{1,0:T(8,128)(2,1)} %pad_maximum_fusion.2.held_ref), channel_id=1, source_target_pairs={{0,3},{1,2},{2,1},{3,0},{4,7},{5,6},{6,5},{7,4},{8,11},{9,10},{10,... | collective-permute-start | bytes 1916936 | tf_op jit(solution)/shard_map/ppermute | solution.py:429
  39.0 17.9 %collective-permute-start.5 = (bf16[128,4992]{1,0:T(8,128)(2,1)S(1)}, bf16[128,4992]{1,0:T(8,128)(2,1)S(1)}, u32[]{:S(2)}, u32[]{:S(2)}) collective-permute-start(bf16[128,4992]{1,0:T(8,128)(2,1)S(1)} %join.9.held_ref), channel_id=1, source_target_pairs={{0,32},{1,33},{2,34},{3,35},{4,36},{5,37},{6,38},{7,39},{8,40},{9,... | collective-permute-start | bytes 3833864 | tf_op jit(solution)/shard_map/ppermute | solution.py:429
  42.3 21.1 %collective-permute-start.11 = (bf16[128,4992]{1,0:T(8,128)(2,1)S(1)}, bf16[128,4992]{1,0:T(8,128)(2,1)S(1)}, u32[]{:S(2)}, u32[]{:S(2)}) collective-permute-start(bf16[128,4992]{1,0:T(8,128)(2,1)S(1)} %join.10.held_ref), channel_id=1, source_target_pairs={{0,3},{1,2},{2,1},{3,0},{4,7},{5,6},{6,5},{7,4},{8,11},{9,10},{10,... | collective-permute-start | bytes 3833864 | tf_op jit(solution)/shard_map/ppermute | solution.py:429
  44.7 18.8 %collective-permute-start.16 = (bf16[128,4992]{1,0:T(8,128)(2,1)S(1)}, bf16[128,4992]{1,0:T(8,128)(2,1)S(1)}, u32[]{:S(2)}, u32[]{:S(2)}) collective-permute-start(bf16[128,4992]{1,0:T(8,128)(2,1)S(1)} %join.12.held_ref), channel_id=1, source_target_pairs={{0,12},{1,13},{2,14},{3,15},{4,8},{5,9},{6,10},{7,11},{8,4},{9,5},... | collective-permute-start | bytes 3833864 | tf_op jit(solution)/shard_map/ppermute | solution.py:429
  57.0 23.4 %collective-permute-start.17 = (bf16[256,1920]{1,0:T(8,128)(2,1)S(1)}, bf16[256,1920]{1,0:T(8,128)(2,1)S(1)}, u32[]{:S(2)}, u32[]{:S(2)}) collective-permute-start(bf16[256,1920]{1,0:T(8,128)(2,1)S(1)} %join.14.refs_0_), channel_id=1, source_target_pairs={{0,1},{1,0},{2,3},{3,2},{4,5},{5,4},{6,7},{7,6},{8,9},{9,8},{10,11... | collective-permute-start | bytes 2949128 | tf_op jit(solution)/shard_map/ppermute | solution.py:429
  63.6 16.8 %collective-permute-start.18 = (bf16[256,1920]{1,0:T(8,128)(2,1)S(1)}, bf16[256,1920]{1,0:T(8,128)(2,1)S(1)}, u32[]{:S(2)}, u32[]{:S(2)}) collective-permute-start(bf16[256,1920]{1,0:T(8,128)(2,1)S(1)} %join.15.refs_1_), channel_id=1, source_target_pairs={{0,32},{1,33},{2,34},{3,35},{4,36},{5,37},{6,38},{7,39},{8,40},{9,... | collective-permute-start | bytes 2949128 | tf_op jit(solution)/shard_map/ppermute | solution.py:429
  66.6 13.7 %collective-permute-start.19 = (bf16[256,1920]{1,0:T(8,128)(2,1)S(1)}, bf16[256,1920]{1,0:T(8,128)(2,1)S(1)}, u32[]{:S(2)}, u32[]{:S(2)}) collective-permute-start(bf16[256,1920]{1,0:T(8,128)(2,1)S(1)} %join.11.refs_2_), channel_id=1, source_target_pairs={{0,12},{1,13},{2,14},{3,15},{4,8},{5,9},{6,10},{7,11},{8,4},{9,5},... | collective-permute-start | bytes 2949128 | tf_op jit(solution)/shard_map/ppermute | solution.py:429
  70.1 36.5 %collective-permute-start.21 = (bf16[256,3072]{1,0:T(8,128)(2,1)S(1)}, bf16[256,3072]{1,0:T(8,128)(2,1)S(1)}, u32[]{:S(2)}, u32[]{:S(2)}) collective-permute-start(bf16[256,3072]{1,0:T(8,128)(2,1)S(1)} %join.16.refs_0_), channel_id=1, source_target_pairs={{0,1},{1,0},{2,3},{3,2},{4,5},{5,4},{6,7},{7,6},{8,9},{9,8},{10,11... | collective-permute-start | bytes 4718600 | tf_op jit(solution)/shard_map/ppermute | solution.py:429
  70.3 36.3 %collective-permute-start.22 = (bf16[256,3072]{1,0:T(8,128)(2,1)S(1)}, bf16[256,3072]{1,0:T(8,128)(2,1)S(1)}, u32[]{:S(2)}, u32[]{:S(2)}) collective-permute-start(bf16[256,3072]{1,0:T(8,128)(2,1)S(1)} %join.17.refs_2_), channel_id=1, source_target_pairs={{0,32},{1,33},{2,34},{3,35},{4,36},{5,37},{6,38},{7,39},{8,40},{9,... | collective-permute-start | bytes 4718600 | tf_op jit(solution)/shard_map/ppermute | solution.py:429
  80.3 26.3 %collective-permute-start.23 = (bf16[256,3072]{1,0:T(8,128)(2,1)S(1)}, bf16[256,3072]{1,0:T(8,128)(2,1)S(1)}, u32[]{:S(2)}, u32[]{:S(2)}) collective-permute-start(bf16[256,3072]{1,0:T(8,128)(2,1)S(1)} %join.13.refs_4_), channel_id=1, source_target_pairs={{0,12},{1,13},{2,14},{3,15},{4,8},{5,9},{6,10},{7,11},{8,4},{9,5},... | collective-permute-start | bytes 4718600 | tf_op jit(solution)/shard_map/ppermute | solution.py:429
  89.8 16.8 %collective-permute-start.20 = (f32[1536,128]{1,0:T(8,128)S(1)}, f32[1536,128]{1,0:T(8,128)S(1)}, u32[]{:S(2)}, u32[]{:S(2)}) collective-permute-start(f32[1536,128]{1,0:T(8,128)S(1)} %get-tuple-element.39), channel_id=1, source_target_pairs={{0,16},{1,17},{2,18},{3,19},{4,20},{5,21},{6,22},{7,23},{8,24},{9,... | collective-permute-start | bytes 2359304 | tf_op jit(solution)/shard_map/ppermute | solution.py:429
  111.7 7.9 %collective-permute-start.24 = (f32[1536,384]{1,0:T(8,128)S(1)}, f32[1536,384]{1,0:T(8,128)S(1)}, u32[]{:S(2)}, u32[]{:S(2)}) collective-permute-start(f32[1536,384]{1,0:T(8,128)S(1)} %get-tuple-element.48), channel_id=1, source_target_pairs={{0,16},{1,17},{2,18},{3,19},{4,20},{5,21},{6,22},{7,23},{8,24},{9,... | collective-permute-start | bytes 7077896 | tf_op jit(solution)/shard_map/ppermute | solution.py:429
  113.1 6.5 %collective-permute-start.25 = (f32[384,128]{1,0:T(8,128)S(1)}, f32[384,128]{1,0:T(8,128)S(1)}, u32[]{:S(2)}, u32[]{:S(2)}) collective-permute-start(f32[384,128]{1,0:T(8,128)S(1)} %get-tuple-element.50), channel_id=1, source_target_pairs={{0,16},{1,17},{2,18},{3,19},{4,20},{5,21},{6,22},{7,23},{8,24},{9,... | collective-permute-start | bytes 589832 | tf_op jit(solution)/shard_map/ppermute | solution.py:429
  (9 other events, 107.5 us)

commit v12 on v9

--- a/solution.py
+++ b/solution.py
@@ -504,11 +504,12 @@
     moved[0], both, places = lax.optimization_barrier((moved[0], both, row_places(me, core)))
     early, late = zip(*[join(h, m, cut, 2 * half) for h, m in zip(held, moved)])
     late = list(late)
+    early = list(early)
+    early[1], late[0], late[2] = lax.optimization_barrier((early[1], late[0], late[2]))
     moved = moved_over(early, 5)
     begun = project(both, early)
     moved[0], begun = lax.optimization_barrier((moved[0], begun))
-    for c in range(COLOURS):
-        moved[c], late[c] = lax.optimization_barrier((moved[c], late[c]))
+    moved[2], late[1] = lax.optimization_barrier((moved[2], late[1]))
     late = [piece for two in zip(late, moved_over(late, 5)) for piece in two]
 
     projected = project(both, moved, begun)

time: 117 us -> 117 us (level)
  starting transfers between devices: 30.2 us -> 28.4 us
    ppermute x26, starting transfers between devices: 30.2 us -> 28.4 us  [hop(): lax.ppermute(value, EVERYONE, [(d, d ^ mask_of(d // CORE % 2)) for d in r...]
  transfers between devices with their start and end apart: 26 -> 26, of which waited for: 11 -> 9; matrix products, arithmetic and copies ran while one was open for 9% -> 9% of each run, Pallas kernels for 26% -> 26%
where the time goes in v12:
time: 117 us; the launch traced here: 116 us
  Pallas kernels  39.3 us (34%)
  waiting for transfers between devices  35.9 us (31%)
  starting transfers between devices  28.4 us (24%)
  matrix products  5.78 us (5%)
  other arithmetic  3.48 us (3%)
  local copies, waits for them, and re-layouts  2.4 us (2%)
    ppermute x26, waiting for transfers between devices, hop(): lax.ppermute(value, EVERYONE, [(d, d ^ mask_of(d // CORE % 2)) for d in r...  35.9 us
    ppermute x26, starting transfers between devices, hop(): lax.ppermute(value, EVERYONE, [(d, d ^ mask_of(d // CORE % 2)) for d in r...  28.4 us
    pallas_call x2, Pallas kernels, scan(): pl.pallas_call(functools.partial(scan_kernel, which), in_specs=[scalars]...  12.2 us
    pallas_call x2, Pallas kernels, out_share(): pl.pallas_call(functools.partial(share_kernel, which), in_specs=[scalars]...  10.3 us
    pallas_call x2, Pallas kernels, project(): pl.pallas_call(functools.partial(project_kernel, first), in_specs=[whole]...  6.48 us
    pallas_call x6, Pallas kernels, join(): pl.pallas_call(join_kernel, in_specs=[whole] * 2, out_specs=[whole] * len...  6.11 us
    dot_general x1, matrix products, body(): both = jnp.dot(both, pick.astype(BF), preferred_element_type=F32).astype(BF)  5.78 us
    squeeze x1, local copies, waits for them, and re-layouts, body(): own = lax.dynamic_index_in_dim(tokens, unit_id, 0, keepdims=False)  2.36 us
  transfers between devices with their start and end apart: 26, of which 9 were waited for; matrix products, arithmetic and copies ran while one was open for 9% of the time, Pallas kernels for 26%

profile of v12, /device:TPU:1, one launch (start us, length us, event | category | flops | bytes accessed | tf_op | source)
XLA Modules:
  0.0 116.3 jit_solution(7260090386035421527)
XLA Ops:
  1.3 1.9 %shards.1 = (bf16[12,4992]{1,0:T(8,128)(2,1)}, bf16[12,4992]{1,0:T(8,128)(2,1)}) custom-call(s32[2]{0:T(128)} %pad_add_fusion.meta_ref, s32[16]{0:T(128)} %lengths_ref.1, f32[12,3072]{1,0:T(8,128)} %input_ref.1, f32[12,256]{1,0:T(8,128)} %state_ref.1, f32[12,48]{1,0:T(8,128)} %step_ref.1, f32[12,3072]{1,0:T(8,128)} %gate_ref.1, f32[12,3072]{1,0:T(8,128)} %out_ref.1), custom_call_target="tpu_custom_call" | custom-call | tf_op jit(solution)/shard_map/shards/pallas_call | solution.py:227
  6.9 3.9 %collective-permute-start.13 = (bf16[8,4992]{1,0:T(8,128)(2,1)S(1)}, bf16[8,4992]{1,0:T(8,128)(2,1)S(1)}, u32[]{:S(2)}, u32[]{:S(2)}) collective-permute-start(bf16[8,4992]{1,0:T(8,128)(2,1)S(1)} %get-tuple-element.68), channel_id=1, source_target_pairs={{0,32},{1,33},{2,34},{3,35},{4,36},{5,37},{6,38},{7,39},{8,40},{9,... | collective-permute-start | bytes 239624 | tf_op jit(solution)/shard_map/ppermute | solution.py:413
  10.8 2.7 %collective-permute-start.8 = (bf16[8,4992]{1,0:T(8,128)(2,1)S(1)}, bf16[8,4992]{1,0:T(8,128)(2,1)S(1)}, u32[]{:S(2)}, u32[]{:S(2)}) collective-permute-start(bf16[8,4992]{1,0:T(8,128)(2,1)S(1)} %get-tuple-element.69), channel_id=1, source_target_pairs={{0,1},{1,0},{2,3},{3,2},{4,5},{5,4},{6,7},{7,6},{8,9},{9,8},{10,11... | collective-permute-start | bytes 239624 | tf_op jit(solution)/shard_map/ppermute | solution.py:413
  13.6 2.5 %collective-permute-start.1 = (bf16[8,4992]{1,0:T(8,128)(2,1)S(1)}, bf16[8,4992]{1,0:T(8,128)(2,1)S(1)}, u32[]{:S(2)}, u32[]{:S(2)}) collective-permute-start(bf16[8,4992]{1,0:T(8,128)(2,1)S(1)} %get-tuple-element.70), channel_id=1, source_target_pairs={{0,4},{1,5},{2,6},{3,7},{4,0},{5,1},{6,2},{7,3},{8,12},{9,13},{10,... | collective-permute-start | bytes 239624 | tf_op jit(solution)/shard_map/ppermute | solution.py:413
  16.2 1.9 %collective-permute-start.9 = (bf16[16,4992]{1,0:T(8,128)(2,1)S(1)}, bf16[16,4992]{1,0:T(8,128)(2,1)S(1)}, u32[]{:S(2)}, u32[]{:S(2)}) collective-permute-start(bf16[16,4992]{1,0:T(8,128)(2,1)S(1)} %pad_maximum_fusion.8), channel_id=1, source_target_pairs={{0,4},{1,5},{2,6},{3,7},{4,0},{5,1},{6,2},{7,3},{8,12},{9,13},{10,... | collective-permute-start | bytes 479240 | tf_op jit(solution)/shard_map/ppermute | solution.py:413
  18.2 3.6 %collective-permute-done.14 = bf16[16,4992]{1,0:T(8,128)(2,1)S(1)} collective-permute-done((bf16[16,4992]{1,0:T(8,128)(2,1)S(1)}, bf16[16,4992]{1,0:T(8,128)(2,1)S(1)}, u32[]{:S(2)}, u32[]{:S(2)}) %collective-permute-start.14) | collective-permute-done | bytes 159776 | tf_op jit(solution)/shard_map/ppermute | solution.py:413
  22.7 6.5 %collective-permute-done.15 = bf16[32,4992]{1,0:T(8,128)(2,1)S(1)} collective-permute-done((bf16[32,4992]{1,0:T(8,128)(2,1)S(1)}, bf16[32,4992]{1,0:T(8,128)(2,1)S(1)}, u32[]{:S(2)}, u32[]{:S(2)}) %collective-permute-start.15) | collective-permute-done | bytes 319520 | tf_op jit(solution)/shard_map/ppermute | solution.py:413
  29.7 9.2 %collective-permute-done.16.moved_ref = bf16[64,4992]{1,0:T(8,128)(2,1)S(1)} collective-permute-done((bf16[64,4992]{1,0:T(8,128)(2,1)S(1)}, bf16[64,4992]{1,0:T(8,128)(2,1)S(1)}, u32[]{:S(2)}, u32[]{:S(2)}) %collective-permute-start.16) | collective-permute-done | bytes 639008 | tf_op jit(solution)/shard_map/ppermute | solution.py:413
  40.0 2.4 %dynamic-slice_bitcast_fusion = bf16[384,1536]{1,0:T(8,128)(2,1)} fusion(bf16[16,384,1536]{2,1,0:T(8,128)(2,1)} %param.12, s32[]{:T(128)S(6)} %select_n.464), kind=kLoop, calls=%fused_computation.8 | loop fusion | bytes 2359300 | tf_op jit(solution)/shard_map/jit(dynamic_index_in_dim)/squeeze | solution.py:500
  43.9 2.6 %collective-permute-start.5 = (bf16[128,4992]{1,0:T(8,128)(2,1)S(1)}, bf16[128,4992]{1,0:T(8,128)(2,1)}, u32[]{:S(2)}, u32[]{:S(2)}) collective-permute-start(bf16[128,4992]{1,0:T(8,128)(2,1)S(1)} %join.6.held_ref), channel_id=1, source_target_pairs={{0,32},{1,33},{2,34},{3,35},{4,36},{5,37},{6,38},{7,39},{8,40},{9,... | collective-permute-start | bytes 3833864 | tf_op jit(solution)/shard_map/ppermute | solution.py:413
  47.9 8.8 %collective-permute-done.17.moved_ref = bf16[128,4992]{1,0:T(8,128)(2,1)} collective-permute-done((bf16[128,4992]{1,0:T(8,128)(2,1)}, bf16[128,4992]{1,0:T(8,128)(2,1)}, u32[]{:S(2)}, u32[]{:S(2)}) %collective-permute-start.17) | collective-permute-done | bytes 1277984 | tf_op jit(solution)/shard_map/ppermute | solution.py:413
  56.8 1.9 %join.11 = (bf16[256,1920]{1,0:T(8,128)(2,1)S(1)}, bf16[256,3072]{1,0:T(8,128)(2,1)S(1)}) custom-call(bf16[128,4992]{1,0:T(8,128)(2,1)} %join.10.held_ref, bf16[128,4992]{1,0:T(8,128)(2,1)} %collective-permute-done.17.moved_ref), custom_call_target="tpu_custom_call" | custom-call | bytes 5111808 | tf_op jit(solution)/shard_map/join/pallas_call | solution.py:248
  58.7 5.8 %fusion.2.tokens_ref = bf16[768,1536]{1,0:T(8,128)(2,1)S(1)} fusion(s32[1536]{0:T(1024)S(1)} %select_subtract_fusion, bf16[384,1536]{1,0:T(8,128)(2,1)} %collective-permute-done.6, bf16[384,1536]{1,0:T(8,128)(2,1)} %dynamic-slice_bitcast_fusion), kind=kOutput, calls=%fused_computation.3 | convolution fusion | flops 3632136192 | bytes 4724736 | tf_op jit(solution)/shard_map/dot_general | solution.py:503
  67.6 1.8 %collective-permute-start.18 = (bf16[256,1920]{1,0:T(8,128)(2,1)S(1)}, bf16[256,1920]{1,0:T(8,128)(2,1)S(1)}, u32[]{:S(2)}, u32[]{:S(2)}) collective-permute-start(bf16[256,1920]{1,0:T(8,128)(2,1)S(1)} %get-tuple-element.44.refs_1_), channel_id=1, source_target_pairs={{0,32},{1,33},{2,34},{3,35},{4,36},{5,37},{6,38},{7,39},{8,40},{9,... | collective-permute-start | bytes 2949128 | tf_op jit(solution)/shard_map/ppermute | solution.py:413
  71.8 1.8 %collective-permute-done.19.refs_3_ = bf16[256,1920]{1,0:T(8,128)(2,1)S(1)} collective-permute-done((bf16[256,1920]{1,0:T(8,128)(2,1)S(1)}, bf16[256,1920]{1,0:T(8,128)(2,1)S(1)}, u32[]{:S(2)}, u32[]{:S(2)}) %collective-permute-start.19) | collective-permute-done | bytes 983072 | tf_op jit(solution)/shard_map/ppermute | solution.py:413
  74.4 3.2 %project.2.refs_0_ = f32[768,1920]{1,0:T(8,128)S(1)} custom-call(bf16[768,1536]{1,0:T(8,128)(2,1)S(1)} %fusion.2.tokens_ref, bf16[256,1920]{1,0:T(8,128)(2,1)S(1)} %get-tuple-element.40.refs_0_, bf16[256,1920]{1,0:T(8,128)(2,1)S(1)} %get-tuple-element.44.refs_1_, bf16[256,1920]{1,0:T(8,128)(2,1)S(1)} %get-tuple-element.45.refs_2_), custom_call_target="tpu_custom_call" | custom-call | flops 2264924160 | bytes 10485760 | tf_op jit(solution)/shard_map/project/pallas_call | solution.py:289
  77.7 2.8 %collective-permute-done.7.refs_1_ = bf16[256,1920]{1,0:T(8,128)(2,1)S(1)} collective-permute-done((bf16[256,1920]{1,0:T(8,128)(2,1)S(1)}, bf16[256,1920]{1,0:T(8,128)(2,1)S(1)}, u32[]{:S(2)}, u32[]{:S(2)}) %collective-permute-start.7) | collective-permute-done | bytes 983072 | tf_op jit(solution)/shard_map/ppermute | solution.py:413
  82.1 3.3 %project.3.projected_ref = bf16[768,1920]{1,0:T(8,128)(2,1)S(1)} custom-call(bf16[768,1536]{1,0:T(8,128)(2,1)S(1)} %fusion.2.tokens_ref, f32[768,1920]{1,0:T(8,128)S(1)} %project.2.refs_0_, bf16[256,1920]{1,0:T(8,128)(2,1)S(1)} %collective-permute-done.7.refs_1_, bf16[256,1920]{1,0:T(8,128)(2,1)S(1)} %collective-permute-done.18.refs_2_, ...), custom_call_target="tpu_custom_call" | custom-call | flops 2264924160 | bytes 10485760 | tf_op jit(solution)/shard_map/project/pallas_call | solution.py:289
  85.4 6.1 %scan.2 = (f32[384,1536]{1,0:T(8,128)S(1)}, f32[1536,128]{1,0:T(8,128)S(1)}) custom-call(s32[2]{0:T(128)S(1)} %copy-done.2, bf16[12,4992]{1,0:T(8,128)(2,1)S(1)} %collective-permute-done.shard_ref, bf16[768,1920]{1,0:T(8,128)(2,1)S(1)} %project.3.projected_ref, f32[4,3328]{1,0:T(4,128)S(1)} %copy-done.3, f32[1,48]{1,0:T(1,128)S(1)} %bitcast.11, ...), custom_call_target="tpu_custom_call" | custom-call | flops 754974720 | bytes 5242880 | tf_op jit(solution)/shard_map/scan/pallas_call | solution.py:177
  91.6 3.0 %collective-permute-start.20 = (f32[1536,128]{1,0:T(8,128)S(1)}, f32[1536,128]{1,0:T(8,128)S(1)}, u32[]{:S(2)}, u32[]{:S(2)}) collective-permute-start(f32[1536,128]{1,0:T(8,128)S(1)} %get-tuple-element.52), channel_id=1, source_target_pairs={{0,16},{1,17},{2,18},{3,19},{4,20},{5,21},{6,22},{7,23},{8,24},{9,... | collective-permute-start | bytes 2359304 | tf_op jit(solution)/shard_map/ppermute | solution.py:413
  94.6 6.1 %scan.3 = (f32[384,1536]{1,0:T(8,128)S(1)}, f32[1536,128]{1,0:T(8,128)S(1)}) custom-call(s32[2]{0:T(128)S(1)} %copy-done.2, bf16[12,4992]{1,0:T(8,128)(2,1)S(1)} %copy-done, bf16[768,1920]{1,0:T(8,128)(2,1)S(1)} %project.3.projected_ref, f32[4,3328]{1,0:T(4,128)S(1)} %copy-done.3, f32[1,48]{1,0:T(1,128)S(1)} %bitcast.12, f32[1,48]{1,0:T(1,128)S(1)} %bitcast.14, ...), custom_call_target="tpu_custom_call" | custom-call | flops 754974720 | bytes 5242880 | tf_op jit(solution)/shard_map/scan/pallas_call | solution.py:177
  100.8 5.1 %out_share.3 = (f32[1536,384]{1,0:T(8,128)S(1)}, f32[384,128]{1,0:T(8,128)S(1)}) custom-call(s32[2]{0:T(128)S(1)} %copy-done.2, s32[192]{0:T(256)S(1)} %multiply_add_fusion.places_ref, bf16[768,1536]{1,0:T(8,128)(2,1)S(1)} %fusion.2.tokens_ref, f32[384,1536]{1,0:T(8,128)S(1)} %get-tuple-element.58.scanned_ref, f32[1,3072]{1,0:T(1,128)S(1)} %bitcast.9, ...), custom_call_target="tpu_custom_call" | custom-call | flops 3623878656 | bytes 16777216 | tf_op jit(solution)/shard_map/out_share/pallas_call | solution.py:342
  108.9 5.1 %out_share.2 = (f32[1536,384]{1,0:T(8,128)S(1)}, f32[384,128]{1,0:T(8,128)S(1)}) custom-call(s32[2]{0:T(128)S(1)} %copy-done.2, s32[192]{0:T(256)S(1)} %multiply_add_fusion.places_ref, bf16[768,1536]{1,0:T(8,128)(2,1)S(1)} %fusion.2.tokens_ref, f32[384,1536]{1,0:T(8,128)S(1)} %get-tuple-element.53.scanned_ref, f32[1,3072]{1,0:T(1,128)S(1)} %bitcast.10, ...), custom_call_target="tpu_custom_call" | custom-call | flops 3623878656 | bytes 16777216 | tf_op jit(solution)/shard_map/out_share/pallas_call | solution.py:342
  114.1 2.3 %mix.1 = bf16[384,1536]{1,0:T(8,128)(2,1)} custom-call(bf16[12,4992]{1,0:T(8,128)(2,1)S(1)} %copy-done, f32[1536,384]{1,0:T(8,128)S(1)} %get-tuple-element.57.mine_ref, f32[1536,384]{1,0:T(8,128)S(1)} %collective-permute-done.24.other_ref, f32[384,128]{1,0:T(8,128)S(1)} %get-tuple-element.60.sq_mine, f32[384,128]{1,0:T(8,128)S(1)} %collective-permute-done.25.sq_other, ...), custom_call_target="tpu_custom_call" | custom-call | flops 452984832 | bytes 8388608 | tf_op jit(solution)/shard_map/mix/pallas_call | solution.py:384
  (76 shorter events, 20.9 us)
Async XLA Ops:
  6.9 9.1 %collective-permute-start.13 = (bf16[8,4992]{1,0:T(8,128)(2,1)S(1)}, bf16[8,4992]{1,0:T(8,128)(2,1)S(1)}, u32[]{:S(2)}, u32[]{:S(2)}) collective-permute-start(bf16[8,4992]{1,0:T(8,128)(2,1)S(1)} %get-tuple-element.68), channel_id=1, source_target_pairs={{0,32},{1,33},{2,34},{3,35},{4,36},{5,37},{6,38},{7,39},{8,40},{9,... | collective-permute-start | bytes 239624 | tf_op jit(solution)/shard_map/ppermute | solution.py:413
  10.8 5.3 %collective-permute-start.8 = (bf16[8,4992]{1,0:T(8,128)(2,1)S(1)}, bf16[8,4992]{1,0:T(8,128)(2,1)S(1)}, u32[]{:S(2)}, u32[]{:S(2)}) collective-permute-start(bf16[8,4992]{1,0:T(8,128)(2,1)S(1)} %get-tuple-element.69), channel_id=1, source_target_pairs={{0,1},{1,0},{2,3},{3,2},{4,5},{5,4},{6,7},{7,6},{8,9},{9,8},{10,11... | collective-permute-start | bytes 239624 | tf_op jit(solution)/shard_map/ppermute | solution.py:413
  16.1 5.7 %collective-permute-start.14 = (bf16[16,4992]{1,0:T(8,128)(2,1)S(1)}, bf16[16,4992]{1,0:T(8,128)(2,1)S(1)}, u32[]{:S(2)}, u32[]{:S(2)}) collective-permute-start(bf16[16,4992]{1,0:T(8,128)(2,1)S(1)} %pad_maximum_fusion.9), channel_id=1, source_target_pairs={{0,1},{1,0},{2,3},{3,2},{4,5},{5,4},{6,7},{7,6},{8,9},{9,8},{10,11... | collective-permute-start | bytes 479240 | tf_op jit(solution)/shard_map/ppermute | solution.py:413
  16.2 5.7 %collective-permute-start.9 = (bf16[16,4992]{1,0:T(8,128)(2,1)S(1)}, bf16[16,4992]{1,0:T(8,128)(2,1)S(1)}, u32[]{:S(2)}, u32[]{:S(2)}) collective-permute-start(bf16[16,4992]{1,0:T(8,128)(2,1)S(1)} %pad_maximum_fusion.8), channel_id=1, source_target_pairs={{0,4},{1,5},{2,6},{3,7},{4,0},{5,1},{6,2},{7,3},{8,12},{9,13},{10,... | collective-permute-start | bytes 479240 | tf_op jit(solution)/shard_map/ppermute | solution.py:413
  18.1 4.5 %collective-permute-start.2 = (bf16[16,4992]{1,0:T(8,128)(2,1)S(1)}, bf16[16,4992]{1,0:T(8,128)(2,1)S(1)}, u32[]{:S(2)}, u32[]{:S(2)}) collective-permute-start(bf16[16,4992]{1,0:T(8,128)(2,1)S(1)} %pad_maximum_fusion.7), channel_id=1, source_target_pairs={{0,96},{1,97},{2,98},{3,99},{4,100},{5,101},{6,102},{7,103},{8,104... | collective-permute-start | bytes 479240 | tf_op jit(solution)/shard_map/ppermute | solution.py:413
  21.8 7.4 %collective-permute-start.15 = (bf16[32,4992]{1,0:T(8,128)(2,1)S(1)}, bf16[32,4992]{1,0:T(8,128)(2,1)S(1)}, u32[]{:S(2)}, u32[]{:S(2)}) collective-permute-start(bf16[32,4992]{1,0:T(8,128)(2,1)S(1)} %pad_maximum_fusion.6), channel_id=1, source_target_pairs={{0,4},{1,5},{2,6},{3,7},{4,0},{5,1},{6,2},{7,3},{8,12},{9,13},{10,... | collective-permute-start | bytes 958472 | tf_op jit(solution)/shard_map/ppermute | solution.py:413
  21.9 7.4 %collective-permute-start.10 = (bf16[32,4992]{1,0:T(8,128)(2,1)S(1)}, bf16[32,4992]{1,0:T(8,128)(2,1)S(1)}, u32[]{:S(2)}, u32[]{:S(2)}) collective-permute-start(bf16[32,4992]{1,0:T(8,128)(2,1)S(1)} %pad_maximum_fusion.5), channel_id=1, source_target_pairs={{0,96},{1,97},{2,98},{3,99},{4,100},{5,101},{6,102},{7,103},{8,104... | collective-permute-start | bytes 958472 | tf_op jit(solution)/shard_map/ppermute | solution.py:413
  22.6 6.9 %collective-permute-start.3 = (bf16[32,4992]{1,0:T(8,128)(2,1)S(1)}, bf16[32,4992]{1,0:T(8,128)(2,1)S(1)}, u32[]{:S(2)}, u32[]{:S(2)}) collective-permute-start(bf16[32,4992]{1,0:T(8,128)(2,1)S(1)} %pad_maximum_fusion.4), channel_id=1, source_target_pairs={{0,3},{1,2},{2,1},{3,0},{4,7},{5,6},{6,5},{7,4},{8,11},{9,10},{10,... | collective-permute-start | bytes 958472 | tf_op jit(solution)/shard_map/ppermute | solution.py:413
  29.3 9.6 %collective-permute-start.16 = (bf16[64,4992]{1,0:T(8,128)(2,1)S(1)}, bf16[64,4992]{1,0:T(8,128)(2,1)S(1)}, u32[]{:S(2)}, u32[]{:S(2)}) collective-permute-start(bf16[64,4992]{1,0:T(8,128)(2,1)S(1)} %pad_maximum_fusion.3.held_ref), channel_id=1, source_target_pairs={{0,96},{1,97},{2,98},{3,99},{4,100},{5,101},{6,102},{7,103},{8,104... | collective-permute-start | bytes 1916936 | tf_op jit(solution)/shard_map/ppermute | solution.py:413
  29.4 17.1 %collective-permute-start.11 = (bf16[64,4992]{1,0:T(8,128)(2,1)S(1)}, bf16[64,4992]{1,0:T(8,128)(2,1)S(1)}, u32[]{:S(2)}, u32[]{:S(2)}) collective-permute-start(bf16[64,4992]{1,0:T(8,128)(2,1)S(1)} %pad_maximum_fusion.2.held_ref), channel_id=1, source_target_pairs={{0,3},{1,2},{2,1},{3,0},{4,7},{5,6},{6,5},{7,4},{8,11},{9,10},{10,... | collective-permute-start | bytes 1916936 | tf_op jit(solution)/shard_map/ppermute | solution.py:413
  29.6 14.2 %collective-permute-start.4 = (bf16[64,4992]{1,0:T(8,128)(2,1)S(1)}, bf16[64,4992]{1,0:T(8,128)(2,1)S(1)}, u32[]{:S(2)}, u32[]{:S(2)}) collective-permute-start(bf16[64,4992]{1,0:T(8,128)(2,1)S(1)} %pad_maximum_fusion.1.held_ref), channel_id=1, source_target_pairs={{0,12},{1,13},{2,14},{3,15},{4,8},{5,9},{6,10},{7,11},{8,4},{9,5},... | collective-permute-start | bytes 1916936 | tf_op jit(solution)/shard_map/ppermute | solution.py:413
  40.0 16.7 %collective-permute-start.17 = (bf16[128,4992]{1,0:T(8,128)(2,1)}, bf16[128,4992]{1,0:T(8,128)(2,1)}, u32[]{:S(2)}, u32[]{:S(2)}) collective-permute-start(bf16[128,4992]{1,0:T(8,128)(2,1)} %join.10.held_ref), channel_id=1, source_target_pairs={{0,3},{1,2},{2,1},{3,0},{4,7},{5,6},{6,5},{7,4},{8,11},{9,10},{10,... | collective-permute-start | bytes 3833864 | tf_op jit(solution)/shard_map/ppermute | solution.py:413
  42.4 16.3 %collective-permute-start.6 = (bf16[384,1536]{1,0:T(8,128)(2,1)}, bf16[384,1536]{1,0:T(8,128)(2,1)}, u32[]{:S(2)}, u32[]{:S(2)}) collective-permute-start(bf16[384,1536]{1,0:T(8,128)(2,1)} %dynamic-slice_bitcast_fusion), channel_id=1, source_target_pairs={{0,16},{1,17},{2,18},{3,19},{4,20},{5,21},{6,22},{7,23},{8,24},{9,... | collective-permute-start | bytes 3538952 | tf_op jit(solution)/shard_map/ppermute | solution.py:413
  43.9 20.6 %collective-permute-start.5 = (bf16[128,4992]{1,0:T(8,128)(2,1)S(1)}, bf16[128,4992]{1,0:T(8,128)(2,1)}, u32[]{:S(2)}, u32[]{:S(2)}) collective-permute-start(bf16[128,4992]{1,0:T(8,128)(2,1)S(1)} %join.6.held_ref), channel_id=1, source_target_pairs={{0,32},{1,33},{2,34},{3,35},{4,36},{5,37},{6,38},{7,39},{8,40},{9,... | collective-permute-start | bytes 3833864 | tf_op jit(solution)/shard_map/ppermute | solution.py:413
  46.6 19.5 %collective-permute-start.12 = (bf16[128,4992]{1,0:T(8,128)(2,1)S(1)}, bf16[128,4992]{1,0:T(8,128)(2,1)}, u32[]{:S(2)}, u32[]{:S(2)}) collective-permute-start(bf16[128,4992]{1,0:T(8,128)(2,1)S(1)} %join.8.held_ref), channel_id=1, source_target_pairs={{0,12},{1,13},{2,14},{3,15},{4,8},{5,9},{6,10},{7,11},{8,4},{9,5},... | collective-permute-start | bytes 3833864 | tf_op jit(solution)/shard_map/ppermute | solution.py:413
  58.6 15.0 %collective-permute-start.19 = (bf16[256,1920]{1,0:T(8,128)(2,1)S(1)}, bf16[256,1920]{1,0:T(8,128)(2,1)S(1)}, u32[]{:S(2)}, u32[]{:S(2)}) collective-permute-start(bf16[256,1920]{1,0:T(8,128)(2,1)S(1)} %get-tuple-element.45.refs_2_), channel_id=1, source_target_pairs={{0,12},{1,13},{2,14},{3,15},{4,8},{5,9},{6,10},{7,11},{8,4},{9,5},... | collective-permute-start | bytes 2949128 | tf_op jit(solution)/shard_map/ppermute | solution.py:413
  66.0 14.5 %collective-permute-start.7 = (bf16[256,1920]{1,0:T(8,128)(2,1)S(1)}, bf16[256,1920]{1,0:T(8,128)(2,1)S(1)}, u32[]{:S(2)}, u32[]{:S(2)}) collective-permute-start(bf16[256,1920]{1,0:T(8,128)(2,1)S(1)} %get-tuple-element.40.refs_0_), channel_id=1, source_target_pairs={{0,1},{1,0},{2,3},{3,2},{4,5},{5,4},{6,7},{7,6},{8,9},{9,8},{10,11... | collective-permute-start | bytes 2949128 | tf_op jit(solution)/shard_map/ppermute | solution.py:413
  67.6 14.5 %collective-permute-start.18 = (bf16[256,1920]{1,0:T(8,128)(2,1)S(1)}, bf16[256,1920]{1,0:T(8,128)(2,1)S(1)}, u32[]{:S(2)}, u32[]{:S(2)}) collective-permute-start(bf16[256,1920]{1,0:T(8,128)(2,1)S(1)} %get-tuple-element.44.refs_1_), channel_id=1, source_target_pairs={{0,32},{1,33},{2,34},{3,35},{4,36},{5,37},{6,38},{7,39},{8,40},{9,... | collective-permute-start | bytes 2949128 | tf_op jit(solution)/shard_map/ppermute | solution.py:413
  69.4 31.4 %collective-permute-start.21 = (bf16[256,3072]{1,0:T(8,128)(2,1)S(1)}, bf16[256,3072]{1,0:T(8,128)(2,1)S(1)}, u32[]{:S(2)}, u32[]{:S(2)}) collective-permute-start(bf16[256,3072]{1,0:T(8,128)(2,1)S(1)} %get-tuple-element.54.refs_0_), channel_id=1, source_target_pairs={{0,1},{1,0},{2,3},{3,2},{4,5},{5,4},{6,7},{7,6},{8,9},{9,8},{10,11... | collective-permute-start | bytes 4718600 | tf_op jit(solution)/shard_map/ppermute | solution.py:413
  70.4 30.4 %collective-permute-start.23 = (bf16[256,3072]{1,0:T(8,128)(2,1)S(1)}, bf16[256,3072]{1,0:T(8,128)(2,1)S(1)}, u32[]{:S(2)}, u32[]{:S(2)}) collective-permute-start(bf16[256,3072]{1,0:T(8,128)(2,1)S(1)} %get-tuple-element.56.refs_4_), channel_id=1, source_target_pairs={{0,12},{1,13},{2,14},{3,15},{4,8},{5,9},{6,10},{7,11},{8,4},{9,5},... | collective-permute-start | bytes 4718600 | tf_op jit(solution)/shard_map/ppermute | solution.py:413
  73.6 27.2 %collective-permute-start.22 = (bf16[256,3072]{1,0:T(8,128)(2,1)S(1)}, bf16[256,3072]{1,0:T(8,128)(2,1)S(1)}, u32[]{:S(2)}, u32[]{:S(2)}) collective-permute-start(bf16[256,3072]{1,0:T(8,128)(2,1)S(1)} %get-tuple-element.55.refs_2_), channel_id=1, source_target_pairs={{0,32},{1,33},{2,34},{3,35},{4,36},{5,37},{6,38},{7,39},{8,40},{9,... | collective-permute-start | bytes 4718600 | tf_op jit(solution)/shard_map/ppermute | solution.py:413
  91.6 9.2 %collective-permute-start.20 = (f32[1536,128]{1,0:T(8,128)S(1)}, f32[1536,128]{1,0:T(8,128)S(1)}, u32[]{:S(2)}, u32[]{:S(2)}) collective-permute-start(f32[1536,128]{1,0:T(8,128)S(1)} %get-tuple-element.52), channel_id=1, source_target_pairs={{0,16},{1,17},{2,18},{3,19},{4,20},{5,21},{6,22},{7,23},{8,24},{9,... | collective-permute-start | bytes 2359304 | tf_op jit(solution)/shard_map/ppermute | solution.py:413
  105.9 8.1 %collective-permute-start.24 = (f32[1536,384]{1,0:T(8,128)S(1)}, f32[1536,384]{1,0:T(8,128)S(1)}, u32[]{:S(2)}, u32[]{:S(2)}) collective-permute-start(f32[1536,384]{1,0:T(8,128)S(1)} %get-tuple-element.59), channel_id=1, source_target_pairs={{0,16},{1,17},{2,18},{3,19},{4,20},{5,21},{6,22},{7,23},{8,24},{9,... | collective-permute-start | bytes 7077896 | tf_op jit(solution)/shard_map/ppermute | solution.py:413
  108.9 5.2 %collective-permute-start.25 = (f32[384,128]{1,0:T(8,128)S(1)}, f32[384,128]{1,0:T(8,128)S(1)}, u32[]{:S(2)}, u32[]{:S(2)}) collective-permute-start(f32[384,128]{1,0:T(8,128)S(1)} %get-tuple-element.61), channel_id=1, source_target_pairs={{0,16},{1,17},{2,18},{3,19},{4,20},{5,21},{6,22},{7,23},{8,24},{9,... | collective-permute-start | bytes 589832 | tf_op jit(solution)/shard_map/ppermute | solution.py:413
  (9 other events, 64.2 us)

commit v13 on v9

--- a/solution.py
+++ b/solution.py
@@ -494,6 +494,7 @@
     held = [pair[8 * c : 8 * c + 8] for c in range(COLOURS)]
     for step in range(3):
         held = joined(held, moved_over(held, step))
+    held[2], unit_id = lax.optimization_barrier((held[2], unit_id))
     held = [join(h, m, cut + 2 * half)[0] for h, m in zip(held, moved_over(held, 3))]
     moved = moved_over(held, 4)
 
@@ -507,8 +508,7 @@
     moved = moved_over(early, 5)
     begun = project(both, early)
     moved[0], begun = lax.optimization_barrier((moved[0], begun))
-    for c in range(COLOURS):
-        moved[c], late[c] = lax.optimization_barrier((moved[c], late[c]))
+    moved[0], late[0] = lax.optimization_barrier((moved[0], late[0]))
     late = [piece for two in zip(late, moved_over(late, 5)) for piece in two]
 
     projected = project(both, moved, begun)

time: 117 us -> 112 us (0.957)
  Pallas kernels: 39.3 us -> 36.3 us
  starting transfers between devices: 30.2 us -> 28.6 us
    pallas_call x6, Pallas kernels: 6.11 us -> 3.15 us  [join(): pl.pallas_call(join_kernel, in_specs=[whole] * 2, out_specs=[whole] * len...]
    ppermute x26, starting transfers between devices: 30.2 us -> 28.6 us  [hop(): lax.ppermute(value, EVERYONE, [(d, d ^ mask_of(d // CORE % 2)) for d in r...]
  transfers between devices with their start and end apart: 26 -> 26, of which waited for: 11 -> 9; matrix products, arithmetic and copies ran while one was open for 9% -> 9% of each run, Pallas kernels for 26% -> 24%
where the time goes in v13:
time: 112 us
  Pallas kernels  36.3 us (32%)
  waiting for transfers between devices  34.5 us (31%)
  starting transfers between devices  28.6 us (26%)
  matrix products  5.79 us (5%)
  other arithmetic  3.4 us (3%)
  local copies, waits for them, and re-layouts  2.4 us (2%)
    ppermute x26, waiting for transfers between devices, hop(): lax.ppermute(value, EVERYONE, [(d, d ^ mask_of(d // CORE % 2)) for d in r...  34.5 us
    ppermute x26, starting transfers between devices, hop(): lax.ppermute(value, EVERYONE, [(d, d ^ mask_of(d // CORE % 2)) for d in r...  28.6 us
    pallas_call x2, Pallas kernels, scan(): pl.pallas_call(functools.partial(scan_kernel, which), in_specs=[scalars]...  12.2 us
    pallas_call x2, Pallas kernels, out_share(): pl.pallas_call(functools.partial(share_kernel, which), in_specs=[scalars]...  10.4 us
    pallas_call x2, Pallas kernels, project(): pl.pallas_call(functools.partial(project_kernel, first), in_specs=[whole]...  6.43 us
    dot_general x1, matrix products, body(): both = jnp.dot(both, pick.astype(BF), preferred_element_type=F32).astype(BF)  5.79 us
    pallas_call x6, Pallas kernels, join(): pl.pallas_call(join_kernel, in_specs=[whole] * 2, out_specs=[whole] * len...  3.15 us
    squeeze x1, local copies, waits for them, and re-layouts, body(): own = lax.dynamic_index_in_dim(tokens, unit_id, 0, keepdims=False)  2.37 us
  transfers between devices with their start and end apart: 26, of which 9 were waited for; matrix products, arithmetic and copies ran while one was open for 9% of the time, Pallas kernels for 24%

profile of v13, /device:TPU:1, one launch (start us, length us, event | category | flops | bytes accessed | tf_op | source)
XLA Modules:
  0.0 112.0 jit_solution(6545174253160765227)
XLA Ops:
  1.3 1.9 %shards.1 = (bf16[12,4992]{1,0:T(8,128)(2,1)}, bf16[12,4992]{1,0:T(8,128)(2,1)}) custom-call(s32[2]{0:T(128)} %pad_add_fusion.meta_ref, s32[16]{0:T(128)} %lengths_ref.1, f32[12,3072]{1,0:T(8,128)} %input_ref.1, f32[12,256]{1,0:T(8,128)} %state_ref.1, f32[12,48]{1,0:T(8,128)} %step_ref.1, f32[12,3072]{1,0:T(8,128)} %gate_ref.1, f32[12,3072]{1,0:T(8,128)} %out_ref.1), custom_call_target="tpu_custom_call" | custom-call | tf_op jit(solution)/shard_map/shards/pallas_call | solution.py:227
  6.8 3.9 %collective-permute-start.6 = (bf16[8,4992]{1,0:T(8,128)(2,1)S(1)}, bf16[8,4992]{1,0:T(8,128)(2,1)S(1)}, u32[]{:S(2)}, u32[]{:S(2)}) collective-permute-start(bf16[8,4992]{1,0:T(8,128)(2,1)S(1)} %get-tuple-element.68), channel_id=1, source_target_pairs={{0,32},{1,33},{2,34},{3,35},{4,36},{5,37},{6,38},{7,39},{8,40},{9,... | collective-permute-start | bytes 239624 | tf_op jit(solution)/shard_map/ppermute | solution.py:413
  10.8 2.7 %collective-permute-start.11 = (bf16[8,4992]{1,0:T(8,128)(2,1)S(1)}, bf16[8,4992]{1,0:T(8,128)(2,1)S(1)}, u32[]{:S(2)}, u32[]{:S(2)}) collective-permute-start(bf16[8,4992]{1,0:T(8,128)(2,1)S(1)} %get-tuple-element.66), channel_id=1, source_target_pairs={{0,1},{1,0},{2,3},{3,2},{4,5},{5,4},{6,7},{7,6},{8,9},{9,8},{10,11... | collective-permute-start | bytes 239624 | tf_op jit(solution)/shard_map/ppermute | solution.py:413
  13.5 2.5 %collective-permute-start.1 = (bf16[8,4992]{1,0:T(8,128)(2,1)S(1)}, bf16[8,4992]{1,0:T(8,128)(2,1)S(1)}, u32[]{:S(2)}, u32[]{:S(2)}) collective-permute-start(bf16[8,4992]{1,0:T(8,128)(2,1)S(1)} %get-tuple-element.67), channel_id=1, source_target_pairs={{0,4},{1,5},{2,6},{3,7},{4,0},{5,1},{6,2},{7,3},{8,12},{9,13},{10,... | collective-permute-start | bytes 239624 | tf_op jit(solution)/shard_map/ppermute | solution.py:413
  16.1 1.9 %collective-permute-start.12 = (bf16[16,4992]{1,0:T(8,128)(2,1)S(1)}, bf16[16,4992]{1,0:T(8,128)(2,1)S(1)}, u32[]{:S(2)}, u32[]{:S(2)}) collective-permute-start(bf16[16,4992]{1,0:T(8,128)(2,1)S(1)} %pad_maximum_fusion.9), channel_id=1, source_target_pairs={{0,4},{1,5},{2,6},{3,7},{4,0},{5,1},{6,2},{7,3},{8,12},{9,13},{10,... | collective-permute-start | bytes 479240 | tf_op jit(solution)/shard_map/ppermute | solution.py:413
  18.1 3.6 %collective-permute-done.7 = bf16[16,4992]{1,0:T(8,128)(2,1)S(1)} collective-permute-done((bf16[16,4992]{1,0:T(8,128)(2,1)S(1)}, bf16[16,4992]{1,0:T(8,128)(2,1)S(1)}, u32[]{:S(2)}, u32[]{:S(2)}) %collective-permute-start.7) | collective-permute-done | bytes 159776 | tf_op jit(solution)/shard_map/ppermute | solution.py:413
  22.6 6.5 %collective-permute-done.8 = bf16[32,4992]{1,0:T(8,128)(2,1)S(1)} collective-permute-done((bf16[32,4992]{1,0:T(8,128)(2,1)S(1)}, bf16[32,4992]{1,0:T(8,128)(2,1)S(1)}, u32[]{:S(2)}, u32[]{:S(2)}) %collective-permute-start.8) | collective-permute-done | bytes 319520 | tf_op jit(solution)/shard_map/ppermute | solution.py:413
  29.3 2.4 %dynamic-slice_bitcast_fusion = bf16[384,1536]{1,0:T(8,128)(2,1)} fusion(bf16[16,384,1536]{2,1,0:T(8,128)(2,1)} %param.12, s32[]{:T(128)S(6)} %select_n.465), kind=kLoop, calls=%fused_computation.8 | loop fusion | bytes 2359300 | tf_op jit(solution)/shard_map/jit(dynamic_index_in_dim)/squeeze | solution.py:501
  33.6 7.9 %collective-permute-done.4.moved_ref = bf16[64,4992]{1,0:T(8,128)(2,1)S(1)} collective-permute-done((bf16[64,4992]{1,0:T(8,128)(2,1)S(1)}, bf16[64,4992]{1,0:T(8,128)(2,1)S(1)}, u32[]{:S(2)}, u32[]{:S(2)}) %collective-permute-start.4) | collective-permute-done | bytes 639008 | tf_op jit(solution)/shard_map/ppermute | solution.py:413
  44.8 5.8 %fusion.2.tokens_ref = bf16[768,1536]{1,0:T(8,128)(2,1)S(1)} fusion(s32[1536]{0:T(1024)S(1)} %select_subtract_fusion, bf16[384,1536]{1,0:T(8,128)(2,1)} %collective-permute-done.9, bf16[384,1536]{1,0:T(8,128)(2,1)} %dynamic-slice_bitcast_fusion), kind=kOutput, calls=%fused_computation.3 | convolution fusion | flops 3632136192 | bytes 4724736 | tf_op jit(solution)/shard_map/dot_general | solution.py:504
  50.6 8.7 %collective-permute-done.5.moved_ref = bf16[128,4992]{1,0:T(8,128)(2,1)} collective-permute-done((bf16[128,4992]{1,0:T(8,128)(2,1)S(1)}, bf16[128,4992]{1,0:T(8,128)(2,1)}, u32[]{:S(2)}, u32[]{:S(2)}) %collective-permute-start.5) | collective-permute-done | bytes 1277984 | tf_op jit(solution)/shard_map/ppermute | solution.py:413
  60.7 1.9 %collective-permute-start.10 = (bf16[256,1920]{1,0:T(8,128)(2,1)S(1)}, bf16[256,1920]{1,0:T(8,128)(2,1)S(1)}, u32[]{:S(2)}, u32[]{:S(2)}) collective-permute-start(bf16[256,1920]{1,0:T(8,128)(2,1)S(1)} %get-tuple-element.40.refs_0_), channel_id=1, source_target_pairs={{0,1},{1,0},{2,3},{3,2},{4,5},{5,4},{6,7},{7,6},{8,9},{9,8},{10,11... | collective-permute-start | bytes 2949128 | tf_op jit(solution)/shard_map/ppermute | solution.py:413
  64.7 2.6 %collective-permute-start.22 = (bf16[256,3072]{1,0:T(8,128)(2,1)S(1)}, bf16[256,3072]{1,0:T(8,128)(2,1)S(1)}, u32[]{:S(2)}, u32[]{:S(2)}) collective-permute-start(bf16[256,3072]{1,0:T(8,128)(2,1)S(1)} %get-tuple-element.53.refs_2_), channel_id=1, source_target_pairs={{0,32},{1,33},{2,34},{3,35},{4,36},{5,37},{6,38},{7,39},{8,40},{9,... | collective-permute-start | bytes 4718600 | tf_op jit(solution)/shard_map/ppermute | solution.py:413
  67.3 3.2 %project.2.refs_0_ = f32[768,1920]{1,0:T(8,128)S(1)} custom-call(bf16[768,1536]{1,0:T(8,128)(2,1)S(1)} %fusion.2.tokens_ref, bf16[256,1920]{1,0:T(8,128)(2,1)S(1)} %get-tuple-element.40.refs_0_, bf16[256,1920]{1,0:T(8,128)(2,1)S(1)} %get-tuple-element.41.refs_1_, bf16[256,1920]{1,0:T(8,128)(2,1)S(1)} %get-tuple-element.43.refs_2_), custom_call_target="tpu_custom_call" | custom-call | flops 2264924160 | bytes 10485760 | tf_op jit(solution)/shard_map/project/pallas_call | solution.py:289
  70.5 4.7 %collective-permute-done.10.refs_1_ = bf16[256,1920]{1,0:T(8,128)(2,1)S(1)} collective-permute-done((bf16[256,1920]{1,0:T(8,128)(2,1)S(1)}, bf16[256,1920]{1,0:T(8,128)(2,1)S(1)}, u32[]{:S(2)}, u32[]{:S(2)}) %collective-permute-start.10) | collective-permute-done | bytes 983072 | tf_op jit(solution)/shard_map/ppermute | solution.py:413
  75.3 2.1 %collective-permute-start.21 = (bf16[256,3072]{1,0:T(8,128)(2,1)S(1)}, bf16[256,3072]{1,0:T(8,128)(2,1)S(1)}, u32[]{:S(2)}, u32[]{:S(2)}) collective-permute-start(bf16[256,3072]{1,0:T(8,128)(2,1)S(1)} %get-tuple-element.52.refs_0_), channel_id=1, source_target_pairs={{0,1},{1,0},{2,3},{3,2},{4,5},{5,4},{6,7},{7,6},{8,9},{9,8},{10,11... | collective-permute-start | bytes 4718600 | tf_op jit(solution)/shard_map/ppermute | solution.py:413
  78.8 3.2 %project.3.projected_ref = bf16[768,1920]{1,0:T(8,128)(2,1)S(1)} custom-call(bf16[768,1536]{1,0:T(8,128)(2,1)S(1)} %fusion.2.tokens_ref, f32[768,1920]{1,0:T(8,128)S(1)} %project.2.refs_0_, bf16[256,1920]{1,0:T(8,128)(2,1)S(1)} %collective-permute-done.10.refs_1_, bf16[256,1920]{1,0:T(8,128)(2,1)S(1)} %collective-permute-done.18.refs_2_, ...), custom_call_target="tpu_custom_call" | custom-call | flops 2264924160 | bytes 10485760 | tf_op jit(solution)/shard_map/project/pallas_call | solution.py:289
  82.1 6.1 %scan.2 = (f32[384,1536]{1,0:T(8,128)S(1)}, f32[1536,128]{1,0:T(8,128)S(1)}) custom-call(s32[2]{0:T(128)S(1)} %copy-done.2, bf16[12,4992]{1,0:T(8,128)(2,1)S(1)} %collective-permute-done.shard_ref, bf16[768,1920]{1,0:T(8,128)(2,1)S(1)} %project.3.projected_ref, f32[4,3328]{1,0:T(4,128)S(1)} %copy-done.3, f32[1,48]{1,0:T(1,128)S(1)} %bitcast.11, ...), custom_call_target="tpu_custom_call" | custom-call | flops 754974720 | bytes 5242880 | tf_op jit(solution)/shard_map/scan/pallas_call | solution.py:177
  88.3 1.8 %collective-permute-start.20 = (f32[1536,128]{1,0:T(8,128)S(1)}, f32[1536,128]{1,0:T(8,128)S(1)}, u32[]{:S(2)}, u32[]{:S(2)}) collective-permute-start(f32[1536,128]{1,0:T(8,128)S(1)} %get-tuple-element.50), channel_id=1, source_target_pairs={{0,16},{1,17},{2,18},{3,19},{4,20},{5,21},{6,22},{7,23},{8,24},{9,... | collective-permute-start | bytes 2359304 | tf_op jit(solution)/shard_map/ppermute | solution.py:413
  90.1 6.1 %scan.3 = (f32[384,1536]{1,0:T(8,128)S(1)}, f32[1536,128]{1,0:T(8,128)S(1)}) custom-call(s32[2]{0:T(128)S(1)} %copy-done.2, bf16[12,4992]{1,0:T(8,128)(2,1)S(1)} %copy-done, bf16[768,1920]{1,0:T(8,128)(2,1)S(1)} %project.3.projected_ref, f32[4,3328]{1,0:T(4,128)S(1)} %copy-done.3, f32[1,48]{1,0:T(1,128)S(1)} %bitcast.12, f32[1,48]{1,0:T(1,128)S(1)} %bitcast.14, ...), custom_call_target="tpu_custom_call" | custom-call | flops 754974720 | bytes 5242880 | tf_op jit(solution)/shard_map/scan/pallas_call | solution.py:177
  96.3 5.2 %out_share.3 = (f32[1536,384]{1,0:T(8,128)S(1)}, f32[384,128]{1,0:T(8,128)S(1)}) custom-call(s32[2]{0:T(128)S(1)} %copy-done.2, s32[192]{0:T(256)S(1)} %multiply_add_fusion.places_ref, bf16[768,1536]{1,0:T(8,128)(2,1)S(1)} %fusion.2.tokens_ref, f32[384,1536]{1,0:T(8,128)S(1)} %get-tuple-element.56.scanned_ref, f32[1,3072]{1,0:T(1,128)S(1)} %bitcast.9, ...), custom_call_target="tpu_custom_call" | custom-call | flops 3623878656 | bytes 16777216 | tf_op jit(solution)/shard_map/out_share/pallas_call | solution.py:342
  101.5 1.6 %collective-permute-start.24 = (f32[1536,384]{1,0:T(8,128)S(1)}, f32[1536,384]{1,0:T(8,128)S(1)}, u32[]{:S(2)}, u32[]{:S(2)}) collective-permute-start(f32[1536,384]{1,0:T(8,128)S(1)} %get-tuple-element.57), channel_id=1, source_target_pairs={{0,16},{1,17},{2,18},{3,19},{4,20},{5,21},{6,22},{7,23},{8,24},{9,... | collective-permute-start | bytes 7077896 | tf_op jit(solution)/shard_map/ppermute | solution.py:413
  104.6 5.2 %out_share.2 = (f32[1536,384]{1,0:T(8,128)S(1)}, f32[384,128]{1,0:T(8,128)S(1)}) custom-call(s32[2]{0:T(128)S(1)} %copy-done.2, s32[192]{0:T(256)S(1)} %multiply_add_fusion.places_ref, bf16[768,1536]{1,0:T(8,128)(2,1)S(1)} %fusion.2.tokens_ref, f32[384,1536]{1,0:T(8,128)S(1)} %get-tuple-element.51.scanned_ref, f32[1,3072]{1,0:T(1,128)S(1)} %bitcast.10, ...), custom_call_target="tpu_custom_call" | custom-call | flops 3623878656 | bytes 16777216 | tf_op jit(solution)/shard_map/out_share/pallas_call | solution.py:342
  109.8 2.2 %mix.1 = bf16[384,1536]{1,0:T(8,128)(2,1)} custom-call(bf16[12,4992]{1,0:T(8,128)(2,1)S(1)} %copy-done, f32[1536,384]{1,0:T(8,128)S(1)} %get-tuple-element.55.mine_ref, f32[1536,384]{1,0:T(8,128)S(1)} %collective-permute-done.24.other_ref, f32[384,128]{1,0:T(8,128)S(1)} %get-tuple-element.58.sq_mine, f32[384,128]{1,0:T(8,128)S(1)} %collective-permute-done.25.sq_other, ...), custom_call_target="tpu_custom_call" | custom-call | flops 452984832 | bytes 8388608 | tf_op jit(solution)/shard_map/mix/pallas_call | solution.py:384
  (76 shorter events, 17.3 us)
Async XLA Ops:
  6.8 9.1 %collective-permute-start.6 = (bf16[8,4992]{1,0:T(8,128)(2,1)S(1)}, bf16[8,4992]{1,0:T(8,128)(2,1)S(1)}, u32[]{:S(2)}, u32[]{:S(2)}) collective-permute-start(bf16[8,4992]{1,0:T(8,128)(2,1)S(1)} %get-tuple-element.68), channel_id=1, source_target_pairs={{0,32},{1,33},{2,34},{3,35},{4,36},{5,37},{6,38},{7,39},{8,40},{9,... | collective-permute-start | bytes 239624 | tf_op jit(solution)/shard_map/ppermute | solution.py:413
  10.8 5.3 %collective-permute-start.11 = (bf16[8,4992]{1,0:T(8,128)(2,1)S(1)}, bf16[8,4992]{1,0:T(8,128)(2,1)S(1)}, u32[]{:S(2)}, u32[]{:S(2)}) collective-permute-start(bf16[8,4992]{1,0:T(8,128)(2,1)S(1)} %get-tuple-element.66), channel_id=1, source_target_pairs={{0,1},{1,0},{2,3},{3,2},{4,5},{5,4},{6,7},{7,6},{8,9},{9,8},{10,11... | collective-permute-start | bytes 239624 | tf_op jit(solution)/shard_map/ppermute | solution.py:413
  16.0 5.7 %collective-permute-start.7 = (bf16[16,4992]{1,0:T(8,128)(2,1)S(1)}, bf16[16,4992]{1,0:T(8,128)(2,1)S(1)}, u32[]{:S(2)}, u32[]{:S(2)}) collective-permute-start(bf16[16,4992]{1,0:T(8,128)(2,1)S(1)} %pad_maximum_fusion.8), channel_id=1, source_target_pairs={{0,1},{1,0},{2,3},{3,2},{4,5},{5,4},{6,7},{7,6},{8,9},{9,8},{10,11... | collective-permute-start | bytes 479240 | tf_op jit(solution)/shard_map/ppermute | solution.py:413
  16.1 5.7 %collective-permute-start.12 = (bf16[16,4992]{1,0:T(8,128)(2,1)S(1)}, bf16[16,4992]{1,0:T(8,128)(2,1)S(1)}, u32[]{:S(2)}, u32[]{:S(2)}) collective-permute-start(bf16[16,4992]{1,0:T(8,128)(2,1)S(1)} %pad_maximum_fusion.9), channel_id=1, source_target_pairs={{0,4},{1,5},{2,6},{3,7},{4,0},{5,1},{6,2},{7,3},{8,12},{9,13},{10,... | collective-permute-start | bytes 479240 | tf_op jit(solution)/shard_map/ppermute | solution.py:413
  18.0 4.5 %collective-permute-start.2 = (bf16[16,4992]{1,0:T(8,128)(2,1)S(1)}, bf16[16,4992]{1,0:T(8,128)(2,1)S(1)}, u32[]{:S(2)}, u32[]{:S(2)}) collective-permute-start(bf16[16,4992]{1,0:T(8,128)(2,1)S(1)} %pad_maximum_fusion.7), channel_id=1, source_target_pairs={{0,96},{1,97},{2,98},{3,99},{4,100},{5,101},{6,102},{7,103},{8,104... | collective-permute-start | bytes 479240 | tf_op jit(solution)/shard_map/ppermute | solution.py:413
  21.7 7.4 %collective-permute-start.8 = (bf16[32,4992]{1,0:T(8,128)(2,1)S(1)}, bf16[32,4992]{1,0:T(8,128)(2,1)S(1)}, u32[]{:S(2)}, u32[]{:S(2)}) collective-permute-start(bf16[32,4992]{1,0:T(8,128)(2,1)S(1)} %pad_maximum_fusion.5), channel_id=1, source_target_pairs={{0,4},{1,5},{2,6},{3,7},{4,0},{5,1},{6,2},{7,3},{8,12},{9,13},{10,... | collective-permute-start | bytes 958472 | tf_op jit(solution)/shard_map/ppermute | solution.py:413
  21.9 10.3 %collective-permute-start.13 = (bf16[32,4992]{1,0:T(8,128)(2,1)S(1)}, bf16[32,4992]{1,0:T(8,128)(2,1)S(1)}, u32[]{:S(2)}, u32[]{:S(2)}) collective-permute-start(bf16[32,4992]{1,0:T(8,128)(2,1)S(1)} %pad_maximum_fusion.6), channel_id=1, source_target_pairs={{0,96},{1,97},{2,98},{3,99},{4,100},{5,101},{6,102},{7,103},{8,104... | collective-permute-start | bytes 958472 | tf_op jit(solution)/shard_map/ppermute | solution.py:413
  22.5 9.1 %collective-permute-start.3 = (bf16[32,4992]{1,0:T(8,128)(2,1)S(1)}, bf16[32,4992]{1,0:T(8,128)(2,1)S(1)}, u32[]{:S(2)}, u32[]{:S(2)}) collective-permute-start(bf16[32,4992]{1,0:T(8,128)(2,1)S(1)} %pad_maximum_fusion.4), channel_id=1, source_target_pairs={{0,3},{1,2},{2,1},{3,0},{4,7},{5,6},{6,5},{7,4},{8,11},{9,10},{10,... | collective-permute-start | bytes 958472 | tf_op jit(solution)/shard_map/ppermute | solution.py:413
  29.2 13.0 %collective-permute-start.16 = (bf16[64,4992]{1,0:T(8,128)(2,1)S(1)}, bf16[64,4992]{1,0:T(8,128)(2,1)S(1)}, u32[]{:S(2)}, u32[]{:S(2)}) collective-permute-start(bf16[64,4992]{1,0:T(8,128)(2,1)S(1)} %pad_maximum_fusion.2.held_ref), channel_id=1, source_target_pairs={{0,96},{1,97},{2,98},{3,99},{4,100},{5,101},{6,102},{7,103},{8,104... | collective-permute-start | bytes 1916936 | tf_op jit(solution)/shard_map/ppermute | solution.py:413
  31.7 13.1 %collective-permute-start.9 = (bf16[384,1536]{1,0:T(8,128)(2,1)}, bf16[384,1536]{1,0:T(8,128)(2,1)}, u32[]{:S(2)}, u32[]{:S(2)}) collective-permute-start(bf16[384,1536]{1,0:T(8,128)(2,1)} %dynamic-slice_bitcast_fusion), channel_id=1, source_target_pairs={{0,16},{1,17},{2,18},{3,19},{4,20},{5,21},{6,22},{7,23},{8,24},{9,... | collective-permute-start | bytes 3538952 | tf_op jit(solution)/shard_map/ppermute | solution.py:413
  31.7 9.7 %collective-permute-start.4 = (bf16[64,4992]{1,0:T(8,128)(2,1)S(1)}, bf16[64,4992]{1,0:T(8,128)(2,1)S(1)}, u32[]{:S(2)}, u32[]{:S(2)}) collective-permute-start(bf16[64,4992]{1,0:T(8,128)(2,1)S(1)} %pad_maximum_fusion.1.held_ref), channel_id=1, source_target_pairs={{0,12},{1,13},{2,14},{3,15},{4,8},{5,9},{6,10},{7,11},{8,4},{9,5},... | collective-permute-start | bytes 1916936 | tf_op jit(solution)/shard_map/ppermute | solution.py:413
  32.2 10.2 %collective-permute-start.14 = (bf16[64,4992]{1,0:T(8,128)(2,1)S(1)}, bf16[64,4992]{1,0:T(8,128)(2,1)}, u32[]{:S(2)}, u32[]{:S(2)}) collective-permute-start(bf16[64,4992]{1,0:T(8,128)(2,1)S(1)} %pad_maximum_fusion.3.held_ref), channel_id=1, source_target_pairs={{0,3},{1,2},{2,1},{3,0},{4,7},{5,6},{6,5},{7,4},{8,11},{9,10},{10,... | collective-permute-start | bytes 1916936 | tf_op jit(solution)/shard_map/ppermute | solution.py:413
  41.6 17.7 %collective-permute-start.5 = (bf16[128,4992]{1,0:T(8,128)(2,1)S(1)}, bf16[128,4992]{1,0:T(8,128)(2,1)}, u32[]{:S(2)}, u32[]{:S(2)}) collective-permute-start(bf16[128,4992]{1,0:T(8,128)(2,1)S(1)} %join.6.held_ref), channel_id=1, source_target_pairs={{0,32},{1,33},{2,34},{3,35},{4,36},{5,37},{6,38},{7,39},{8,40},{9,... | collective-permute-start | bytes 3833864 | tf_op jit(solution)/shard_map/ppermute | solution.py:413
  42.3 20.4 %collective-permute-start.17 = (bf16[128,4992]{1,0:T(8,128)(2,1)S(1)}, bf16[128,4992]{1,0:T(8,128)(2,1)S(1)}, u32[]{:S(2)}, u32[]{:S(2)}) collective-permute-start(bf16[128,4992]{1,0:T(8,128)(2,1)S(1)} %join.10.held_ref), channel_id=1, source_target_pairs={{0,3},{1,2},{2,1},{3,0},{4,7},{5,6},{6,5},{7,4},{8,11},{9,10},{10,... | collective-permute-start | bytes 3833864 | tf_op jit(solution)/shard_map/ppermute | solution.py:413
  43.5 20.6 %collective-permute-start.15 = (bf16[128,4992]{1,0:T(8,128)(2,1)S(1)}, bf16[128,4992]{1,0:T(8,128)(2,1)S(1)}, u32[]{:S(2)}, u32[]{:S(2)}) collective-permute-start(bf16[128,4992]{1,0:T(8,128)(2,1)S(1)} %join.8.held_ref), channel_id=1, source_target_pairs={{0,12},{1,13},{2,14},{3,15},{4,8},{5,9},{6,10},{7,11},{8,4},{9,5},... | collective-permute-start | bytes 3833864 | tf_op jit(solution)/shard_map/ppermute | solution.py:413
  60.7 14.5 %collective-permute-start.10 = (bf16[256,1920]{1,0:T(8,128)(2,1)S(1)}, bf16[256,1920]{1,0:T(8,128)(2,1)S(1)}, u32[]{:S(2)}, u32[]{:S(2)}) collective-permute-start(bf16[256,1920]{1,0:T(8,128)(2,1)S(1)} %get-tuple-element.40.refs_0_), channel_id=1, source_target_pairs={{0,1},{1,0},{2,3},{3,2},{4,5},{5,4},{6,7},{7,6},{8,9},{9,8},{10,11... | collective-permute-start | bytes 2949128 | tf_op jit(solution)/shard_map/ppermute | solution.py:413
  62.8 14.6 %collective-permute-start.19 = (bf16[256,1920]{1,0:T(8,128)(2,1)S(1)}, bf16[256,1920]{1,0:T(8,128)(2,1)S(1)}, u32[]{:S(2)}, u32[]{:S(2)}) collective-permute-start(bf16[256,1920]{1,0:T(8,128)(2,1)S(1)} %get-tuple-element.43.refs_2_), channel_id=1, source_target_pairs={{0,12},{1,13},{2,14},{3,15},{4,8},{5,9},{6,10},{7,11},{8,4},{9,5},... | collective-permute-start | bytes 2949128 | tf_op jit(solution)/shard_map/ppermute | solution.py:413
  64.3 14.5 %collective-permute-start.18 = (bf16[256,1920]{1,0:T(8,128)(2,1)S(1)}, bf16[256,1920]{1,0:T(8,128)(2,1)S(1)}, u32[]{:S(2)}, u32[]{:S(2)}) collective-permute-start(bf16[256,1920]{1,0:T(8,128)(2,1)S(1)} %get-tuple-element.41.refs_1_), channel_id=1, source_target_pairs={{0,32},{1,33},{2,34},{3,35},{4,36},{5,37},{6,38},{7,39},{8,40},{9,... | collective-permute-start | bytes 2949128 | tf_op jit(solution)/shard_map/ppermute | solution.py:413
  64.4 31.8 %collective-permute-start.23 = (bf16[256,3072]{1,0:T(8,128)(2,1)S(1)}, bf16[256,3072]{1,0:T(8,128)(2,1)S(1)}, u32[]{:S(2)}, u32[]{:S(2)}) collective-permute-start(bf16[256,3072]{1,0:T(8,128)(2,1)S(1)} %get-tuple-element.54.refs_4_), channel_id=1, source_target_pairs={{0,12},{1,13},{2,14},{3,15},{4,8},{5,9},{6,10},{7,11},{8,4},{9,5},... | collective-permute-start | bytes 4718600 | tf_op jit(solution)/shard_map/ppermute | solution.py:413
  64.7 31.5 %collective-permute-start.22 = (bf16[256,3072]{1,0:T(8,128)(2,1)S(1)}, bf16[256,3072]{1,0:T(8,128)(2,1)S(1)}, u32[]{:S(2)}, u32[]{:S(2)}) collective-permute-start(bf16[256,3072]{1,0:T(8,128)(2,1)S(1)} %get-tuple-element.53.refs_2_), channel_id=1, source_target_pairs={{0,32},{1,33},{2,34},{3,35},{4,36},{5,37},{6,38},{7,39},{8,40},{9,... | collective-permute-start | bytes 4718600 | tf_op jit(solution)/shard_map/ppermute | solution.py:413
  75.3 21.0 %collective-permute-start.21 = (bf16[256,3072]{1,0:T(8,128)(2,1)S(1)}, bf16[256,3072]{1,0:T(8,128)(2,1)S(1)}, u32[]{:S(2)}, u32[]{:S(2)}) collective-permute-start(bf16[256,3072]{1,0:T(8,128)(2,1)S(1)} %get-tuple-element.52.refs_0_), channel_id=1, source_target_pairs={{0,1},{1,0},{2,3},{3,2},{4,5},{5,4},{6,7},{7,6},{8,9},{9,8},{10,11... | collective-permute-start | bytes 4718600 | tf_op jit(solution)/shard_map/ppermute | solution.py:413
  88.3 7.9 %collective-permute-start.20 = (f32[1536,128]{1,0:T(8,128)S(1)}, f32[1536,128]{1,0:T(8,128)S(1)}, u32[]{:S(2)}, u32[]{:S(2)}) collective-permute-start(f32[1536,128]{1,0:T(8,128)S(1)} %get-tuple-element.50), channel_id=1, source_target_pairs={{0,16},{1,17},{2,18},{3,19},{4,20},{5,21},{6,22},{7,23},{8,24},{9,... | collective-permute-start | bytes 2359304 | tf_op jit(solution)/shard_map/ppermute | solution.py:413
  101.5 8.3 %collective-permute-start.24 = (f32[1536,384]{1,0:T(8,128)S(1)}, f32[1536,384]{1,0:T(8,128)S(1)}, u32[]{:S(2)}, u32[]{:S(2)}) collective-permute-start(f32[1536,384]{1,0:T(8,128)S(1)} %get-tuple-element.57), channel_id=1, source_target_pairs={{0,16},{1,17},{2,18},{3,19},{4,20},{5,21},{6,22},{7,23},{8,24},{9,... | collective-permute-start | bytes 7077896 | tf_op jit(solution)/shard_map/ppermute | solution.py:413
  104.6 5.2 %collective-permute-start.25 = (f32[384,128]{1,0:T(8,128)S(1)}, f32[384,128]{1,0:T(8,128)S(1)}, u32[]{:S(2)}, u32[]{:S(2)}) collective-permute-start(f32[384,128]{1,0:T(8,128)S(1)} %get-tuple-element.59), channel_id=1, source_target_pairs={{0,16},{1,17},{2,18},{3,19},{4,20},{5,21},{6,22},{7,23},{8,24},{9,... | collective-permute-start | bytes 589832 | tf_op jit(solution)/shard_map/ppermute | solution.py:413
  (9 other events, 57.2 us)

commit v14 on v13

--- a/solution.py
+++ b/solution.py
@@ -494,7 +494,7 @@
     held = [pair[8 * c : 8 * c + 8] for c in range(COLOURS)]
     for step in range(3):
         held = joined(held, moved_over(held, step))
-    held[2], unit_id = lax.optimization_barrier((held[2], unit_id))
+    held[0], unit_id = lax.optimization_barrier((held[0], unit_id))
     held = [join(h, m, cut + 2 * half)[0] for h, m in zip(held, moved_over(held, 3))]
     moved = moved_over(held, 4)
 

time: 112 us -> 118 us (1.054)
  starting transfers between devices: 28.6 us -> 34.1 us
  waiting for transfers between devices: 34.5 us -> 32.9 us
    ppermute x26, starting transfers between devices: 28.6 us -> 34.1 us  [hop(): lax.ppermute(value, EVERYONE, [(d, d ^ mask_of(d // CORE % 2)) for d in r...]
    ppermute x26, waiting for transfers between devices: 34.5 us -> 32.9 us  [hop(): lax.ppermute(value, EVERYONE, [(d, d ^ mask_of(d // CORE % 2)) for d in r...]
  transfers between devices with their start and end apart: 26 -> 26, of which waited for: 9 -> 8; matrix products, arithmetic and copies ran while one was open for 9% -> 9% of each run, Pallas kernels for 24% -> 24%
where the time goes in v14:
time: 118 us
  Pallas kernels  37.4 us (32%)
  starting transfers between devices  34.1 us (29%)
  waiting for transfers between devices  32.9 us (28%)
  matrix products  5.78 us (5%)
  other arithmetic  4.38 us (4%)
  local copies, waits for them, and re-layouts  2.39 us (2%)
    ppermute x26, starting transfers between devices, hop(): lax.ppermute(value, EVERYONE, [(d, d ^ mask_of(d // CORE % 2)) for d in r...  34.1 us
    ppermute x26, waiting for transfers between devices, hop(): lax.ppermute(value, EVERYONE, [(d, d ^ mask_of(d // CORE % 2)) for d in r...  32.9 us
    pallas_call x2, Pallas kernels, scan(): pl.pallas_call(functools.partial(scan_kernel, which), in_specs=[scalars]...  12.2 us
    pallas_call x2, Pallas kernels, out_share(): pl.pallas_call(functools.partial(share_kernel, which), in_specs=[scalars]...  10.4 us
    pallas_call x2, Pallas kernels, project(): pl.pallas_call(functools.partial(project_kernel, first), in_specs=[whole]...  6.42 us
    dot_general x1, matrix products, body(): both = jnp.dot(both, pick.astype(BF), preferred_element_type=F32).astype(BF)  5.78 us
    pallas_call x6, Pallas kernels, join(): pl.pallas_call(join_kernel, in_specs=[whole] * 2, out_specs=[whole] * len...  4.23 us
  transfers between devices with their start and end apart: 26, of which 8 were waited for; matrix products, arithmetic and copies ran while one was open for 9% of the time, Pallas kernels for 24%

profile of v14, /device:TPU:1, one launch (start us, length us, event | category | flops | bytes accessed | tf_op | source)
XLA Modules:
  0.0 117.9 jit_solution(13849388697213974056)
XLA Ops:
  1.3 1.9 %shards.1 = (bf16[12,4992]{1,0:T(8,128)(2,1)}, bf16[12,4992]{1,0:T(8,128)(2,1)}) custom-call(s32[2]{0:T(128)} %pad_add_fusion.meta_ref, s32[16]{0:T(128)} %lengths_ref.1, f32[12,3072]{1,0:T(8,128)} %input_ref.1, f32[12,256]{1,0:T(8,128)} %state_ref.1, f32[12,48]{1,0:T(8,128)} %step_ref.1, f32[12,3072]{1,0:T(8,128)} %gate_ref.1, f32[12,3072]{1,0:T(8,128)} %out_ref.1), custom_call_target="tpu_custom_call" | custom-call | tf_op jit(solution)/shard_map/shards/pallas_call | solution.py:227
  6.8 3.9 %collective-permute-start.13 = (bf16[8,4992]{1,0:T(8,128)(2,1)S(1)}, bf16[8,4992]{1,0:T(8,128)(2,1)S(1)}, u32[]{:S(2)}, u32[]{:S(2)}) collective-permute-start(bf16[8,4992]{1,0:T(8,128)(2,1)S(1)} %get-tuple-element.66), channel_id=1, source_target_pairs={{0,32},{1,33},{2,34},{3,35},{4,36},{5,37},{6,38},{7,39},{8,40},{9,... | collective-permute-start | bytes 239624 | tf_op jit(solution)/shard_map/ppermute | solution.py:413
  10.8 2.7 %collective-permute-start.8 = (bf16[8,4992]{1,0:T(8,128)(2,1)S(1)}, bf16[8,4992]{1,0:T(8,128)(2,1)S(1)}, u32[]{:S(2)}, u32[]{:S(2)}) collective-permute-start(bf16[8,4992]{1,0:T(8,128)(2,1)S(1)} %get-tuple-element.67), channel_id=1, source_target_pairs={{0,1},{1,0},{2,3},{3,2},{4,5},{5,4},{6,7},{7,6},{8,9},{9,8},{10,11... | collective-permute-start | bytes 239624 | tf_op jit(solution)/shard_map/ppermute | solution.py:413
  13.5 2.5 %collective-permute-start.1 = (bf16[8,4992]{1,0:T(8,128)(2,1)S(1)}, bf16[8,4992]{1,0:T(8,128)(2,1)S(1)}, u32[]{:S(2)}, u32[]{:S(2)}) collective-permute-start(bf16[8,4992]{1,0:T(8,128)(2,1)S(1)} %get-tuple-element.68), channel_id=1, source_target_pairs={{0,4},{1,5},{2,6},{3,7},{4,0},{5,1},{6,2},{7,3},{8,12},{9,13},{10,... | collective-permute-start | bytes 239624 | tf_op jit(solution)/shard_map/ppermute | solution.py:413
  16.1 1.9 %collective-permute-start.9 = (bf16[16,4992]{1,0:T(8,128)(2,1)S(1)}, bf16[16,4992]{1,0:T(8,128)(2,1)S(1)}, u32[]{:S(2)}, u32[]{:S(2)}) collective-permute-start(bf16[16,4992]{1,0:T(8,128)(2,1)S(1)} %pad_maximum_fusion.8), channel_id=1, source_target_pairs={{0,4},{1,5},{2,6},{3,7},{4,0},{5,1},{6,2},{7,3},{8,12},{9,13},{10,... | collective-permute-start | bytes 479240 | tf_op jit(solution)/shard_map/ppermute | solution.py:413
  18.1 3.6 %collective-permute-done.14 = bf16[16,4992]{1,0:T(8,128)(2,1)S(1)} collective-permute-done((bf16[16,4992]{1,0:T(8,128)(2,1)S(1)}, bf16[16,4992]{1,0:T(8,128)(2,1)S(1)}, u32[]{:S(2)}, u32[]{:S(2)}) %collective-permute-start.14) | collective-permute-done | bytes 159776 | tf_op jit(solution)/shard_map/ppermute | solution.py:413
  22.6 6.5 %collective-permute-done.15 = bf16[32,4992]{1,0:T(8,128)(2,1)S(1)} collective-permute-done((bf16[32,4992]{1,0:T(8,128)(2,1)S(1)}, bf16[32,4992]{1,0:T(8,128)(2,1)S(1)}, u32[]{:S(2)}, u32[]{:S(2)}) %collective-permute-start.15) | collective-permute-done | bytes 319520 | tf_op jit(solution)/shard_map/ppermute | solution.py:413
  29.8 2.4 %dynamic-slice_bitcast_fusion = bf16[384,1536]{1,0:T(8,128)(2,1)} fusion(bf16[16,384,1536]{2,1,0:T(8,128)(2,1)} %param.12, s32[]{:T(128)S(6)} %select_n.464), kind=kLoop, calls=%fused_computation.8 | loop fusion | bytes 2359300 | tf_op jit(solution)/shard_map/jit(dynamic_index_in_dim)/squeeze | solution.py:501
  32.2 4.3 %collective-permute-start.6 = (bf16[384,1536]{1,0:T(8,128)(2,1)}, bf16[384,1536]{1,0:T(8,128)(2,1)}, u32[]{:S(2)}, u32[]{:S(2)}) collective-permute-start(bf16[384,1536]{1,0:T(8,128)(2,1)} %dynamic-slice_bitcast_fusion), channel_id=1, source_target_pairs={{0,16},{1,17},{2,18},{3,19},{4,20},{5,21},{6,22},{7,23},{8,24},{9,... | collective-permute-start | bytes 3538952 | tf_op jit(solution)/shard_map/ppermute | solution.py:413
  37.8 8.3 %collective-permute-done.4.moved_ref = bf16[64,4992]{1,0:T(8,128)(2,1)S(1)} collective-permute-done((bf16[64,4992]{1,0:T(8,128)(2,1)S(1)}, bf16[64,4992]{1,0:T(8,128)(2,1)S(1)}, u32[]{:S(2)}, u32[]{:S(2)}) %collective-permute-start.4) | collective-permute-done | bytes 639008 | tf_op jit(solution)/shard_map/ppermute | solution.py:413
  50.4 5.8 %fusion.2.tokens_ref = bf16[768,1536]{1,0:T(8,128)(2,1)S(1)} fusion(s32[1536]{0:T(1024)S(1)} %select_subtract_fusion, bf16[384,1536]{1,0:T(8,128)(2,1)} %collective-permute-done.6, bf16[384,1536]{1,0:T(8,128)(2,1)} %dynamic-slice_bitcast_fusion), kind=kOutput, calls=%fused_computation.3 | convolution fusion | flops 3632136192 | bytes 4724736 | tf_op jit(solution)/shard_map/dot_general | solution.py:504
  56.2 7.8 %collective-permute-done.5.moved_ref = bf16[128,4992]{1,0:T(8,128)(2,1)} collective-permute-done((bf16[128,4992]{1,0:T(8,128)(2,1)S(1)}, bf16[128,4992]{1,0:T(8,128)(2,1)}, u32[]{:S(2)}, u32[]{:S(2)}) %collective-permute-start.5) | collective-permute-done | bytes 1277984 | tf_op jit(solution)/shard_map/ppermute | solution.py:413
  65.4 2.0 %collective-permute-start.7 = (bf16[256,1920]{1,0:T(8,128)(2,1)S(1)}, bf16[256,1920]{1,0:T(8,128)(2,1)S(1)}, u32[]{:S(2)}, u32[]{:S(2)}) collective-permute-start(bf16[256,1920]{1,0:T(8,128)(2,1)S(1)} %get-tuple-element.41.refs_0_), channel_id=1, source_target_pairs={{0,1},{1,0},{2,3},{3,2},{4,5},{5,4},{6,7},{7,6},{8,9},{9,8},{10,11... | collective-permute-start | bytes 2949128 | tf_op jit(solution)/shard_map/ppermute | solution.py:413
  70.4 1.7 %collective-permute-start.22 = (bf16[256,3072]{1,0:T(8,128)(2,1)S(1)}, bf16[256,3072]{1,0:T(8,128)(2,1)S(1)}, u32[]{:S(2)}, u32[]{:S(2)}) collective-permute-start(bf16[256,3072]{1,0:T(8,128)(2,1)S(1)} %get-tuple-element.53.refs_2_), channel_id=1, source_target_pairs={{0,32},{1,33},{2,34},{3,35},{4,36},{5,37},{6,38},{7,39},{8,40},{9,... | collective-permute-start | bytes 4718600 | tf_op jit(solution)/shard_map/ppermute | solution.py:413
  72.0 3.2 %project.2.refs_0_ = f32[768,1920]{1,0:T(8,128)S(1)} custom-call(bf16[768,1536]{1,0:T(8,128)(2,1)S(1)} %fusion.2.tokens_ref, bf16[256,1920]{1,0:T(8,128)(2,1)S(1)} %get-tuple-element.41.refs_0_, bf16[256,1920]{1,0:T(8,128)(2,1)S(1)} %get-tuple-element.42.refs_1_, bf16[256,1920]{1,0:T(8,128)(2,1)S(1)} %get-tuple-element.43.refs_2_), custom_call_target="tpu_custom_call" | custom-call | flops 2264924160 | bytes 10485760 | tf_op jit(solution)/shard_map/project/pallas_call | solution.py:289
  75.2 4.7 %collective-permute-done.7.refs_1_ = bf16[256,1920]{1,0:T(8,128)(2,1)S(1)} collective-permute-done((bf16[256,1920]{1,0:T(8,128)(2,1)S(1)}, bf16[256,1920]{1,0:T(8,128)(2,1)S(1)}, u32[]{:S(2)}, u32[]{:S(2)}) %collective-permute-start.7) | collective-permute-done | bytes 983072 | tf_op jit(solution)/shard_map/ppermute | solution.py:413
  80.0 2.2 %collective-permute-start.21 = (bf16[256,3072]{1,0:T(8,128)(2,1)S(1)}, bf16[256,3072]{1,0:T(8,128)(2,1)S(1)}, u32[]{:S(2)}, u32[]{:S(2)}) collective-permute-start(bf16[256,3072]{1,0:T(8,128)(2,1)S(1)} %get-tuple-element.52.refs_0_), channel_id=1, source_target_pairs={{0,1},{1,0},{2,3},{3,2},{4,5},{5,4},{6,7},{7,6},{8,9},{9,8},{10,11... | collective-permute-start | bytes 4718600 | tf_op jit(solution)/shard_map/ppermute | solution.py:413
  82.6 3.2 %project.3.projected_ref = bf16[768,1920]{1,0:T(8,128)(2,1)S(1)} custom-call(bf16[768,1536]{1,0:T(8,128)(2,1)S(1)} %fusion.2.tokens_ref, f32[768,1920]{1,0:T(8,128)S(1)} %project.2.refs_0_, bf16[256,1920]{1,0:T(8,128)(2,1)S(1)} %collective-permute-done.7.refs_1_, bf16[256,1920]{1,0:T(8,128)(2,1)S(1)} %collective-permute-done.18.refs_2_, ...), custom_call_target="tpu_custom_call" | custom-call | flops 2264924160 | bytes 10485760 | tf_op jit(solution)/shard_map/project/pallas_call | solution.py:289
  85.9 6.1 %scan.2 = (f32[384,1536]{1,0:T(8,128)S(1)}, f32[1536,128]{1,0:T(8,128)S(1)}) custom-call(s32[2]{0:T(128)S(1)} %copy-done.2, bf16[12,4992]{1,0:T(8,128)(2,1)S(1)} %collective-permute-done.shard_ref, bf16[768,1920]{1,0:T(8,128)(2,1)S(1)} %project.3.projected_ref, f32[4,3328]{1,0:T(4,128)S(1)} %copy-done.3, f32[1,48]{1,0:T(1,128)S(1)} %bitcast.11, ...), custom_call_target="tpu_custom_call" | custom-call | flops 754974720 | bytes 5242880 | tf_op jit(solution)/shard_map/scan/pallas_call | solution.py:177
  92.0 4.3 %collective-permute-start.20 = (f32[1536,128]{1,0:T(8,128)S(1)}, f32[1536,128]{1,0:T(8,128)S(1)}, u32[]{:S(2)}, u32[]{:S(2)}) collective-permute-start(f32[1536,128]{1,0:T(8,128)S(1)} %get-tuple-element.50), channel_id=1, source_target_pairs={{0,16},{1,17},{2,18},{3,19},{4,20},{5,21},{6,22},{7,23},{8,24},{9,... | collective-permute-start | bytes 2359304 | tf_op jit(solution)/shard_map/ppermute | solution.py:413
  96.3 6.1 %scan.3 = (f32[384,1536]{1,0:T(8,128)S(1)}, f32[1536,128]{1,0:T(8,128)S(1)}) custom-call(s32[2]{0:T(128)S(1)} %copy-done.2, bf16[12,4992]{1,0:T(8,128)(2,1)S(1)} %copy-done, bf16[768,1920]{1,0:T(8,128)(2,1)S(1)} %project.3.projected_ref, f32[4,3328]{1,0:T(4,128)S(1)} %copy-done.3, f32[1,48]{1,0:T(1,128)S(1)} %bitcast.12, f32[1,48]{1,0:T(1,128)S(1)} %bitcast.14, ...), custom_call_target="tpu_custom_call" | custom-call | flops 754974720 | bytes 5242880 | tf_op jit(solution)/shard_map/scan/pallas_call | solution.py:177
  102.5 5.2 %out_share.3 = (f32[1536,384]{1,0:T(8,128)S(1)}, f32[384,128]{1,0:T(8,128)S(1)}) custom-call(s32[2]{0:T(128)S(1)} %copy-done.2, s32[192]{0:T(256)S(1)} %multiply_add_fusion.places_ref, bf16[768,1536]{1,0:T(8,128)(2,1)S(1)} %fusion.2.tokens_ref, f32[384,1536]{1,0:T(8,128)S(1)} %get-tuple-element.56.scanned_ref, f32[1,3072]{1,0:T(1,128)S(1)} %bitcast.9, ...), custom_call_target="tpu_custom_call" | custom-call | flops 3623878656 | bytes 16777216 | tf_op jit(solution)/shard_map/out_share/pallas_call | solution.py:342
  110.5 5.2 %out_share.2 = (f32[1536,384]{1,0:T(8,128)S(1)}, f32[384,128]{1,0:T(8,128)S(1)}) custom-call(s32[2]{0:T(128)S(1)} %copy-done.2, s32[192]{0:T(256)S(1)} %multiply_add_fusion.places_ref, bf16[768,1536]{1,0:T(8,128)(2,1)S(1)} %fusion.2.tokens_ref, f32[384,1536]{1,0:T(8,128)S(1)} %get-tuple-element.51.scanned_ref, f32[1,3072]{1,0:T(1,128)S(1)} %bitcast.10, ...), custom_call_target="tpu_custom_call" | custom-call | flops 3623878656 | bytes 16777216 | tf_op jit(solution)/shard_map/out_share/pallas_call | solution.py:342
  115.7 2.2 %mix.1 = bf16[384,1536]{1,0:T(8,128)(2,1)} custom-call(bf16[12,4992]{1,0:T(8,128)(2,1)S(1)} %copy-done, f32[1536,384]{1,0:T(8,128)S(1)} %get-tuple-element.55.mine_ref, f32[1536,384]{1,0:T(8,128)S(1)} %collective-permute-done.24.other_ref, f32[384,128]{1,0:T(8,128)S(1)} %get-tuple-element.58.sq_mine, f32[384,128]{1,0:T(8,128)S(1)} %collective-permute-done.25.sq_other, ...), custom_call_target="tpu_custom_call" | custom-call | flops 452984832 | bytes 8388608 | tf_op jit(solution)/shard_map/mix/pallas_call | solution.py:384
  (76 shorter events, 19.3 us)
Async XLA Ops:
  6.8 9.1 %collective-permute-start.13 = (bf16[8,4992]{1,0:T(8,128)(2,1)S(1)}, bf16[8,4992]{1,0:T(8,128)(2,1)S(1)}, u32[]{:S(2)}, u32[]{:S(2)}) collective-permute-start(bf16[8,4992]{1,0:T(8,128)(2,1)S(1)} %get-tuple-element.66), channel_id=1, source_target_pairs={{0,32},{1,33},{2,34},{3,35},{4,36},{5,37},{6,38},{7,39},{8,40},{9,... | collective-permute-start | bytes 239624 | tf_op jit(solution)/shard_map/ppermute | solution.py:413
  10.8 5.3 %collective-permute-start.8 = (bf16[8,4992]{1,0:T(8,128)(2,1)S(1)}, bf16[8,4992]{1,0:T(8,128)(2,1)S(1)}, u32[]{:S(2)}, u32[]{:S(2)}) collective-permute-start(bf16[8,4992]{1,0:T(8,128)(2,1)S(1)} %get-tuple-element.67), channel_id=1, source_target_pairs={{0,1},{1,0},{2,3},{3,2},{4,5},{5,4},{6,7},{7,6},{8,9},{9,8},{10,11... | collective-permute-start | bytes 239624 | tf_op jit(solution)/shard_map/ppermute | solution.py:413
  16.0 5.7 %collective-permute-start.14 = (bf16[16,4992]{1,0:T(8,128)(2,1)S(1)}, bf16[16,4992]{1,0:T(8,128)(2,1)S(1)}, u32[]{:S(2)}, u32[]{:S(2)}) collective-permute-start(bf16[16,4992]{1,0:T(8,128)(2,1)S(1)} %pad_maximum_fusion.9), channel_id=1, source_target_pairs={{0,1},{1,0},{2,3},{3,2},{4,5},{5,4},{6,7},{7,6},{8,9},{9,8},{10,11... | collective-permute-start | bytes 479240 | tf_op jit(solution)/shard_map/ppermute | solution.py:413
  16.1 5.7 %collective-permute-start.9 = (bf16[16,4992]{1,0:T(8,128)(2,1)S(1)}, bf16[16,4992]{1,0:T(8,128)(2,1)S(1)}, u32[]{:S(2)}, u32[]{:S(2)}) collective-permute-start(bf16[16,4992]{1,0:T(8,128)(2,1)S(1)} %pad_maximum_fusion.8), channel_id=1, source_target_pairs={{0,4},{1,5},{2,6},{3,7},{4,0},{5,1},{6,2},{7,3},{8,12},{9,13},{10,... | collective-permute-start | bytes 479240 | tf_op jit(solution)/shard_map/ppermute | solution.py:413
  18.0 4.5 %collective-permute-start.2 = (bf16[16,4992]{1,0:T(8,128)(2,1)S(1)}, bf16[16,4992]{1,0:T(8,128)(2,1)S(1)}, u32[]{:S(2)}, u32[]{:S(2)}) collective-permute-start(bf16[16,4992]{1,0:T(8,128)(2,1)S(1)} %pad_maximum_fusion.7), channel_id=1, source_target_pairs={{0,96},{1,97},{2,98},{3,99},{4,100},{5,101},{6,102},{7,103},{8,104... | collective-permute-start | bytes 479240 | tf_op jit(solution)/shard_map/ppermute | solution.py:413
  21.7 7.4 %collective-permute-start.15 = (bf16[32,4992]{1,0:T(8,128)(2,1)S(1)}, bf16[32,4992]{1,0:T(8,128)(2,1)S(1)}, u32[]{:S(2)}, u32[]{:S(2)}) collective-permute-start(bf16[32,4992]{1,0:T(8,128)(2,1)S(1)} %pad_maximum_fusion.6), channel_id=1, source_target_pairs={{0,4},{1,5},{2,6},{3,7},{4,0},{5,1},{6,2},{7,3},{8,12},{9,13},{10,... | collective-permute-start | bytes 958472 | tf_op jit(solution)/shard_map/ppermute | solution.py:413
  21.9 14.9 %collective-permute-start.10 = (bf16[32,4992]{1,0:T(8,128)(2,1)S(1)}, bf16[32,4992]{1,0:T(8,128)(2,1)}, u32[]{:S(2)}, u32[]{:S(2)}) collective-permute-start(bf16[32,4992]{1,0:T(8,128)(2,1)S(1)} %pad_maximum_fusion.5), channel_id=1, source_target_pairs={{0,96},{1,97},{2,98},{3,99},{4,100},{5,101},{6,102},{7,103},{8,104... | collective-permute-start | bytes 958472 | tf_op jit(solution)/shard_map/ppermute | solution.py:413
  22.5 6.7 %collective-permute-start.3 = (bf16[32,4992]{1,0:T(8,128)(2,1)S(1)}, bf16[32,4992]{1,0:T(8,128)(2,1)S(1)}, u32[]{:S(2)}, u32[]{:S(2)}) collective-permute-start(bf16[32,4992]{1,0:T(8,128)(2,1)S(1)} %pad_maximum_fusion.4), channel_id=1, source_target_pairs={{0,3},{1,2},{2,1},{3,0},{4,7},{5,6},{6,5},{7,4},{8,11},{9,10},{10,... | collective-permute-start | bytes 958472 | tf_op jit(solution)/shard_map/ppermute | solution.py:413
  29.3 17.3 %collective-permute-start.16 = (bf16[64,4992]{1,0:T(8,128)(2,1)S(1)}, bf16[64,4992]{1,0:T(8,128)(2,1)}, u32[]{:S(2)}, u32[]{:S(2)}) collective-permute-start(bf16[64,4992]{1,0:T(8,128)(2,1)S(1)} %pad_maximum_fusion.3.held_ref), channel_id=1, source_target_pairs={{0,96},{1,97},{2,98},{3,99},{4,100},{5,101},{6,102},{7,103},{8,104... | collective-permute-start | bytes 1916936 | tf_op jit(solution)/shard_map/ppermute | solution.py:413
  32.2 18.2 %collective-permute-start.6 = (bf16[384,1536]{1,0:T(8,128)(2,1)}, bf16[384,1536]{1,0:T(8,128)(2,1)}, u32[]{:S(2)}, u32[]{:S(2)}) collective-permute-start(bf16[384,1536]{1,0:T(8,128)(2,1)} %dynamic-slice_bitcast_fusion), channel_id=1, source_target_pairs={{0,16},{1,17},{2,18},{3,19},{4,20},{5,21},{6,22},{7,23},{8,24},{9,... | collective-permute-start | bytes 3538952 | tf_op jit(solution)/shard_map/ppermute | solution.py:413
  36.5 9.7 %collective-permute-start.4 = (bf16[64,4992]{1,0:T(8,128)(2,1)S(1)}, bf16[64,4992]{1,0:T(8,128)(2,1)S(1)}, u32[]{:S(2)}, u32[]{:S(2)}) collective-permute-start(bf16[64,4992]{1,0:T(8,128)(2,1)S(1)} %pad_maximum_fusion.1.held_ref), channel_id=1, source_target_pairs={{0,12},{1,13},{2,14},{3,15},{4,8},{5,9},{6,10},{7,11},{8,4},{9,5},... | collective-permute-start | bytes 1916936 | tf_op jit(solution)/shard_map/ppermute | solution.py:413
  37.8 10.1 %collective-permute-start.11 = (bf16[64,4992]{1,0:T(8,128)(2,1)S(1)}, bf16[64,4992]{1,0:T(8,128)(2,1)}, u32[]{:S(2)}, u32[]{:S(2)}) collective-permute-start(bf16[64,4992]{1,0:T(8,128)(2,1)S(1)} %pad_maximum_fusion.2.held_ref), channel_id=1, source_target_pairs={{0,3},{1,2},{2,1},{3,0},{4,7},{5,6},{6,5},{7,4},{8,11},{9,10},{10,... | collective-permute-start | bytes 1916936 | tf_op jit(solution)/shard_map/ppermute | solution.py:413
  46.2 17.7 %collective-permute-start.5 = (bf16[128,4992]{1,0:T(8,128)(2,1)S(1)}, bf16[128,4992]{1,0:T(8,128)(2,1)}, u32[]{:S(2)}, u32[]{:S(2)}) collective-permute-start(bf16[128,4992]{1,0:T(8,128)(2,1)S(1)} %join.6.held_ref), channel_id=1, source_target_pairs={{0,32},{1,33},{2,34},{3,35},{4,36},{5,37},{6,38},{7,39},{8,40},{9,... | collective-permute-start | bytes 3833864 | tf_op jit(solution)/shard_map/ppermute | solution.py:413
  47.8 19.6 %collective-permute-start.17 = (bf16[128,4992]{1,0:T(8,128)(2,1)S(1)}, bf16[128,4992]{1,0:T(8,128)(2,1)S(1)}, u32[]{:S(2)}, u32[]{:S(2)}) collective-permute-start(bf16[128,4992]{1,0:T(8,128)(2,1)S(1)} %join.10.held_ref), channel_id=1, source_target_pairs={{0,3},{1,2},{2,1},{3,0},{4,7},{5,6},{6,5},{7,4},{8,11},{9,10},{10,... | collective-permute-start | bytes 3833864 | tf_op jit(solution)/shard_map/ppermute | solution.py:413
  49.1 18.8 %collective-permute-start.12 = (bf16[128,4992]{1,0:T(8,128)(2,1)S(1)}, bf16[128,4992]{1,0:T(8,128)(2,1)S(1)}, u32[]{:S(2)}, u32[]{:S(2)}) collective-permute-start(bf16[128,4992]{1,0:T(8,128)(2,1)S(1)} %join.8.held_ref), channel_id=1, source_target_pairs={{0,12},{1,13},{2,14},{3,15},{4,8},{5,9},{6,10},{7,11},{8,4},{9,5},... | collective-permute-start | bytes 3833864 | tf_op jit(solution)/shard_map/ppermute | solution.py:413
  65.4 14.5 %collective-permute-start.7 = (bf16[256,1920]{1,0:T(8,128)(2,1)S(1)}, bf16[256,1920]{1,0:T(8,128)(2,1)S(1)}, u32[]{:S(2)}, u32[]{:S(2)}) collective-permute-start(bf16[256,1920]{1,0:T(8,128)(2,1)S(1)} %get-tuple-element.41.refs_0_), channel_id=1, source_target_pairs={{0,1},{1,0},{2,3},{3,2},{4,5},{5,4},{6,7},{7,6},{8,9},{9,8},{10,11... | collective-permute-start | bytes 2949128 | tf_op jit(solution)/shard_map/ppermute | solution.py:413
  67.6 14.6 %collective-permute-start.19 = (bf16[256,1920]{1,0:T(8,128)(2,1)S(1)}, bf16[256,1920]{1,0:T(8,128)(2,1)S(1)}, u32[]{:S(2)}, u32[]{:S(2)}) collective-permute-start(bf16[256,1920]{1,0:T(8,128)(2,1)S(1)} %get-tuple-element.43.refs_2_), channel_id=1, source_target_pairs={{0,12},{1,13},{2,14},{3,15},{4,8},{5,9},{6,10},{7,11},{8,4},{9,5},... | collective-permute-start | bytes 2949128 | tf_op jit(solution)/shard_map/ppermute | solution.py:413
  68.1 14.5 %collective-permute-start.18 = (bf16[256,1920]{1,0:T(8,128)(2,1)S(1)}, bf16[256,1920]{1,0:T(8,128)(2,1)S(1)}, u32[]{:S(2)}, u32[]{:S(2)}) collective-permute-start(bf16[256,1920]{1,0:T(8,128)(2,1)S(1)} %get-tuple-element.42.refs_1_), channel_id=1, source_target_pairs={{0,32},{1,33},{2,34},{3,35},{4,36},{5,37},{6,38},{7,39},{8,40},{9,... | collective-permute-start | bytes 2949128 | tf_op jit(solution)/shard_map/ppermute | solution.py:413
  69.4 33.1 %collective-permute-start.23 = (bf16[256,3072]{1,0:T(8,128)(2,1)S(1)}, bf16[256,3072]{1,0:T(8,128)(2,1)S(1)}, u32[]{:S(2)}, u32[]{:S(2)}) collective-permute-start(bf16[256,3072]{1,0:T(8,128)(2,1)S(1)} %get-tuple-element.54.refs_4_), channel_id=1, source_target_pairs={{0,12},{1,13},{2,14},{3,15},{4,8},{5,9},{6,10},{7,11},{8,4},{9,5},... | collective-permute-start | bytes 4718600 | tf_op jit(solution)/shard_map/ppermute | solution.py:413
  70.4 32.1 %collective-permute-start.22 = (bf16[256,3072]{1,0:T(8,128)(2,1)S(1)}, bf16[256,3072]{1,0:T(8,128)(2,1)S(1)}, u32[]{:S(2)}, u32[]{:S(2)}) collective-permute-start(bf16[256,3072]{1,0:T(8,128)(2,1)S(1)} %get-tuple-element.53.refs_2_), channel_id=1, source_target_pairs={{0,32},{1,33},{2,34},{3,35},{4,36},{5,37},{6,38},{7,39},{8,40},{9,... | collective-permute-start | bytes 4718600 | tf_op jit(solution)/shard_map/ppermute | solution.py:413
  80.0 22.5 %collective-permute-start.21 = (bf16[256,3072]{1,0:T(8,128)(2,1)S(1)}, bf16[256,3072]{1,0:T(8,128)(2,1)S(1)}, u32[]{:S(2)}, u32[]{:S(2)}) collective-permute-start(bf16[256,3072]{1,0:T(8,128)(2,1)S(1)} %get-tuple-element.52.refs_0_), channel_id=1, source_target_pairs={{0,1},{1,0},{2,3},{3,2},{4,5},{5,4},{6,7},{7,6},{8,9},{9,8},{10,11... | collective-permute-start | bytes 4718600 | tf_op jit(solution)/shard_map/ppermute | solution.py:413
  92.0 10.4 %collective-permute-start.20 = (f32[1536,128]{1,0:T(8,128)S(1)}, f32[1536,128]{1,0:T(8,128)S(1)}, u32[]{:S(2)}, u32[]{:S(2)}) collective-permute-start(f32[1536,128]{1,0:T(8,128)S(1)} %get-tuple-element.50), channel_id=1, source_target_pairs={{0,16},{1,17},{2,18},{3,19},{4,20},{5,21},{6,22},{7,23},{8,24},{9,... | collective-permute-start | bytes 2359304 | tf_op jit(solution)/shard_map/ppermute | solution.py:413
  107.7 8.0 %collective-permute-start.24 = (f32[1536,384]{1,0:T(8,128)S(1)}, f32[1536,384]{1,0:T(8,128)S(1)}, u32[]{:S(2)}, u32[]{:S(2)}) collective-permute-start(f32[1536,384]{1,0:T(8,128)S(1)} %get-tuple-element.57), channel_id=1, source_target_pairs={{0,16},{1,17},{2,18},{3,19},{4,20},{5,21},{6,22},{7,23},{8,24},{9,... | collective-permute-start | bytes 7077896 | tf_op jit(solution)/shard_map/ppermute | solution.py:413
  110.5 5.2 %collective-permute-start.25 = (f32[384,128]{1,0:T(8,128)S(1)}, f32[384,128]{1,0:T(8,128)S(1)}, u32[]{:S(2)}, u32[]{:S(2)}) collective-permute-start(f32[384,128]{1,0:T(8,128)S(1)} %get-tuple-element.59), channel_id=1, source_target_pairs={{0,16},{1,17},{2,18},{3,19},{4,20},{5,21},{6,22},{7,23},{8,24},{9,... | collective-permute-start | bytes 589832 | tf_op jit(solution)/shard_map/ppermute | solution.py:413
  (9 other events, 57.6 us)
